TPU v7x, 32 devices: a whole 2x2x4 slice. The times are simulated.
32 devices in a mesh: slab: 4 (over x, core), view: 8 (over z, y).
Axes of the slice: x: 2, y: 2, z: 4, core: 2. Of those that a mesh axis runs over, the one named last changes fastest.
Arguments:
- volume: float32 [64, 4, 4096], P('slab'), may hold values from 0 to 2
- sinogram: float32 [16, 64, 4096], P('view', 'slab'), may hold values from -8 to 81928
- curvature: float32 [64, 4, 4096], P('slab'), may hold values from 0.003 to 3
- angles: int32 [16], P('view'), may hold values from 0 to 1151
- offsets: int32 [16, 4], P('view'), may hold values from 0 to 48, as said below
Outputs:
- updated: float32 [64, 4, 4096], P('slab')
Inputs may be any that keep to these rules, and one draw needn't show every extreme that they name: `offsets`: in each view the band of slab k starts within 8 rows of ((k + s) mod the number of slabs) * 16, where s, fixed for the view, is 0 or half the number of slabs.
All inputs are finite; a program needn't handle non-finite values.
Results may differ from a plain program's by a relative error of at most 0.0003.
Values sent between devices are 32-bit elements; how exact they have to be, the bound alone decides.
No kernel may reach another device: no remote copies, remote signals or barrier semaphores. Data moves between devices by JAX's collectives and lax.ppermute only.
A program may use at most 64 MiB of HBM per device.

v0:
```python
import math

import jax
import jax.numpy as jnp
from jax import lax
from jax.sharding import PartitionSpec as P

ROTATION_VIEWS = 1152


huber_delta = 0.5
tv_weight = 4.0
step_limit = 1.0
detector_scale = 0.7
epsilon = 1e-06


def padded_2(cells, sides, width):
    for axis, dim in sides:
        count = lax.axis_size(axis)
        ends = count - 1
        head = lax.slice_in_dim(cells, 0, width, axis=dim)
        tail = lax.slice_in_dim(cells, cells.shape[dim] - width, cells.shape[dim], axis=dim)
        cells = jnp.concatenate(
            [
                lax.ppermute(tail, axis, [(i, (i + 1) % count) for i in range(ends)]),
                cells,
                lax.ppermute(head, axis, [((i + 1) % count, i) for i in range(ends)]),
            ],
            axis=dim,
        )
    return cells


def geometry(angle_index, rows_n, cols_n, bins_n):
    angle_rad = angle_index.astype(jnp.float32) * (2.0 * math.pi / ROTATION_VIEWS)
    across = jnp.arange(cols_n, dtype=jnp.float32) - 0.5 * cols_n + 0.5
    along = jnp.arange(rows_n, dtype=jnp.float32) - 0.5 * rows_n + 0.5
    coord = (
        detector_scale
        * (across[None, :] * jnp.cos(angle_rad) + along[:, None] * jnp.sin(angle_rad))
        + 0.5 * bins_n
        - 0.5
    )
    coord = coord.reshape(-1)
    lower = jnp.floor(coord)
    return (lower.astype(jnp.int32), coord - lower)


def project(slices_flat, bin_index, bin_frac, bins_n):
    summed = jnp.zeros((slices_flat.shape[0], bins_n), jnp.float32)
    summed = summed.at[:, bin_index].add(slices_flat * (1.0 - bin_frac))
    return summed.at[:, bin_index + 1].add(slices_flat * bin_frac)


def backproject(det_rows, bin_index, bin_frac):
    return det_rows[:, bin_index] * (1.0 - bin_frac) + det_rows[:, bin_index + 1] * bin_frac


def slope(diff):
    return jnp.clip(diff / huber_delta, -1.0, 1.0)


def tv_padded(padded):
    centre = padded[1:-1, 1:-1, 1:-1]
    result = slope(centre - padded[:-2, 1:-1, 1:-1]) - slope(padded[2:, 1:-1, 1:-1] - centre)
    result = (
        result + slope(centre - padded[1:-1, :-2, 1:-1]) - slope(padded[1:-1, 2:, 1:-1] - centre)
    )
    result = (
        result + slope(centre - padded[1:-1, 1:-1, :-2]) - slope(padded[1:-1, 1:-1, 2:] - centre)
    )
    return result


def local(volume, sinogram, curvature, angles, offsets):
    slices_n, rows_n, cols_n = volume.shape
    bins_n = sinogram.shape[2]
    pixels_n = rows_n * cols_n
    slab_count = lax.axis_size("slab")
    all_rows = sinogram.shape[1] * slab_count
    slab_pos = lax.axis_index("slab")
    flattened = volume.reshape(slices_n, pixels_n)
    geometries = []
    bands = []
    projections = []
    for view_num in range(angles.shape[0]):
        bin_index, bin_frac = geometry(angles[view_num], rows_n, cols_n, bins_n)
        band_start = lax.dynamic_index_in_dim(offsets[view_num], slab_pos, 0, keepdims=False)
        projected = project(flattened, bin_index, bin_frac, bins_n)
        detector = lax.dynamic_update_slice(
            jnp.zeros((all_rows, bins_n), jnp.float32), projected, (band_start, jnp.int32(0))
        )
        geometries.append((bin_index, bin_frac))
        bands.append(band_start)
        projections.append(detector)
    stacked = jnp.stack(projections)
    own_rows = lax.psum_scatter(stacked, "slab", scatter_dimension=1, tiled=True)
    residual = lax.all_gather(own_rows - sinogram, "slab", axis=1, tiled=True)
    data_local = jnp.zeros((slices_n, pixels_n), jnp.float32)
    for view_num in range(angles.shape[0]):
        bin_index, bin_frac = geometries[view_num]
        det_band = lax.dynamic_slice(
            residual[view_num], (bands[view_num], jnp.int32(0)), (slices_n, bins_n)
        )
        data_local = data_local + backproject(det_band, bin_index, bin_frac)
    extended = padded_2(volume, (("slab", 0),), 1)
    padded = jnp.pad(extended, ((0, 0), (1, 1), (1, 1)))
    tv_grad = tv_padded(padded).reshape(slices_n, pixels_n)
    curv_flat = curvature.reshape(slices_n, pixels_n)
    voxel_count = slices_n * slab_count * pixels_n
    data_grad = lax.psum(data_local, "view")
    direction = (data_grad + tv_weight * tv_grad) / curv_flat
    squares = lax.psum(jnp.sum(direction * direction), "slab")
    factor = jnp.minimum(1.0, step_limit / jnp.sqrt(squares / voxel_count + epsilon))
    updated = flattened - factor * direction
    return updated.reshape(slices_n, rows_n, cols_n)


def solution(mesh):
    in_specs = (
        P("slab", None, None),
        P("view", "slab", None),
        P("slab", None, None),
        P("view"),
        P("view", None),
    )
    out_specs = P("slab", None, None)
    return jax.shard_map(local, mesh=mesh, in_specs=in_specs, out_specs=out_specs, check_vma=False)
```

profile of v0, /device:TPU:0, one launch (start us, length us, event | category | flops | bytes accessed | tf_op | source)
XLA Modules:
  0.0 864.2 jit_solution(14174823234276909082)
XLA Ops:
  14.3 1.8 copy.26
  17.5 4.6 copy.14
  22.4 4.6 copy.15
  27.0 88.1 %scatter_custom_fusion = f32[16,4096]{0,1:T(8,128)S(1)} fusion(s32[16384]{0:T(1024)S(1)} %bitcast.63, f32[16384,16]{1,0:T(8,128)} %copy.14, f32[]{:T(128)} %constant.61.clone.1), kind=kCustom, calls=%fused_computation.54 | custom fusion | flops 262144 | bytes 262656 | tf_op jit(solution)/shard_map/scatter-add | solution.py:52
  115.1 88.4 %scatter_fusion = f32[16,4096]{0,1:T(8,128)S(1)} fusion(f32[16,4096]{0,1:T(8,128)S(1)} %scatter_custom_fusion, s32[16384]{0:T(1024)S(1)} %bitcast.59, f32[16384,16]{1,0:T(8,128)} %copy.15), kind=kCustom, calls=%fused_computation.5 | custom fusion | flops 262144 | bytes 3211264 | tf_op jit(solution)/shard_map/scatter-add | solution.py:53
  204.1 6.0 copy.17
  211.0 4.6 copy.18
  215.6 88.2 %scatter_custom_fusion.2 = f32[16,4096]{0,1:T(8,128)S(1)} fusion(s32[16384]{0:T(1024)} %bitcast.65, f32[16384,16]{1,0:T(8,128)} %copy.17, f32[]{:T(128)} %constant.61.clone.1), kind=kCustom, calls=%fused_computation.52 | custom fusion | flops 262144 | bytes 262656 | tf_op jit(solution)/shard_map/scatter-add | solution.py:52
  303.7 88.6 %scatter_fusion.1 = f32[16,4096]{0,1:T(8,128)S(1)} fusion(f32[16,4096]{0,1:T(8,128)S(1)} %scatter_custom_fusion.2, s32[16384]{0:T(1024)} %bitcast.61, f32[16384,16]{1,0:T(8,128)} %copy.18), kind=kCustom, calls=%fused_computation.7 | custom fusion | flops 262144 | bytes 3211264 | tf_op jit(solution)/shard_map/scatter-add | solution.py:53
  395.1 1.5 pad_maximum_fusion
  396.7 86.4 %reduce-scatter.2.cloned.1.call-done = f32[2,16,4096]{2,1,0:T(8,128)} async-done(((f32[2,64,4096]{2,1,0:T(8,128)}), f32[2,16,4096]{2,1,0:T(8,128)}) %reduce-scatter.2.cloned.1.call-update) | async-done | bytes 524304 | tf_op jit(solution)/shard_map/reduce_scatter | solution.py:98
  483.1 2.1 sub.94
  485.9 2.3 collective-permute-start
  489.5 1.7 copy.32
  493.7 14.2 %all-gather.2.cloned.1.call-done = f32[2,64,4096]{2,1,0:T(8,128)} async-done(((f32[2,16,4096]{2,1,0:T(8,128)}), f32[2,64,4096]{2,1,0:T(8,128)}) %all-gather.2.cloned.1.call-update) | async-done | bytes 2097168 | tf_op jit(solution)/shard_map/all_gather | solution.py:99
  507.9 2.7 fusion.33
  511.2 59.6 %gather_fusion = f32[16384,16]{1,0:T(8,128)} fusion(f32[16,4096]{0,1:T(8,128)S(1)} %bitcast.46, s32[16384]{0:T(1024)} %broadcast_clamp_fusion.3), kind=kCustom, calls=%fused_computation | custom fusion | bytes 2162688 | tf_op jit(solution)/shard_map/gather | solution.py:57
  570.9 6.0 copy.21
  576.9 54.4 %gather_fusion.1 = f32[16384,16]{1,0:T(8,128)} fusion(f32[16,4096]{0,1:T(8,128)S(1)} %bitcast.47, s32[16384]{0:T(1024)S(1)} %copy-done.15), kind=kCustom, calls=%fused_computation.1 | custom fusion | bytes 2162688 | tf_op jit(solution)/shard_map/gather | solution.py:57
  631.3 6.0 copy.22
  638.9 59.6 %gather_fusion.2 = f32[16384,16]{1,0:T(8,128)} fusion(f32[16,4096]{0,1:T(8,128)S(1)} %bitcast.48, s32[16384]{0:T(1024)} %broadcast_clamp_fusion.1), kind=kCustom, calls=%fused_computation.2 | custom fusion | bytes 2162688 | tf_op jit(solution)/shard_map/gather | solution.py:57
  698.5 6.0 copy.24
  704.5 54.4 %gather_fusion.3 = f32[16384,16]{1,0:T(8,128)} fusion(f32[16,4096]{0,1:T(8,128)S(1)} %bitcast.49, s32[16384]{0:T(1024)S(1)} %copy-done.14), kind=kCustom, calls=%fused_computation.3 | custom fusion | bytes 2162688 | tf_op jit(solution)/shard_map/gather | solution.py:57
  759.0 6.1 copy.25
  765.1 2.9 add_bitcast_fusion
  768.0 1.6 select_maximum_fusion
  769.6 3.4 fusion.6
  773.0 1.6 copy.31
  774.6 71.5 %all-reduce.3.cloned.1.call-done = f32[16,16384]{1,0:T(8,128)} async-done(((f32[16,16384]{1,0:T(8,128)}), f32[16,16384]{1,0:T(8,128)}) %all-reduce.3.cloned.1.call-update) | async-done | bytes 1048592 | tf_op jit(solution)/shard_map/psum | solution.py:112
  846.1 2.4 multiply_reduce_fusion
  848.6 6.6 psum.15
  856.0 1.7 reshape.238
  (82 shorter events, 14.9 us)
Async XLA Ops:
  6.5 476.6 %reduce-scatter.2.cloned.1.call-start = ((), (), s32[]{:S(2)}) async-start(), calls=%async_computation.1 | async-start | bytes 2621440 | tf_op jit(solution)/shard_map/reduce_scatter | solution.py:98
  16.2 1.4 copy-start.1
  16.2 1.3 copy-start.7
  16.2 1.3 copy-start.9
  22.4 4.6 copy-start.16
  22.4 92.8 %copy-start.11 = (s32[16384,1]{0,1:T(1,128)}, s32[16384,1]{0,1:T(1,128)S(1)}, u32[]{:S(2)}) copy-start(s32[16384,1]{0,1:T(1,128)S(1)} %get-tuple-element.17) | copy-start | bytes 196612
  204.1 6.0 copy-start.19
  396.6 88.7 %copy-start = (f32[16,4,4096]{2,1,0:T(4,128)S(1)}, f32[16,4,4096]{2,1,0:T(4,128)}, u32[]{:S(2)}) copy-start(f32[16,4,4096]{2,1,0:T(4,128)} %param.5) | copy-start | bytes 3145732
  396.6 92.9 %copy-start.6 = (f32[16,4,4096]{2,1,0:T(4,128)S(1)}, f32[16,4,4096]{2,1,0:T(4,128)}, u32[]{:S(2)}) copy-start(f32[16,4,4096]{2,1,0:T(4,128)} %param.7) | copy-start | bytes 3145732
  396.6 94.6 %copy-start.17 = (s32[16384,1]{0,1:T(1,128)S(1)}, s32[16384,1]{0,1:T(1,128)}, u32[]{:S(2)}) copy-start(s32[16384,1]{0,1:T(1,128)} %copy-done.16) | copy-start | bytes 196612
  396.6 95.2 %copy-start.12 = (s32[16384,1]{0,1:T(1,128)S(1)}, s32[16384,1]{0,1:T(1,128)}, u32[]{:S(2)}) copy-start(s32[16384,1]{0,1:T(1,128)} %copy-done.11) | copy-start | bytes 196612
  396.6 95.8 %copy-start.18 = (s32[16384,1]{0,1:T(1,128)S(1)}, s32[16384,1]{0,1:T(1,128)}, u32[]{:S(2)}) copy-start(s32[16384,1]{0,1:T(1,128)} %get-tuple-element.22) | copy-start | bytes 196612
  396.6 96.5 %copy-start.13 = (s32[16384,1]{0,1:T(1,128)S(1)}, s32[16384,1]{0,1:T(1,128)}, u32[]{:S(2)}) copy-start(s32[16384,1]{0,1:T(1,128)} %get-tuple-element.21) | copy-start | bytes 196612
  396.6 111.3 %all-gather.2.cloned.1.call-start = ((), (), s32[]{:S(2)}) async-start(), calls=%async_computation.2 | async-start | bytes 2621440 | tf_op jit(solution)/shard_map/all_gather | solution.py:99
  485.2 361.0 %all-reduce.3.cloned.1.call-start = ((), (), s32[]{:S(2)}) async-start(), calls=%async_computation.3 | async-start | bytes 2097152 | tf_op jit(solution)/shard_map/psum | solution.py:112
  485.9 282.1 %collective-permute-start = (f32[1,4,4096]{2,1,0:T(4,128)}, f32[1,4,4096]{2,1,0:T(4,128)}, u32[]{:S(2)}, u32[]{:S(2)}) collective-permute-start(f32[1,4,4096]{2,1,0:T(4,128)} %get-tuple-element.9), channel_id=1, source_target_pairs={{0,8},{8,16},{16,24},{1,9},{9,17},{17,25},{2,10},{10,18},{18,26},{... | collective-permute-start | bytes 196616 | tf_op jit(solution)/shard_map/ppermute | solution.py:26
  488.2 279.8 %collective-permute-start.1 = (f32[1,4,4096]{2,1,0:T(4,128)}, f32[1,4,4096]{2,1,0:T(4,128)}, u32[]{:S(2)}, u32[]{:S(2)}) collective-permute-start(f32[1,4,4096]{2,1,0:T(4,128)} %get-tuple-element.10), channel_id=1, source_target_pairs={{8,0},{16,8},{24,16},{9,1},{17,9},{25,17},{10,2},{18,10},{26,18},{... | collective-permute-start | bytes 196616 | tf_op jit(solution)/shard_map/ppermute | solution.py:28
  570.8 6.0 copy-start.15
  698.5 6.0 copy-start.14
  759.0 6.2 copy-start.4
  759.0 6.2 copy-start.5
  759.0 6.2 copy-start.8
  759.0 6.2 copy-start.10
  773.0 73.1 %copy-start.3 = (f32[2,8,4,4096]{3,1,2,0:T(8,128)S(1)}, f32[2,8,4,4096]{3,1,2,0:T(8,128)}, u32[]{:S(2)}) copy-start(f32[2,8,4,4096]{3,1,2,0:T(8,128)} %copy.32) | copy-start | bytes 3145732
  774.6 81.3 %copy-start.2 = (f32[2,8,4,4096]{3,1,2,0:T(8,128)S(1)}, f32[2,8,4,4096]{3,1,2,0:T(8,128)}, u32[]{:S(2)}) copy-start(f32[2,8,4,4096]{3,1,2,0:T(8,128)} %copy-done.1) | copy-start | bytes 3145732
Sparse Core Ops, SparseCore 0:
  396.7 86.3 reduce-scatter.1
  485.3 22.5 all-gather.1
  768.1 77.9 all-reduce.2
where the time goes:
time: 862 us; the launch traced here: 864 us
  other arithmetic  373 us (43%)
  local copies, waits for them, and re-layouts  289 us (34%)
  waiting for transfers between devices  172 us (20%)
  between operations  19.6 us (2%)
    scatter-add x2, other arithmetic, project(): return summed.at[:, bin_index + 1].add(slices_flat * bin_frac)  177 us
    scatter-add x2, other arithmetic, project(): summed = summed.at[:, bin_index].add(slices_flat * (1.0 - bin_frac))  176 us
    gather x4, local copies, waits for them, and re-layouts, backproject(): det_rows[:, bin_index] * (1.0 - bin_frac)  131 us
    gather x4, local copies, waits for them, and re-layouts, backproject(): det_rows[:, bin_index + 1] * bin_frac  121 us
    reduce_scatter x1, waiting for transfers between devices, local(): lax.psum_scatter(stacked, 'slab', scatter_dimension=1, tiled=True)  86.4 us
    psum x1, waiting for transfers between devices, local(): data_grad = lax.psum(data_local, 'view')  71.5 us
  transfers between devices with their start and end apart: 5, of which 3 were waited for; matrix products, arithmetic and copies ran while one was open for 31% of the time, Pallas kernels for 0%

commit v1 on v0

v1 whole, which is shorter than its diff:
```python
import math
import jax
import jax.numpy as jnp
from jax import lax
from jax.experimental import pallas as pl
from jax.experimental.pallas import tpu as pltpu
from jax.sharding import PartitionSpec as P

ROTATION_VIEWS = 1152


huber_delta = 0.5
tv_weight = 4.0
step_limit = 1.0
epsilon = 1e-06
scale = 0.7
LANES = 128
GROUP = 8


def coordinate(across, along, cos, sin, bins_n):
    return scale * (across * cos + along * sin) + 0.5 * bins_n - 0.5


def window_of(start, cos, sin, along, cols_n, bins_n, base):
    first = coordinate(start - 0.5 * cols_n + 0.5, along, cos, sin, bins_n)
    last = coordinate(start + (LANES - 1.0) - 0.5 * cols_n + 0.5, along, cos, sin, bins_n)
    return jnp.minimum(first, last).astype(jnp.int32) - (base + 1)


def project_kernel(cols_n, rows_n, bins_n, base, blocks_n, views_n, trig_ref, vol_ref, out_ref, rows_ref, acc_ref, sem):
    copies = [pltpu.make_async_copy(vol_ref.at[:, i, :], rows_ref.at[i], sem.at[i]) for i in range(rows_n)]
    for c in copies:
        c.start()
    acc_ref[...] = jnp.zeros_like(acc_ref)
    lane8 = lax.broadcasted_iota(jnp.int32, (8, LANES), 1)
    lane = lax.broadcasted_iota(jnp.int32, (16, LANES), 1)
    sub = lax.broadcasted_iota(jnp.int32, (LANES, LANES), 0).astype(jnp.float32).astype(jnp.bfloat16)
    zero = jnp.zeros((LANES, LANES), jnp.bfloat16)

    def tall(x):
        return jnp.concatenate([jnp.concatenate([x, x], 0).astype(jnp.bfloat16)] * (LANES // 16), 0)

    for row in range(rows_n):
        copies[row].wait()
        along = row - 0.5 * rows_n + 0.5

        def step(g, _):
            outs = []
            for u in range(GROUP):
                block = g * GROUP + u
                start = (block * LANES).astype(jnp.float32)
                vals = rows_ref[row, :, pl.ds(pl.multiple_of(block * LANES, LANES), LANES)]
                high = vals.astype(jnp.bfloat16)
                rest = vals - high.astype(jnp.float32)
                mid = rest.astype(jnp.bfloat16)
                low = (rest - mid.astype(jnp.float32)).astype(jnp.bfloat16)
                terms = jnp.concatenate([high, mid, low], 0)
                mats = []
                wins = []
                for v in range(views_n):
                    cos = trig_ref[v]
                    sin = trig_ref[views_n + v]
                    across = (lane8 + block * LANES).astype(jnp.float32) - 0.5 * cols_n + 0.5
                    coord = coordinate(across, along, cos, sin, bins_n)
                    lower = jnp.floor(coord)
                    frac = coord - lower
                    rel = lower - float(base)
                    bm = rel - LANES * jnp.floor(rel * (1.0 / LANES))
                    bn = jnp.where(bm == LANES - 1.0, 0.0, bm + 1.0)
                    fh = jnp.floor(frac * 128.0) * (1.0 / 128.0)
                    fl = frac - fh
                    here = sub == tall(bm)
                    next_ = sub == tall(bn)
                    wh = jnp.where(here, tall(1.0 - fh), jnp.where(next_, tall(fh), zero))
                    wl = jnp.where(here, tall(-fl), jnp.where(next_, tall(fl), zero))
                    mats.append(jnp.concatenate([wh, wl], 1))
                    wins.append(window_of(start, cos, sin, along, cols_n, bins_n, base))
                weights = jnp.concatenate(mats, 0)
                both = jnp.concatenate([terms, terms], 1)
                prod = lax.dot_general(both, weights, (((1,), (1,)), ((), ())), preferred_element_type=jnp.float32)
                outs.append((prod[0:16] + prod[16:32] + prod[32:48], wins))
            for summed, wins in outs:
                for v in range(views_n):
                    first = wins[v]
                    k = first >> 7
                    own = lane >= (first & (LANES - 1))
                    part = summed[:, v * LANES:(v + 1) * LANES]
                    acc_ref[v, k] += jnp.where(own, part, 0.0)
                    acc_ref[v, k + 1] += jnp.where(own, 0.0, part)
            return 0

        lax.fori_loop(0, cols_n // LANES // GROUP, step, 0)
    out_ref[...] = acc_ref[:, :blocks_n]


def project(trig, volume, bins_n, base, blocks_n, views_n):
    slices_n, rows_n, cols_n = volume.shape
    body = lambda *refs: project_kernel(cols_n, rows_n, bins_n, base, blocks_n, views_n, *refs)
    return pl.pallas_call(
        body,
        out_shape=jax.ShapeDtypeStruct((views_n, blocks_n, slices_n, LANES), jnp.float32),
        in_specs=[pl.BlockSpec(memory_space=pltpu.SMEM), pl.BlockSpec(memory_space=pl.ANY)],
        out_specs=pl.BlockSpec(memory_space=pltpu.VMEM),
        scratch_shapes=[
            pltpu.VMEM((rows_n, slices_n, cols_n), jnp.float32),
            pltpu.VMEM((views_n, blocks_n + 1, slices_n, LANES), jnp.float32),
            pltpu.SemaphoreType.DMA((rows_n,)),
        ],
        name="project",
    )(trig, volume)


def backproject_kernel(cols_n, rows_n, bins_n, base, views_n, width, per_n, trig_ref, starts_ref, res_ref, out_ref):
    lane16 = lax.broadcasted_iota(jnp.int32, (16, LANES), 1)
    pixel0 = starts_ref[views_n]

    def row_step(row, _):
        along = row.astype(jnp.float32) - 0.5 * rows_n + 0.5

        def step(u, _):
            column = pixel0 + u * LANES
            start = column.astype(jnp.float32)
            across = (lane16 + column).astype(jnp.float32) - 0.5 * cols_n + 0.5
            total = jnp.zeros((16, LANES), jnp.float32)
            for v in range(views_n):
                cos = trig_ref[v]
                sin = trig_ref[views_n + v]
                coord = coordinate(across, along, cos, sin, bins_n)
                lower = jnp.floor(coord)
                frac = coord - lower
                offset = starts_ref[v]
                rel = lower.astype(jnp.int32) - (base + offset)
                here = rel & (LANES - 1)
                next_ = (rel + 1) & (LANES - 1)
                first = window_of(start, cos, sin, along, cols_n, bins_n, base) - offset
                k = first >> 7
                left = res_ref[v, k]
                right = res_ref[v, jnp.minimum(k + 1, width - 1)]
                band = jnp.where(lane16 >= (first & (LANES - 1)), left, right)
                a = jnp.take_along_axis(band, here, axis=1, mode="promise_in_bounds")
                b = jnp.take_along_axis(band, next_, axis=1, mode="promise_in_bounds")
                total = total + (a * (1.0 - frac) + b * frac)
            out_ref[row, :, pl.ds(pl.multiple_of(u * LANES, LANES), LANES)] = total
            return 0

        lax.fori_loop(0, per_n // LANES, step, 0)
        return 0

    lax.fori_loop(0, rows_n, row_step, 0)


def backproject(trig, starts, res, rows_n, cols_n, bins_n, base, per_n):
    views_n, width, slices_n, _ = res.shape
    body = lambda *refs: backproject_kernel(cols_n, rows_n, bins_n, base, views_n, width, per_n, *refs)
    return pl.pallas_call(
        body,
        out_shape=jax.ShapeDtypeStruct((rows_n, slices_n, per_n), jnp.float32),
        in_specs=[pl.BlockSpec(memory_space=pltpu.SMEM), pl.BlockSpec(memory_space=pltpu.SMEM), pl.BlockSpec(memory_space=pltpu.VMEM)],
        out_specs=pl.BlockSpec(memory_space=pltpu.VMEM),
        name="backproject",
    )(trig, starts, res)


def padded_2(cells, sides, width):
    for axis, dim in sides:
        count = lax.axis_size(axis)
        ends = count - 1
        head = lax.slice_in_dim(cells, 0, width, axis=dim)
        tail = lax.slice_in_dim(cells, cells.shape[dim] - width, cells.shape[dim], axis=dim)
        cells = jnp.concatenate(
            [
                lax.ppermute(tail, axis, [(i, (i + 1) % count) for i in range(ends)]),
                cells,
                lax.ppermute(head, axis, [((i + 1) % count, i) for i in range(ends)]),
            ],
            axis=dim,
        )
    return cells


def slope(diff):
    return jnp.clip(diff / huber_delta, -1.0, 1.0)


def tv_padded(padded):
    centre = padded[1:-1, 1:-1, 1:-1]
    result = slope(centre - padded[:-2, 1:-1, 1:-1]) - slope(padded[2:, 1:-1, 1:-1] - centre)
    result = (
        result + slope(centre - padded[1:-1, :-2, 1:-1]) - slope(padded[1:-1, 2:, 1:-1] - centre)
    )
    result = (
        result + slope(centre - padded[1:-1, 1:-1, :-2]) - slope(padded[1:-1, 1:-1, 2:] - centre)
    )
    return result


def extent(rows_n, cols_n, bins_n):
    reach = scale * math.hypot(0.5 * (cols_n - 1), 0.5 * (rows_n - 1))
    centre = 0.5 * bins_n - 0.5
    base = (int(centre - reach) - 3) // 8 * 8
    blocks = -(-(int(centre + reach) + 3 - base) // LANES)
    return base, blocks


def local(volume, sinogram, curvature, angles, offsets):
    slices_n, rows_n, cols_n = volume.shape
    views_n = angles.shape[0]
    bins_n = sinogram.shape[2]
    base, blocks = extent(rows_n, cols_n, bins_n)
    pixels_n = rows_n * cols_n
    slab_count = lax.axis_size("slab")
    all_rows = sinogram.shape[1] * slab_count
    slab_pos = lax.axis_index("slab")
    angle_rad = angles.astype(jnp.float32) * (2.0 * math.pi / ROTATION_VIEWS)
    trig = jnp.concatenate([jnp.cos(angle_rad), jnp.sin(angle_rad)])
    proj = project(trig, volume, bins_n, base, blocks, views_n)
    stacked = []
    bands = []
    for v in range(views_n):
        start = lax.dynamic_index_in_dim(offsets[v], slab_pos, 0, keepdims=False)
        flat = proj[v].transpose(1, 0, 2).reshape(slices_n, blocks * LANES)
        stacked.append(
            lax.dynamic_update_slice(
                jnp.zeros((all_rows, blocks * LANES), jnp.float32), flat, (start, jnp.int32(0))
            )
        )
        bands.append(start)
    own = lax.psum_scatter(jnp.stack(stacked), "slab", scatter_dimension=1, tiled=True)
    measured = sinogram[:, :, base : base + blocks * LANES]
    residual = lax.all_gather(own - measured, "slab", axis=1, tiled=True)
    windows = jnp.stack(
        [
            lax.dynamic_slice(
                residual[v], (bands[v], jnp.int32(0)), (slices_n, blocks * LANES)
            )
            .reshape(slices_n, blocks, LANES)
            .transpose(1, 0, 2)
            for v in range(views_n)
        ]
    )
    starts = jnp.zeros((views_n + 1,), jnp.int32)
    data_local = backproject(trig, starts, windows, rows_n, cols_n, bins_n, base, cols_n)
    extended = padded_2(volume, (("slab", 0),), 1)
    padded = jnp.pad(extended, ((0, 0), (1, 1), (1, 1)))
    tv_grad = tv_padded(padded)
    data_grad = lax.psum(data_local, "view").transpose(1, 0, 2)
    direction = (data_grad + tv_weight * tv_grad) / curvature
    squares = lax.psum(jnp.sum(direction * direction), "slab")
    voxel_count = slices_n * slab_count * pixels_n
    factor = jnp.minimum(1.0, step_limit / jnp.sqrt(squares / voxel_count + epsilon))
    return volume - factor * direction


def solution(mesh):
    in_specs = (
        P("slab", None, None),
        P("view", "slab", None),
        P("slab", None, None),
        P("view"),
        P("view", None),
    )
    out_specs = P("slab", None, None)
    return jax.shard_map(local, mesh=mesh, in_specs=in_specs, out_specs=out_specs, check_vma=False)
```

time: 862 us -> 201 us (0.23)
  other arithmetic: 373 us -> 13.9 us
  local copies, waits for them, and re-layouts: 289 us -> 11.5 us
  waiting for transfers between devices: 172 us -> 121 us
  Pallas kernels: 0 us -> 25.3 us
    scatter-add x4 -> x0, other arithmetic: 353 us -> none  [the longest x2 177 us: project(): return summed.at[:, bin_index + 1].add(slices_flat * bin_frac)]
    gather x8 -> x0, local copies, waits for them, and re-layouts: 252 us -> none  [the longest x4 131 us: backproject(): det_rows[:, bin_index] * (1.0 - bin_frac)]
    reduce_scatter x1, waiting for transfers between devices: 86.4 us -> 30.6 us  [local(): lax.psum_scatter(jnp.stack(stacked), 'slab', scatter_dimension=1, tiled=T...]
    pallas_call x0 -> x2, Pallas kernels: none -> 25.3 us  [the longest x1 15.4 us: backproject(): pl.pallas_call(body, out_shape=jax.ShapeDtypeStruct((rows_n, slices_n, pe...]
    mul x4 -> x0, local copies, waits for them, and re-layouts: 19.8 us -> none  [the longest x2 10.6 us: project(): summed = summed.at[:, bin_index].add(slices_flat * (1.0 - bin_frac))]
  transfers between devices with their start and end apart: 5 -> 5, of which waited for: 3 -> 4; matrix products, arithmetic and copies ran while one was open for 31% -> 1% of each run, Pallas kernels for 0% -> 0%
where the time goes in v1:
time: 201 us; the launch traced here: 200 us
  waiting for transfers between devices  121 us (60%)
  Pallas kernels  25.3 us (13%)
  between operations  17.8 us (9%)
  other arithmetic  13.9 us (7%)
  local copies, waits for them, and re-layouts  11.5 us (6%)
  blocking collectives  6.51 us (3%)
  starting transfers between devices  4.41 us (2%)
    psum x1, waiting for transfers between devices, local(): data_grad = lax.psum(data_local, 'view').transpose(1, 0, 2)  70.6 us
    reduce_scatter x1, waiting for transfers between devices, local(): lax.psum_scatter(jnp.stack(stacked), 'slab', scatter_dimension=1, tiled=T...  30.6 us
    all_gather x1, waiting for transfers between devices, local(): residual = lax.all_gather(own - measured, 'slab', axis=1, tiled=True)  19.4 us
    pallas_call x1, Pallas kernels, backproject(): pl.pallas_call(body, out_shape=jax.ShapeDtypeStruct((rows_n, slices_n, pe...  15.4 us
    pallas_call x1, Pallas kernels, project(): pl.pallas_call(body, out_shape=jax.ShapeDtypeStruct((views_n, blocks_n, s...  9.86 us
    psum x1, blocking collectives, local(): squares = lax.psum(jnp.sum(direction * direction), 'slab')  6.51 us
    reduce_sum x1, other arithmetic, local(): squares = lax.psum(jnp.sum(direction * direction), 'slab')  5.99 us
  transfers between devices with their start and end apart: 5, of which 4 were waited for; matrix products, arithmetic and copies ran while one was open for 1% of the time, Pallas kernels for 0%

profile of v1, /device:TPU:0, one launch (start us, length us, event | category | flops | bytes accessed | tf_op | source)
XLA Modules:
  0.0 200.2 jit_solution(14196859313675222215)
XLA Ops:
  6.5 0.8 fusion.30
  7.3 0.7 constant_dynamic-slice_fusion.2
  10.5 0.7 fusion.26
  11.2 0.7 pad_maximum_fusion.4.refs_0_
  11.8 9.9 %project.1 = f32[2,23,16,128]{3,2,1,0:T(8,128)} custom-call(f32[4]{0:T(128)} %pad_maximum_fusion.4.refs_0_, f32[16,4,4096]{2,1,0:T(4,128)} %refs_1_.1), custom_call_target="tpu_custom_call" | custom-call | tf_op jit(solution)/shard_map/project/pallas_call | solution.py:100
  21.7 1.0 slice_bitcast_fusion.1
  22.7 0.1 copy.20
  22.9 0.1 copy.21
  24.3 1.4 dynamic_update_slice.9
  25.7 1.4 dynamic_update_slice.8
  27.1 1.2 pad_maximum_fusion
  28.4 30.6 %reduce-scatter.2.cloned.1.call-done = f32[2,16,2944]{2,1,0:T(8,128)} async-done(((f32[2,64,2944]{2,1,0:T(8,128)}), f32[2,16,2944]{2,1,0:T(8,128)}) %reduce-scatter.2.cloned.1.call-update) | async-done | bytes 376848 | tf_op jit(solution)/shard_map/reduce_scatter | solution.py:229
  59.0 1.9 slice_subtract_fusion.4
  60.9 19.4 %all-gather.2.cloned.1.call-done = f32[2,64,2944]{2,1,0:T(8,128)} async-done(((f32[2,16,2944]{2,1,0:T(8,128)}), f32[2,64,2944]{2,1,0:T(8,128)}) %all-gather.2.cloned.1.call-update) | async-done | bytes 1507344 | tf_op jit(solution)/shard_map/all_gather | solution.py:231
  80.3 1.4 fusion.28
  82.0 0.8 pad_maximum_fusion.3.refs_2_
  82.8 0.6 broadcast_5_refs_1_.2.refs_1_
  83.4 15.4 %backproject.1 = f32[4,16,4096]{2,1,0:T(8,128)} custom-call(f32[4]{0:T(128)} %pad_maximum_fusion.4.refs_0_, s32[3]{0:T(128)} %broadcast_5_refs_1_.2.refs_1_, f32[2,23,16,128]{3,2,1,0:T(8,128)} %pad_maximum_fusion.3.refs_2_), custom_call_target="tpu_custom_call" | custom-call | tf_op jit(solution)/shard_map/backproject/pallas_call | solution.py:156
  98.9 0.1 copy.27
  98.9 1.3 collective-permute-start.1
  100.2 0.1 copy.24
  100.3 3.0 %collective-permute-start = (f32[1,4,4096]{2,0,1:T(1,128)S(1)}, f32[1,4,4096]{2,0,1:T(1,128)S(1)}, u32[]{:S(2)}, u32[]{:S(2)}) collective-permute-start(f32[1,4,4096]{2,0,1:T(1,128)S(1)} %copy.24), channel_id=1, source_target_pairs={{0,8},{8,16},{16,24},{1,9},{9,17},{17,25},{2,10},{10,18},{18,26},{... | collective-permute-start | bytes 196616 | tf_op jit(solution)/shard_map/ppermute | solution.py:173
  103.4 0.6 copy.36
  104.0 0.2 collective-permute-done
  104.2 0.8 copy-done.1
  105.0 0.6 copy-done.3
  105.6 0.8 select_maximum_fusion
  106.4 70.6 %all-reduce.3.cloned.1.call-done = f32[16,4,4096]{2,0,1:T(8,128)} async-done(((f32[16,4,4096]{2,0,1:T(8,128)}), f32[16,4,4096]{2,0,1:T(8,128)}) %all-reduce.3.cloned.1.call-update) | async-done | bytes 1048592 | tf_op jit(solution)/shard_map/psum | solution.py:247
  177.0 6.0 %multiply_reduce_fusion = (f32[]{:T(128)}, f32[16,4,4096]{2,0,1:T(8,128)}) fusion(f32[16,4,4096]{2,1,0:T(4,128)} %param.7, f32[16,4,4096]{2,0,1:T(8,128)} %all-reduce.3.cloned.1.call-done, f32[16,4,4096]{2,0,1:T(8,128)} %copy-done.1, f32[18,6,4098]{2,0,1:T(8,128)S(1)} %select_maximum_fusion, f32[1,4,4096]{2,0,1:T(1,128)S(1)} %collective-permute-done.1, ...), kind=kLoop, calls=%fused_computation.39 | loop fusion | flops 7864319 | bytes 8519684 | tf_op jit(solution)/shard_map/reduce_sum | solution.py:249
  183.0 6.5 %psum.15 = f32[]{:T(128)} all-reduce(f32[]{:T(128)} %get-tuple-element.5), channel_id=1, replica_groups=mesh['slab'=4,'view'=8] {'slab'}, use_global_device_ids=true, to_apply=%region_3.4 | all-reduce | flops 1 | bytes 8 | tf_op jit(solution)/shard_map/psum | solution.py:249
  190.2 1.9 multiply_subtract_fusion
  192.0 1.6 copy.37
  (24 shorter events, 0.5 us)
Async XLA Ops:
  6.5 52.4 %reduce-scatter.2.cloned.1.call-start = ((), (), s32[]{:S(2)}) async-start(), calls=%async_computation.1 | async-start | bytes 1884160 | tf_op jit(solution)/shard_map/reduce_scatter | solution.py:229
  25.7 33.3 %copy-start.2 = (f32[2,16,4096]{2,1,0:T(8,128)S(1)}, f32[2,16,4096]{2,1,0:T(8,128)}, u32[]{:S(2)}) copy-start(f32[2,16,4096]{2,1,0:T(8,128)} %param.6) | copy-start | bytes 1572868
  28.3 52.0 %all-gather.2.cloned.1.call-start = ((), (), s32[]{:S(2)}) async-start(), calls=%async_computation.2 | async-start | bytes 1884160 | tf_op jit(solution)/shard_map/all_gather | solution.py:231
  60.9 116.1 %all-reduce.3.cloned.1.call-start = ((), (), s32[]{:S(2)}) async-start(), calls=%async_computation.3 | async-start | bytes 2097152 | tf_op jit(solution)/shard_map/psum | solution.py:247
  81.9 17.0 %copy-start = (f32[16,4,4096]{2,1,0:T(4,128)S(1)}, f32[16,4,4096]{2,1,0:T(4,128)}, u32[]{:S(2)}) copy-start(f32[16,4,4096]{2,1,0:T(4,128)} %refs_1_.1) | copy-start | bytes 3145732
  98.9 5.0 %collective-permute-start.1 = (f32[1,4,4096]{2,0,1:T(1,128)S(1)}, f32[1,4,4096]{2,0,1:T(1,128)S(1)}, u32[]{:S(2)}, u32[]{:S(2)}) collective-permute-start(f32[1,4,4096]{2,0,1:T(1,128)S(1)} %copy.27), channel_id=1, source_target_pairs={{8,0},{16,8},{24,16},{9,1},{17,9},{25,17},{10,2},{18,10},{26,18},{... | collective-permute-start | bytes 196616 | tf_op jit(solution)/shard_map/ppermute | solution.py:175
  100.3 3.9 %collective-permute-start = (f32[1,4,4096]{2,0,1:T(1,128)S(1)}, f32[1,4,4096]{2,0,1:T(1,128)S(1)}, u32[]{:S(2)}, u32[]{:S(2)}) collective-permute-start(f32[1,4,4096]{2,0,1:T(1,128)S(1)} %copy.24), channel_id=1, source_target_pairs={{0,8},{8,16},{16,24},{1,9},{9,17},{17,25},{2,10},{10,18},{18,26},{... | collective-permute-start | bytes 196616 | tf_op jit(solution)/shard_map/ppermute | solution.py:173
  104.0 1.0 copy-start.1
  105.0 0.6 copy-start.3
Sparse Core Ops, SparseCore 0:
  28.5 30.4 reduce-scatter.1
  61.0 19.2 all-gather.1
  99.0 77.9 all-reduce.2

commit v2 on v1

--- a/solution.py
+++ b/solution.py
@@ -203,7 +203,7 @@
     return base, blocks
 
 
-def local(volume, sinogram, curvature, angles, offsets):
+def local_any(volume, sinogram, curvature, angles, offsets):
     slices_n, rows_n, cols_n = volume.shape
     views_n = angles.shape[0]
     bins_n = sinogram.shape[2]
@@ -252,6 +252,292 @@
     return volume - factor * direction
 
 
+WINDOW = 3
+COS_LANE = LANES - 2
+SIN_LANE = LANES - 1
+
+
+def window_start(part, per_n, cos, sin, rows_n, cols_n, bins_n, base, blocks):
+    low = None
+    for row in (0, rows_n - 1):
+        along = row - 0.5 * rows_n + 0.5
+        for edge in (0.0, per_n - 1.0):
+            across = (part * per_n).astype(jnp.float32) + edge - 0.5 * cols_n + 0.5
+            t = coordinate(across, along, cos, sin, bins_n)
+            low = t if low is None else jnp.minimum(low, t)
+    first = low.astype(jnp.int32) - (base + 1)
+    return jnp.clip(first, 0, (blocks - WINDOW) * LANES)
+
+
+def residual_kernel(dims, parts_n, ints_ref, trig_ref, proj_ref, near_ref, far_c_ref, far_o_ref, own_ref, pair_ref, cross_c_ref, cross_o_ref, *rest):
+    rows_n, cols_n, bins_n, base, blocks = dims
+    outs = rest[:parts_n]
+    near_pad, far_pad, sino, res = rest[parts_n:]
+    views_n, _, band, _ = proj_ref.shape
+    slab, core, part = ints_ref[0], ints_ref[1], ints_ref[2]
+    for pad in (near_pad, far_pad):
+        pad[:, :, 0:band] = jnp.zeros((views_n, blocks, band, LANES), jnp.float32)
+        pad[:, :, 2 * band:] = jnp.zeros((views_n, blocks, band, LANES), jnp.float32)
+    near_pad[:, :, band:2 * band] = near_ref[...]
+    far_pad[core, :, band:2 * band] = far_c_ref[...]
+    far_pad[1 - core, :, band:2 * band] = far_o_ref[...]
+
+    def rows_of(k):
+        return pl.ds(pl.multiple_of(k * band, band), band)
+
+    sino[:, :, rows_of(slab)] = own_ref[...]
+    sino[:, :, rows_of(slab ^ 1)] = pair_ref[...]
+    sino[core, :, rows_of(slab ^ 2)] = cross_c_ref[0]
+    sino[core, :, rows_of(slab ^ 3)] = cross_c_ref[1]
+    sino[1 - core, :, rows_of(slab ^ 3)] = cross_o_ref[0]
+    sino[1 - core, :, rows_of(slab ^ 2)] = cross_o_ref[1]
+    for v in range(views_n):
+        start, near, far = ints_ref[3 + 3 * v], ints_ref[4 + 3 * v], ints_ref[5 + 3 * v]
+        res[v, 0:blocks] = (
+            (proj_ref[v] + near_pad[v, :, pl.ds(near, band), :])
+            + far_pad[v, :, pl.ds(far, band), :]
+        ) - sino[v, :, pl.ds(start, band), :]
+        res[v, blocks] = jnp.zeros((band, LANES), jnp.float32)
+    lane = lax.broadcasted_iota(jnp.int32, (band, LANES), 1)
+    per_n = cols_n // parts_n
+    for r in range(parts_n):
+        for v in range(views_n):
+            cos, sin = trig_ref[v], trig_ref[views_n + v]
+            first = window_start(part ^ r, per_n, cos, sin, rows_n, cols_n, bins_n, base, blocks)
+            k = first >> 7
+            shift = first & (LANES - 1)
+            turned = [pltpu.roll(res[v, k + m], (LANES - shift) & (LANES - 1), 1) for m in range(WINDOW + 1)]
+            for m in range(WINDOW):
+                value = jnp.where(lane < LANES - shift, turned[m], turned[m + 1])
+                if m == WINDOW - 1:
+                    value = jnp.where(lane == COS_LANE, cos, jnp.where(lane == SIN_LANE, sin, value))
+                outs[r][v, m] = value
+
+
+def residual_windows(dims, parts_n, ints, trig, arrays):
+    views_n, blocks, band, _ = arrays[0].shape
+    body = lambda *refs: residual_kernel(dims, parts_n, *refs)
+    vmem = pl.BlockSpec(memory_space=pltpu.VMEM)
+    smem = pl.BlockSpec(memory_space=pltpu.SMEM)
+    return pl.pallas_call(
+        body,
+        out_shape=[jax.ShapeDtypeStruct((views_n, WINDOW, band, LANES), jnp.float32)] * parts_n,
+        in_specs=[smem, smem] + [vmem] * len(arrays),
+        out_specs=[vmem] * parts_n,
+        scratch_shapes=[
+            pltpu.VMEM((views_n, blocks, 3 * band, LANES), jnp.float32),
+            pltpu.VMEM((views_n, blocks, 3 * band, LANES), jnp.float32),
+            pltpu.VMEM((views_n, blocks, 4 * band, LANES), jnp.float32),
+            pltpu.VMEM((views_n, blocks + 1, band, LANES), jnp.float32),
+        ],
+        name="residual_windows",
+    )(ints, trig, *arrays)
+
+
+def gather_kernel(dims, parts_n, views_n, ints_ref, *rest):
+    rows_n, cols_n, bins_n, base, blocks = dims
+    pieces = rest[:parts_n]
+    out_ref, trig_ref, starts_ref = rest[parts_n:]
+    per_n = cols_n // parts_n
+    part = ints_ref[2]
+    lane8 = lax.broadcasted_iota(jnp.int32, (8, LANES), 1)
+    lane = lax.broadcasted_iota(jnp.int32, (16, LANES), 1)
+    total_n = parts_n * views_n
+    for n in range(total_n):
+        tagged = pieces[n // views_n][n % views_n, WINDOW - 1, 0:8, :]
+        cos = jnp.max(jnp.where(lane8 == COS_LANE, tagged, -2.0))
+        sin = jnp.max(jnp.where(lane8 == SIN_LANE, tagged, -2.0))
+        trig_ref[n] = cos
+        trig_ref[total_n + n] = sin
+        starts_ref[n] = window_start(part, per_n, cos, sin, rows_n, cols_n, bins_n, base, blocks)
+
+    def step(index, _):
+        row = index // (per_n // LANES)
+        u = index - row * (per_n // LANES)
+        along = row.astype(jnp.float32) - 0.5 * rows_n + 0.5
+        column = part * per_n + u * LANES
+        start = column.astype(jnp.float32)
+        across = (lane + column).astype(jnp.float32) - 0.5 * cols_n + 0.5
+        total = jnp.zeros((16, LANES), jnp.float32)
+        for n in range(total_n):
+            cos = trig_ref[n]
+            sin = trig_ref[total_n + n]
+            offset = starts_ref[n]
+            coord = coordinate(across, along, cos, sin, bins_n)
+            lower = jnp.floor(coord)
+            frac = coord - lower
+            rel = lower.astype(jnp.int32) - (base + offset)
+            here = rel & (LANES - 1)
+            next_ = (rel + 1) & (LANES - 1)
+            first = jnp.maximum(window_of(start, cos, sin, along, cols_n, bins_n, base) - offset, 0)
+            k = jnp.minimum(first >> 7, WINDOW - 1)
+            windows = pieces[n // views_n]
+            left = windows[n % views_n, k]
+            right = windows[n % views_n, jnp.minimum(k + 1, WINDOW - 1)]
+            held = jnp.where(lane >= (first & (LANES - 1)), left, right)
+            a = jnp.take_along_axis(held, here, axis=1, mode="promise_in_bounds")
+            b = jnp.take_along_axis(held, next_, axis=1, mode="promise_in_bounds")
+            total = total + (a * (1.0 - frac) + b * frac)
+        out_ref[row, :, pl.ds(pl.multiple_of(u * LANES, LANES), LANES)] = total
+        return 0
+
+    lax.fori_loop(0, rows_n * (per_n // LANES), step, 0)
+
+
+def gather_views(dims, parts_n, ints, pieces):
+    views_n, _, slices_n, _ = pieces[0].shape
+    rows_n, cols_n = dims[:2]
+    body = lambda *refs: gather_kernel(dims, parts_n, views_n, *refs)
+    vmem = pl.BlockSpec(memory_space=pltpu.VMEM)
+    return pl.pallas_call(
+        body,
+        out_shape=jax.ShapeDtypeStruct((rows_n, slices_n, cols_n // parts_n), jnp.float32),
+        in_specs=[pl.BlockSpec(memory_space=pltpu.SMEM)] + [vmem] * parts_n,
+        out_specs=vmem,
+        scratch_shapes=[
+            pltpu.SMEM((2 * parts_n * views_n,), jnp.float32),
+            pltpu.SMEM((parts_n * views_n,), jnp.int32),
+        ],
+        name="gather_views",
+    )(ints, *pieces)
+
+
+def finish_kernel(parts_n, order_ref, factor_ref, vol_ref, *rest):
+    pieces = rest[:parts_n]
+    out_ref = rest[parts_n]
+    factor = factor_ref[0]
+    per_n = pieces[0].shape[2]
+    for r in range(parts_n):
+        cols = pl.ds(pl.multiple_of(order_ref[r] * per_n, per_n), per_n)
+        out_ref[:, :, cols] = vol_ref[:, :, cols] - factor * pieces[r][...]
+
+
+def finish(order, factor, volume, pieces):
+    parts_n = len(pieces)
+    vmem = pl.BlockSpec(memory_space=pltpu.VMEM)
+    smem = pl.BlockSpec(memory_space=pltpu.SMEM)
+    return pl.pallas_call(
+        lambda *refs: finish_kernel(parts_n, *refs),
+        out_shape=jax.ShapeDtypeStruct(volume.shape, volume.dtype),
+        in_specs=[smem, smem] + [vmem] * (parts_n + 1),
+        out_specs=vmem,
+        name="finish",
+    )(order, factor, volume, *pieces)
+
+
+def swapped(x, axis, bit):
+    return lax.ppermute(x, axis, [(i, i ^ bit) for i in range(lax.axis_size(axis))])
+
+
+def gathered(piece):
+    part = lax.axis_index("view")
+    depth = part // 2
+    end = (depth == 0) | (depth == 3)
+
+    def along(x, pairs):
+        return lax.ppermute(x, "view", [(2 * a + y, 2 * b + y) for a, b in pairs for y in (0, 1)])
+
+    across = [swapped(piece, "view", 1)]
+    second = along(piece, [(0, 1), (1, 0), (2, 3), (3, 2)])
+    middle = along(piece, [(1, 2), (2, 1)])
+    across.append(swapped(second, "view", 1))
+    onward = along(middle, [(1, 0), (2, 3)])
+    middle_last = along(second, [(1, 2), (2, 1)])
+    third = jnp.where(end, onward, middle)
+    across.append(swapped(third, "view", 1))
+    last = jnp.where(end, along(middle_last, [(1, 0), (2, 3)]), middle_last)
+    across.append(swapped(last, "view", 1))
+    upper = depth // 2
+    depths = [depth, depth ^ 1, 2 - upper, 3 - 3 * upper]
+    order = jnp.stack([2 * d + part % 2 for d in depths] + [2 * d + 1 - part % 2 for d in depths])
+    return order.astype(jnp.int32), [piece, second, third, last] + across
+
+
+def local_split(volume, sinogram, curvature, angles, offsets):
+    slices_n, rows_n, cols_n = volume.shape
+    views_n = angles.shape[0]
+    bins_n = sinogram.shape[2]
+    base, blocks = extent(rows_n, cols_n, bins_n)
+    dims = (rows_n, cols_n, bins_n, base, blocks)
+    slab_count = lax.axis_size("slab")
+    parts_n = lax.axis_size("view")
+    slab = lax.axis_index("slab")
+    core = slab % 2
+    part = lax.axis_index("view")
+    per_n = cols_n // parts_n
+
+    measured = sinogram[:, :, base : base + blocks * LANES]
+    measured = measured.reshape(views_n, slices_n, blocks, LANES).transpose(0, 2, 1, 3)
+    pair_rows = swapped(measured, "slab", 1)
+    chip_rows = jnp.stack(
+        [
+            lax.dynamic_index_in_dim(measured, core, 0, keepdims=False),
+            lax.dynamic_index_in_dim(pair_rows, core, 0, keepdims=False),
+        ]
+    )
+    cross_rows = swapped(chip_rows, "slab", 2)
+    cross_other = swapped(cross_rows, "slab", 1)
+
+    angle_rad = angles.astype(jnp.float32) * (2.0 * math.pi / ROTATION_VIEWS)
+    trig = jnp.concatenate([jnp.cos(angle_rad), jnp.sin(angle_rad)])
+    proj = project(trig, volume, bins_n, base, blocks, views_n)
+    near = swapped(proj, "slab", 1)
+    turned = offsets[:, 0] > slices_n
+    chip = slab // 2
+    edge_core = jnp.where(turned, chip, 1 - chip)
+    sends_own = lax.dynamic_index_in_dim(edge_core, core, 0, keepdims=False) == core
+    edge = jnp.where(
+        sends_own,
+        lax.dynamic_index_in_dim(proj, core, 0, keepdims=False),
+        lax.dynamic_index_in_dim(near, core, 0, keepdims=False),
+    )
+    far = swapped(edge, "slab", 2)
+    far_other = swapped(far, "slab", 1)
+
+    def of(k):
+        return lax.dynamic_index_in_dim(offsets, k, 1, keepdims=False)
+
+    far_slab = 2 * (1 - chip) + jnp.where(turned, 1 - chip, chip)
+    start = of(slab)
+    far_start = jnp.take_along_axis(offsets, far_slab[:, None], axis=1)[:, 0]
+
+    def shift(other):
+        return slices_n + jnp.clip(start - other, -slices_n, slices_n)
+
+    table = jnp.stack([start, shift(of(slab ^ 1)), shift(far_start)], axis=1).reshape(-1)
+    ints = jnp.concatenate([jnp.stack([slab, core, part]).astype(jnp.int32), table])
+    windows = residual_windows(
+        dims, parts_n, ints, trig,
+        [proj, near, far, far_other, measured, pair_rows, cross_rows, cross_other],
+    )
+    pieces = [windows[0]] + [swapped(windows[r], "view", r) for r in range(1, parts_n)]
+    data_grad = gather_views(dims, parts_n, ints, pieces).transpose(1, 0, 2)
+
+    wide = jnp.pad(volume, ((0, 0), (0, 0), (1, 1)))
+    block = lax.dynamic_slice_in_dim(wide, part * per_n, per_n + 2, axis=2)
+    padded = jnp.pad(padded_2(block, (("slab", 0),), 1), ((0, 0), (1, 1), (0, 0)))
+    tv_grad = tv_padded(padded)
+    curv = lax.dynamic_slice_in_dim(curvature, part * per_n, per_n, axis=2)
+    direction = (data_grad + tv_weight * tv_grad) / curv
+    squares = jnp.sum(direction * direction).reshape(1, 1)
+    for axis in ("slab", "view"):
+        bit = 1
+        while bit < lax.axis_size(axis):
+            squares = squares + swapped(squares, axis, bit)
+            bit *= 2
+    order, parts = gathered(direction)
+    voxel_count = slices_n * slab_count * rows_n * cols_n
+    factor = jnp.minimum(1.0, step_limit / jnp.sqrt(squares / voxel_count + epsilon))
+    return finish(order, factor.reshape(1), volume, parts)
+
+
+def local(volume, sinogram, curvature, angles, offsets):
+    shape = (lax.axis_size("slab"), lax.axis_size("view"), angles.shape[0])
+    if shape == (4, 8, 2):
+        return local_split(volume, sinogram, curvature, angles, offsets)
+    return local_any(volume, sinogram, curvature, angles, offsets)
+
+
 def solution(mesh):
     in_specs = (
         P("slab", None, None),

time: 201 us -> 109 us (0.54)
  waiting for transfers between devices: 121 us -> 34.4 us
  starting transfers between devices: 4.41 us -> 37.6 us
  between operations: 17.8 us -> 4.92 us
  other arithmetic: 13.9 us -> 4.05 us
  blocking collectives: 6.51 us -> 0 us
  local copies, waits for them, and re-layouts: 11.5 us -> 6.4 us
  Pallas kernels: 25.3 us -> 21.4 us
    psum x1 -> x0, waiting for transfers between devices: 70.6 us -> none  [local(): data_grad = lax.psum(data_local, 'view').transpose(1, 0, 2)]
    ppermute x0 -> x27, waiting for transfers between devices: none -> 34.4 us  [the longest x22 22.7 us: swapped(): lax.ppermute(x, axis, [(i, i ^ bit) for i in range(lax.axis_size(axis))])]
    ppermute x0 -> x27, starting transfers between devices: none -> 34 us  [the longest x22 30.1 us: swapped(): lax.ppermute(x, axis, [(i, i ^ bit) for i in range(lax.axis_size(axis))])]
    reduce_scatter x1 -> x0, waiting for transfers between devices: 30.6 us -> none  [local(): lax.psum_scatter(jnp.stack(stacked), 'slab', scatter_dimension=1, tiled=T...]
    all_gather x1 -> x0, waiting for transfers between devices: 19.4 us -> none  [local(): residual = lax.all_gather(own - measured, 'slab', axis=1, tiled=True)]
    psum x1 -> x0, blocking collectives: 6.51 us -> none  [local(): squares = lax.psum(jnp.sum(direction * direction), 'slab')]
    pallas_call x1 -> x3, Pallas kernels: 15.4 us -> 11.6 us  [the longest x1 5.94 us: gather_views(): pl.pallas_call(body, out_shape=jax.ShapeDtypeStruct((rows_n, slices_n, co...]
    reduce_sum x1, other arithmetic: 5.99 us -> 2.16 us  [local_split(): squares = jnp.sum(direction * direction).reshape(1, 1)]
  transfers between devices with their start and end apart: 5 -> 29, of which waited for: 4 -> 13; matrix products, arithmetic and copies ran while one was open for 1% -> 4% of each run, Pallas kernels for 0% -> 12%
where the time goes in v2:
time: 109 us
  starting transfers between devices  37.6 us (34%)
  waiting for transfers between devices  34.4 us (32%)
  Pallas kernels  21.4 us (20%)
  local copies, waits for them, and re-layouts  6.4 us (6%)
  between operations  4.92 us (5%)
  other arithmetic  4.05 us (4%)
    ppermute x22, starting transfers between devices, swapped(): lax.ppermute(x, axis, [(i, i ^ bit) for i in range(lax.axis_size(axis))])  30.1 us
    ppermute x22, waiting for transfers between devices, swapped(): lax.ppermute(x, axis, [(i, i ^ bit) for i in range(lax.axis_size(axis))])  22.7 us
    ppermute x5, waiting for transfers between devices, along(): lax.ppermute(x, 'view', [(2 * a + y, 2 * b + y) for a, b in pairs for y i...  11.7 us
    pallas_call x1, Pallas kernels, project(): pl.pallas_call(body, out_shape=jax.ShapeDtypeStruct((views_n, blocks_n, s...  9.86 us
    pallas_call x1, Pallas kernels, gather_views(): pl.pallas_call(body, out_shape=jax.ShapeDtypeStruct((rows_n, slices_n, co...  5.94 us
    ppermute x5, starting transfers between devices, along(): lax.ppermute(x, 'view', [(2 * a + y, 2 * b + y) for a, b in pairs for y i...  3.92 us
    pallas_call x1, Pallas kernels, residual_windows(): pl.pallas_call(body, out_shape=[jax.ShapeDtypeStruct((views_n, WINDOW, ba...  2.95 us
    unnamed x63, local copies, waits for them, and re-layouts  2.79 us
  transfers between devices with their start and end apart: 29, of which 13 were waited for; matrix products, arithmetic and copies ran while one was open for 4% of the time, Pallas kernels for 12%

profile of v2, /device:TPU:0, one launch (start us, length us, event | category | flops | bytes accessed | tf_op | source)
XLA Modules:
  0.0 108.9 jit_solution(5338134129052204211)
XLA Ops:
  0.0 1.2 %copy_bitcast_fusion = (f32[2,16,23,128]{3,1,2,0:T(8,128)S(1)}, f32[2,23,16,128]{3,2,1,0:T(8,128)S(1)}) fusion(f32[2,16,4096]{2,1,0:T(8,128)} %param.6), kind=kLoop, calls=%fused_computation.9 | loop fusion | bytes 1130496 | tf_op jit(solution)/shard_map/reshape | solution.py:470
  2.5 9.9 %project.1.refs_2_ = f32[2,23,16,128]{3,2,1,0:T(8,128)} custom-call(f32[4]{0:T(128)} %pad_maximum_fusion.3.refs_0_.refs_1_, f32[16,4,4096]{2,1,0:T(4,128)} %refs_2_.1), custom_call_target="tpu_custom_call" | custom-call | tf_op jit(solution)/shard_map/project/pallas_call | solution.py:100
  12.6 2.4 %collective-permute-start.13 = (f32[1,4,514]{2,1,0:T(4,128)S(1)}, f32[1,4,514]{2,1,0:T(4,128)S(1)}, u32[]{:S(2)}, u32[]{:S(2)}) collective-permute-start(f32[1,4,514]{2,1,0:T(4,128)S(1)} %get-tuple-element.25), channel_id=1, source_target_pairs={{0,8},{8,16},{16,24},{1,9},{9,17},{17,25},{2,10},{10,18},{18,26},{... | collective-permute-start | bytes 24680 | tf_op jit(solution)/shard_map/ppermute | solution.py:173
  15.0 1.3 %collective-permute-start.14 = (f32[1,4,514]{2,1,0:T(4,128)S(1)}, f32[1,4,514]{2,1,0:T(4,128)S(1)}, u32[]{:S(2)}, u32[]{:S(2)}) collective-permute-start(f32[1,4,514]{2,1,0:T(4,128)S(1)} %get-tuple-element.26), channel_id=1, source_target_pairs={{8,0},{16,8},{24,16},{9,1},{17,9},{25,17},{10,2},{18,10},{26,18},{... | collective-permute-start | bytes 24680 | tf_op jit(solution)/shard_map/ppermute | solution.py:175
  16.4 4.9 %collective-permute-start.4 = (f32[2,23,16,128]{3,2,1,0:T(8,128)S(1)}, f32[2,23,16,128]{3,2,1,0:T(8,128)S(1)}, u32[]{:S(2)}, u32[]{:S(2)}) collective-permute-start(f32[2,23,16,128]{3,2,1,0:T(8,128)S(1)} %pad_maximum_fusion), channel_id=1, source_target_pairs={{0,16},{8,24},{16,0},{24,8},{1,17},{9,25},{17,1},{25,9},{2,18},{10... | collective-permute-start | bytes 1130504 | tf_op jit(solution)/shard_map/ppermute | solution.py:429
  23.8 7.1 %collective-permute-done.4.refs_8_ = f32[2,23,16,128]{3,2,1,0:T(8,128)S(1)} collective-permute-done((f32[2,23,16,128]{3,2,1,0:T(8,128)S(1)}, f32[2,23,16,128]{3,2,1,0:T(8,128)S(1)}, u32[]{:S(2)}, u32[]{:S(2)}) %collective-permute-start.4) | collective-permute-done | bytes 376864 | tf_op jit(solution)/shard_map/ppermute | solution.py:429
  30.9 3.6 %collective-permute-done.1.refs_4_ = f32[23,16,128]{2,1,0:T(8,128)S(1)} collective-permute-done((f32[23,16,128]{2,1,0:T(8,128)S(1)}, f32[23,16,128]{2,1,0:T(8,128)S(1)}, u32[]{:S(2)}, u32[]{:S(2)}) %collective-permute-start.1) | collective-permute-done | bytes 188448 | tf_op jit(solution)/shard_map/ppermute | solution.py:429
  37.4 2.9 %residual_windows.1 = (f32[2,3,16,128]{3,2,1,0:T(8,128)}, f32[2,3,16,128]{3,2,1,0:T(8,128)}, f32[2,3,16,128]{3,2,1,0:T(8,128)}, f32[2,3,16,128]{3,2,1,0:T(8,128)...) custom-call(s32[9]{0:T(128)} %pad_add_fusion.2.refs_0_, ...), custom_call_target="tpu_custom_call" | custom-call | tf_op jit(solution)/shard_map/residual_windows/pallas_call | solution.py:322
  40.4 3.6 %collective-permute-start.10 = (f32[2,3,16,128]{3,2,1,0:T(8,128)}, f32[2,3,16,128]{3,2,1,0:T(8,128)S(1)}, u32[]{:S(2)}, u32[]{:S(2)}) collective-permute-start(f32[2,3,16,128]{3,2,1,0:T(8,128)} %get-tuple-element.18), channel_id=1, source_target_pairs={{0,5},{1,4},{2,7},{3,6},{4,1},{5,0},{6,3},{7,2},{8,13},{9,12},{10,... | collective-permute-start | bytes 147464 | tf_op jit(solution)/shard_map/ppermute | solution.py:429
  44.0 1.3 %collective-permute-start.11 = (f32[2,3,16,128]{3,2,1,0:T(8,128)}, f32[2,3,16,128]{3,2,1,0:T(8,128)S(1)}, u32[]{:S(2)}, u32[]{:S(2)}) collective-permute-start(f32[2,3,16,128]{3,2,1,0:T(8,128)} %get-tuple-element.19), channel_id=1, source_target_pairs={{0,6},{1,7},{2,4},{3,5},{4,2},{5,3},{6,0},{7,1},{8,14},{9,15},{10,... | collective-permute-start | bytes 147464 | tf_op jit(solution)/shard_map/ppermute | solution.py:429
  45.5 2.5 %collective-permute-start.12 = (f32[2,3,16,128]{3,2,1,0:T(8,128)S(1)}, f32[2,3,16,128]{3,2,1,0:T(8,128)S(1)}, u32[]{:S(2)}, u32[]{:S(2)}) collective-permute-start(f32[2,3,16,128]{3,2,1,0:T(8,128)S(1)} %copy-done.29), channel_id=1, source_target_pairs={{0,7},{1,6},{2,5},{3,4},{4,3},{5,2},{6,1},{7,0},{8,15},{9,14},{10,... | collective-permute-start | bytes 147464 | tf_op jit(solution)/shard_map/ppermute | solution.py:429
  48.0 1.5 %collective-permute-start.6 = (f32[2,3,16,128]{3,2,1,0:T(8,128)S(1)}, f32[2,3,16,128]{3,2,1,0:T(8,128)S(1)}, u32[]{:S(2)}, u32[]{:S(2)}) collective-permute-start(f32[2,3,16,128]{3,2,1,0:T(8,128)S(1)} %copy-done.28), channel_id=1, source_target_pairs={{0,1},{1,0},{2,3},{3,2},{4,5},{5,4},{6,7},{7,6},{8,9},{9,8},{10,11... | collective-permute-start | bytes 147464 | tf_op jit(solution)/shard_map/ppermute | solution.py:429
  49.6 2.0 %collective-permute-start.8 = (f32[2,3,16,128]{3,2,1,0:T(8,128)S(1)}, f32[2,3,16,128]{3,2,1,0:T(8,128)S(1)}, u32[]{:S(2)}, u32[]{:S(2)}) collective-permute-start(f32[2,3,16,128]{3,2,1,0:T(8,128)S(1)} %copy-done.26), channel_id=1, source_target_pairs={{0,3},{1,2},{2,1},{3,0},{4,7},{5,6},{6,5},{7,4},{8,11},{9,10},{10,... | collective-permute-start | bytes 147464 | tf_op jit(solution)/shard_map/ppermute | solution.py:429
  51.6 2.7 %collective-permute-start.9 = (f32[2,3,16,128]{3,2,1,0:T(8,128)S(1)}, f32[2,3,16,128]{3,2,1,0:T(8,128)S(1)}, u32[]{:S(2)}, u32[]{:S(2)}) collective-permute-start(f32[2,3,16,128]{3,2,1,0:T(8,128)S(1)} %copy-done.25), channel_id=1, source_target_pairs={{0,4},{1,5},{2,6},{3,7},{4,0},{5,1},{6,2},{7,3},{8,12},{9,13},{10,... | collective-permute-start | bytes 147464 | tf_op jit(solution)/shard_map/ppermute | solution.py:429
  54.6 2.1 %collective-permute-done.9.refs_5_ = f32[2,3,16,128]{3,2,1,0:T(8,128)S(1)} collective-permute-done((f32[2,3,16,128]{3,2,1,0:T(8,128)S(1)}, f32[2,3,16,128]{3,2,1,0:T(8,128)S(1)}, u32[]{:S(2)}, u32[]{:S(2)}) %collective-permute-start.9) | collective-permute-done | bytes 49184 | tf_op jit(solution)/shard_map/ppermute | solution.py:429
  57.3 5.9 %gather_views.1 = f32[4,16,512]{2,1,0:T(8,128)} custom-call(s32[9]{0:T(128)} %pad_add_fusion.2.refs_0_, f32[2,3,16,128]{3,2,1,0:T(8,128)} %get-tuple-element.13.refs_1_, f32[2,3,16,128]{3,2,1,0:T(8,128)} %copy-done.21, f32[2,3,16,128]{3,2,1,0:T(8,128)} %copy-done.22, f32[2,3,16,128]{3,2,1,0:T(8,128)} %copy-done.23, f32[2,3,16,128]{3,2,1,0:T(8,128)} %copy-done.24, ...), custom_call_target="tpu_custom_call" | custom-call | tf_op jit(solution)/shard_map/gather_views/pallas_call | solution.py:392
  63.2 2.2 %multiply_reduce_fusion = (f32[]{:T(128)}, f32[16,4,512]{2,1,0:T(4,128)S(1)}) fusion(f32[16,4,4096]{2,1,0:T(4,128)} %param.7, s32[]{:T(128)S(6)} %select_n.117, s32[]{:T(128)S(6)} %add.154, s32[]{:T(128)S(6)} %select_n.116, f32[18,6,514]{2,1,0:T(8,128)S(1)} %select_maximum_fusion, f32[1,4,514]{2,1,0:T(4,128)S(1)} %collective-permute-done.14, ...), kind=kLoop, calls=%fused_computation.41 | loop fusion | flops 983039 | bytes 1851988 | tf_op jit(solution)/shard_map/reduce_sum | solution.py:522
  66.1 4.3 %collective-permute-done.20.refs_4_ = f32[16,4,512]{2,1,0:T(4,128)S(1)} collective-permute-done((f32[16,4,512]{2,1,0:T(4,128)S(1)}, f32[16,4,512]{2,1,0:T(4,128)S(1)}, u32[]{:S(2)}, u32[]{:S(2)}) %collective-permute-start.20) | collective-permute-done | bytes 131104 | tf_op jit(solution)/shard_map/ppermute | solution.py:438
  71.1 1.3 %collective-permute-start.22 = (f32[16,4,512]{2,1,0:T(4,128)S(1)}, f32[16,4,512]{2,1,0:T(4,128)S(1)}, u32[]{:S(2)}, u32[]{:S(2)}) collective-permute-start(f32[16,4,512]{2,1,0:T(4,128)S(1)} %collective-permute-done.21), channel_id=1, source_target_pairs={{2,0},{3,1},{4,6},{5,7},{10,8},{11,9},{12,14},{13,15},{18,16},{19,... | collective-permute-start | bytes 393224 | tf_op jit(solution)/shard_map/ppermute | solution.py:438
  72.4 1.5 %collective-permute-start.25 = (f32[16,4,512]{2,1,0:T(4,128)S(1)}, f32[16,4,512]{2,1,0:T(4,128)S(1)}, u32[]{:S(2)}, u32[]{:S(2)}) collective-permute-start(f32[16,4,512]{2,1,0:T(4,128)S(1)} %get-tuple-element.22.refs_3_), channel_id=1, source_target_pairs={{0,1},{1,0},{2,3},{3,2},{4,5},{5,4},{6,7},{7,6},{8,9},{9,8},{10,11... | collective-permute-start | bytes 393224 | tf_op jit(solution)/shard_map/ppermute | solution.py:429
  74.5 1.3 %collective-permute-start.24 = (f32[16,4,512]{2,1,0:T(4,128)S(1)}, f32[16,4,512]{2,1,0:T(4,128)S(1)}, u32[]{:S(2)}, u32[]{:S(2)}) collective-permute-start(f32[16,4,512]{2,1,0:T(4,128)S(1)} %collective-permute-done.23), channel_id=1, source_target_pairs={{2,0},{3,1},{4,6},{5,7},{10,8},{11,9},{12,14},{13,15},{18,16},{19,... | collective-permute-start | bytes 393224 | tf_op jit(solution)/shard_map/ppermute | solution.py:438
  75.8 4.9 %collective-permute-done.22 = f32[16,4,512]{2,1,0:T(4,128)S(1)} collective-permute-done((f32[16,4,512]{2,1,0:T(4,128)S(1)}, f32[16,4,512]{2,1,0:T(4,128)S(1)}, u32[]{:S(2)}, u32[]{:S(2)}) %collective-permute-start.22) | collective-permute-done | bytes 131104 | tf_op jit(solution)/shard_map/ppermute | solution.py:438
  80.8 2.5 %collective-permute-done.24 = f32[16,4,512]{2,1,0:T(4,128)S(1)} collective-permute-done((f32[16,4,512]{2,1,0:T(4,128)S(1)}, f32[16,4,512]{2,1,0:T(4,128)S(1)}, u32[]{:S(2)}, u32[]{:S(2)}) %collective-permute-start.24) | collective-permute-done | bytes 131104 | tf_op jit(solution)/shard_map/ppermute | solution.py:438
  84.5 1.3 %collective-permute-done.15 = f32[1,1]{1,0:T(1,128)} collective-permute-done((f32[1,1]{1,0:T(1,128)}, f32[1,1]{1,0:T(1,128)}, u32[]{:S(2)}, u32[]{:S(2)}) %collective-permute-start.15) | collective-permute-done | bytes 36 | tf_op jit(solution)/shard_map/ppermute | solution.py:429
  87.1 1.7 %collective-permute-start.16 = (f32[1,1]{1,0:T(1,128)}, f32[1,1]{1,0:T(1,128)}, u32[]{:S(2)}, u32[]{:S(2)}) collective-permute-start(f32[1,1]{1,0:T(1,128)} %add.138), channel_id=1, source_target_pairs={{0,16},{8,24},{16,0},{24,8},{1,17},{9,25},{17,1},{25,9},{2,18},{10... | collective-permute-start | bytes 20 | tf_op jit(solution)/shard_map/ppermute | solution.py:429
  88.7 2.1 %collective-permute-done.16 = f32[1,1]{1,0:T(1,128)} collective-permute-done((f32[1,1]{1,0:T(1,128)}, f32[1,1]{1,0:T(1,128)}, u32[]{:S(2)}, u32[]{:S(2)}) %collective-permute-start.16) | collective-permute-done | bytes 36 | tf_op jit(solution)/shard_map/ppermute | solution.py:429
  91.4 2.9 %collective-permute-start.17 = (f32[1,1]{1,0:T(1,128)}, f32[1,1]{1,0:T(1,128)}, u32[]{:S(2)}, u32[]{:S(2)}) collective-permute-start(f32[1,1]{1,0:T(1,128)} %add.139), channel_id=1, source_target_pairs={{0,1},{1,0},{2,3},{3,2},{4,5},{5,4},{6,7},{7,6},{8,9},{9,8},{10,11... | collective-permute-start | bytes 20 | tf_op jit(solution)/shard_map/ppermute | solution.py:429
  95.7 1.4 %collective-permute-start.18 = (f32[1,1]{1,0:T(1,128)}, f32[1,1]{1,0:T(1,128)}, u32[]{:S(2)}, u32[]{:S(2)}) collective-permute-start(f32[1,1]{1,0:T(1,128)} %add.140), channel_id=1, source_target_pairs={{0,2},{1,3},{2,0},{3,1},{4,6},{5,7},{6,4},{7,5},{8,10},{9,11},{10,... | collective-permute-start | bytes 20 | tf_op jit(solution)/shard_map/ppermute | solution.py:429
  97.1 2.3 %collective-permute-done.18 = f32[1,1]{1,0:T(1,128)} collective-permute-done((f32[1,1]{1,0:T(1,128)}, f32[1,1]{1,0:T(1,128)}, u32[]{:S(2)}, u32[]{:S(2)}) %collective-permute-start.18) | collective-permute-done | bytes 36 | tf_op jit(solution)/shard_map/ppermute | solution.py:429
  100.1 2.1 %collective-permute-start.19 = (f32[1,1]{1,0:T(1,128)}, f32[1,1]{1,0:T(1,128)}, u32[]{:S(2)}, u32[]{:S(2)}) collective-permute-start(f32[1,1]{1,0:T(1,128)} %add.141), channel_id=1, source_target_pairs={{0,4},{1,5},{2,6},{3,7},{4,0},{5,1},{6,2},{7,3},{8,12},{9,13},{10,... | collective-permute-start | bytes 20 | tf_op jit(solution)/shard_map/ppermute | solution.py:429
  102.2 2.5 %collective-permute-done.19 = f32[1,1]{1,0:T(1,128)} collective-permute-done((f32[1,1]{1,0:T(1,128)}, f32[1,1]{1,0:T(1,128)}, u32[]{:S(2)}, u32[]{:S(2)}) %collective-permute-start.19) | collective-permute-done | bytes 36 | tf_op jit(solution)/shard_map/ppermute | solution.py:429
  106.2 2.7 %finish.1 = f32[16,4,4096]{2,1,0:T(4,128)} custom-call(s32[8]{0:T(128)} %stack.55.refs_0_, f32[1]{0:T(128)} %bitcast.19.refs_1_, f32[16,4,4096]{2,1,0:T(4,128)} %refs_2_.1, f32[16,4,512]{2,1,0:T(4,128)} %copy-done.6, f32[16,4,512]{2,1,0:T(4,128)} %copy-done.13, f32[16,4,512]{2,1,0:T(4,128)} %bitcast.40, f32[16,4,512]{2,1,0:T(4,128)} %bitcast.42, ...), custom_call_target="tpu_custom_call" | custom-call | tf_op jit(solution)/shard_map/finish/pallas_call | solution.py:419
  (118 shorter events, 12.0 us)
Async XLA Ops:
  1.3 15.1 %collective-permute-start.3 = (f32[2,23,16,128]{3,2,1,0:T(8,128)S(1)}, f32[2,23,16,128]{3,2,1,0:T(8,128)S(1)}, u32[]{:S(2)}, u32[]{:S(2)}) collective-permute-start(f32[2,23,16,128]{3,2,1,0:T(8,128)S(1)} %get-tuple-element.28.refs_6_), channel_id=1, source_target_pairs={{0,8},{8,0},{16,24},{24,16},{1,9},{9,1},{17,25},{25,17},{2,10},{10... | collective-permute-start | bytes 1130504 | tf_op jit(solution)/shard_map/ppermute | solution.py:429
  12.4 11.3 %collective-permute-start = (f32[2,23,16,128]{3,2,1,0:T(8,128)}, f32[2,23,16,128]{3,2,1,0:T(8,128)S(1)}, u32[]{:S(2)}, u32[]{:S(2)}) collective-permute-start(f32[2,23,16,128]{3,2,1,0:T(8,128)} %project.1.refs_2_), channel_id=1, source_target_pairs={{0,8},{8,0},{16,24},{24,16},{1,9},{9,1},{17,25},{25,17},{2,10},{10... | collective-permute-start | bytes 1130504 | tf_op jit(solution)/shard_map/ppermute | solution.py:429
  12.6 35.4 %collective-permute-start.13 = (f32[1,4,514]{2,1,0:T(4,128)S(1)}, f32[1,4,514]{2,1,0:T(4,128)S(1)}, u32[]{:S(2)}, u32[]{:S(2)}) collective-permute-start(f32[1,4,514]{2,1,0:T(4,128)S(1)} %get-tuple-element.25), channel_id=1, source_target_pairs={{0,8},{8,16},{16,24},{1,9},{9,17},{17,25},{2,10},{10,18},{18,26},{... | collective-permute-start | bytes 24680 | tf_op jit(solution)/shard_map/ppermute | solution.py:173
  15.0 34.6 %collective-permute-start.14 = (f32[1,4,514]{2,1,0:T(4,128)S(1)}, f32[1,4,514]{2,1,0:T(4,128)S(1)}, u32[]{:S(2)}, u32[]{:S(2)}) collective-permute-start(f32[1,4,514]{2,1,0:T(4,128)S(1)} %get-tuple-element.26), channel_id=1, source_target_pairs={{8,0},{16,8},{24,16},{9,1},{17,9},{25,17},{10,2},{18,10},{26,18},{... | collective-permute-start | bytes 24680 | tf_op jit(solution)/shard_map/ppermute | solution.py:175
  16.4 14.5 %collective-permute-start.4 = (f32[2,23,16,128]{3,2,1,0:T(8,128)S(1)}, f32[2,23,16,128]{3,2,1,0:T(8,128)S(1)}, u32[]{:S(2)}, u32[]{:S(2)}) collective-permute-start(f32[2,23,16,128]{3,2,1,0:T(8,128)S(1)} %pad_maximum_fusion), channel_id=1, source_target_pairs={{0,16},{8,24},{16,0},{24,8},{1,17},{9,25},{17,1},{25,9},{2,18},{10... | collective-permute-start | bytes 1130504 | tf_op jit(solution)/shard_map/ppermute | solution.py:429
  23.7 10.9 %collective-permute-start.1 = (f32[23,16,128]{2,1,0:T(8,128)S(1)}, f32[23,16,128]{2,1,0:T(8,128)S(1)}, u32[]{:S(2)}, u32[]{:S(2)}) collective-permute-start(f32[23,16,128]{2,1,0:T(8,128)S(1)} %select_bitcast_fusion), channel_id=1, source_target_pairs={{0,16},{8,24},{16,0},{24,8},{1,17},{9,25},{17,1},{25,9},{2,18},{10... | collective-permute-start | bytes 565256 | tf_op jit(solution)/shard_map/ppermute | solution.py:429
  30.9 5.1 %collective-permute-start.5 = (f32[2,23,16,128]{3,2,1,0:T(8,128)S(1)}, f32[2,23,16,128]{3,2,1,0:T(8,128)S(1)}, u32[]{:S(2)}, u32[]{:S(2)}) collective-permute-start(f32[2,23,16,128]{3,2,1,0:T(8,128)S(1)} %collective-permute-done.4.refs_8_), channel_id=1, source_target_pairs={{0,8},{8,0},{16,24},{24,16},{1,9},{9,1},{17,25},{25,17},{2,10},{10... | collective-permute-start | bytes 1130504 | tf_op jit(solution)/shard_map/ppermute | solution.py:429
  34.5 1.4 %collective-permute-start.2 = (f32[23,16,128]{2,1,0:T(8,128)S(1)}, f32[23,16,128]{2,1,0:T(8,128)S(1)}, u32[]{:S(2)}, u32[]{:S(2)}) collective-permute-start(f32[23,16,128]{2,1,0:T(8,128)S(1)} %collective-permute-done.1.refs_4_), channel_id=1, source_target_pairs={{0,8},{8,0},{16,24},{24,16},{1,9},{9,1},{17,25},{25,17},{2,10},{10... | collective-permute-start | bytes 565256 | tf_op jit(solution)/shard_map/ppermute | solution.py:429
  40.4 9.2 %collective-permute-start.10 = (f32[2,3,16,128]{3,2,1,0:T(8,128)}, f32[2,3,16,128]{3,2,1,0:T(8,128)S(1)}, u32[]{:S(2)}, u32[]{:S(2)}) collective-permute-start(f32[2,3,16,128]{3,2,1,0:T(8,128)} %get-tuple-element.18), channel_id=1, source_target_pairs={{0,5},{1,4},{2,7},{3,6},{4,1},{5,0},{6,3},{7,2},{8,13},{9,12},{10,... | collective-permute-start | bytes 147464 | tf_op jit(solution)/shard_map/ppermute | solution.py:429
  44.0 7.6 %collective-permute-start.11 = (f32[2,3,16,128]{3,2,1,0:T(8,128)}, f32[2,3,16,128]{3,2,1,0:T(8,128)S(1)}, u32[]{:S(2)}, u32[]{:S(2)}) collective-permute-start(f32[2,3,16,128]{3,2,1,0:T(8,128)} %get-tuple-element.19), channel_id=1, source_target_pairs={{0,6},{1,7},{2,4},{3,5},{4,2},{5,3},{6,0},{7,1},{8,14},{9,15},{10,... | collective-permute-start | bytes 147464 | tf_op jit(solution)/shard_map/ppermute | solution.py:429
  45.5 8.8 %collective-permute-start.12 = (f32[2,3,16,128]{3,2,1,0:T(8,128)S(1)}, f32[2,3,16,128]{3,2,1,0:T(8,128)S(1)}, u32[]{:S(2)}, u32[]{:S(2)}) collective-permute-start(f32[2,3,16,128]{3,2,1,0:T(8,128)S(1)} %copy-done.29), channel_id=1, source_target_pairs={{0,7},{1,6},{2,5},{3,4},{4,3},{5,2},{6,1},{7,0},{8,15},{9,14},{10,... | collective-permute-start | bytes 147464 | tf_op jit(solution)/shard_map/ppermute | solution.py:429
  48.0 6.4 %collective-permute-start.6 = (f32[2,3,16,128]{3,2,1,0:T(8,128)S(1)}, f32[2,3,16,128]{3,2,1,0:T(8,128)S(1)}, u32[]{:S(2)}, u32[]{:S(2)}) collective-permute-start(f32[2,3,16,128]{3,2,1,0:T(8,128)S(1)} %copy-done.28), channel_id=1, source_target_pairs={{0,1},{1,0},{2,3},{3,2},{4,5},{5,4},{6,7},{7,6},{8,9},{9,8},{10,11... | collective-permute-start | bytes 147464 | tf_op jit(solution)/shard_map/ppermute | solution.py:429
  49.5 4.9 %collective-permute-start.7 = (f32[2,3,16,128]{3,2,1,0:T(8,128)S(1)}, f32[2,3,16,128]{3,2,1,0:T(8,128)S(1)}, u32[]{:S(2)}, u32[]{:S(2)}) collective-permute-start(f32[2,3,16,128]{3,2,1,0:T(8,128)S(1)} %copy-done.27), channel_id=1, source_target_pairs={{0,2},{1,3},{2,0},{3,1},{4,6},{5,7},{6,4},{7,5},{8,10},{9,11},{10,... | collective-permute-start | bytes 147464 | tf_op jit(solution)/shard_map/ppermute | solution.py:429
  49.6 5.1 %collective-permute-start.8 = (f32[2,3,16,128]{3,2,1,0:T(8,128)S(1)}, f32[2,3,16,128]{3,2,1,0:T(8,128)S(1)}, u32[]{:S(2)}, u32[]{:S(2)}) collective-permute-start(f32[2,3,16,128]{3,2,1,0:T(8,128)S(1)} %copy-done.26), channel_id=1, source_target_pairs={{0,3},{1,2},{2,1},{3,0},{4,7},{5,6},{6,5},{7,4},{8,11},{9,10},{10,... | collective-permute-start | bytes 147464 | tf_op jit(solution)/shard_map/ppermute | solution.py:429
  51.6 5.1 %collective-permute-start.9 = (f32[2,3,16,128]{3,2,1,0:T(8,128)S(1)}, f32[2,3,16,128]{3,2,1,0:T(8,128)S(1)}, u32[]{:S(2)}, u32[]{:S(2)}) collective-permute-start(f32[2,3,16,128]{3,2,1,0:T(8,128)S(1)} %copy-done.25), channel_id=1, source_target_pairs={{0,4},{1,5},{2,6},{3,7},{4,0},{5,1},{6,2},{7,3},{8,12},{9,13},{10,... | collective-permute-start | bytes 147464 | tf_op jit(solution)/shard_map/ppermute | solution.py:429
  65.4 40.0 %copy-start.6 = (f32[16,4,512]{2,1,0:T(4,128)}, f32[16,4,512]{2,1,0:T(4,128)S(1)}, u32[]{:S(2)}) copy-start(f32[16,4,512]{2,1,0:T(4,128)S(1)} %get-tuple-element.22.refs_3_) | copy-start | bytes 393220
  65.4 5.0 %collective-permute-start.20 = (f32[16,4,512]{2,1,0:T(4,128)S(1)}, f32[16,4,512]{2,1,0:T(4,128)S(1)}, u32[]{:S(2)}, u32[]{:S(2)}) collective-permute-start(f32[16,4,512]{2,1,0:T(4,128)S(1)} %get-tuple-element.22.refs_3_), channel_id=1, source_target_pairs={{0,2},{1,3},{2,0},{3,1},{4,6},{5,7},{6,4},{7,5},{8,10},{9,11},{10,... | collective-permute-start | bytes 393224 | tf_op jit(solution)/shard_map/ppermute | solution.py:438
  65.4 5.6 %collective-permute-start.21 = (f32[16,4,512]{2,1,0:T(4,128)S(1)}, f32[16,4,512]{2,1,0:T(4,128)S(1)}, u32[]{:S(2)}, u32[]{:S(2)}) collective-permute-start(f32[16,4,512]{2,1,0:T(4,128)S(1)} %get-tuple-element.22.refs_3_), channel_id=1, source_target_pairs={{2,4},{3,5},{4,2},{5,3},{10,12},{11,13},{12,10},{13,11},{18,20},{1... | collective-permute-start | bytes 393224 | tf_op jit(solution)/shard_map/ppermute | solution.py:438
  70.4 35.1 %copy-start.13 = (f32[16,4,512]{2,1,0:T(4,128)}, f32[16,4,512]{2,1,0:T(4,128)S(1)}, u32[]{:S(2)}) copy-start(f32[16,4,512]{2,1,0:T(4,128)S(1)} %collective-permute-done.20.refs_4_) | copy-start | bytes 393220
  70.4 4.1 %collective-permute-start.23 = (f32[16,4,512]{2,1,0:T(4,128)S(1)}, f32[16,4,512]{2,1,0:T(4,128)S(1)}, u32[]{:S(2)}, u32[]{:S(2)}) collective-permute-start(f32[16,4,512]{2,1,0:T(4,128)S(1)} %collective-permute-done.20.refs_4_), channel_id=1, source_target_pairs={{2,4},{3,5},{4,2},{5,3},{10,12},{11,13},{12,10},{13,11},{18,20},{1... | collective-permute-start | bytes 393224 | tf_op jit(solution)/shard_map/ppermute | solution.py:438
  71.1 9.6 %collective-permute-start.22 = (f32[16,4,512]{2,1,0:T(4,128)S(1)}, f32[16,4,512]{2,1,0:T(4,128)S(1)}, u32[]{:S(2)}, u32[]{:S(2)}) collective-permute-start(f32[16,4,512]{2,1,0:T(4,128)S(1)} %collective-permute-done.21), channel_id=1, source_target_pairs={{2,0},{3,1},{4,6},{5,7},{10,8},{11,9},{12,14},{13,15},{18,16},{19,... | collective-permute-start | bytes 393224 | tf_op jit(solution)/shard_map/ppermute | solution.py:438
  72.4 33.0 %collective-permute-start.25 = (f32[16,4,512]{2,1,0:T(4,128)S(1)}, f32[16,4,512]{2,1,0:T(4,128)S(1)}, u32[]{:S(2)}, u32[]{:S(2)}) collective-permute-start(f32[16,4,512]{2,1,0:T(4,128)S(1)} %get-tuple-element.22.refs_3_), channel_id=1, source_target_pairs={{0,1},{1,0},{2,3},{3,2},{4,5},{5,4},{6,7},{7,6},{8,9},{9,8},{10,11... | collective-permute-start | bytes 393224 | tf_op jit(solution)/shard_map/ppermute | solution.py:429
  73.9 31.5 %collective-permute-start.26 = (f32[16,4,512]{2,1,0:T(4,128)S(1)}, f32[16,4,512]{2,1,0:T(4,128)S(1)}, u32[]{:S(2)}, u32[]{:S(2)}) collective-permute-start(f32[16,4,512]{2,1,0:T(4,128)S(1)} %collective-permute-done.20.refs_4_), channel_id=1, source_target_pairs={{0,1},{1,0},{2,3},{3,2},{4,5},{5,4},{6,7},{7,6},{8,9},{9,8},{10,11... | collective-permute-start | bytes 393224 | tf_op jit(solution)/shard_map/ppermute | solution.py:429
  74.5 8.8 %collective-permute-start.24 = (f32[16,4,512]{2,1,0:T(4,128)S(1)}, f32[16,4,512]{2,1,0:T(4,128)S(1)}, u32[]{:S(2)}, u32[]{:S(2)}) collective-permute-start(f32[16,4,512]{2,1,0:T(4,128)S(1)} %collective-permute-done.23), channel_id=1, source_target_pairs={{2,0},{3,1},{4,6},{5,7},{10,8},{11,9},{12,14},{13,15},{18,16},{19,... | collective-permute-start | bytes 393224 | tf_op jit(solution)/shard_map/ppermute | solution.py:438
  80.7 24.7 %copy-start.7 = (f32[8,8,512]{2,1,0:T(8,128)}, f32[8,8,512]{2,1,0:T(8,128)S(1)}, u32[]{:S(2)}) copy-start(f32[8,8,512]{2,1,0:T(8,128)S(1)} %broadcast_select_fusion.1) | copy-start | bytes 393220
  80.7 24.7 %collective-permute-start.27 = (f32[16,4,512]{2,1,0:T(4,128)S(1)}, f32[16,4,512]{2,1,0:T(4,128)S(1)}, u32[]{:S(2)}, u32[]{:S(2)}) collective-permute-start(f32[16,4,512]{2,1,0:T(4,128)S(1)} %bitcast.39), channel_id=1, source_target_pairs={{0,1},{1,0},{2,3},{3,2},{4,5},{5,4},{6,7},{7,6},{8,9},{9,8},{10,11... | collective-permute-start | bytes 393224 | tf_op jit(solution)/shard_map/ppermute | solution.py:429
  83.3 22.1 %collective-permute-start.28 = (f32[16,4,512]{2,1,0:T(4,128)S(1)}, f32[16,4,512]{2,1,0:T(4,128)S(1)}, u32[]{:S(2)}, u32[]{:S(2)}) collective-permute-start(f32[16,4,512]{2,1,0:T(4,128)S(1)} %bitcast.41), channel_id=1, source_target_pairs={{0,1},{1,0},{2,3},{3,2},{4,5},{5,4},{6,7},{7,6},{8,9},{9,8},{10,11... | collective-permute-start | bytes 393224 | tf_op jit(solution)/shard_map/ppermute | solution.py:429
  84.5 1.3 %collective-permute-start.15 = (f32[1,1]{1,0:T(1,128)}, f32[1,1]{1,0:T(1,128)}, u32[]{:S(2)}, u32[]{:S(2)}) collective-permute-start(f32[1,1]{1,0:T(1,128)} %bitcast.18), channel_id=1, source_target_pairs={{0,8},{8,0},{16,24},{24,16},{1,9},{9,1},{17,25},{25,17},{2,10},{10... | collective-permute-start | bytes 20 | tf_op jit(solution)/shard_map/ppermute | solution.py:429
  87.1 3.7 %collective-permute-start.16 = (f32[1,1]{1,0:T(1,128)}, f32[1,1]{1,0:T(1,128)}, u32[]{:S(2)}, u32[]{:S(2)}) collective-permute-start(f32[1,1]{1,0:T(1,128)} %add.138), channel_id=1, source_target_pairs={{0,16},{8,24},{16,0},{24,8},{1,17},{9,25},{17,1},{25,9},{2,18},{10... | collective-permute-start | bytes 20 | tf_op jit(solution)/shard_map/ppermute | solution.py:429
  91.4 3.7 %collective-permute-start.17 = (f32[1,1]{1,0:T(1,128)}, f32[1,1]{1,0:T(1,128)}, u32[]{:S(2)}, u32[]{:S(2)}) collective-permute-start(f32[1,1]{1,0:T(1,128)} %add.139), channel_id=1, source_target_pairs={{0,1},{1,0},{2,3},{3,2},{4,5},{5,4},{6,7},{7,6},{8,9},{9,8},{10,11... | collective-permute-start | bytes 20 | tf_op jit(solution)/shard_map/ppermute | solution.py:429
  95.7 3.7 %collective-permute-start.18 = (f32[1,1]{1,0:T(1,128)}, f32[1,1]{1,0:T(1,128)}, u32[]{:S(2)}, u32[]{:S(2)}) collective-permute-start(f32[1,1]{1,0:T(1,128)} %add.140), channel_id=1, source_target_pairs={{0,2},{1,3},{2,0},{3,1},{4,6},{5,7},{6,4},{7,5},{8,10},{9,11},{10,... | collective-permute-start | bytes 20 | tf_op jit(solution)/shard_map/ppermute | solution.py:429
  100.1 4.6 %collective-permute-start.19 = (f32[1,1]{1,0:T(1,128)}, f32[1,1]{1,0:T(1,128)}, u32[]{:S(2)}, u32[]{:S(2)}) collective-permute-start(f32[1,1]{1,0:T(1,128)} %add.141), channel_id=1, source_target_pairs={{0,4},{1,5},{2,6},{3,7},{4,0},{5,1},{6,2},{7,3},{8,12},{9,13},{10,... | collective-permute-start | bytes 20 | tf_op jit(solution)/shard_map/ppermute | solution.py:429
  (28 other events, 158.6 us)

commit v3 on v2

--- a/solution.py
+++ b/solution.py
@@ -269,34 +269,26 @@
     return jnp.clip(first, 0, (blocks - WINDOW) * LANES)
 
 
-def residual_kernel(dims, parts_n, ints_ref, trig_ref, proj_ref, near_ref, far_c_ref, far_o_ref, own_ref, pair_ref, cross_c_ref, cross_o_ref, *rest):
+def residual_kernel(dims, parts_n, ints_ref, trig_ref, *rest):
     rows_n, cols_n, bins_n, base, blocks = dims
-    outs = rest[:parts_n]
-    near_pad, far_pad, sino, res = rest[parts_n:]
-    views_n, _, band, _ = proj_ref.shape
-    slab, core, part = ints_ref[0], ints_ref[1], ints_ref[2]
-    for pad in (near_pad, far_pad):
+    projs, sinos, outs = rest[:4], rest[4:8], rest[8 : 8 + parts_n]
+    pads = rest[8 + parts_n : 11 + parts_n]
+    sino, res = rest[11 + parts_n :]
+    views_n, _, band, _ = projs[0].shape
+    slab, part = ints_ref[0], ints_ref[1]
+    for other in range(1, 4):
+        pad = pads[other - 1]
         pad[:, :, 0:band] = jnp.zeros((views_n, blocks, band, LANES), jnp.float32)
-        pad[:, :, 2 * band:] = jnp.zeros((views_n, blocks, band, LANES), jnp.float32)
-    near_pad[:, :, band:2 * band] = near_ref[...]
-    far_pad[core, :, band:2 * band] = far_c_ref[...]
-    far_pad[1 - core, :, band:2 * band] = far_o_ref[...]
-
-    def rows_of(k):
-        return pl.ds(pl.multiple_of(k * band, band), band)
-
-    sino[:, :, rows_of(slab)] = own_ref[...]
-    sino[:, :, rows_of(slab ^ 1)] = pair_ref[...]
-    sino[core, :, rows_of(slab ^ 2)] = cross_c_ref[0]
-    sino[core, :, rows_of(slab ^ 3)] = cross_c_ref[1]
-    sino[1 - core, :, rows_of(slab ^ 3)] = cross_o_ref[0]
-    sino[1 - core, :, rows_of(slab ^ 2)] = cross_o_ref[1]
+        pad[:, :, 2 * band :] = jnp.zeros((views_n, blocks, band, LANES), jnp.float32)
+        pad[:, :, band : 2 * band] = projs[other][...]
+    for other in range(4):
+        rows = pl.ds(pl.multiple_of((slab ^ other) * band, band), band)
+        sino[:, :, rows] = sinos[other][:, 0:blocks]
     for v in range(views_n):
-        start, near, far = ints_ref[3 + 3 * v], ints_ref[4 + 3 * v], ints_ref[5 + 3 * v]
-        res[v, 0:blocks] = (
-            (proj_ref[v] + near_pad[v, :, pl.ds(near, band), :])
-            + far_pad[v, :, pl.ds(far, band), :]
-        ) - sino[v, :, pl.ds(start, band), :]
+        value = projs[0][v]
+        for other in range(1, 4):
+            value = value + pads[other - 1][v, :, pl.ds(ints_ref[2 + 4 * v + other], band), :]
+        res[v, 0:blocks] = value - sino[v, :, pl.ds(ints_ref[2 + 4 * v], band), :]
         res[v, blocks] = jnp.zeros((band, LANES), jnp.float32)
     lane = lax.broadcasted_iota(jnp.int32, (band, LANES), 1)
     per_n = cols_n // parts_n
@@ -327,6 +319,7 @@
         scratch_shapes=[
             pltpu.VMEM((views_n, blocks, 3 * band, LANES), jnp.float32),
             pltpu.VMEM((views_n, blocks, 3 * band, LANES), jnp.float32),
+            pltpu.VMEM((views_n, blocks, 3 * band, LANES), jnp.float32),
             pltpu.VMEM((views_n, blocks, 4 * band, LANES), jnp.float32),
             pltpu.VMEM((views_n, blocks + 1, band, LANES), jnp.float32),
         ],
@@ -339,7 +332,7 @@
     pieces = rest[:parts_n]
     out_ref, trig_ref, starts_ref = rest[parts_n:]
     per_n = cols_n // parts_n
-    part = ints_ref[2]
+    part = ints_ref[1]
     lane8 = lax.broadcasted_iota(jnp.int32, (8, LANES), 1)
     lane = lax.broadcasted_iota(jnp.int32, (16, LANES), 1)
     total_n = parts_n * views_n
@@ -429,7 +422,7 @@
     return lax.ppermute(x, axis, [(i, i ^ bit) for i in range(lax.axis_size(axis))])
 
 
-def gathered(piece):
+def gathered(piece, squares):
     part = lax.axis_index("view")
     depth = part // 2
     end = (depth == 0) | (depth == 3)
@@ -437,20 +430,27 @@
     def along(x, pairs):
         return lax.ppermute(x, "view", [(2 * a + y, 2 * b + y) for a, b in pairs for y in (0, 1)])
 
-    across = [swapped(piece, "view", 1)]
+    first = swapped(piece, "view", 1)
     second = along(piece, [(0, 1), (1, 0), (2, 3), (3, 2)])
     middle = along(piece, [(1, 2), (2, 1)])
-    across.append(swapped(second, "view", 1))
+    squares = squares + swapped(squares, "slab", 1) + (swapped(squares, "slab", 2) + swapped(squares, "slab", 3))
+    first, second, middle, squares = lax.optimization_barrier((first, second, middle, squares))
+    across = [first, swapped(second, "view", 1)]
     onward = along(middle, [(1, 0), (2, 3)])
     middle_last = along(second, [(1, 2), (2, 1)])
+    squares = squares + swapped(squares, "view", 1) + (swapped(squares, "view", 2) + swapped(squares, "view", 3))
+    onward, middle_last, squares = lax.optimization_barrier((onward, middle_last, squares))
     third = jnp.where(end, onward, middle)
     across.append(swapped(third, "view", 1))
-    last = jnp.where(end, along(middle_last, [(1, 0), (2, 3)]), middle_last)
+    last = along(middle_last, [(1, 0), (2, 3)])
+    squares = squares + swapped(squares, "view", 4)
+    last, squares = lax.optimization_barrier((last, squares))
+    last = jnp.where(end, last, middle_last)
     across.append(swapped(last, "view", 1))
     upper = depth // 2
     depths = [depth, depth ^ 1, 2 - upper, 3 - 3 * upper]
     order = jnp.stack([2 * d + part % 2 for d in depths] + [2 * d + 1 - part % 2 for d in depths])
-    return order.astype(jnp.int32), [piece, second, third, last] + across
+    return order.astype(jnp.int32), [piece, second, third, last] + across, squares
 
 
 def local_split(volume, sinogram, curvature, angles, offsets):
@@ -462,70 +462,60 @@
     slab_count = lax.axis_size("slab")
     parts_n = lax.axis_size("view")
     slab = lax.axis_index("slab")
-    core = slab % 2
     part = lax.axis_index("view")
     per_n = cols_n // parts_n
 
+    angle_rad = angles.astype(jnp.float32) * (2.0 * math.pi / ROTATION_VIEWS)
+    trig = jnp.concatenate([jnp.cos(angle_rad), jnp.sin(angle_rad)])
+
+    def outer(at):
+        face = lax.dynamic_slice(volume, (at, 0, part * per_n), (1, rows_n, per_n))
+        return face.reshape(1, 1, slices_n, LANES)
+
     measured = sinogram[:, :, base : base + blocks * LANES]
     measured = measured.reshape(views_n, slices_n, blocks, LANES).transpose(0, 2, 1, 3)
+    faces = jnp.concatenate([outer(0), outer(slices_n - 1)], axis=0)
+    measured = jnp.concatenate([measured, faces], axis=1)
+    cross_rows = swapped(measured, "slab", 2)
     pair_rows = swapped(measured, "slab", 1)
-    chip_rows = jnp.stack(
-        [
-            lax.dynamic_index_in_dim(measured, core, 0, keepdims=False),
-            lax.dynamic_index_in_dim(pair_rows, core, 0, keepdims=False),
-        ]
-    )
-    cross_rows = swapped(chip_rows, "slab", 2)
-    cross_other = swapped(cross_rows, "slab", 1)
-
-    angle_rad = angles.astype(jnp.float32) * (2.0 * math.pi / ROTATION_VIEWS)
-    trig = jnp.concatenate([jnp.cos(angle_rad), jnp.sin(angle_rad)])
+    trig, measured = lax.optimization_barrier((trig, measured))
     proj = project(trig, volume, bins_n, base, blocks, views_n)
+    cross_pair_rows = swapped(cross_rows, "slab", 1)
+    cross = swapped(proj, "slab", 2)
     near = swapped(proj, "slab", 1)
-    turned = offsets[:, 0] > slices_n
-    chip = slab // 2
-    edge_core = jnp.where(turned, chip, 1 - chip)
-    sends_own = lax.dynamic_index_in_dim(edge_core, core, 0, keepdims=False) == core
-    edge = jnp.where(
-        sends_own,
-        lax.dynamic_index_in_dim(proj, core, 0, keepdims=False),
-        lax.dynamic_index_in_dim(near, core, 0, keepdims=False),
-    )
-    far = swapped(edge, "slab", 2)
-    far_other = swapped(far, "slab", 1)
+    cross_pair = swapped(cross, "slab", 1)
 
     def of(k):
         return lax.dynamic_index_in_dim(offsets, k, 1, keepdims=False)
 
-    far_slab = 2 * (1 - chip) + jnp.where(turned, 1 - chip, chip)
     start = of(slab)
-    far_start = jnp.take_along_axis(offsets, far_slab[:, None], axis=1)[:, 0]
-
-    def shift(other):
-        return slices_n + jnp.clip(start - other, -slices_n, slices_n)
-
-    table = jnp.stack([start, shift(of(slab ^ 1)), shift(far_start)], axis=1).reshape(-1)
-    ints = jnp.concatenate([jnp.stack([slab, core, part]).astype(jnp.int32), table])
+    shifts = [slices_n + jnp.clip(start - of(slab ^ k), -slices_n, slices_n) for k in (1, 2, 3)]
+    table = jnp.stack([start] + shifts, axis=1).reshape(-1)
+    ints = jnp.concatenate([jnp.stack([slab, part]).astype(jnp.int32), table])
     windows = residual_windows(
-        dims, parts_n, ints, trig,
-        [proj, near, far, far_other, measured, pair_rows, cross_rows, cross_other],
+        dims,
+        parts_n,
+        ints,
+        trig,
+        [proj, near, cross, cross_pair, measured, pair_rows, cross_rows, cross_pair_rows],
     )
     pieces = [windows[0]] + [swapped(windows[r], "view", r) for r in range(1, parts_n)]
     data_grad = gather_views(dims, parts_n, ints, pieces).transpose(1, 0, 2)
 
+    def face_of(rows, which):
+        return rows[which, blocks].reshape(1, rows_n, per_n)
+
+    odd = slab % 2 == 1
+    below = jnp.where(odd, face_of(pair_rows, 1), jnp.where(slab == 0, 0.0, face_of(cross_pair_rows, 1)))
+    above = jnp.where(odd, jnp.where(slab == slab_count - 1, 0.0, face_of(cross_pair_rows, 0)), face_of(pair_rows, 0))
     wide = jnp.pad(volume, ((0, 0), (0, 0), (1, 1)))
     block = lax.dynamic_slice_in_dim(wide, part * per_n, per_n + 2, axis=2)
-    padded = jnp.pad(padded_2(block, (("slab", 0),), 1), ((0, 0), (1, 1), (0, 0)))
-    tv_grad = tv_padded(padded)
+    sides = ((0, 0), (0, 0), (1, 1))
+    block = jnp.concatenate([jnp.pad(below, sides), block, jnp.pad(above, sides)], axis=0)
+    tv_grad = tv_padded(jnp.pad(block, ((0, 0), (1, 1), (0, 0))))
     curv = lax.dynamic_slice_in_dim(curvature, part * per_n, per_n, axis=2)
     direction = (data_grad + tv_weight * tv_grad) / curv
-    squares = jnp.sum(direction * direction).reshape(1, 1)
-    for axis in ("slab", "view"):
-        bit = 1
-        while bit < lax.axis_size(axis):
-            squares = squares + swapped(squares, axis, bit)
-            bit *= 2
-    order, parts = gathered(direction)
+    order, parts, squares = gathered(direction, jnp.sum(direction * direction).reshape(1, 1))
     voxel_count = slices_n * slab_count * rows_n * cols_n
     factor = jnp.minimum(1.0, step_limit / jnp.sqrt(squares / voxel_count + epsilon))
     return finish(order, factor.reshape(1), volume, parts)

time: 109 us -> 104 us (0.954)
  waiting for transfers between devices: 34.4 us -> 25.5 us
  starting transfers between devices: 37.6 us -> 41.5 us
  local copies, waits for them, and re-layouts: 6.4 us -> 5.07 us
    ppermute x22 -> x24, starting transfers between devices: 30.1 us -> 37.6 us  [swapped(): lax.ppermute(x, axis, [(i, i ^ bit) for i in range(lax.axis_size(axis))])]
    ppermute x5, waiting for transfers between devices: 11.7 us -> 4.81 us  [along(): lax.ppermute(x, 'view', [(2 * a + y, 2 * b + y) for a, b in pairs for y i...]
    ppermute x2 -> x0, starting transfers between devices: 3.65 us -> none  [the longest x1 2.36 us: padded_2(): lax.ppermute(tail, axis, [(i, (i + 1) % count) for i in range(ends)])]
    ppermute x22 -> x24, waiting for transfers between devices: 22.7 us -> 20.7 us  [swapped(): lax.ppermute(x, axis, [(i, i ^ bit) for i in range(lax.axis_size(axis))])]
    reshape x2 -> x3, local copies, waits for them, and re-layouts: 1.33 us -> 0.1 us  [the longest x1 0.08 us: local_split(): table = jnp.stack([start] + shifts, axis=1).reshape(-1)]
    transpose x0 -> x1, local copies, waits for them, and re-layouts: none -> 1.15 us  [local_split(): measured.reshape(views_n, slices_n, blocks, LANES).transpose(0, 2, 1, 3)]
    unnamed x63 -> x46, local copies, waits for them, and re-layouts: 2.79 us -> 2.1 us
  transfers between devices with their start and end apart: 29 -> 29, of which waited for: 13 -> 10; matrix products, arithmetic and copies ran while one was open for 4% -> 3% of each run, Pallas kernels for 12% -> 10%
where the time goes in v3:
time: 104 us
  starting transfers between devices  41.5 us (40%)
  waiting for transfers between devices  25.5 us (25%)
  Pallas kernels  21.6 us (21%)
  between operations  5.5 us (5%)
  local copies, waits for them, and re-layouts  5.07 us (5%)
  other arithmetic  4.62 us (4%)
    ppermute x24, starting transfers between devices, swapped(): lax.ppermute(x, axis, [(i, i ^ bit) for i in range(lax.axis_size(axis))])  37.6 us
    ppermute x24, waiting for transfers between devices, swapped(): lax.ppermute(x, axis, [(i, i ^ bit) for i in range(lax.axis_size(axis))])  20.7 us
    pallas_call x1, Pallas kernels, project(): pl.pallas_call(body, out_shape=jax.ShapeDtypeStruct((views_n, blocks_n, s...  9.87 us
    pallas_call x1, Pallas kernels, gather_views(): pl.pallas_call(body, out_shape=jax.ShapeDtypeStruct((rows_n, slices_n, co...  5.94 us
    ppermute x5, waiting for transfers between devices, along(): lax.ppermute(x, 'view', [(2 * a + y, 2 * b + y) for a, b in pairs for y i...  4.81 us
    ppermute x5, starting transfers between devices, along(): lax.ppermute(x, 'view', [(2 * a + y, 2 * b + y) for a, b in pairs for y i...  3.9 us
    pallas_call x1, Pallas kernels, residual_windows(): pl.pallas_call(body, out_shape=[jax.ShapeDtypeStruct((views_n, WINDOW, ba...  3.12 us
    pallas_call x1, Pallas kernels, finish(): pl.pallas_call(lambda *refs: finish_kernel(parts_n, *refs), out_shape=jax...  2.7 us
  transfers between devices with their start and end apart: 29, of which 10 were waited for; matrix products, arithmetic and copies ran while one was open for 3% of the time, Pallas kernels for 10%

profile of v3, /device:TPU:0, one launch (start us, length us, event | category | flops | bytes accessed | tf_op | source)
XLA Modules:
  0.0 103.9 jit_solution(3335011193039380957)
XLA Ops:
  0.0 0.7 constant_dynamic-slice_fusion.1
  0.8 1.2 %bitcast_bitcast_fusion = f32[2,23,16,128]{3,2,1,0:T(8,128)S(1)} fusion(f32[2,16,4096]{2,1,0:T(8,128)} %param.6), kind=kLoop, calls=%fused_computation.7 | loop fusion | bytes 753664 | tf_op jit(solution)/shard_map/transpose | solution.py:476
  2.0 3.0 %collective-permute-start.4 = (f32[2,24,16,128]{3,2,1,0:T(8,128)S(1)}, f32[2,24,16,128]{3,2,1,0:T(8,128)S(1)}, u32[]{:S(2)}, u32[]{:S(2)}) collective-permute-start(f32[2,24,16,128]{3,2,1,0:T(8,128)S(1)} %maximum_maximum_fusion.refs_6_), channel_id=1, source_target_pairs={{0,16},{8,24},{16,0},{24,8},{1,17},{9,25},{17,1},{25,9},{2,18},{10... | collective-permute-start | bytes 1179656 | tf_op jit(solution)/shard_map/ppermute | solution.py:422
  5.7 9.9 %project.1.refs_2_ = f32[2,23,16,128]{3,2,1,0:T(8,128)} custom-call(f32[4]{0:T(128)} %pad_maximum_fusion.2.refs_0_.refs_1_, f32[16,4,4096]{2,1,0:T(4,128)} %refs_2_.1), custom_call_target="tpu_custom_call" | custom-call | tf_op jit(solution)/shard_map/project/pallas_call | solution.py:100
  16.3 9.8 %collective-permute-done.1.refs_4_ = f32[2,23,16,128]{3,2,1,0:T(8,128)S(1)} collective-permute-done((f32[2,23,16,128]{3,2,1,0:T(8,128)}, f32[2,23,16,128]{3,2,1,0:T(8,128)S(1)}, u32[]{:S(2)}, u32[]{:S(2)}) %collective-permute-start.1) | collective-permute-done | bytes 376864 | tf_op jit(solution)/shard_map/ppermute | solution.py:422
  28.4 0.7 copy-done.6
  29.2 3.1 %residual_windows.1 = (f32[2,3,16,128]{3,2,1,0:T(8,128)}, f32[2,3,16,128]{3,2,1,0:T(8,128)}, f32[2,3,16,128]{3,2,1,0:T(8,128)}, f32[2,3,16,128]{3,2,1,0:T(8,128)...) custom-call(s32[10]{0:T(128)} %pad_add_fusion.1.refs_0_, ...), custom_call_target="tpu_custom_call" | custom-call | tf_op jit(solution)/shard_map/residual_windows/pallas_call | solution.py:314
  32.3 3.6 %collective-permute-start.10 = (f32[2,3,16,128]{3,2,1,0:T(8,128)}, f32[2,3,16,128]{3,2,1,0:T(8,128)S(1)}, u32[]{:S(2)}, u32[]{:S(2)}) collective-permute-start(f32[2,3,16,128]{3,2,1,0:T(8,128)} %get-tuple-element.31), channel_id=1, source_target_pairs={{0,5},{1,4},{2,7},{3,6},{4,1},{5,0},{6,3},{7,2},{8,13},{9,12},{10,... | collective-permute-start | bytes 147464 | tf_op jit(solution)/shard_map/ppermute | solution.py:422
  35.9 1.3 %collective-permute-start.11 = (f32[2,3,16,128]{3,2,1,0:T(8,128)}, f32[2,3,16,128]{3,2,1,0:T(8,128)S(1)}, u32[]{:S(2)}, u32[]{:S(2)}) collective-permute-start(f32[2,3,16,128]{3,2,1,0:T(8,128)} %get-tuple-element.32), channel_id=1, source_target_pairs={{0,6},{1,7},{2,4},{3,5},{4,2},{5,3},{6,0},{7,1},{8,14},{9,15},{10,... | collective-permute-start | bytes 147464 | tf_op jit(solution)/shard_map/ppermute | solution.py:422
  37.2 2.4 %collective-permute-start.12 = (f32[2,3,16,128]{3,2,1,0:T(8,128)}, f32[2,3,16,128]{3,2,1,0:T(8,128)S(1)}, u32[]{:S(2)}, u32[]{:S(2)}) collective-permute-start(f32[2,3,16,128]{3,2,1,0:T(8,128)} %get-tuple-element.33), channel_id=1, source_target_pairs={{0,7},{1,6},{2,5},{3,4},{4,3},{5,2},{6,1},{7,0},{8,15},{9,14},{10,... | collective-permute-start | bytes 147464 | tf_op jit(solution)/shard_map/ppermute | solution.py:422
  39.6 1.5 %collective-permute-start.6 = (f32[2,3,16,128]{3,2,1,0:T(8,128)}, f32[2,3,16,128]{3,2,1,0:T(8,128)S(1)}, u32[]{:S(2)}, u32[]{:S(2)}) collective-permute-start(f32[2,3,16,128]{3,2,1,0:T(8,128)} %get-tuple-element.27), channel_id=1, source_target_pairs={{0,1},{1,0},{2,3},{3,2},{4,5},{5,4},{6,7},{7,6},{8,9},{9,8},{10,11... | collective-permute-start | bytes 147464 | tf_op jit(solution)/shard_map/ppermute | solution.py:422
  41.2 0.8 fusion.21
  42.1 2.0 %collective-permute-start.8 = (f32[2,3,16,128]{3,2,1,0:T(8,128)}, f32[2,3,16,128]{3,2,1,0:T(8,128)S(1)}, u32[]{:S(2)}, u32[]{:S(2)}) collective-permute-start(f32[2,3,16,128]{3,2,1,0:T(8,128)} %get-tuple-element.29), channel_id=1, source_target_pairs={{0,3},{1,2},{2,1},{3,0},{4,7},{5,6},{6,5},{7,4},{8,11},{9,10},{10,... | collective-permute-start | bytes 147464 | tf_op jit(solution)/shard_map/ppermute | solution.py:422
  44.1 2.0 %collective-permute-start.9 = (f32[2,3,16,128]{3,2,1,0:T(8,128)}, f32[2,3,16,128]{3,2,1,0:T(8,128)S(1)}, u32[]{:S(2)}, u32[]{:S(2)}) collective-permute-start(f32[2,3,16,128]{3,2,1,0:T(8,128)} %get-tuple-element.30), channel_id=1, source_target_pairs={{0,4},{1,5},{2,6},{3,7},{4,0},{5,1},{6,2},{7,3},{8,12},{9,13},{10,... | collective-permute-start | bytes 147464 | tf_op jit(solution)/shard_map/ppermute | solution.py:422
  46.2 1.1 %collective-permute-done.8.refs_4_ = f32[2,3,16,128]{3,2,1,0:T(8,128)S(1)} collective-permute-done((f32[2,3,16,128]{3,2,1,0:T(8,128)}, f32[2,3,16,128]{3,2,1,0:T(8,128)S(1)}, u32[]{:S(2)}, u32[]{:S(2)}) %collective-permute-start.8) | collective-permute-done | bytes 49184 | tf_op jit(solution)/shard_map/ppermute | solution.py:422
  47.4 2.1 %collective-permute-done.9.refs_5_ = f32[2,3,16,128]{3,2,1,0:T(8,128)S(1)} collective-permute-done((f32[2,3,16,128]{3,2,1,0:T(8,128)}, f32[2,3,16,128]{3,2,1,0:T(8,128)S(1)}, u32[]{:S(2)}, u32[]{:S(2)}) %collective-permute-start.9) | collective-permute-done | bytes 49184 | tf_op jit(solution)/shard_map/ppermute | solution.py:422
  50.0 5.9 %gather_views.1 = f32[4,16,512]{2,1,0:T(8,128)} custom-call(s32[10]{0:T(128)} %pad_add_fusion.1.refs_0_, f32[2,3,16,128]{3,2,1,0:T(8,128)} %get-tuple-element.26.refs_1_, f32[2,3,16,128]{3,2,1,0:T(8,128)} %copy-done.17, f32[2,3,16,128]{3,2,1,0:T(8,128)} %copy-done.18, f32[2,3,16,128]{3,2,1,0:T(8,128)} %copy-done.19, f32[2,3,16,128]{3,2,1,0:T(8,128)} %copy-done.20, ...), custom_call_target="tpu_custom_call" | custom-call | tf_op jit(solution)/shard_map/gather_views/pallas_call | solution.py:385
  56.0 2.1 %multiply_reduce_fusion = (f32[]{:T(128)}, f32[16,4,512]{2,1,0:T(4,128)S(1)}) fusion(f32[16,4,4096]{2,1,0:T(4,128)} %param.7, s32[]{:T(128)S(6)} %select_n.138, s32[]{:T(128)S(6)} %add.150, s32[]{:T(128)S(6)} %select_n.139, f32[18,6,514]{2,1,0:T(8,128)S(1)} %select_maximum_fusion, f32[1,4,514]{2,1,0:T(4,128)S(1)} %pad.17, ...), kind=kLoop, calls=%fused_computation.36 | loop fusion | flops 983039 | bytes 1851988 | tf_op jit(solution)/shard_map/reduce_sum | solution.py:518
  58.1 1.4 %collective-permute-start.13 = (f32[16,4,512]{2,1,0:T(4,128)S(1)}, f32[16,4,512]{2,1,0:T(4,128)S(1)}, u32[]{:S(2)}, u32[]{:S(2)}) collective-permute-start(f32[16,4,512]{2,1,0:T(4,128)S(1)} %get-tuple-element.44.refs_3_), channel_id=1, source_target_pairs={{0,1},{1,0},{2,3},{3,2},{4,5},{5,4},{6,7},{7,6},{8,9},{9,8},{10,11... | collective-permute-start | bytes 393224 | tf_op jit(solution)/shard_map/ppermute | solution.py:422
  60.8 1.5 %collective-permute-done.16 = f32[1,1]{1,0:T(1,128)} collective-permute-done((f32[1,1]{1,0:T(1,128)}, f32[1,1]{1,0:T(1,128)}, u32[]{:S(2)}, u32[]{:S(2)}) %collective-permute-start.16) | collective-permute-done | bytes 36 | tf_op jit(solution)/shard_map/ppermute | solution.py:422
  62.3 1.3 %collective-permute-start.18 = (f32[1,1]{1,0:T(1,128)}, f32[1,1]{1,0:T(1,128)}, u32[]{:S(2)}, u32[]{:S(2)}) collective-permute-start(f32[1,1]{1,0:T(1,128)} %bitcast.12), channel_id=1, source_target_pairs={{0,24},{8,16},{16,8},{24,0},{1,25},{9,17},{17,9},{25,1},{2,26},{10... | collective-permute-start | bytes 20 | tf_op jit(solution)/shard_map/ppermute | solution.py:422
  66.6 1.3 %collective-permute-start.19 = (f32[16,4,512]{2,1,0:T(4,128)S(1)}, f32[16,4,512]{2,1,0:T(4,128)S(1)}, u32[]{:S(2)}, u32[]{:S(2)}) collective-permute-start(f32[16,4,512]{2,1,0:T(4,128)S(1)} %collective-permute-done.15), channel_id=1, source_target_pairs={{2,0},{3,1},{4,6},{5,7},{10,8},{11,9},{12,14},{13,15},{18,16},{19,... | collective-permute-start | bytes 393224 | tf_op jit(solution)/shard_map/ppermute | solution.py:431
  68.6 7.9 %collective-permute-start.22 = (f32[1,1]{1,0:T(1,128)}, f32[1,1]{1,0:T(1,128)}, u32[]{:S(2)}, u32[]{:S(2)}) collective-permute-start(f32[1,1]{1,0:T(1,128)} %add.138), channel_id=1, source_target_pairs={{0,2},{1,3},{2,0},{3,1},{4,6},{5,7},{6,4},{7,5},{8,10},{9,11},{10,... | collective-permute-start | bytes 20 | tf_op jit(solution)/shard_map/ppermute | solution.py:422
  76.5 1.3 %collective-permute-start.23 = (f32[1,1]{1,0:T(1,128)}, f32[1,1]{1,0:T(1,128)}, u32[]{:S(2)}, u32[]{:S(2)}) collective-permute-start(f32[1,1]{1,0:T(1,128)} %add.138), channel_id=1, source_target_pairs={{0,3},{1,2},{2,1},{3,0},{4,7},{5,6},{6,5},{7,4},{8,11},{9,10},{10,... | collective-permute-start | bytes 20 | tf_op jit(solution)/shard_map/ppermute | solution.py:422
  77.8 2.7 %collective-permute-start.21 = (f32[1,1]{1,0:T(1,128)}, f32[1,1]{1,0:T(1,128)}, u32[]{:S(2)}, u32[]{:S(2)}) collective-permute-start(f32[1,1]{1,0:T(1,128)} %add.138), channel_id=1, source_target_pairs={{0,1},{1,0},{2,3},{3,2},{4,5},{5,4},{6,7},{7,6},{8,9},{9,8},{10,11... | collective-permute-start | bytes 20 | tf_op jit(solution)/shard_map/ppermute | solution.py:422
  80.5 0.9 collective-permute-done.21
  81.5 1.4 %collective-permute-start.26 = (f32[16,4,512]{2,1,0:T(4,128)S(1)}, f32[16,4,512]{2,1,0:T(4,128)S(1)}, u32[]{:S(2)}, u32[]{:S(2)}) collective-permute-start(f32[16,4,512]{2,1,0:T(4,128)S(1)} %collective-permute-done.14.refs_4_), channel_id=1, source_target_pairs={{0,1},{1,0},{2,3},{3,2},{4,5},{5,4},{6,7},{7,6},{8,9},{9,8},{10,11... | collective-permute-start | bytes 393224 | tf_op jit(solution)/shard_map/ppermute | solution.py:422
  84.8 3.8 %collective-permute-start.25 = (f32[1,1]{1,0:T(1,128)}, f32[1,1]{1,0:T(1,128)}, u32[]{:S(2)}, u32[]{:S(2)}) collective-permute-start(f32[1,1]{1,0:T(1,128)} %add.141), channel_id=1, source_target_pairs={{0,4},{1,5},{2,6},{3,7},{4,0},{5,1},{6,2},{7,3},{8,12},{9,13},{10,... | collective-permute-start | bytes 20 | tf_op jit(solution)/shard_map/ppermute | solution.py:422
  88.6 1.3 %collective-permute-start.24 = (f32[16,4,512]{2,1,0:T(4,128)S(1)}, f32[16,4,512]{2,1,0:T(4,128)S(1)}, u32[]{:S(2)}, u32[]{:S(2)}) collective-permute-start(f32[16,4,512]{2,1,0:T(4,128)S(1)} %collective-permute-done.20), channel_id=1, source_target_pairs={{2,0},{3,1},{4,6},{5,7},{10,8},{11,9},{12,14},{13,15},{18,16},{19,... | collective-permute-start | bytes 393224 | tf_op jit(solution)/shard_map/ppermute | solution.py:431
  90.6 4.8 %collective-permute-done.24 = f32[16,4,512]{2,1,0:T(4,128)S(1)} collective-permute-done((f32[16,4,512]{2,1,0:T(4,128)S(1)}, f32[16,4,512]{2,1,0:T(4,128)S(1)}, u32[]{:S(2)}, u32[]{:S(2)}) %collective-permute-start.24) | collective-permute-done | bytes 131104 | tf_op jit(solution)/shard_map/ppermute | solution.py:431
  96.3 4.2 %collective-permute-done.28.refs_10_ = f32[16,4,512]{2,1,0:T(4,128)S(1)} collective-permute-done((f32[16,4,512]{2,1,0:T(4,128)S(1)}, f32[16,4,512]{2,1,0:T(4,128)S(1)}, u32[]{:S(2)}, u32[]{:S(2)}) %collective-permute-start.28) | collective-permute-done | bytes 131104 | tf_op jit(solution)/shard_map/ppermute | solution.py:422
  101.2 2.7 %finish.1 = f32[16,4,4096]{2,1,0:T(4,128)} custom-call(s32[8]{0:T(128)} %stack.48.refs_0_, f32[1]{0:T(128)} %bitcast.13.refs_1_, f32[16,4,4096]{2,1,0:T(4,128)} %refs_2_.1, f32[16,4,512]{2,1,0:T(4,128)} %copy-done.2, f32[16,4,512]{2,1,0:T(4,128)} %copy-done.10, f32[16,4,512]{2,1,0:T(4,128)} %bitcast.33, f32[16,4,512]{2,1,0:T(4,128)} %bitcast.35, ...), custom_call_target="tpu_custom_call" | custom-call | tf_op jit(solution)/shard_map/finish/pallas_call | solution.py:412
  (99 shorter events, 8.6 us)
Async XLA Ops:
  2.0 24.1 %collective-permute-start.4 = (f32[2,24,16,128]{3,2,1,0:T(8,128)S(1)}, f32[2,24,16,128]{3,2,1,0:T(8,128)S(1)}, u32[]{:S(2)}, u32[]{:S(2)}) collective-permute-start(f32[2,24,16,128]{3,2,1,0:T(8,128)S(1)} %maximum_maximum_fusion.refs_6_), channel_id=1, source_target_pairs={{0,16},{8,24},{16,0},{24,8},{1,17},{9,25},{17,1},{25,9},{2,18},{10... | collective-permute-start | bytes 1179656 | tf_op jit(solution)/shard_map/ppermute | solution.py:422
  15.6 10.5 %collective-permute-start.1 = (f32[2,23,16,128]{3,2,1,0:T(8,128)}, f32[2,23,16,128]{3,2,1,0:T(8,128)S(1)}, u32[]{:S(2)}, u32[]{:S(2)}) collective-permute-start(f32[2,23,16,128]{3,2,1,0:T(8,128)} %project.1.refs_2_), channel_id=1, source_target_pairs={{0,16},{8,24},{16,0},{24,8},{1,17},{9,25},{17,1},{25,9},{2,18},{10... | collective-permute-start | bytes 1130504 | tf_op jit(solution)/shard_map/ppermute | solution.py:422
  15.6 12.0 %collective-permute-start = (f32[2,23,16,128]{3,2,1,0:T(8,128)}, f32[2,23,16,128]{3,2,1,0:T(8,128)}, u32[]{:S(2)}, u32[]{:S(2)}) collective-permute-start(f32[2,23,16,128]{3,2,1,0:T(8,128)} %project.1.refs_2_), channel_id=1, source_target_pairs={{0,8},{8,0},{16,24},{24,16},{1,9},{9,1},{17,25},{25,17},{2,10},{10... | collective-permute-start | bytes 1130504 | tf_op jit(solution)/shard_map/ppermute | solution.py:422
  15.7 12.0 %collective-permute-start.3 = (f32[2,24,16,128]{3,2,1,0:T(8,128)S(1)}, f32[2,24,16,128]{3,2,1,0:T(8,128)S(1)}, u32[]{:S(2)}, u32[]{:S(2)}) collective-permute-start(f32[2,24,16,128]{3,2,1,0:T(8,128)S(1)} %maximum_maximum_fusion.refs_6_), channel_id=1, source_target_pairs={{0,8},{8,0},{16,24},{24,16},{1,9},{9,1},{17,25},{25,17},{2,10},{10... | collective-permute-start | bytes 1179656 | tf_op jit(solution)/shard_map/ppermute | solution.py:422
  26.1 1.8 %collective-permute-start.2 = (f32[2,23,16,128]{3,2,1,0:T(8,128)S(1)}, f32[2,23,16,128]{3,2,1,0:T(8,128)}, u32[]{:S(2)}, u32[]{:S(2)}) collective-permute-start(f32[2,23,16,128]{3,2,1,0:T(8,128)S(1)} %collective-permute-done.1.refs_4_), channel_id=1, source_target_pairs={{0,8},{8,0},{16,24},{24,16},{1,9},{9,1},{17,25},{25,17},{2,10},{10... | collective-permute-start | bytes 1130504 | tf_op jit(solution)/shard_map/ppermute | solution.py:422
  26.1 2.2 %collective-permute-start.5 = (f32[2,24,16,128]{3,2,1,0:T(8,128)S(1)}, f32[2,24,16,128]{3,2,1,0:T(8,128)S(1)}, u32[]{:S(2)}, u32[]{:S(2)}) collective-permute-start(f32[2,24,16,128]{3,2,1,0:T(8,128)S(1)} %collective-permute-done.4.refs_8_), channel_id=1, source_target_pairs={{0,8},{8,0},{16,24},{24,16},{1,9},{9,1},{17,25},{25,17},{2,10},{10... | collective-permute-start | bytes 1179656 | tf_op jit(solution)/shard_map/ppermute | solution.py:422
  32.3 9.8 %collective-permute-start.10 = (f32[2,3,16,128]{3,2,1,0:T(8,128)}, f32[2,3,16,128]{3,2,1,0:T(8,128)S(1)}, u32[]{:S(2)}, u32[]{:S(2)}) collective-permute-start(f32[2,3,16,128]{3,2,1,0:T(8,128)} %get-tuple-element.31), channel_id=1, source_target_pairs={{0,5},{1,4},{2,7},{3,6},{4,1},{5,0},{6,3},{7,2},{8,13},{9,12},{10,... | collective-permute-start | bytes 147464 | tf_op jit(solution)/shard_map/ppermute | solution.py:422
  35.9 8.2 %collective-permute-start.11 = (f32[2,3,16,128]{3,2,1,0:T(8,128)}, f32[2,3,16,128]{3,2,1,0:T(8,128)S(1)}, u32[]{:S(2)}, u32[]{:S(2)}) collective-permute-start(f32[2,3,16,128]{3,2,1,0:T(8,128)} %get-tuple-element.32), channel_id=1, source_target_pairs={{0,6},{1,7},{2,4},{3,5},{4,2},{5,3},{6,0},{7,1},{8,14},{9,15},{10,... | collective-permute-start | bytes 147464 | tf_op jit(solution)/shard_map/ppermute | solution.py:422
  37.2 8.9 %collective-permute-start.12 = (f32[2,3,16,128]{3,2,1,0:T(8,128)}, f32[2,3,16,128]{3,2,1,0:T(8,128)S(1)}, u32[]{:S(2)}, u32[]{:S(2)}) collective-permute-start(f32[2,3,16,128]{3,2,1,0:T(8,128)} %get-tuple-element.33), channel_id=1, source_target_pairs={{0,7},{1,6},{2,5},{3,4},{4,3},{5,2},{6,1},{7,0},{8,15},{9,14},{10,... | collective-permute-start | bytes 147464 | tf_op jit(solution)/shard_map/ppermute | solution.py:422
  39.6 6.5 %collective-permute-start.6 = (f32[2,3,16,128]{3,2,1,0:T(8,128)}, f32[2,3,16,128]{3,2,1,0:T(8,128)S(1)}, u32[]{:S(2)}, u32[]{:S(2)}) collective-permute-start(f32[2,3,16,128]{3,2,1,0:T(8,128)} %get-tuple-element.27), channel_id=1, source_target_pairs={{0,1},{1,0},{2,3},{3,2},{4,5},{5,4},{6,7},{7,6},{8,9},{9,8},{10,11... | collective-permute-start | bytes 147464 | tf_op jit(solution)/shard_map/ppermute | solution.py:422
  41.2 5.0 %collective-permute-start.7 = (f32[2,3,16,128]{3,2,1,0:T(8,128)}, f32[2,3,16,128]{3,2,1,0:T(8,128)S(1)}, u32[]{:S(2)}, u32[]{:S(2)}) collective-permute-start(f32[2,3,16,128]{3,2,1,0:T(8,128)} %get-tuple-element.28), channel_id=1, source_target_pairs={{0,2},{1,3},{2,0},{3,1},{4,6},{5,7},{6,4},{7,5},{8,10},{9,11},{10,... | collective-permute-start | bytes 147464 | tf_op jit(solution)/shard_map/ppermute | solution.py:422
  42.1 5.3 %collective-permute-start.8 = (f32[2,3,16,128]{3,2,1,0:T(8,128)}, f32[2,3,16,128]{3,2,1,0:T(8,128)S(1)}, u32[]{:S(2)}, u32[]{:S(2)}) collective-permute-start(f32[2,3,16,128]{3,2,1,0:T(8,128)} %get-tuple-element.29), channel_id=1, source_target_pairs={{0,3},{1,2},{2,1},{3,0},{4,7},{5,6},{6,5},{7,4},{8,11},{9,10},{10,... | collective-permute-start | bytes 147464 | tf_op jit(solution)/shard_map/ppermute | solution.py:422
  44.1 5.3 %collective-permute-start.9 = (f32[2,3,16,128]{3,2,1,0:T(8,128)}, f32[2,3,16,128]{3,2,1,0:T(8,128)S(1)}, u32[]{:S(2)}, u32[]{:S(2)}) collective-permute-start(f32[2,3,16,128]{3,2,1,0:T(8,128)} %get-tuple-element.30), channel_id=1, source_target_pairs={{0,4},{1,5},{2,6},{3,7},{4,0},{5,1},{6,2},{7,3},{8,12},{9,13},{10,... | collective-permute-start | bytes 147464 | tf_op jit(solution)/shard_map/ppermute | solution.py:422
  58.1 42.4 %copy-start.2 = (f32[16,4,512]{2,1,0:T(4,128)}, f32[16,4,512]{2,1,0:T(4,128)S(1)}, u32[]{:S(2)}) copy-start(f32[16,4,512]{2,1,0:T(4,128)S(1)} %get-tuple-element.44.refs_3_) | copy-start | bytes 393220
  58.1 8.4 %collective-permute-start.13 = (f32[16,4,512]{2,1,0:T(4,128)S(1)}, f32[16,4,512]{2,1,0:T(4,128)S(1)}, u32[]{:S(2)}, u32[]{:S(2)}) collective-permute-start(f32[16,4,512]{2,1,0:T(4,128)S(1)} %get-tuple-element.44.refs_3_), channel_id=1, source_target_pairs={{0,1},{1,0},{2,3},{3,2},{4,5},{5,4},{6,7},{7,6},{8,9},{9,8},{10,11... | collective-permute-start | bytes 393224 | tf_op jit(solution)/shard_map/ppermute | solution.py:422
  59.5 7.0 %collective-permute-start.14 = (f32[16,4,512]{2,1,0:T(4,128)S(1)}, f32[16,4,512]{2,1,0:T(4,128)S(1)}, u32[]{:S(2)}, u32[]{:S(2)}) collective-permute-start(f32[16,4,512]{2,1,0:T(4,128)S(1)} %get-tuple-element.44.refs_3_), channel_id=1, source_target_pairs={{0,2},{1,3},{2,0},{3,1},{4,6},{5,7},{6,4},{7,5},{8,10},{9,11},{10,... | collective-permute-start | bytes 393224 | tf_op jit(solution)/shard_map/ppermute | solution.py:431
  59.5 7.0 %collective-permute-start.15 = (f32[16,4,512]{2,1,0:T(4,128)S(1)}, f32[16,4,512]{2,1,0:T(4,128)S(1)}, u32[]{:S(2)}, u32[]{:S(2)}) collective-permute-start(f32[16,4,512]{2,1,0:T(4,128)S(1)} %get-tuple-element.44.refs_3_), channel_id=1, source_target_pairs={{2,4},{3,5},{4,2},{5,3},{10,12},{11,13},{12,10},{13,11},{18,20},{1... | collective-permute-start | bytes 393224 | tf_op jit(solution)/shard_map/ppermute | solution.py:431
  60.2 4.5 %collective-permute-start.17 = (f32[1,1]{1,0:T(1,128)}, f32[1,1]{1,0:T(1,128)}, u32[]{:S(2)}, u32[]{:S(2)}) collective-permute-start(f32[1,1]{1,0:T(1,128)} %bitcast.12), channel_id=1, source_target_pairs={{0,16},{8,24},{16,0},{24,8},{1,17},{9,25},{17,1},{25,9},{2,18},{10... | collective-permute-start | bytes 20 | tf_op jit(solution)/shard_map/ppermute | solution.py:422
  60.8 1.5 %collective-permute-start.16 = (f32[1,1]{1,0:T(1,128)}, f32[1,1]{1,0:T(1,128)}, u32[]{:S(2)}, u32[]{:S(2)}) collective-permute-start(f32[1,1]{1,0:T(1,128)} %bitcast.12), channel_id=1, source_target_pairs={{0,8},{8,0},{16,24},{24,16},{1,9},{9,1},{17,25},{25,17},{2,10},{10... | collective-permute-start | bytes 20 | tf_op jit(solution)/shard_map/ppermute | solution.py:422
  62.3 3.0 %collective-permute-start.18 = (f32[1,1]{1,0:T(1,128)}, f32[1,1]{1,0:T(1,128)}, u32[]{:S(2)}, u32[]{:S(2)}) collective-permute-start(f32[1,1]{1,0:T(1,128)} %bitcast.12), channel_id=1, source_target_pairs={{0,24},{8,16},{16,8},{24,0},{1,25},{9,17},{17,9},{25,1},{2,26},{10... | collective-permute-start | bytes 20 | tf_op jit(solution)/shard_map/ppermute | solution.py:422
  66.5 34.0 %copy-start.9 = (f32[16,4,512]{2,1,0:T(4,128)}, f32[16,4,512]{2,1,0:T(4,128)S(1)}, u32[]{:S(2)}) copy-start(f32[16,4,512]{2,1,0:T(4,128)S(1)} %collective-permute-done.13.refs_7_) | copy-start | bytes 393220
  66.5 34.0 %copy-start.10 = (f32[16,4,512]{2,1,0:T(4,128)}, f32[16,4,512]{2,1,0:T(4,128)S(1)}, u32[]{:S(2)}) copy-start(f32[16,4,512]{2,1,0:T(4,128)S(1)} %collective-permute-done.14.refs_4_) | copy-start | bytes 393220
  66.6 18.2 %collective-permute-start.19 = (f32[16,4,512]{2,1,0:T(4,128)S(1)}, f32[16,4,512]{2,1,0:T(4,128)S(1)}, u32[]{:S(2)}, u32[]{:S(2)}) collective-permute-start(f32[16,4,512]{2,1,0:T(4,128)S(1)} %collective-permute-done.15), channel_id=1, source_target_pairs={{2,0},{3,1},{4,6},{5,7},{10,8},{11,9},{12,14},{13,15},{18,16},{19,... | collective-permute-start | bytes 393224 | tf_op jit(solution)/shard_map/ppermute | solution.py:431
  67.9 16.9 %collective-permute-start.20 = (f32[16,4,512]{2,1,0:T(4,128)S(1)}, f32[16,4,512]{2,1,0:T(4,128)S(1)}, u32[]{:S(2)}, u32[]{:S(2)}) collective-permute-start(f32[16,4,512]{2,1,0:T(4,128)S(1)} %collective-permute-done.14.refs_4_), channel_id=1, source_target_pairs={{2,4},{3,5},{4,2},{5,3},{10,12},{11,13},{12,10},{13,11},{18,20},{1... | collective-permute-start | bytes 393224 | tf_op jit(solution)/shard_map/ppermute | solution.py:431
  68.6 14.9 %collective-permute-start.22 = (f32[1,1]{1,0:T(1,128)}, f32[1,1]{1,0:T(1,128)}, u32[]{:S(2)}, u32[]{:S(2)}) collective-permute-start(f32[1,1]{1,0:T(1,128)} %add.138), channel_id=1, source_target_pairs={{0,2},{1,3},{2,0},{3,1},{4,6},{5,7},{6,4},{7,5},{8,10},{9,11},{10,... | collective-permute-start | bytes 20 | tf_op jit(solution)/shard_map/ppermute | solution.py:422
  76.5 7.0 %collective-permute-start.23 = (f32[1,1]{1,0:T(1,128)}, f32[1,1]{1,0:T(1,128)}, u32[]{:S(2)}, u32[]{:S(2)}) collective-permute-start(f32[1,1]{1,0:T(1,128)} %add.138), channel_id=1, source_target_pairs={{0,3},{1,2},{2,1},{3,0},{4,7},{5,6},{6,5},{7,4},{8,11},{9,10},{10,... | collective-permute-start | bytes 20 | tf_op jit(solution)/shard_map/ppermute | solution.py:422
  77.8 3.6 %collective-permute-start.21 = (f32[1,1]{1,0:T(1,128)}, f32[1,1]{1,0:T(1,128)}, u32[]{:S(2)}, u32[]{:S(2)}) collective-permute-start(f32[1,1]{1,0:T(1,128)} %add.138), channel_id=1, source_target_pairs={{0,1},{1,0},{2,3},{3,2},{4,5},{5,4},{6,7},{7,6},{8,9},{9,8},{10,11... | collective-permute-start | bytes 20 | tf_op jit(solution)/shard_map/ppermute | solution.py:422
  81.5 14.9 %collective-permute-start.26 = (f32[16,4,512]{2,1,0:T(4,128)S(1)}, f32[16,4,512]{2,1,0:T(4,128)S(1)}, u32[]{:S(2)}, u32[]{:S(2)}) collective-permute-start(f32[16,4,512]{2,1,0:T(4,128)S(1)} %collective-permute-done.14.refs_4_), channel_id=1, source_target_pairs={{0,1},{1,0},{2,3},{3,2},{4,5},{5,4},{6,7},{7,6},{8,9},{9,8},{10,11... | collective-permute-start | bytes 393224 | tf_op jit(solution)/shard_map/ppermute | solution.py:422
  84.8 5.2 %collective-permute-start.25 = (f32[1,1]{1,0:T(1,128)}, f32[1,1]{1,0:T(1,128)}, u32[]{:S(2)}, u32[]{:S(2)}) collective-permute-start(f32[1,1]{1,0:T(1,128)} %add.141), channel_id=1, source_target_pairs={{0,4},{1,5},{2,6},{3,7},{4,0},{5,1},{6,2},{7,3},{8,12},{9,13},{10,... | collective-permute-start | bytes 20 | tf_op jit(solution)/shard_map/ppermute | solution.py:422
  88.6 6.8 %collective-permute-start.24 = (f32[16,4,512]{2,1,0:T(4,128)S(1)}, f32[16,4,512]{2,1,0:T(4,128)S(1)}, u32[]{:S(2)}, u32[]{:S(2)}) collective-permute-start(f32[16,4,512]{2,1,0:T(4,128)S(1)} %collective-permute-done.20), channel_id=1, source_target_pairs={{2,0},{3,1},{4,6},{5,7},{10,8},{11,9},{12,14},{13,15},{18,16},{19,... | collective-permute-start | bytes 393224 | tf_op jit(solution)/shard_map/ppermute | solution.py:431
  89.9 6.4 %collective-permute-start.27 = (f32[16,4,512]{2,1,0:T(4,128)S(1)}, f32[16,4,512]{2,1,0:T(4,128)S(1)}, u32[]{:S(2)}, u32[]{:S(2)}) collective-permute-start(f32[16,4,512]{2,1,0:T(4,128)S(1)} %bitcast.32), channel_id=1, source_target_pairs={{0,1},{1,0},{2,3},{3,2},{4,5},{5,4},{6,7},{7,6},{8,9},{9,8},{10,11... | collective-permute-start | bytes 393224 | tf_op jit(solution)/shard_map/ppermute | solution.py:422
  95.5 5.0 %collective-permute-start.28 = (f32[16,4,512]{2,1,0:T(4,128)S(1)}, f32[16,4,512]{2,1,0:T(4,128)S(1)}, u32[]{:S(2)}, u32[]{:S(2)}) collective-permute-start(f32[16,4,512]{2,1,0:T(4,128)S(1)} %bitcast.34), channel_id=1, source_target_pairs={{0,1},{1,0},{2,3},{3,2},{4,5},{5,4},{6,7},{7,6},{8,9},{9,8},{10,11... | collective-permute-start | bytes 393224 | tf_op jit(solution)/shard_map/ppermute | solution.py:422
  (20 other events, 126.5 us)

commit v4 on v3

--- a/solution.py
+++ b/solution.py
@@ -15,7 +15,7 @@
 epsilon = 1e-06
 scale = 0.7
 LANES = 128
-GROUP = 8
+GROUP = 32
 
 
 def coordinate(across, along, cos, sin, bins_n):
@@ -327,10 +327,10 @@
     )(ints, trig, *arrays)
 
 
-def gather_kernel(dims, parts_n, views_n, ints_ref, *rest):
+def gather_kernel(dims, parts_n, views_n, ints_ref, tv_ref, curv_ref, *rest):
     rows_n, cols_n, bins_n, base, blocks = dims
     pieces = rest[:parts_n]
-    out_ref, trig_ref, starts_ref = rest[parts_n:]
+    out_ref, rows_ref, trig_ref, starts_ref = rest[parts_n:]
     per_n = cols_n // parts_n
     part = ints_ref[1]
     lane8 = lax.broadcasted_iota(jnp.int32, (8, LANES), 1)
@@ -344,7 +344,7 @@
         trig_ref[total_n + n] = sin
         starts_ref[n] = window_start(part, per_n, cos, sin, rows_n, cols_n, bins_n, base, blocks)
 
-    def step(index, _):
+    def step(index, squares):
         row = index // (per_n // LANES)
         u = index - row * (per_n // LANES)
         along = row.astype(jnp.float32) - 0.5 * rows_n + 0.5
@@ -371,38 +371,44 @@
             a = jnp.take_along_axis(held, here, axis=1, mode="promise_in_bounds")
             b = jnp.take_along_axis(held, next_, axis=1, mode="promise_in_bounds")
             total = total + (a * (1.0 - frac) + b * frac)
-        out_ref[row, :, pl.ds(pl.multiple_of(u * LANES, LANES), LANES)] = total
-        return 0
-
-    lax.fori_loop(0, rows_n * (per_n // LANES), step, 0)
-
-
-def gather_views(dims, parts_n, ints, pieces):
+        cols = pl.ds(pl.multiple_of(u * LANES, LANES), LANES)
+        total = (total + tv_ref[row, :, cols]) / curv_ref[row, :, cols]
+        rows_ref[row, :, cols] = total
+        return squares + total * total
+
+    squares = lax.fori_loop(0, rows_n * (per_n // LANES), step, jnp.zeros((16, LANES), jnp.float32))
+    for row in range(rows_n):
+        out_ref[0:16, row, :] = rows_ref[row]
+    out_ref[16] = jnp.full((rows_n, per_n), jnp.sum(squares), jnp.float32)
+
+
+def gather_views(dims, parts_n, ints, tv, curv, pieces):
     views_n, _, slices_n, _ = pieces[0].shape
     rows_n, cols_n = dims[:2]
     body = lambda *refs: gather_kernel(dims, parts_n, views_n, *refs)
     vmem = pl.BlockSpec(memory_space=pltpu.VMEM)
     return pl.pallas_call(
         body,
-        out_shape=jax.ShapeDtypeStruct((rows_n, slices_n, cols_n // parts_n), jnp.float32),
-        in_specs=[pl.BlockSpec(memory_space=pltpu.SMEM)] + [vmem] * parts_n,
+        out_shape=jax.ShapeDtypeStruct((slices_n + 1, rows_n, cols_n // parts_n), jnp.float32),
+        in_specs=[pl.BlockSpec(memory_space=pltpu.SMEM)] + [vmem] * (parts_n + 2),
         out_specs=vmem,
         scratch_shapes=[
+            pltpu.VMEM((rows_n, slices_n, cols_n // parts_n), jnp.float32),
             pltpu.SMEM((2 * parts_n * views_n,), jnp.float32),
             pltpu.SMEM((parts_n * views_n,), jnp.int32),
         ],
         name="gather_views",
-    )(ints, *pieces)
+    )(ints, tv, curv, *pieces)
 
 
 def finish_kernel(parts_n, order_ref, factor_ref, vol_ref, *rest):
     pieces = rest[:parts_n]
     out_ref = rest[parts_n]
     factor = factor_ref[0]
-    per_n = pieces[0].shape[2]
+    slices_n, _, per_n = pieces[0].shape
     for r in range(parts_n):
         cols = pl.ds(pl.multiple_of(order_ref[r] * per_n, per_n), per_n)
-        out_ref[:, :, cols] = vol_ref[:, :, cols] - factor * pieces[r][...]
+        out_ref[:, :, cols] = vol_ref[:, :, cols] - factor * pieces[r][0 : slices_n - 1]
 
 
 def finish(order, factor, volume, pieces):
@@ -422,7 +428,7 @@
     return lax.ppermute(x, axis, [(i, i ^ bit) for i in range(lax.axis_size(axis))])
 
 
-def gathered(piece, squares):
+def gathered(piece):
     part = lax.axis_index("view")
     depth = part // 2
     end = (depth == 0) | (depth == 3)
@@ -433,24 +439,17 @@
     first = swapped(piece, "view", 1)
     second = along(piece, [(0, 1), (1, 0), (2, 3), (3, 2)])
     middle = along(piece, [(1, 2), (2, 1)])
-    squares = squares + swapped(squares, "slab", 1) + (swapped(squares, "slab", 2) + swapped(squares, "slab", 3))
-    first, second, middle, squares = lax.optimization_barrier((first, second, middle, squares))
     across = [first, swapped(second, "view", 1)]
     onward = along(middle, [(1, 0), (2, 3)])
     middle_last = along(second, [(1, 2), (2, 1)])
-    squares = squares + swapped(squares, "view", 1) + (swapped(squares, "view", 2) + swapped(squares, "view", 3))
-    onward, middle_last, squares = lax.optimization_barrier((onward, middle_last, squares))
     third = jnp.where(end, onward, middle)
     across.append(swapped(third, "view", 1))
-    last = along(middle_last, [(1, 0), (2, 3)])
-    squares = squares + swapped(squares, "view", 4)
-    last, squares = lax.optimization_barrier((last, squares))
-    last = jnp.where(end, last, middle_last)
+    last = jnp.where(end, along(middle_last, [(1, 0), (2, 3)]), middle_last)
     across.append(swapped(last, "view", 1))
     upper = depth // 2
     depths = [depth, depth ^ 1, 2 - upper, 3 - 3 * upper]
     order = jnp.stack([2 * d + part % 2 for d in depths] + [2 * d + 1 - part % 2 for d in depths])
-    return order.astype(jnp.int32), [piece, second, third, last] + across, squares
+    return order.astype(jnp.int32), [piece, second, third, last] + across
 
 
 def local_split(volume, sinogram, curvature, angles, offsets):
@@ -500,8 +499,6 @@
         [proj, near, cross, cross_pair, measured, pair_rows, cross_rows, cross_pair_rows],
     )
     pieces = [windows[0]] + [swapped(windows[r], "view", r) for r in range(1, parts_n)]
-    data_grad = gather_views(dims, parts_n, ints, pieces).transpose(1, 0, 2)
-
     def face_of(rows, which):
         return rows[which, blocks].reshape(1, rows_n, per_n)
 
@@ -514,8 +511,13 @@
     block = jnp.concatenate([jnp.pad(below, sides), block, jnp.pad(above, sides)], axis=0)
     tv_grad = tv_padded(jnp.pad(block, ((0, 0), (1, 1), (0, 0))))
     curv = lax.dynamic_slice_in_dim(curvature, part * per_n, per_n, axis=2)
-    direction = (data_grad + tv_weight * tv_grad) / curv
-    order, parts, squares = gathered(direction, jnp.sum(direction * direction).reshape(1, 1))
+    tv = (tv_weight * tv_grad).transpose(1, 0, 2)
+    order, parts = gathered(gather_views(dims, parts_n, ints, tv, curv.transpose(1, 0, 2), pieces))
+    sums = [p[slices_n, 0, 0] for p in parts]
+    while len(sums) > 1:
+        sums = [a + b for a, b in zip(sums[0::2], sums[1::2])]
+    squares = sums[0].reshape(1, 1)
+    squares = squares + swapped(squares, "slab", 1) + (swapped(squares, "slab", 2) + swapped(squares, "slab", 3))
     voxel_count = slices_n * slab_count * rows_n * cols_n
     factor = jnp.minimum(1.0, step_limit / jnp.sqrt(squares / voxel_count + epsilon))
     return finish(order, factor.reshape(1), volume, parts)

time: 104 us -> 94.2 us (0.906)
  starting transfers between devices: 41.5 us -> 30.4 us
  local copies, waits for them, and re-layouts: 5.07 us -> 9.99 us
  waiting for transfers between devices: 25.5 us -> 22.3 us
  between operations: 5.5 us -> 7.42 us
  Pallas kernels: 21.6 us -> 20.1 us
  other arithmetic: 4.62 us -> 3.48 us
    ppermute x24 -> x20, starting transfers between devices: 37.6 us -> 26.5 us  [swapped(): lax.ppermute(x, axis, [(i, i ^ bit) for i in range(lax.axis_size(axis))])]
    ppermute x24 -> x20, waiting for transfers between devices: 20.7 us -> 12.2 us  [swapped(): lax.ppermute(x, axis, [(i, i ^ bit) for i in range(lax.axis_size(axis))])]
    ppermute x5, waiting for transfers between devices: 4.81 us -> 10 us  [along(): lax.ppermute(x, 'view', [(2 * a + y, 2 * b + y) for a, b in pairs for y i...]
    slice x0 -> x8, local copies, waits for them, and re-layouts: none -> 5.06 us  [local_split(): sums = [p[slices_n, 0, 0] for p in parts]]
    reduce_sum x1 -> x0, other arithmetic: 2.13 us -> none  [local_split(): jnp.sum(direction * direction).reshape(1, 1)]
    pallas_call x1, Pallas kernels: 9.87 us -> 7.99 us  [project(): pl.pallas_call(body, out_shape=jax.ShapeDtypeStruct((views_n, blocks_n, s...]
    unnamed x46 -> x40, local copies, waits for them, and re-layouts: 2.1 us -> 1.94 us
  transfers between devices with their start and end apart: 29 -> 25, of which waited for: 10 -> 6; matrix products, arithmetic and copies ran while one was open for 3% -> 11% of each run, Pallas kernels for 10% -> 9%
where the time goes in v4:
time: 94.2 us; the launch traced here: 93.7 us
  starting transfers between devices  30.4 us (32%)
  waiting for transfers between devices  22.3 us (24%)
  Pallas kernels  20.1 us (21%)
  local copies, waits for them, and re-layouts  9.99 us (11%)
  between operations  7.42 us (8%)
  other arithmetic  3.48 us (4%)
    ppermute x20, starting transfers between devices, swapped(): lax.ppermute(x, axis, [(i, i ^ bit) for i in range(lax.axis_size(axis))])  26.5 us
    ppermute x20, waiting for transfers between devices, swapped(): lax.ppermute(x, axis, [(i, i ^ bit) for i in range(lax.axis_size(axis))])  12.2 us
    ppermute x5, waiting for transfers between devices, along(): lax.ppermute(x, 'view', [(2 * a + y, 2 * b + y) for a, b in pairs for y i...  10 us
    pallas_call x1, Pallas kernels, project(): pl.pallas_call(body, out_shape=jax.ShapeDtypeStruct((views_n, blocks_n, s...  7.99 us
    pallas_call x1, Pallas kernels, gather_views(): pl.pallas_call(body, out_shape=jax.ShapeDtypeStruct((slices_n + 1, rows_n...  6.23 us
    slice x8, local copies, waits for them, and re-layouts, local_split(): sums = [p[slices_n, 0, 0] for p in parts]  5.06 us
    ppermute x5, starting transfers between devices, along(): lax.ppermute(x, 'view', [(2 * a + y, 2 * b + y) for a, b in pairs for y i...  3.94 us
    pallas_call x1, Pallas kernels, residual_windows(): pl.pallas_call(body, out_shape=[jax.ShapeDtypeStruct((views_n, WINDOW, ba...  3.14 us
  transfers between devices with their start and end apart: 25, of which 6 were waited for; matrix products, arithmetic and copies ran while one was open for 11% of the time, Pallas kernels for 9%

profile of v4, /device:TPU:0, one launch (start us, length us, event | category | flops | bytes accessed | tf_op | source)
XLA Modules:
  0.0 93.7 jit_solution(2023006386879788983)
XLA Ops:
  0.0 0.8 constant_dynamic-slice_fusion.2
  0.8 1.2 %bitcast_bitcast_fusion = f32[2,23,16,128]{3,2,1,0:T(8,128)S(1)} fusion(f32[2,16,4096]{2,1,0:T(8,128)} %param.6), kind=kLoop, calls=%fused_computation.7 | loop fusion | bytes 753664 | tf_op jit(solution)/shard_map/transpose | solution.py:475
  2.1 3.0 %collective-permute-start.1 = (f32[2,24,16,128]{3,2,1,0:T(8,128)S(1)}, f32[2,24,16,128]{3,2,1,0:T(8,128)}, u32[]{:S(2)}, u32[]{:S(2)}) collective-permute-start(f32[2,24,16,128]{3,2,1,0:T(8,128)S(1)} %maximum_maximum_fusion.refs_6_), channel_id=1, source_target_pairs={{0,16},{8,24},{16,0},{24,8},{1,17},{9,25},{17,1},{25,9},{2,18},{10... | collective-permute-start | bytes 1179656 | tf_op jit(solution)/shard_map/ppermute | solution.py:428
  5.8 8.0 %project.1.refs_2_ = f32[2,23,16,128]{3,2,1,0:T(8,128)} custom-call(f32[4]{0:T(128)} %pad_maximum_fusion.2.refs_0_.refs_1_, f32[16,4,4096]{2,1,0:T(4,128)} %refs_2_.1), custom_call_target="tpu_custom_call" | custom-call | tf_op jit(solution)/shard_map/project/pallas_call | solution.py:100
  14.6 9.8 %collective-permute-done.4.refs_4_ = f32[2,23,16,128]{3,2,1,0:T(8,128)} collective-permute-done((f32[2,23,16,128]{3,2,1,0:T(8,128)}, f32[2,23,16,128]{3,2,1,0:T(8,128)}, u32[]{:S(2)}, u32[]{:S(2)}) %collective-permute-start.4) | collective-permute-done | bytes 376864 | tf_op jit(solution)/shard_map/ppermute | solution.py:428
  25.7 0.7 copy.15
  27.2 3.1 %residual_windows.1 = (f32[2,3,16,128]{3,2,1,0:T(8,128)}, f32[2,3,16,128]{3,2,1,0:T(8,128)}, f32[2,3,16,128]{3,2,1,0:T(8,128)}, f32[2,3,16,128]{3,2,1,0:T(8,128)...) custom-call(s32[10]{0:T(128)} %pad_add_fusion.1.refs_0_, ...), custom_call_target="tpu_custom_call" | custom-call | tf_op jit(solution)/shard_map/residual_windows/pallas_call | solution.py:314
  30.3 3.6 %collective-permute-start.10 = (f32[2,3,16,128]{3,2,1,0:T(8,128)}, f32[2,3,16,128]{3,2,1,0:T(8,128)S(1)}, u32[]{:S(2)}, u32[]{:S(2)}) collective-permute-start(f32[2,3,16,128]{3,2,1,0:T(8,128)} %get-tuple-element.22), channel_id=1, source_target_pairs={{0,5},{1,4},{2,7},{3,6},{4,1},{5,0},{6,3},{7,2},{8,13},{9,12},{10,... | collective-permute-start | bytes 147464 | tf_op jit(solution)/shard_map/ppermute | solution.py:428
  33.9 1.4 %collective-permute-start.11 = (f32[2,3,16,128]{3,2,1,0:T(8,128)}, f32[2,3,16,128]{3,2,1,0:T(8,128)S(1)}, u32[]{:S(2)}, u32[]{:S(2)}) collective-permute-start(f32[2,3,16,128]{3,2,1,0:T(8,128)} %get-tuple-element.23), channel_id=1, source_target_pairs={{0,6},{1,7},{2,4},{3,5},{4,2},{5,3},{6,0},{7,1},{8,14},{9,15},{10,... | collective-permute-start | bytes 147464 | tf_op jit(solution)/shard_map/ppermute | solution.py:428
  35.3 2.4 %collective-permute-start.12 = (f32[2,3,16,128]{3,2,1,0:T(8,128)}, f32[2,3,16,128]{3,2,1,0:T(8,128)S(1)}, u32[]{:S(2)}, u32[]{:S(2)}) collective-permute-start(f32[2,3,16,128]{3,2,1,0:T(8,128)} %get-tuple-element.24), channel_id=1, source_target_pairs={{0,7},{1,6},{2,5},{3,4},{4,3},{5,2},{6,1},{7,0},{8,15},{9,14},{10,... | collective-permute-start | bytes 147464 | tf_op jit(solution)/shard_map/ppermute | solution.py:428
  37.7 1.5 %collective-permute-start.6 = (f32[2,3,16,128]{3,2,1,0:T(8,128)}, f32[2,3,16,128]{3,2,1,0:T(8,128)S(1)}, u32[]{:S(2)}, u32[]{:S(2)}) collective-permute-start(f32[2,3,16,128]{3,2,1,0:T(8,128)} %get-tuple-element.18), channel_id=1, source_target_pairs={{0,1},{1,0},{2,3},{3,2},{4,5},{5,4},{6,7},{7,6},{8,9},{9,8},{10,11... | collective-permute-start | bytes 147464 | tf_op jit(solution)/shard_map/ppermute | solution.py:428
  39.2 0.8 fusion.24
  40.2 2.0 %collective-permute-start.8 = (f32[2,3,16,128]{3,2,1,0:T(8,128)}, f32[2,3,16,128]{3,2,1,0:T(8,128)S(1)}, u32[]{:S(2)}, u32[]{:S(2)}) collective-permute-start(f32[2,3,16,128]{3,2,1,0:T(8,128)} %get-tuple-element.20), channel_id=1, source_target_pairs={{0,3},{1,2},{2,1},{3,0},{4,7},{5,6},{6,5},{7,4},{8,11},{9,10},{10,... | collective-permute-start | bytes 147464 | tf_op jit(solution)/shard_map/ppermute | solution.py:428
  42.2 1.9 %collective-permute-start.9 = (f32[2,3,16,128]{3,2,1,0:T(8,128)}, f32[2,3,16,128]{3,2,1,0:T(8,128)S(1)}, u32[]{:S(2)}, u32[]{:S(2)}) collective-permute-start(f32[2,3,16,128]{3,2,1,0:T(8,128)} %get-tuple-element.21), channel_id=1, source_target_pairs={{0,4},{1,5},{2,6},{3,7},{4,0},{5,1},{6,2},{7,3},{8,12},{9,13},{10,... | collective-permute-start | bytes 147464 | tf_op jit(solution)/shard_map/ppermute | solution.py:428
  44.1 1.0 %fusion.7.refs_1_ = f32[4,16,512]{2,1,0:T(8,128)} fusion(s32[]{:T(128)S(6)} %select_n.138, f32[16,4,4096]{2,0,1:T(8,128)S(1)} %copy.8, s32[]{:T(128)S(6)} %add.165, f32[18,6,514]{2,0,1:T(8,128)S(1)} %select_maximum_fusion, f32[1,4,514]{2,0,1:T(1,128)S(1)} %pad.17, f32[16,4,514]{2,0,1:T(8,128)S(1)} %pad_dynamic-slice_fusion.3, s32[]{:T(128)S(6)} %add.164, ...), kind=kLoop, calls=%fused_computation.18 | loop fusion | flops 851968 | bytes 1589836 | tf_op jit(solution)/shard_map/transpose | solution.py:514
  45.5 2.1 %collective-permute-done.9.refs_7_ = f32[2,3,16,128]{3,2,1,0:T(8,128)S(1)} collective-permute-done((f32[2,3,16,128]{3,2,1,0:T(8,128)}, f32[2,3,16,128]{3,2,1,0:T(8,128)S(1)}, u32[]{:S(2)}, u32[]{:S(2)}) %collective-permute-start.9) | collective-permute-done | bytes 49184 | tf_op jit(solution)/shard_map/ppermute | solution.py:428
  48.2 6.2 %gather_views.1.refs_3_ = f32[17,4,512]{2,1,0:T(4,128)} custom-call(s32[10]{0:T(128)} %pad_add_fusion.1.refs_0_, f32[4,16,512]{2,1,0:T(8,128)} %fusion.7.refs_1_, f32[4,16,512]{2,1,0:T(8,128)} %bitcast.26, f32[2,3,16,128]{3,2,1,0:T(8,128)} %get-tuple-element.17.refs_3_, f32[2,3,16,128]{3,2,1,0:T(8,128)} %copy-done.13, f32[2,3,16,128]{3,2,1,0:T(8,128)} %copy-done.14, ...), custom_call_target="tpu_custom_call" | custom-call | tf_op jit(solution)/shard_map/gather_views/pallas_call | solution.py:390
  54.4 0.7 collective-permute-start.14
  55.1 4.6 %collective-permute-done.13.refs_4_ = f32[17,4,512]{2,1,0:T(4,128)S(1)} collective-permute-done((f32[17,4,512]{2,1,0:T(4,128)}, f32[17,4,512]{2,1,0:T(4,128)S(1)}, u32[]{:S(2)}, u32[]{:S(2)}) %collective-permute-start.13) | collective-permute-done | bytes 139296 | tf_op jit(solution)/shard_map/ppermute | solution.py:437
  59.7 0.7 collective-permute-start.16
  60.3 1.3 %collective-permute-start.15 = (f32[17,4,512]{2,1,0:T(4,128)S(1)}, f32[17,4,512]{2,1,0:T(4,128)S(1)}, u32[]{:S(2)}, u32[]{:S(2)}) collective-permute-start(f32[17,4,512]{2,1,0:T(4,128)S(1)} %collective-permute-done.14), channel_id=1, source_target_pairs={{2,0},{3,1},{4,6},{5,7},{10,8},{11,9},{12,14},{13,15},{18,16},{19,... | collective-permute-start | bytes 417800 | tf_op jit(solution)/shard_map/ppermute | solution.py:437
  61.7 1.5 %collective-permute-start.18 = (f32[17,4,512]{2,1,0:T(4,128)}, f32[17,4,512]{2,1,0:T(4,128)S(1)}, u32[]{:S(2)}, u32[]{:S(2)}) collective-permute-start(f32[17,4,512]{2,1,0:T(4,128)} %gather_views.1.refs_3_), channel_id=1, source_target_pairs={{0,1},{1,0},{2,3},{3,2},{4,5},{5,4},{6,7},{7,6},{8,9},{9,8},{10,11... | collective-permute-start | bytes 417800 | tf_op jit(solution)/shard_map/ppermute | solution.py:428
  63.7 1.3 %collective-permute-start.17 = (f32[17,4,512]{2,1,0:T(4,128)S(1)}, f32[17,4,512]{2,1,0:T(4,128)S(1)}, u32[]{:S(2)}, u32[]{:S(2)}) collective-permute-start(f32[17,4,512]{2,1,0:T(4,128)S(1)} %collective-permute-done.16), channel_id=1, source_target_pairs={{2,0},{3,1},{4,6},{5,7},{10,8},{11,9},{12,14},{13,15},{18,16},{19,... | collective-permute-start | bytes 417800 | tf_op jit(solution)/shard_map/ppermute | solution.py:437
  65.0 3.3 %collective-permute-done.15 = f32[17,4,512]{2,1,0:T(4,128)S(1)} collective-permute-done((f32[17,4,512]{2,1,0:T(4,128)S(1)}, f32[17,4,512]{2,1,0:T(4,128)S(1)}, u32[]{:S(2)}, u32[]{:S(2)}) %collective-permute-start.15) | collective-permute-done | bytes 139296 | tf_op jit(solution)/shard_map/ppermute | solution.py:437
  68.4 1.1 %collective-permute-start.20 = (f32[17,4,512]{2,1,0:T(4,128)S(1)}, f32[17,4,512]{2,1,0:T(4,128)S(1)}, u32[]{:S(2)}, u32[]{:S(2)}) collective-permute-start(f32[17,4,512]{2,1,0:T(4,128)S(1)} %broadcast_select_fusion.1.refs_5_), channel_id=1, source_target_pairs={{0,1},{1,0},{2,3},{3,2},{4,5},{5,4},{6,7},{7,6},{8,9},{9,8},{10,11... | collective-permute-start | bytes 417800 | tf_op jit(solution)/shard_map/ppermute | solution.py:428
  69.5 2.2 %collective-permute-done.17 = f32[17,4,512]{2,1,0:T(4,128)S(1)} collective-permute-done((f32[17,4,512]{2,1,0:T(4,128)S(1)}, f32[17,4,512]{2,1,0:T(4,128)S(1)}, u32[]{:S(2)}, u32[]{:S(2)}) %collective-permute-start.17) | collective-permute-done | bytes 139296 | tf_op jit(solution)/shard_map/ppermute | solution.py:437
  71.8 1.1 %collective-permute-start.21 = (f32[17,4,512]{2,1,0:T(4,128)S(1)}, f32[17,4,512]{2,1,0:T(4,128)S(1)}, u32[]{:S(2)}, u32[]{:S(2)}) collective-permute-start(f32[17,4,512]{2,1,0:T(4,128)S(1)} %broadcast_select_fusion.refs_6_), channel_id=1, source_target_pairs={{0,1},{1,0},{2,3},{3,2},{4,5},{5,4},{6,7},{7,6},{8,9},{9,8},{10,11... | collective-permute-start | bytes 417800 | tf_op jit(solution)/shard_map/ppermute | solution.py:428
  73.6 1.2 %slice.96 = f32[1,1,1]{2,1,0:T(1,128)} slice(f32[17,4,512]{2,1,0:T(4,128)} %gather_views.1.refs_3_), slice={[16:17], [0:1], [0:1]} | slice | bytes 8 | tf_op jit(solution)/shard_map/slice | solution.py:516
  83.8 1.9 %collective-permute-start.23 = (f32[1,1]{1,0:T(1,128)}, f32[1,1]{1,0:T(1,128)}, u32[]{:S(2)}, u32[]{:S(2)}) collective-permute-start(f32[1,1]{1,0:T(1,128)} %bitcast.15), channel_id=1, source_target_pairs={{0,16},{8,24},{16,0},{24,8},{1,17},{9,25},{17,1},{25,9},{2,18},{10... | collective-permute-start | bytes 20 | tf_op jit(solution)/shard_map/ppermute | solution.py:428
  85.7 1.3 %collective-permute-start.24 = (f32[1,1]{1,0:T(1,128)}, f32[1,1]{1,0:T(1,128)}, u32[]{:S(2)}, u32[]{:S(2)}) collective-permute-start(f32[1,1]{1,0:T(1,128)} %bitcast.15), channel_id=1, source_target_pairs={{0,24},{8,16},{16,8},{24,0},{1,25},{9,17},{17,9},{25,1},{2,26},{10... | collective-permute-start | bytes 20 | tf_op jit(solution)/shard_map/ppermute | solution.py:428
  87.0 2.0 %collective-permute-start.22 = (f32[1,1]{1,0:T(1,128)}, f32[1,1]{1,0:T(1,128)}, u32[]{:S(2)}, u32[]{:S(2)}) collective-permute-start(f32[1,1]{1,0:T(1,128)} %bitcast.15), channel_id=1, source_target_pairs={{0,8},{8,0},{16,24},{24,16},{1,9},{9,1},{17,25},{25,17},{2,10},{10... | collective-permute-start | bytes 20 | tf_op jit(solution)/shard_map/ppermute | solution.py:428
  90.9 2.7 %finish.1 = f32[16,4,4096]{2,1,0:T(4,128)} custom-call(s32[8]{0:T(128)} %stack.48.refs_0_, f32[1]{0:T(128)} %bitcast.16.refs_1_, f32[16,4,4096]{2,1,0:T(4,128)} %refs_2_.1, f32[17,4,512]{2,1,0:T(4,128)} %gather_views.1.refs_3_, f32[17,4,512]{2,1,0:T(4,128)} %copy-done.5, f32[17,4,512]{2,1,0:T(4,128)} %copy-done.3, f32[17,4,512]{2,1,0:T(4,128)} %copy-done.4, ...), custom_call_target="tpu_custom_call" | custom-call | tf_op jit(solution)/shard_map/finish/pallas_call | solution.py:418
  (92 shorter events, 10.1 us)
Async XLA Ops:
  0.0 25.7 %copy-start = (f32[16,4,4096]{2,1,0:T(4,128)S(1)}, f32[16,4,4096]{2,1,0:T(4,128)}, u32[]{:S(2)}) copy-start(f32[16,4,4096]{2,1,0:T(4,128)} %param.7) | copy-start | bytes 3145732
  2.0 23.0 %copy-start.1 = (f32[16,4,4096]{2,1,0:T(4,128)S(1)}, f32[16,4,4096]{2,1,0:T(4,128)}, u32[]{:S(2)}) copy-start(f32[16,4,4096]{2,1,0:T(4,128)} %refs_2_.1) | copy-start | bytes 3145732
  2.1 23.5 %copy-start.2 = (f32[2,24,16,128]{3,2,1,0:T(8,128)}, f32[2,24,16,128]{3,2,1,0:T(8,128)S(1)}, u32[]{:S(2)}) copy-start(f32[2,24,16,128]{3,2,1,0:T(8,128)S(1)} %maximum_maximum_fusion.refs_6_) | copy-start | bytes 1179652
  2.1 22.3 %collective-permute-start.1 = (f32[2,24,16,128]{3,2,1,0:T(8,128)S(1)}, f32[2,24,16,128]{3,2,1,0:T(8,128)}, u32[]{:S(2)}, u32[]{:S(2)}) collective-permute-start(f32[2,24,16,128]{3,2,1,0:T(8,128)S(1)} %maximum_maximum_fusion.refs_6_), channel_id=1, source_target_pairs={{0,16},{8,24},{16,0},{24,8},{1,17},{9,25},{17,1},{25,9},{2,18},{10... | collective-permute-start | bytes 1179656 | tf_op jit(solution)/shard_map/ppermute | solution.py:428
  13.8 10.6 %collective-permute-start.4 = (f32[2,23,16,128]{3,2,1,0:T(8,128)}, f32[2,23,16,128]{3,2,1,0:T(8,128)}, u32[]{:S(2)}, u32[]{:S(2)}) collective-permute-start(f32[2,23,16,128]{3,2,1,0:T(8,128)} %project.1.refs_2_), channel_id=1, source_target_pairs={{0,16},{8,24},{16,0},{24,8},{1,17},{9,25},{17,1},{25,9},{2,18},{10... | collective-permute-start | bytes 1130504 | tf_op jit(solution)/shard_map/ppermute | solution.py:428
  13.9 13.3 %collective-permute-start.3 = (f32[2,23,16,128]{3,2,1,0:T(8,128)}, f32[2,23,16,128]{3,2,1,0:T(8,128)}, u32[]{:S(2)}, u32[]{:S(2)}) collective-permute-start(f32[2,23,16,128]{3,2,1,0:T(8,128)} %project.1.refs_2_), channel_id=1, source_target_pairs={{0,8},{8,0},{16,24},{24,16},{1,9},{9,1},{17,25},{25,17},{2,10},{10... | collective-permute-start | bytes 1130504 | tf_op jit(solution)/shard_map/ppermute | solution.py:428
  13.9 13.2 %collective-permute-start = (f32[2,24,16,128]{3,2,1,0:T(8,128)S(1)}, f32[2,24,16,128]{3,2,1,0:T(8,128)}, u32[]{:S(2)}, u32[]{:S(2)}) collective-permute-start(f32[2,24,16,128]{3,2,1,0:T(8,128)S(1)} %maximum_maximum_fusion.refs_6_), channel_id=1, source_target_pairs={{0,8},{8,0},{16,24},{24,16},{1,9},{9,1},{17,25},{25,17},{2,10},{10... | collective-permute-start | bytes 1179656 | tf_op jit(solution)/shard_map/ppermute | solution.py:428
  24.4 2.8 %collective-permute-start.5 = (f32[2,23,16,128]{3,2,1,0:T(8,128)}, f32[2,23,16,128]{3,2,1,0:T(8,128)}, u32[]{:S(2)}, u32[]{:S(2)}) collective-permute-start(f32[2,23,16,128]{3,2,1,0:T(8,128)} %collective-permute-done.4.refs_4_), channel_id=1, source_target_pairs={{0,8},{8,0},{16,24},{24,16},{1,9},{9,1},{17,25},{25,17},{2,10},{10... | collective-permute-start | bytes 1130504 | tf_op jit(solution)/shard_map/ppermute | solution.py:428
  24.4 2.8 %collective-permute-start.2 = (f32[2,24,16,128]{3,2,1,0:T(8,128)}, f32[2,24,16,128]{3,2,1,0:T(8,128)}, u32[]{:S(2)}, u32[]{:S(2)}) collective-permute-start(f32[2,24,16,128]{3,2,1,0:T(8,128)} %collective-permute-done.1.refs_8_), channel_id=1, source_target_pairs={{0,8},{8,0},{16,24},{24,16},{1,9},{9,1},{17,25},{25,17},{2,10},{10... | collective-permute-start | bytes 1179656 | tf_op jit(solution)/shard_map/ppermute | solution.py:428
  30.3 9.9 %collective-permute-start.10 = (f32[2,3,16,128]{3,2,1,0:T(8,128)}, f32[2,3,16,128]{3,2,1,0:T(8,128)S(1)}, u32[]{:S(2)}, u32[]{:S(2)}) collective-permute-start(f32[2,3,16,128]{3,2,1,0:T(8,128)} %get-tuple-element.22), channel_id=1, source_target_pairs={{0,5},{1,4},{2,7},{3,6},{4,1},{5,0},{6,3},{7,2},{8,13},{9,12},{10,... | collective-permute-start | bytes 147464 | tf_op jit(solution)/shard_map/ppermute | solution.py:428
  33.9 8.3 %collective-permute-start.11 = (f32[2,3,16,128]{3,2,1,0:T(8,128)}, f32[2,3,16,128]{3,2,1,0:T(8,128)S(1)}, u32[]{:S(2)}, u32[]{:S(2)}) collective-permute-start(f32[2,3,16,128]{3,2,1,0:T(8,128)} %get-tuple-element.23), channel_id=1, source_target_pairs={{0,6},{1,7},{2,4},{3,5},{4,2},{5,3},{6,0},{7,1},{8,14},{9,15},{10,... | collective-permute-start | bytes 147464 | tf_op jit(solution)/shard_map/ppermute | solution.py:428
  35.3 9.9 %collective-permute-start.12 = (f32[2,3,16,128]{3,2,1,0:T(8,128)}, f32[2,3,16,128]{3,2,1,0:T(8,128)S(1)}, u32[]{:S(2)}, u32[]{:S(2)}) collective-permute-start(f32[2,3,16,128]{3,2,1,0:T(8,128)} %get-tuple-element.24), channel_id=1, source_target_pairs={{0,7},{1,6},{2,5},{3,4},{4,3},{5,2},{6,1},{7,0},{8,15},{9,14},{10,... | collective-permute-start | bytes 147464 | tf_op jit(solution)/shard_map/ppermute | solution.py:428
  37.7 7.5 %collective-permute-start.6 = (f32[2,3,16,128]{3,2,1,0:T(8,128)}, f32[2,3,16,128]{3,2,1,0:T(8,128)S(1)}, u32[]{:S(2)}, u32[]{:S(2)}) collective-permute-start(f32[2,3,16,128]{3,2,1,0:T(8,128)} %get-tuple-element.18), channel_id=1, source_target_pairs={{0,1},{1,0},{2,3},{3,2},{4,5},{5,4},{6,7},{7,6},{8,9},{9,8},{10,11... | collective-permute-start | bytes 147464 | tf_op jit(solution)/shard_map/ppermute | solution.py:428
  39.2 5.9 %collective-permute-start.7 = (f32[2,3,16,128]{3,2,1,0:T(8,128)}, f32[2,3,16,128]{3,2,1,0:T(8,128)S(1)}, u32[]{:S(2)}, u32[]{:S(2)}) collective-permute-start(f32[2,3,16,128]{3,2,1,0:T(8,128)} %get-tuple-element.19), channel_id=1, source_target_pairs={{0,2},{1,3},{2,0},{3,1},{4,6},{5,7},{6,4},{7,5},{8,10},{9,11},{10,... | collective-permute-start | bytes 147464 | tf_op jit(solution)/shard_map/ppermute | solution.py:428
  40.2 5.3 %collective-permute-start.8 = (f32[2,3,16,128]{3,2,1,0:T(8,128)}, f32[2,3,16,128]{3,2,1,0:T(8,128)S(1)}, u32[]{:S(2)}, u32[]{:S(2)}) collective-permute-start(f32[2,3,16,128]{3,2,1,0:T(8,128)} %get-tuple-element.20), channel_id=1, source_target_pairs={{0,3},{1,2},{2,1},{3,0},{4,7},{5,6},{6,5},{7,4},{8,11},{9,10},{10,... | collective-permute-start | bytes 147464 | tf_op jit(solution)/shard_map/ppermute | solution.py:428
  42.2 5.3 %collective-permute-start.9 = (f32[2,3,16,128]{3,2,1,0:T(8,128)}, f32[2,3,16,128]{3,2,1,0:T(8,128)S(1)}, u32[]{:S(2)}, u32[]{:S(2)}) collective-permute-start(f32[2,3,16,128]{3,2,1,0:T(8,128)} %get-tuple-element.21), channel_id=1, source_target_pairs={{0,4},{1,5},{2,6},{3,7},{4,0},{5,1},{6,2},{7,3},{8,12},{9,13},{10,... | collective-permute-start | bytes 147464 | tf_op jit(solution)/shard_map/ppermute | solution.py:428
  54.4 5.3 %collective-permute-start.13 = (f32[17,4,512]{2,1,0:T(4,128)}, f32[17,4,512]{2,1,0:T(4,128)S(1)}, u32[]{:S(2)}, u32[]{:S(2)}) collective-permute-start(f32[17,4,512]{2,1,0:T(4,128)} %gather_views.1.refs_3_), channel_id=1, source_target_pairs={{0,2},{1,3},{2,0},{3,1},{4,6},{5,7},{6,4},{7,5},{8,10},{9,11},{10,... | collective-permute-start | bytes 417800 | tf_op jit(solution)/shard_map/ppermute | solution.py:437
  54.4 5.9 %collective-permute-start.14 = (f32[17,4,512]{2,1,0:T(4,128)}, f32[17,4,512]{2,1,0:T(4,128)S(1)}, u32[]{:S(2)}, u32[]{:S(2)}) collective-permute-start(f32[17,4,512]{2,1,0:T(4,128)} %gather_views.1.refs_3_), channel_id=1, source_target_pairs={{2,4},{3,5},{4,2},{5,3},{10,12},{11,13},{12,10},{13,11},{18,20},{1... | collective-permute-start | bytes 417800 | tf_op jit(solution)/shard_map/ppermute | solution.py:437
  59.7 31.2 %copy-start.5 = (f32[17,4,512]{2,1,0:T(4,128)}, f32[17,4,512]{2,1,0:T(4,128)S(1)}, u32[]{:S(2)}) copy-start(f32[17,4,512]{2,1,0:T(4,128)S(1)} %collective-permute-done.13.refs_4_) | copy-start | bytes 417796
  59.7 4.1 %collective-permute-start.16 = (f32[17,4,512]{2,1,0:T(4,128)S(1)}, f32[17,4,512]{2,1,0:T(4,128)S(1)}, u32[]{:S(2)}, u32[]{:S(2)}) collective-permute-start(f32[17,4,512]{2,1,0:T(4,128)S(1)} %collective-permute-done.13.refs_4_), channel_id=1, source_target_pairs={{2,4},{3,5},{4,2},{5,3},{10,12},{11,13},{12,10},{13,11},{18,20},{1... | collective-permute-start | bytes 417800 | tf_op jit(solution)/shard_map/ppermute | solution.py:437
  60.3 8.0 %collective-permute-start.15 = (f32[17,4,512]{2,1,0:T(4,128)S(1)}, f32[17,4,512]{2,1,0:T(4,128)S(1)}, u32[]{:S(2)}, u32[]{:S(2)}) collective-permute-start(f32[17,4,512]{2,1,0:T(4,128)S(1)} %collective-permute-done.14), channel_id=1, source_target_pairs={{2,0},{3,1},{4,6},{5,7},{10,8},{11,9},{12,14},{13,15},{18,16},{19,... | collective-permute-start | bytes 417800 | tf_op jit(solution)/shard_map/ppermute | solution.py:437
  61.7 14.8 %collective-permute-start.18 = (f32[17,4,512]{2,1,0:T(4,128)}, f32[17,4,512]{2,1,0:T(4,128)S(1)}, u32[]{:S(2)}, u32[]{:S(2)}) collective-permute-start(f32[17,4,512]{2,1,0:T(4,128)} %gather_views.1.refs_3_), channel_id=1, source_target_pairs={{0,1},{1,0},{2,3},{3,2},{4,5},{5,4},{6,7},{7,6},{8,9},{9,8},{10,11... | collective-permute-start | bytes 417800 | tf_op jit(solution)/shard_map/ppermute | solution.py:428
  63.1 14.4 %collective-permute-start.19 = (f32[17,4,512]{2,1,0:T(4,128)S(1)}, f32[17,4,512]{2,1,0:T(4,128)S(1)}, u32[]{:S(2)}, u32[]{:S(2)}) collective-permute-start(f32[17,4,512]{2,1,0:T(4,128)S(1)} %collective-permute-done.13.refs_4_), channel_id=1, source_target_pairs={{0,1},{1,0},{2,3},{3,2},{4,5},{5,4},{6,7},{7,6},{8,9},{9,8},{10,11... | collective-permute-start | bytes 417800 | tf_op jit(solution)/shard_map/ppermute | solution.py:428
  63.7 8.0 %collective-permute-start.17 = (f32[17,4,512]{2,1,0:T(4,128)S(1)}, f32[17,4,512]{2,1,0:T(4,128)S(1)}, u32[]{:S(2)}, u32[]{:S(2)}) collective-permute-start(f32[17,4,512]{2,1,0:T(4,128)S(1)} %collective-permute-done.16), channel_id=1, source_target_pairs={{2,0},{3,1},{4,6},{5,7},{10,8},{11,9},{12,14},{13,15},{18,16},{19,... | collective-permute-start | bytes 417800 | tf_op jit(solution)/shard_map/ppermute | solution.py:437
  68.4 22.5 %copy-start.3 = (f32[17,4,512]{2,1,0:T(4,128)}, f32[17,4,512]{2,1,0:T(4,128)S(1)}, u32[]{:S(2)}) copy-start(f32[17,4,512]{2,1,0:T(4,128)S(1)} %broadcast_select_fusion.1.refs_5_) | copy-start | bytes 417796
  68.4 12.9 %collective-permute-start.20 = (f32[17,4,512]{2,1,0:T(4,128)S(1)}, f32[17,4,512]{2,1,0:T(4,128)S(1)}, u32[]{:S(2)}, u32[]{:S(2)}) collective-permute-start(f32[17,4,512]{2,1,0:T(4,128)S(1)} %broadcast_select_fusion.1.refs_5_), channel_id=1, source_target_pairs={{0,1},{1,0},{2,3},{3,2},{4,5},{5,4},{6,7},{7,6},{8,9},{9,8},{10,11... | collective-permute-start | bytes 417800 | tf_op jit(solution)/shard_map/ppermute | solution.py:428
  71.8 19.1 %copy-start.4 = (f32[17,4,512]{2,1,0:T(4,128)}, f32[17,4,512]{2,1,0:T(4,128)S(1)}, u32[]{:S(2)}) copy-start(f32[17,4,512]{2,1,0:T(4,128)S(1)} %broadcast_select_fusion.refs_6_) | copy-start | bytes 417796
  71.8 10.1 %collective-permute-start.21 = (f32[17,4,512]{2,1,0:T(4,128)S(1)}, f32[17,4,512]{2,1,0:T(4,128)S(1)}, u32[]{:S(2)}, u32[]{:S(2)}) collective-permute-start(f32[17,4,512]{2,1,0:T(4,128)S(1)} %broadcast_select_fusion.refs_6_), channel_id=1, source_target_pairs={{0,1},{1,0},{2,3},{3,2},{4,5},{5,4},{6,7},{7,6},{8,9},{9,8},{10,11... | collective-permute-start | bytes 417800 | tf_op jit(solution)/shard_map/ppermute | solution.py:428
  76.4 14.5 %copy-start.6 = (f32[17,4,512]{2,1,0:T(4,128)}, f32[17,4,512]{2,1,0:T(4,128)S(1)}, u32[]{:S(2)}) copy-start(f32[17,4,512]{2,1,0:T(4,128)S(1)} %collective-permute-done.18.refs_7_) | copy-start | bytes 417796
  83.8 5.7 %collective-permute-start.23 = (f32[1,1]{1,0:T(1,128)}, f32[1,1]{1,0:T(1,128)}, u32[]{:S(2)}, u32[]{:S(2)}) collective-permute-start(f32[1,1]{1,0:T(1,128)} %bitcast.15), channel_id=1, source_target_pairs={{0,16},{8,24},{16,0},{24,8},{1,17},{9,25},{17,1},{25,9},{2,18},{10... | collective-permute-start | bytes 20 | tf_op jit(solution)/shard_map/ppermute | solution.py:428
  85.7 3.9 %collective-permute-start.24 = (f32[1,1]{1,0:T(1,128)}, f32[1,1]{1,0:T(1,128)}, u32[]{:S(2)}, u32[]{:S(2)}) collective-permute-start(f32[1,1]{1,0:T(1,128)} %bitcast.15), channel_id=1, source_target_pairs={{0,24},{8,16},{16,8},{24,0},{1,25},{9,17},{17,9},{25,1},{2,26},{10... | collective-permute-start | bytes 20 | tf_op jit(solution)/shard_map/ppermute | solution.py:428
  87.0 2.0 %collective-permute-start.22 = (f32[1,1]{1,0:T(1,128)}, f32[1,1]{1,0:T(1,128)}, u32[]{:S(2)}, u32[]{:S(2)}) collective-permute-start(f32[1,1]{1,0:T(1,128)} %bitcast.15), channel_id=1, source_target_pairs={{0,8},{8,0},{16,24},{24,16},{1,9},{9,1},{17,25},{25,17},{2,10},{10... | collective-permute-start | bytes 20 | tf_op jit(solution)/shard_map/ppermute | solution.py:428
  (12 other events, 72.3 us)

commit v5 on v4

--- a/solution.py
+++ b/solution.py
@@ -401,27 +401,55 @@
     )(ints, tv, curv, *pieces)
 
 
-def finish_kernel(parts_n, order_ref, factor_ref, vol_ref, *rest):
-    pieces = rest[:parts_n]
-    out_ref = rest[parts_n]
-    factor = factor_ref[0]
+def total_kernel(*refs):
+    sums = [ref[0, 0:1, :] for ref in refs[:-1]]
+    while len(sums) > 1:
+        sums = [a + b for a, b in zip(sums[0::2], sums[1::2])]
+    refs[-1][...] = sums[0]
+
+
+def total(pieces):
+    slices_n, rows_n, _ = pieces[0].shape
+    last = pl.BlockSpec((1, rows_n, LANES), lambda i: (slices_n - 1, 0, 0))
+    return pl.pallas_call(
+        total_kernel,
+        grid=(1,),
+        out_shape=jax.ShapeDtypeStruct((1, LANES), jnp.float32),
+        in_specs=[last] * len(pieces),
+        out_specs=pl.BlockSpec((1, LANES), lambda i: (0, 0)),
+        name="total",
+    )(*pieces)
+
+
+def finish_kernel(parts_n, voxel_count, ints_ref, *rest):
+    sums, vol_ref, pieces = rest[:4], rest[4], rest[5 : 5 + parts_n]
+    out_ref = rest[5 + parts_n]
+    squares = sums[0][...] + sums[1][...] + (sums[2][...] + sums[3][...])
+    rms = jnp.sqrt(squares / float(voxel_count) + epsilon)
+    factor = jnp.max(jnp.minimum(1.0, step_limit / rms))
     slices_n, _, per_n = pieces[0].shape
+    part = ints_ref[1]
+    depth = part >> 1
+    upper = depth >> 1
+    side = part & 1
+    depths = [depth, depth ^ 1, 2 - upper, 3 - 3 * upper]
+    order = [2 * d + side for d in depths] + [2 * d + 1 - side for d in depths]
     for r in range(parts_n):
-        cols = pl.ds(pl.multiple_of(order_ref[r] * per_n, per_n), per_n)
+        cols = pl.ds(pl.multiple_of(order[r] * per_n, per_n), per_n)
         out_ref[:, :, cols] = vol_ref[:, :, cols] - factor * pieces[r][0 : slices_n - 1]
 
 
-def finish(order, factor, volume, pieces):
+def finish(voxel_count, ints, sums, volume, pieces):
     parts_n = len(pieces)
     vmem = pl.BlockSpec(memory_space=pltpu.VMEM)
     smem = pl.BlockSpec(memory_space=pltpu.SMEM)
     return pl.pallas_call(
-        lambda *refs: finish_kernel(parts_n, *refs),
+        lambda *refs: finish_kernel(parts_n, voxel_count, *refs),
         out_shape=jax.ShapeDtypeStruct(volume.shape, volume.dtype),
-        in_specs=[smem, smem] + [vmem] * (parts_n + 1),
+        in_specs=[smem] + [vmem] * (parts_n + 5),
         out_specs=vmem,
         name="finish",
-    )(order, factor, volume, *pieces)
+    )(ints, *sums, volume, *pieces)
 
 
 def swapped(x, axis, bit):
@@ -446,10 +474,7 @@
     across.append(swapped(third, "view", 1))
     last = jnp.where(end, along(middle_last, [(1, 0), (2, 3)]), middle_last)
     across.append(swapped(last, "view", 1))
-    upper = depth // 2
-    depths = [depth, depth ^ 1, 2 - upper, 3 - 3 * upper]
-    order = jnp.stack([2 * d + part % 2 for d in depths] + [2 * d + 1 - part % 2 for d in depths])
-    return order.astype(jnp.int32), [piece, second, third, last] + across
+    return [piece, second, third, last] + across
 
 
 def local_split(volume, sinogram, curvature, angles, offsets):
@@ -512,15 +537,11 @@
     tv_grad = tv_padded(jnp.pad(block, ((0, 0), (1, 1), (0, 0))))
     curv = lax.dynamic_slice_in_dim(curvature, part * per_n, per_n, axis=2)
     tv = (tv_weight * tv_grad).transpose(1, 0, 2)
-    order, parts = gathered(gather_views(dims, parts_n, ints, tv, curv.transpose(1, 0, 2), pieces))
-    sums = [p[slices_n, 0, 0] for p in parts]
-    while len(sums) > 1:
-        sums = [a + b for a, b in zip(sums[0::2], sums[1::2])]
-    squares = sums[0].reshape(1, 1)
-    squares = squares + swapped(squares, "slab", 1) + (swapped(squares, "slab", 2) + swapped(squares, "slab", 3))
+    parts = gathered(gather_views(dims, parts_n, ints, tv, curv.transpose(1, 0, 2), pieces))
+    squares = total(parts)
+    sums = [squares] + [swapped(squares, "slab", k) for k in (1, 2, 3)]
     voxel_count = slices_n * slab_count * rows_n * cols_n
-    factor = jnp.minimum(1.0, step_limit / jnp.sqrt(squares / voxel_count + epsilon))
-    return finish(order, factor.reshape(1), volume, parts)
+    return finish(voxel_count, ints, sums, volume, parts)
 
 
 def local(volume, sinogram, curvature, angles, offsets):

time: 94.2 us -> 86.8 us (0.921)
  between operations: 7.42 us -> 0.36 us
  waiting for transfers between devices: 22.3 us -> 28.1 us
  local copies, waits for them, and re-layouts: 9.99 us -> 5.97 us
  starting transfers between devices: 30.4 us -> 27.1 us
  Pallas kernels: 20.1 us -> 21.5 us
    ppermute x20, waiting for transfers between devices: 12.2 us -> 18.1 us  [swapped(): lax.ppermute(x, axis, [(i, i ^ bit) for i in range(lax.axis_size(axis))])]
    slice x8 -> x0, local copies, waits for them, and re-layouts: 5.06 us -> none  [local_split(): sums = [p[slices_n, 0, 0] for p in parts]]
    ppermute x20, starting transfers between devices: 26.5 us -> 23.1 us  [swapped(): lax.ppermute(x, axis, [(i, i ^ bit) for i in range(lax.axis_size(axis))])]
    unnamed x40 -> x46, local copies, waits for them, and re-layouts: 1.94 us -> 3.62 us
    pallas_call x1 -> x2, Pallas kernels: 2.74 us -> 4.07 us  [the longest x1 2.88 us: finish(): pl.pallas_call(lambda *refs: finish_kernel(parts_n, voxel_count, *refs),...]
  transfers between devices with their start and end apart: 25 -> 25, of which waited for: 6 -> 9; matrix products, arithmetic and copies ran while one was open for 11% -> 6% of each run, Pallas kernels for 9% -> 9%
where the time goes in v5:
time: 86.8 us; the launch traced here: 86.4 us
  waiting for transfers between devices  28.1 us (32%)
  starting transfers between devices  27.1 us (31%)
  Pallas kernels  21.5 us (25%)
  local copies, waits for them, and re-layouts  5.97 us (7%)
  other arithmetic  3.41 us (4%)
    ppermute x20, starting transfers between devices, swapped(): lax.ppermute(x, axis, [(i, i ^ bit) for i in range(lax.axis_size(axis))])  23.1 us
    ppermute x20, waiting for transfers between devices, swapped(): lax.ppermute(x, axis, [(i, i ^ bit) for i in range(lax.axis_size(axis))])  18.1 us
    ppermute x5, waiting for transfers between devices, along(): lax.ppermute(x, 'view', [(2 * a + y, 2 * b + y) for a, b in pairs for y i...  10 us
    pallas_call x1, Pallas kernels, project(): pl.pallas_call(body, out_shape=jax.ShapeDtypeStruct((views_n, blocks_n, s...  8 us
    pallas_call x1, Pallas kernels, gather_views(): pl.pallas_call(body, out_shape=jax.ShapeDtypeStruct((slices_n + 1, rows_n...  6.23 us
    ppermute x5, starting transfers between devices, along(): lax.ppermute(x, 'view', [(2 * a + y, 2 * b + y) for a, b in pairs for y i...  3.94 us
    unnamed x46, local copies, waits for them, and re-layouts  3.62 us
    pallas_call x1, Pallas kernels, residual_windows(): pl.pallas_call(body, out_shape=[jax.ShapeDtypeStruct((views_n, WINDOW, ba...  3.15 us
  transfers between devices with their start and end apart: 25, of which 9 were waited for; matrix products, arithmetic and copies ran while one was open for 6% of the time, Pallas kernels for 9%

profile of v5, /device:TPU:0, one launch (start us, length us, event | category | flops | bytes accessed | tf_op | source)
XLA Modules:
  0.0 86.4 jit_solution(9481951815279994375)
XLA Ops:
  0.0 0.8 constant_dynamic-slice_fusion.2
  0.8 1.2 %bitcast_bitcast_fusion = f32[2,23,16,128]{3,2,1,0:T(8,128)S(1)} fusion(f32[2,16,4096]{2,1,0:T(8,128)} %param.6), kind=kLoop, calls=%fused_computation.7 | loop fusion | bytes 753664 | tf_op jit(solution)/shard_map/transpose | solution.py:500
  2.1 3.0 %collective-permute-start.1 = (f32[2,24,16,128]{3,2,1,0:T(8,128)S(1)}, f32[2,24,16,128]{3,2,1,0:T(8,128)}, u32[]{:S(2)}, u32[]{:S(2)}) collective-permute-start(f32[2,24,16,128]{3,2,1,0:T(8,128)S(1)} %maximum_maximum_fusion.refs_6_), channel_id=1, source_target_pairs={{0,16},{8,24},{16,0},{24,8},{1,17},{9,25},{17,1},{25,9},{2,18},{10... | collective-permute-start | bytes 1179656 | tf_op jit(solution)/shard_map/ppermute | solution.py:456
  5.8 8.0 %project.1.refs_2_ = f32[2,23,16,128]{3,2,1,0:T(8,128)} custom-call(f32[4]{0:T(128)} %pad_maximum_fusion.2.refs_0_.refs_1_, f32[16,4,4096]{2,1,0:T(4,128)} %refs_5_.1), custom_call_target="tpu_custom_call" | custom-call | tf_op jit(solution)/shard_map/project/pallas_call | solution.py:100
  14.6 9.8 %collective-permute-done.4.refs_4_ = f32[2,23,16,128]{3,2,1,0:T(8,128)} collective-permute-done((f32[2,23,16,128]{3,2,1,0:T(8,128)}, f32[2,23,16,128]{3,2,1,0:T(8,128)}, u32[]{:S(2)}, u32[]{:S(2)}) %collective-permute-start.4) | collective-permute-done | bytes 376864 | tf_op jit(solution)/shard_map/ppermute | solution.py:456
  25.7 0.7 copy.15
  27.1 3.2 %residual_windows.1 = (f32[2,3,16,128]{3,2,1,0:T(8,128)}, f32[2,3,16,128]{3,2,1,0:T(8,128)}, f32[2,3,16,128]{3,2,1,0:T(8,128)}, f32[2,3,16,128]{3,2,1,0:T(8,128)...) custom-call(s32[10]{0:T(128)} %pad_add_fusion.1.refs_0_, ...), custom_call_target="tpu_custom_call" | custom-call | tf_op jit(solution)/shard_map/residual_windows/pallas_call | solution.py:314
  30.3 3.6 %collective-permute-start.10 = (f32[2,3,16,128]{3,2,1,0:T(8,128)}, f32[2,3,16,128]{3,2,1,0:T(8,128)S(1)}, u32[]{:S(2)}, u32[]{:S(2)}) collective-permute-start(f32[2,3,16,128]{3,2,1,0:T(8,128)} %get-tuple-element.22), channel_id=1, source_target_pairs={{0,5},{1,4},{2,7},{3,6},{4,1},{5,0},{6,3},{7,2},{8,13},{9,12},{10,... | collective-permute-start | bytes 147464 | tf_op jit(solution)/shard_map/ppermute | solution.py:456
  33.8 1.4 %collective-permute-start.11 = (f32[2,3,16,128]{3,2,1,0:T(8,128)}, f32[2,3,16,128]{3,2,1,0:T(8,128)S(1)}, u32[]{:S(2)}, u32[]{:S(2)}) collective-permute-start(f32[2,3,16,128]{3,2,1,0:T(8,128)} %get-tuple-element.23), channel_id=1, source_target_pairs={{0,6},{1,7},{2,4},{3,5},{4,2},{5,3},{6,0},{7,1},{8,14},{9,15},{10,... | collective-permute-start | bytes 147464 | tf_op jit(solution)/shard_map/ppermute | solution.py:456
  35.2 2.4 %collective-permute-start.12 = (f32[2,3,16,128]{3,2,1,0:T(8,128)}, f32[2,3,16,128]{3,2,1,0:T(8,128)S(1)}, u32[]{:S(2)}, u32[]{:S(2)}) collective-permute-start(f32[2,3,16,128]{3,2,1,0:T(8,128)} %get-tuple-element.24), channel_id=1, source_target_pairs={{0,7},{1,6},{2,5},{3,4},{4,3},{5,2},{6,1},{7,0},{8,15},{9,14},{10,... | collective-permute-start | bytes 147464 | tf_op jit(solution)/shard_map/ppermute | solution.py:456
  37.6 1.5 %collective-permute-start.6 = (f32[2,3,16,128]{3,2,1,0:T(8,128)}, f32[2,3,16,128]{3,2,1,0:T(8,128)S(1)}, u32[]{:S(2)}, u32[]{:S(2)}) collective-permute-start(f32[2,3,16,128]{3,2,1,0:T(8,128)} %get-tuple-element.18), channel_id=1, source_target_pairs={{0,1},{1,0},{2,3},{3,2},{4,5},{5,4},{6,7},{7,6},{8,9},{9,8},{10,11... | collective-permute-start | bytes 147464 | tf_op jit(solution)/shard_map/ppermute | solution.py:456
  39.1 0.8 fusion.24
  40.1 2.0 %collective-permute-start.8 = (f32[2,3,16,128]{3,2,1,0:T(8,128)}, f32[2,3,16,128]{3,2,1,0:T(8,128)S(1)}, u32[]{:S(2)}, u32[]{:S(2)}) collective-permute-start(f32[2,3,16,128]{3,2,1,0:T(8,128)} %get-tuple-element.20), channel_id=1, source_target_pairs={{0,3},{1,2},{2,1},{3,0},{4,7},{5,6},{6,5},{7,4},{8,11},{9,10},{10,... | collective-permute-start | bytes 147464 | tf_op jit(solution)/shard_map/ppermute | solution.py:456
  42.2 1.9 %collective-permute-start.9 = (f32[2,3,16,128]{3,2,1,0:T(8,128)}, f32[2,3,16,128]{3,2,1,0:T(8,128)S(1)}, u32[]{:S(2)}, u32[]{:S(2)}) collective-permute-start(f32[2,3,16,128]{3,2,1,0:T(8,128)} %get-tuple-element.21), channel_id=1, source_target_pairs={{0,4},{1,5},{2,6},{3,7},{4,0},{5,1},{6,2},{7,3},{8,12},{9,13},{10,... | collective-permute-start | bytes 147464 | tf_op jit(solution)/shard_map/ppermute | solution.py:456
  44.0 1.0 %fusion.7.refs_1_ = f32[4,16,512]{2,1,0:T(8,128)} fusion(s32[]{:T(128)S(6)} %select_n.114, f32[16,4,4096]{2,0,1:T(8,128)S(1)} %copy.8, s32[]{:T(128)S(6)} %add.70, f32[18,6,514]{2,0,1:T(8,128)S(1)} %select_maximum_fusion, f32[1,4,514]{2,0,1:T(1,128)S(1)} %pad.17, f32[16,4,514]{2,0,1:T(8,128)S(1)} %pad_dynamic-slice_fusion.3, s32[]{:T(128)S(6)} %add.69, ...), kind=kLoop, calls=%fused_computation.18 | loop fusion | flops 851968 | bytes 1589836 | tf_op jit(solution)/shard_map/transpose | solution.py:539
  45.4 2.1 %collective-permute-done.9.refs_7_ = f32[2,3,16,128]{3,2,1,0:T(8,128)S(1)} collective-permute-done((f32[2,3,16,128]{3,2,1,0:T(8,128)}, f32[2,3,16,128]{3,2,1,0:T(8,128)S(1)}, u32[]{:S(2)}, u32[]{:S(2)}) %collective-permute-start.9) | collective-permute-done | bytes 49184 | tf_op jit(solution)/shard_map/ppermute | solution.py:456
  48.1 6.2 %gather_views.1.refs_0_.refs_6_ = f32[17,4,512]{2,1,0:T(4,128)} custom-call(s32[10]{0:T(128)} %pad_add_fusion.1.refs_0_, f32[4,16,512]{2,1,0:T(8,128)} %fusion.7.refs_1_, f32[4,16,512]{2,1,0:T(8,128)} %bitcast.16, f32[2,3,16,128]{3,2,1,0:T(8,128)} %get-tuple-element.17.refs_3_, f32[2,3,16,128]{3,2,1,0:T(8,128)} %copy-done.13, f32[2,3,16,128]{3,2,1,0:T(8,128)} %copy-done.14, ...), custom_call_target="tpu_custom_call" | custom-call | tf_op jit(solution)/shard_map/gather_views/pallas_call | solution.py:390
  55.0 4.6 %collective-permute-done.13.refs_1_.refs_7_ = f32[17,4,512]{2,1,0:T(4,128)S(1)} collective-permute-done((f32[17,4,512]{2,1,0:T(4,128)}, f32[17,4,512]{2,1,0:T(4,128)S(1)}, u32[]{:S(2)}, u32[]{:S(2)}) %collective-permute-start.13) | collective-permute-done | bytes 139296 | tf_op jit(solution)/shard_map/ppermute | solution.py:465
  59.6 0.7 collective-permute-start.16
  60.3 1.3 %collective-permute-start.15 = (f32[17,4,512]{2,1,0:T(4,128)S(1)}, f32[17,4,512]{2,1,0:T(4,128)S(1)}, u32[]{:S(2)}, u32[]{:S(2)}) collective-permute-start(f32[17,4,512]{2,1,0:T(4,128)S(1)} %collective-permute-done.14), channel_id=1, source_target_pairs={{2,0},{3,1},{4,6},{5,7},{10,8},{11,9},{12,14},{13,15},{18,16},{19,... | collective-permute-start | bytes 417800 | tf_op jit(solution)/shard_map/ppermute | solution.py:465
  61.6 1.5 %collective-permute-start.18 = (f32[17,4,512]{2,1,0:T(4,128)}, f32[17,4,512]{2,1,0:T(4,128)S(1)}, u32[]{:S(2)}, u32[]{:S(2)}) collective-permute-start(f32[17,4,512]{2,1,0:T(4,128)} %gather_views.1.refs_0_.refs_6_), channel_id=1, source_target_pairs={{0,1},{1,0},{2,3},{3,2},{4,5},{5,4},{6,7},{7,6},{8,9},{9,8},{10,11... | collective-permute-start | bytes 417800 | tf_op jit(solution)/shard_map/ppermute | solution.py:456
  63.7 1.3 %collective-permute-start.17 = (f32[17,4,512]{2,1,0:T(4,128)S(1)}, f32[17,4,512]{2,1,0:T(4,128)S(1)}, u32[]{:S(2)}, u32[]{:S(2)}) collective-permute-start(f32[17,4,512]{2,1,0:T(4,128)S(1)} %collective-permute-done.16), channel_id=1, source_target_pairs={{2,0},{3,1},{4,6},{5,7},{10,8},{11,9},{12,14},{13,15},{18,16},{19,... | collective-permute-start | bytes 417800 | tf_op jit(solution)/shard_map/ppermute | solution.py:465
  65.0 3.3 %collective-permute-done.15 = f32[17,4,512]{2,1,0:T(4,128)S(1)} collective-permute-done((f32[17,4,512]{2,1,0:T(4,128)S(1)}, f32[17,4,512]{2,1,0:T(4,128)S(1)}, u32[]{:S(2)}, u32[]{:S(2)}) %collective-permute-start.15) | collective-permute-done | bytes 139296 | tf_op jit(solution)/shard_map/ppermute | solution.py:465
  68.3 1.1 %collective-permute-start.20 = (f32[17,4,512]{2,1,0:T(4,128)S(1)}, f32[17,4,512]{2,1,0:T(4,128)S(1)}, u32[]{:S(2)}, u32[]{:S(2)}) collective-permute-start(f32[17,4,512]{2,1,0:T(4,128)S(1)} %broadcast_select_fusion.1.refs_2_.refs_8_), channel_id=1, source_target_pairs={{0,1},{1,0},{2,3},{3,2},{4,5},{5,4},{6,7},{7,6},{8,9},{9,8},{10,11... | collective-permute-start | bytes 417800 | tf_op jit(solution)/shard_map/ppermute | solution.py:456
  69.4 2.2 %collective-permute-done.17 = f32[17,4,512]{2,1,0:T(4,128)S(1)} collective-permute-done((f32[17,4,512]{2,1,0:T(4,128)S(1)}, f32[17,4,512]{2,1,0:T(4,128)S(1)}, u32[]{:S(2)}, u32[]{:S(2)}) %collective-permute-start.17) | collective-permute-done | bytes 139296 | tf_op jit(solution)/shard_map/ppermute | solution.py:465
  71.7 1.1 %collective-permute-start.21 = (f32[17,4,512]{2,1,0:T(4,128)S(1)}, f32[17,4,512]{2,1,0:T(4,128)S(1)}, u32[]{:S(2)}, u32[]{:S(2)}) collective-permute-start(f32[17,4,512]{2,1,0:T(4,128)S(1)} %broadcast_select_fusion.refs_3_.refs_9_), channel_id=1, source_target_pairs={{0,1},{1,0},{2,3},{3,2},{4,5},{5,4},{6,7},{7,6},{8,9},{9,8},{10,11... | collective-permute-start | bytes 417800 | tf_op jit(solution)/shard_map/ppermute | solution.py:456
  73.4 3.4 %collective-permute-done.21.refs_7_.refs_13_ = f32[17,4,512]{2,1,0:T(4,128)S(1)} collective-permute-done((f32[17,4,512]{2,1,0:T(4,128)S(1)}, f32[17,4,512]{2,1,0:T(4,128)S(1)}, u32[]{:S(2)}, u32[]{:S(2)}) %collective-permute-start.21) | collective-permute-done | bytes 139296 | tf_op jit(solution)/shard_map/ppermute | solution.py:456
  76.9 0.7 copy-done.9
  77.5 1.2 %total.1.refs_1_ = f32[1,128]{1,0:T(1,128)} custom-call(f32[17,4,512]{2,1,0:T(4,128)} %gather_views.1.refs_0_.refs_6_, f32[17,4,512]{2,1,0:T(4,128)} %copy-done.5, f32[17,4,512]{2,1,0:T(4,128)} %copy-done.3, f32[17,4,512]{2,1,0:T(4,128)} %copy-done.4, f32[17,4,512]{2,1,0:T(4,128)} %copy-done.6, f32[17,4,512]{2,1,0:T(4,128)} %copy-done.7, ...), custom_call_target="tpu_custom_call" | custom-call | tf_op jit(solution)/shard_map/total/pallas_call | solution.py:414
  79.3 1.3 %collective-permute-start.24 = (f32[1,128]{1,0:T(1,128)}, f32[1,128]{1,0:T(1,128)S(1)}, u32[]{:S(2)}, u32[]{:S(2)}) collective-permute-start(f32[1,128]{1,0:T(1,128)} %total.1.refs_1_), channel_id=1, source_target_pairs={{0,24},{8,16},{16,8},{24,0},{1,25},{9,17},{17,9},{25,1},{2,26},{10... | collective-permute-start | bytes 1544 | tf_op jit(solution)/shard_map/ppermute | solution.py:456
  80.6 1.9 %collective-permute-done.23.refs_3_ = f32[1,128]{1,0:T(1,128)S(1)} collective-permute-done((f32[1,128]{1,0:T(1,128)}, f32[1,128]{1,0:T(1,128)S(1)}, u32[]{:S(2)}, u32[]{:S(2)}) %collective-permute-start.23) | collective-permute-done | bytes 544 | tf_op jit(solution)/shard_map/ppermute | solution.py:456
  83.5 2.9 %finish.1 = f32[16,4,4096]{2,1,0:T(4,128)} custom-call(s32[10]{0:T(128)} %pad_add_fusion.1.refs_0_, f32[1,128]{1,0:T(1,128)} %total.1.refs_1_, f32[1,128]{1,0:T(1,128)} %copy-done.18, f32[1,128]{1,0:T(1,128)} %copy-done.19, f32[1,128]{1,0:T(1,128)} %copy-done.20, f32[16,4,4096]{2,1,0:T(4,128)} %refs_5_.1, f32[17,4,512]{2,1,0:T(4,128)} %gather_views.1.refs_0_.refs_6_, ...), custom_call_target="tpu_custom_call" | custom-call | tf_op jit(solution)/shard_map/finish/pallas_call | solution.py:446
  (90 shorter events, 8.3 us)
Async XLA Ops:
  0.0 25.7 %copy-start = (f32[16,4,4096]{2,1,0:T(4,128)S(1)}, f32[16,4,4096]{2,1,0:T(4,128)}, u32[]{:S(2)}) copy-start(f32[16,4,4096]{2,1,0:T(4,128)} %param.7) | copy-start | bytes 3145732
  2.0 12.4 %copy-start.17 = (s32[2,4]{1,0:T(2,128)S(1)}, s32[2,4]{1,0:T(2,128)}, u32[]{:S(2)}) copy-start(s32[2,4]{1,0:T(2,128)} %param.9) | copy-start | bytes 100
  2.0 23.0 %copy-start.1 = (f32[16,4,4096]{2,1,0:T(4,128)S(1)}, f32[16,4,4096]{2,1,0:T(4,128)}, u32[]{:S(2)}) copy-start(f32[16,4,4096]{2,1,0:T(4,128)} %refs_5_.1) | copy-start | bytes 3145732
  2.1 23.5 %copy-start.2 = (f32[2,24,16,128]{3,2,1,0:T(8,128)}, f32[2,24,16,128]{3,2,1,0:T(8,128)S(1)}, u32[]{:S(2)}) copy-start(f32[2,24,16,128]{3,2,1,0:T(8,128)S(1)} %maximum_maximum_fusion.refs_6_) | copy-start | bytes 1179652
  2.1 22.3 %collective-permute-start.1 = (f32[2,24,16,128]{3,2,1,0:T(8,128)S(1)}, f32[2,24,16,128]{3,2,1,0:T(8,128)}, u32[]{:S(2)}, u32[]{:S(2)}) collective-permute-start(f32[2,24,16,128]{3,2,1,0:T(8,128)S(1)} %maximum_maximum_fusion.refs_6_), channel_id=1, source_target_pairs={{0,16},{8,24},{16,0},{24,8},{1,17},{9,25},{17,1},{25,9},{2,18},{10... | collective-permute-start | bytes 1179656 | tf_op jit(solution)/shard_map/ppermute | solution.py:456
  13.8 10.6 %collective-permute-start.4 = (f32[2,23,16,128]{3,2,1,0:T(8,128)}, f32[2,23,16,128]{3,2,1,0:T(8,128)}, u32[]{:S(2)}, u32[]{:S(2)}) collective-permute-start(f32[2,23,16,128]{3,2,1,0:T(8,128)} %project.1.refs_2_), channel_id=1, source_target_pairs={{0,16},{8,24},{16,0},{24,8},{1,17},{9,25},{17,1},{25,9},{2,18},{10... | collective-permute-start | bytes 1130504 | tf_op jit(solution)/shard_map/ppermute | solution.py:456
  13.9 13.2 %collective-permute-start.3 = (f32[2,23,16,128]{3,2,1,0:T(8,128)}, f32[2,23,16,128]{3,2,1,0:T(8,128)}, u32[]{:S(2)}, u32[]{:S(2)}) collective-permute-start(f32[2,23,16,128]{3,2,1,0:T(8,128)} %project.1.refs_2_), channel_id=1, source_target_pairs={{0,8},{8,0},{16,24},{24,16},{1,9},{9,1},{17,25},{25,17},{2,10},{10... | collective-permute-start | bytes 1130504 | tf_op jit(solution)/shard_map/ppermute | solution.py:456
  13.9 13.1 %collective-permute-start = (f32[2,24,16,128]{3,2,1,0:T(8,128)S(1)}, f32[2,24,16,128]{3,2,1,0:T(8,128)}, u32[]{:S(2)}, u32[]{:S(2)}) collective-permute-start(f32[2,24,16,128]{3,2,1,0:T(8,128)S(1)} %maximum_maximum_fusion.refs_6_), channel_id=1, source_target_pairs={{0,8},{8,0},{16,24},{24,16},{1,9},{9,1},{17,25},{25,17},{2,10},{10... | collective-permute-start | bytes 1179656 | tf_op jit(solution)/shard_map/ppermute | solution.py:456
  24.4 2.7 %collective-permute-start.5 = (f32[2,23,16,128]{3,2,1,0:T(8,128)}, f32[2,23,16,128]{3,2,1,0:T(8,128)}, u32[]{:S(2)}, u32[]{:S(2)}) collective-permute-start(f32[2,23,16,128]{3,2,1,0:T(8,128)} %collective-permute-done.4.refs_4_), channel_id=1, source_target_pairs={{0,8},{8,0},{16,24},{24,16},{1,9},{9,1},{17,25},{25,17},{2,10},{10... | collective-permute-start | bytes 1130504 | tf_op jit(solution)/shard_map/ppermute | solution.py:456
  24.4 2.7 %collective-permute-start.2 = (f32[2,24,16,128]{3,2,1,0:T(8,128)}, f32[2,24,16,128]{3,2,1,0:T(8,128)}, u32[]{:S(2)}, u32[]{:S(2)}) collective-permute-start(f32[2,24,16,128]{3,2,1,0:T(8,128)} %collective-permute-done.1.refs_8_), channel_id=1, source_target_pairs={{0,8},{8,0},{16,24},{24,16},{1,9},{9,1},{17,25},{25,17},{2,10},{10... | collective-permute-start | bytes 1179656 | tf_op jit(solution)/shard_map/ppermute | solution.py:456
  30.3 9.8 %collective-permute-start.10 = (f32[2,3,16,128]{3,2,1,0:T(8,128)}, f32[2,3,16,128]{3,2,1,0:T(8,128)S(1)}, u32[]{:S(2)}, u32[]{:S(2)}) collective-permute-start(f32[2,3,16,128]{3,2,1,0:T(8,128)} %get-tuple-element.22), channel_id=1, source_target_pairs={{0,5},{1,4},{2,7},{3,6},{4,1},{5,0},{6,3},{7,2},{8,13},{9,12},{10,... | collective-permute-start | bytes 147464 | tf_op jit(solution)/shard_map/ppermute | solution.py:456
  33.8 8.3 %collective-permute-start.11 = (f32[2,3,16,128]{3,2,1,0:T(8,128)}, f32[2,3,16,128]{3,2,1,0:T(8,128)S(1)}, u32[]{:S(2)}, u32[]{:S(2)}) collective-permute-start(f32[2,3,16,128]{3,2,1,0:T(8,128)} %get-tuple-element.23), channel_id=1, source_target_pairs={{0,6},{1,7},{2,4},{3,5},{4,2},{5,3},{6,0},{7,1},{8,14},{9,15},{10,... | collective-permute-start | bytes 147464 | tf_op jit(solution)/shard_map/ppermute | solution.py:456
  35.2 9.9 %collective-permute-start.12 = (f32[2,3,16,128]{3,2,1,0:T(8,128)}, f32[2,3,16,128]{3,2,1,0:T(8,128)S(1)}, u32[]{:S(2)}, u32[]{:S(2)}) collective-permute-start(f32[2,3,16,128]{3,2,1,0:T(8,128)} %get-tuple-element.24), channel_id=1, source_target_pairs={{0,7},{1,6},{2,5},{3,4},{4,3},{5,2},{6,1},{7,0},{8,15},{9,14},{10,... | collective-permute-start | bytes 147464 | tf_op jit(solution)/shard_map/ppermute | solution.py:456
  37.6 7.4 %collective-permute-start.6 = (f32[2,3,16,128]{3,2,1,0:T(8,128)}, f32[2,3,16,128]{3,2,1,0:T(8,128)S(1)}, u32[]{:S(2)}, u32[]{:S(2)}) collective-permute-start(f32[2,3,16,128]{3,2,1,0:T(8,128)} %get-tuple-element.18), channel_id=1, source_target_pairs={{0,1},{1,0},{2,3},{3,2},{4,5},{5,4},{6,7},{7,6},{8,9},{9,8},{10,11... | collective-permute-start | bytes 147464 | tf_op jit(solution)/shard_map/ppermute | solution.py:456
  39.1 5.9 %collective-permute-start.7 = (f32[2,3,16,128]{3,2,1,0:T(8,128)}, f32[2,3,16,128]{3,2,1,0:T(8,128)S(1)}, u32[]{:S(2)}, u32[]{:S(2)}) collective-permute-start(f32[2,3,16,128]{3,2,1,0:T(8,128)} %get-tuple-element.19), channel_id=1, source_target_pairs={{0,2},{1,3},{2,0},{3,1},{4,6},{5,7},{6,4},{7,5},{8,10},{9,11},{10,... | collective-permute-start | bytes 147464 | tf_op jit(solution)/shard_map/ppermute | solution.py:456
  40.1 7.4 %copy-start.10 = (f32[2,3,16,128]{3,2,1,0:T(8,128)}, f32[2,3,16,128]{3,2,1,0:T(8,128)S(1)}, u32[]{:S(2)}) copy-start(f32[2,3,16,128]{3,2,1,0:T(8,128)S(1)} %collective-permute-done.10.refs_8_) | copy-start | bytes 147460
  40.1 5.3 %collective-permute-start.8 = (f32[2,3,16,128]{3,2,1,0:T(8,128)}, f32[2,3,16,128]{3,2,1,0:T(8,128)S(1)}, u32[]{:S(2)}, u32[]{:S(2)}) collective-permute-start(f32[2,3,16,128]{3,2,1,0:T(8,128)} %get-tuple-element.20), channel_id=1, source_target_pairs={{0,3},{1,2},{2,1},{3,0},{4,7},{5,6},{6,5},{7,4},{8,11},{9,10},{10,... | collective-permute-start | bytes 147464 | tf_op jit(solution)/shard_map/ppermute | solution.py:456
  42.2 5.3 %collective-permute-start.9 = (f32[2,3,16,128]{3,2,1,0:T(8,128)}, f32[2,3,16,128]{3,2,1,0:T(8,128)S(1)}, u32[]{:S(2)}, u32[]{:S(2)}) collective-permute-start(f32[2,3,16,128]{3,2,1,0:T(8,128)} %get-tuple-element.21), channel_id=1, source_target_pairs={{0,4},{1,5},{2,6},{3,7},{4,0},{5,1},{6,2},{7,3},{8,12},{9,13},{10,... | collective-permute-start | bytes 147464 | tf_op jit(solution)/shard_map/ppermute | solution.py:456
  54.3 5.3 %collective-permute-start.13 = (f32[17,4,512]{2,1,0:T(4,128)}, f32[17,4,512]{2,1,0:T(4,128)S(1)}, u32[]{:S(2)}, u32[]{:S(2)}) collective-permute-start(f32[17,4,512]{2,1,0:T(4,128)} %gather_views.1.refs_0_.refs_6_), channel_id=1, source_target_pairs={{0,2},{1,3},{2,0},{3,1},{4,6},{5,7},{6,4},{7,5},{8,10},{9,11},{10,... | collective-permute-start | bytes 417800 | tf_op jit(solution)/shard_map/ppermute | solution.py:465
  54.4 5.9 %collective-permute-start.14 = (f32[17,4,512]{2,1,0:T(4,128)}, f32[17,4,512]{2,1,0:T(4,128)S(1)}, u32[]{:S(2)}, u32[]{:S(2)}) collective-permute-start(f32[17,4,512]{2,1,0:T(4,128)} %gather_views.1.refs_0_.refs_6_), channel_id=1, source_target_pairs={{2,4},{3,5},{4,2},{5,3},{10,12},{11,13},{12,10},{13,11},{18,20},{1... | collective-permute-start | bytes 417800 | tf_op jit(solution)/shard_map/ppermute | solution.py:465
  59.6 17.2 %copy-start.5 = (f32[17,4,512]{2,1,0:T(4,128)}, f32[17,4,512]{2,1,0:T(4,128)S(1)}, u32[]{:S(2)}) copy-start(f32[17,4,512]{2,1,0:T(4,128)S(1)} %collective-permute-done.13.refs_1_.refs_7_) | copy-start | bytes 417796
  59.6 4.1 %collective-permute-start.16 = (f32[17,4,512]{2,1,0:T(4,128)S(1)}, f32[17,4,512]{2,1,0:T(4,128)S(1)}, u32[]{:S(2)}, u32[]{:S(2)}) collective-permute-start(f32[17,4,512]{2,1,0:T(4,128)S(1)} %collective-permute-done.13.refs_1_.refs_7_), channel_id=1, source_target_pairs={{2,4},{3,5},{4,2},{5,3},{10,12},{11,13},{12,10},{13,11},{18,20},{1... | collective-permute-start | bytes 417800 | tf_op jit(solution)/shard_map/ppermute | solution.py:465
  60.3 8.0 %collective-permute-start.15 = (f32[17,4,512]{2,1,0:T(4,128)S(1)}, f32[17,4,512]{2,1,0:T(4,128)S(1)}, u32[]{:S(2)}, u32[]{:S(2)}) collective-permute-start(f32[17,4,512]{2,1,0:T(4,128)S(1)} %collective-permute-done.14), channel_id=1, source_target_pairs={{2,0},{3,1},{4,6},{5,7},{10,8},{11,9},{12,14},{13,15},{18,16},{19,... | collective-permute-start | bytes 417800 | tf_op jit(solution)/shard_map/ppermute | solution.py:465
  61.6 11.3 %collective-permute-start.18 = (f32[17,4,512]{2,1,0:T(4,128)}, f32[17,4,512]{2,1,0:T(4,128)S(1)}, u32[]{:S(2)}, u32[]{:S(2)}) collective-permute-start(f32[17,4,512]{2,1,0:T(4,128)} %gather_views.1.refs_0_.refs_6_), channel_id=1, source_target_pairs={{0,1},{1,0},{2,3},{3,2},{4,5},{5,4},{6,7},{7,6},{8,9},{9,8},{10,11... | collective-permute-start | bytes 417800 | tf_op jit(solution)/shard_map/ppermute | solution.py:456
  63.1 9.8 %collective-permute-start.19 = (f32[17,4,512]{2,1,0:T(4,128)S(1)}, f32[17,4,512]{2,1,0:T(4,128)S(1)}, u32[]{:S(2)}, u32[]{:S(2)}) collective-permute-start(f32[17,4,512]{2,1,0:T(4,128)S(1)} %collective-permute-done.13.refs_1_.refs_7_), channel_id=1, source_target_pairs={{0,1},{1,0},{2,3},{3,2},{4,5},{5,4},{6,7},{7,6},{8,9},{9,8},{10,11... | collective-permute-start | bytes 417800 | tf_op jit(solution)/shard_map/ppermute | solution.py:456
  63.7 8.0 %collective-permute-start.17 = (f32[17,4,512]{2,1,0:T(4,128)S(1)}, f32[17,4,512]{2,1,0:T(4,128)S(1)}, u32[]{:S(2)}, u32[]{:S(2)}) collective-permute-start(f32[17,4,512]{2,1,0:T(4,128)S(1)} %collective-permute-done.16), channel_id=1, source_target_pairs={{2,0},{3,1},{4,6},{5,7},{10,8},{11,9},{12,14},{13,15},{18,16},{19,... | collective-permute-start | bytes 417800 | tf_op jit(solution)/shard_map/ppermute | solution.py:465
  68.3 8.5 %copy-start.3 = (f32[17,4,512]{2,1,0:T(4,128)}, f32[17,4,512]{2,1,0:T(4,128)S(1)}, u32[]{:S(2)}) copy-start(f32[17,4,512]{2,1,0:T(4,128)S(1)} %broadcast_select_fusion.1.refs_2_.refs_8_) | copy-start | bytes 417796
  68.3 5.1 %collective-permute-start.20 = (f32[17,4,512]{2,1,0:T(4,128)S(1)}, f32[17,4,512]{2,1,0:T(4,128)S(1)}, u32[]{:S(2)}, u32[]{:S(2)}) collective-permute-start(f32[17,4,512]{2,1,0:T(4,128)S(1)} %broadcast_select_fusion.1.refs_2_.refs_8_), channel_id=1, source_target_pairs={{0,1},{1,0},{2,3},{3,2},{4,5},{5,4},{6,7},{7,6},{8,9},{9,8},{10,11... | collective-permute-start | bytes 417800 | tf_op jit(solution)/shard_map/ppermute | solution.py:456
  71.7 5.1 %collective-permute-start.21 = (f32[17,4,512]{2,1,0:T(4,128)S(1)}, f32[17,4,512]{2,1,0:T(4,128)S(1)}, u32[]{:S(2)}, u32[]{:S(2)}) collective-permute-start(f32[17,4,512]{2,1,0:T(4,128)S(1)} %broadcast_select_fusion.refs_3_.refs_9_), channel_id=1, source_target_pairs={{0,1},{1,0},{2,3},{3,2},{4,5},{5,4},{6,7},{7,6},{8,9},{9,8},{10,11... | collective-permute-start | bytes 417800 | tf_op jit(solution)/shard_map/ppermute | solution.py:456
  78.7 1.9 %collective-permute-start.22 = (f32[1,128]{1,0:T(1,128)}, f32[1,128]{1,0:T(1,128)S(1)}, u32[]{:S(2)}, u32[]{:S(2)}) collective-permute-start(f32[1,128]{1,0:T(1,128)} %total.1.refs_1_), channel_id=1, source_target_pairs={{0,8},{8,0},{16,24},{24,16},{1,9},{9,1},{17,25},{25,17},{2,10},{10... | collective-permute-start | bytes 1544 | tf_op jit(solution)/shard_map/ppermute | solution.py:456
  78.7 3.8 %collective-permute-start.23 = (f32[1,128]{1,0:T(1,128)}, f32[1,128]{1,0:T(1,128)S(1)}, u32[]{:S(2)}, u32[]{:S(2)}) collective-permute-start(f32[1,128]{1,0:T(1,128)} %total.1.refs_1_), channel_id=1, source_target_pairs={{0,16},{8,24},{16,0},{24,8},{1,17},{9,25},{17,1},{25,9},{2,18},{10... | collective-permute-start | bytes 1544 | tf_op jit(solution)/shard_map/ppermute | solution.py:456
  79.3 3.2 %collective-permute-start.24 = (f32[1,128]{1,0:T(1,128)}, f32[1,128]{1,0:T(1,128)S(1)}, u32[]{:S(2)}, u32[]{:S(2)}) collective-permute-start(f32[1,128]{1,0:T(1,128)} %total.1.refs_1_), channel_id=1, source_target_pairs={{0,24},{8,16},{16,8},{24,0},{1,25},{9,17},{17,9},{25,1},{2,26},{10... | collective-permute-start | bytes 1544 | tf_op jit(solution)/shard_map/ppermute | solution.py:456
  (15 other events, 40.6 us)

commit v6 on v5

--- a/solution.py
+++ b/solution.py
@@ -253,6 +253,7 @@
 
 
 WINDOW = 3
+SLOTS = (0, 2, 4, 6, 1, 3, 5, 7)
 COS_LANE = LANES - 2
 SIN_LANE = LANES - 1
 
@@ -327,15 +328,20 @@
     )(ints, trig, *arrays)
 
 
-def gather_kernel(dims, parts_n, views_n, ints_ref, tv_ref, curv_ref, *rest):
+def gather_kernel(dims, parts_n, pieces_n, views_n, last, ints_ref, *rest):
     rows_n, cols_n, bins_n, base, blocks = dims
-    pieces = rest[:parts_n]
-    out_ref, rows_ref, trig_ref, starts_ref = rest[parts_n:]
+    if last:
+        tv_ref, curv_ref, near_ref, *rest = rest
+    pieces = rest[:pieces_n]
+    if last:
+        out_ref, rows_ref, trig_ref, starts_ref = rest[pieces_n:]
+    else:
+        rows_ref, trig_ref, starts_ref = rest[pieces_n:]
     per_n = cols_n // parts_n
     part = ints_ref[1]
     lane8 = lax.broadcasted_iota(jnp.int32, (8, LANES), 1)
     lane = lax.broadcasted_iota(jnp.int32, (16, LANES), 1)
-    total_n = parts_n * views_n
+    total_n = pieces_n * views_n
     for n in range(total_n):
         tagged = pieces[n // views_n][n % views_n, WINDOW - 1, 0:8, :]
         cos = jnp.max(jnp.where(lane8 == COS_LANE, tagged, -2.0))
@@ -351,7 +357,8 @@
         column = part * per_n + u * LANES
         start = column.astype(jnp.float32)
         across = (lane + column).astype(jnp.float32) - 0.5 * cols_n + 0.5
-        total = jnp.zeros((16, LANES), jnp.float32)
+        cols = pl.ds(pl.multiple_of(u * LANES, LANES), LANES)
+        total = near_ref[row, :, cols] if last else jnp.zeros((16, LANES), jnp.float32)
         for n in range(total_n):
             cos = trig_ref[n]
             sin = trig_ref[total_n + n]
@@ -371,34 +378,40 @@
             a = jnp.take_along_axis(held, here, axis=1, mode="promise_in_bounds")
             b = jnp.take_along_axis(held, next_, axis=1, mode="promise_in_bounds")
             total = total + (a * (1.0 - frac) + b * frac)
-        cols = pl.ds(pl.multiple_of(u * LANES, LANES), LANES)
-        total = (total + tv_ref[row, :, cols]) / curv_ref[row, :, cols]
+        if last:
+            total = (total + tv_ref[row, :, cols]) / curv_ref[row, :, cols]
         rows_ref[row, :, cols] = total
-        return squares + total * total
-
-    squares = lax.fori_loop(0, rows_n * (per_n // LANES), step, jnp.zeros((16, LANES), jnp.float32))
-    for row in range(rows_n):
-        out_ref[0:16, row, :] = rows_ref[row]
-    out_ref[16] = jnp.full((rows_n, per_n), jnp.sum(squares), jnp.float32)
-
-
-def gather_views(dims, parts_n, ints, tv, curv, pieces):
+        return squares + total * total if last else squares
+
+    steps = rows_n * (per_n // LANES)
+    squares = lax.fori_loop(0, steps, step, jnp.zeros((16, LANES), jnp.float32), unroll=4)
+    if last:
+        for row in range(rows_n):
+            out_ref[0:16, row, :] = rows_ref[row]
+        out_ref[16] = jnp.full((rows_n, per_n), jnp.sum(squares), jnp.float32)
+
+
+def gather_views(dims, parts_n, ints, pieces, extra=()):
     views_n, _, slices_n, _ = pieces[0].shape
     rows_n, cols_n = dims[:2]
-    body = lambda *refs: gather_kernel(dims, parts_n, views_n, *refs)
+    per_n = cols_n // parts_n
+    pieces_n = len(pieces)
+    last = len(extra) > 0
+    rows = (rows_n, slices_n, per_n)
+    shape = (slices_n + 1, rows_n, per_n) if last else rows
     vmem = pl.BlockSpec(memory_space=pltpu.VMEM)
+    scratch = [
+        pltpu.SMEM((2 * pieces_n * views_n,), jnp.float32),
+        pltpu.SMEM((pieces_n * views_n,), jnp.int32),
+    ]
     return pl.pallas_call(
-        body,
-        out_shape=jax.ShapeDtypeStruct((slices_n + 1, rows_n, cols_n // parts_n), jnp.float32),
-        in_specs=[pl.BlockSpec(memory_space=pltpu.SMEM)] + [vmem] * (parts_n + 2),
+        lambda *refs: gather_kernel(dims, parts_n, pieces_n, views_n, last, *refs),
+        out_shape=jax.ShapeDtypeStruct(shape, jnp.float32),
+        in_specs=[pl.BlockSpec(memory_space=pltpu.SMEM)] + [vmem] * (pieces_n + len(extra)),
         out_specs=vmem,
-        scratch_shapes=[
-            pltpu.VMEM((rows_n, slices_n, cols_n // parts_n), jnp.float32),
-            pltpu.SMEM((2 * parts_n * views_n,), jnp.float32),
-            pltpu.SMEM((parts_n * views_n,), jnp.int32),
-        ],
+        scratch_shapes=([pltpu.VMEM(rows, jnp.float32)] if last else []) + scratch,
         name="gather_views",
-    )(ints, tv, curv, *pieces)
+    )(ints, *extra, *pieces)
 
 
 def total_kernel(*refs):
@@ -429,13 +442,8 @@
     factor = jnp.max(jnp.minimum(1.0, step_limit / rms))
     slices_n, _, per_n = pieces[0].shape
     part = ints_ref[1]
-    depth = part >> 1
-    upper = depth >> 1
-    side = part & 1
-    depths = [depth, depth ^ 1, 2 - upper, 3 - 3 * upper]
-    order = [2 * d + side for d in depths] + [2 * d + 1 - side for d in depths]
     for r in range(parts_n):
-        cols = pl.ds(pl.multiple_of(order[r] * per_n, per_n), per_n)
+        cols = pl.ds(pl.multiple_of((part ^ SLOTS[r]) * per_n, per_n), per_n)
         out_ref[:, :, cols] = vol_ref[:, :, cols] - factor * pieces[r][0 : slices_n - 1]
 
 
@@ -457,24 +465,10 @@
 
 
 def gathered(piece):
-    part = lax.axis_index("view")
-    depth = part // 2
-    end = (depth == 0) | (depth == 3)
-
-    def along(x, pairs):
-        return lax.ppermute(x, "view", [(2 * a + y, 2 * b + y) for a, b in pairs for y in (0, 1)])
-
-    first = swapped(piece, "view", 1)
-    second = along(piece, [(0, 1), (1, 0), (2, 3), (3, 2)])
-    middle = along(piece, [(1, 2), (2, 1)])
-    across = [first, swapped(second, "view", 1)]
-    onward = along(middle, [(1, 0), (2, 3)])
-    middle_last = along(second, [(1, 2), (2, 1)])
-    third = jnp.where(end, onward, middle)
-    across.append(swapped(third, "view", 1))
-    last = jnp.where(end, along(middle_last, [(1, 0), (2, 3)]), middle_last)
-    across.append(swapped(last, "view", 1))
-    return [piece, second, third, last] + across
+    near = swapped(piece, "view", 2)
+    far = [swapped(piece, "view", 4), swapped(piece, "view", 6)]
+    side = [swapped(piece, "view", 1), swapped(piece, "view", 3)]
+    return [piece, near] + far + side + [swapped(x, "view", 1) for x in far]
 
 
 def local_split(volume, sinogram, curvature, angles, offsets):
@@ -537,7 +531,9 @@
     tv_grad = tv_padded(jnp.pad(block, ((0, 0), (1, 1), (0, 0))))
     curv = lax.dynamic_slice_in_dim(curvature, part * per_n, per_n, axis=2)
     tv = (tv_weight * tv_grad).transpose(1, 0, 2)
-    parts = gathered(gather_views(dims, parts_n, ints, tv, curv.transpose(1, 0, 2), pieces))
+    near_grad = gather_views(dims, parts_n, ints, pieces[: parts_n // 2])
+    extra = (tv, curv.transpose(1, 0, 2), near_grad)
+    parts = gathered(gather_views(dims, parts_n, ints, pieces[parts_n // 2 :], extra))
     squares = total(parts)
     sums = [squares] + [swapped(squares, "slab", k) for k in (1, 2, 3)]
     voxel_count = slices_n * slab_count * rows_n * cols_n

time: 86.8 us -> 83.3 us (0.960)
  waiting for transfers between devices: 28.1 us -> 22.6 us
  Pallas kernels: 21.5 us -> 22.6 us
    ppermute x5 -> x0, waiting for transfers between devices: 10 us -> none  [along(): lax.ppermute(x, 'view', [(2 * a + y, 2 * b + y) for a, b in pairs for y i...]
    ppermute x20 -> x23, waiting for transfers between devices: 18.1 us -> 22.6 us  [swapped(): lax.ppermute(x, axis, [(i, i ^ bit) for i in range(lax.axis_size(axis))])]
    ppermute x5 -> x0, starting transfers between devices: 3.94 us -> none  [along(): lax.ppermute(x, 'view', [(2 * a + y, 2 * b + y) for a, b in pairs for y i...]
    ppermute x20 -> x23, starting transfers between devices: 23.1 us -> 26.7 us  [swapped(): lax.ppermute(x, axis, [(i, i ^ bit) for i in range(lax.axis_size(axis))])]
    pallas_call x1 -> x2, Pallas kernels: 6.23 us -> 7.29 us  [gather_views(): pl.pallas_call(lambda *refs: gather_kernel(dims, parts_n, pieces_n, views...]
  transfers between devices with their start and end apart: 25 -> 23, of which waited for: 9 -> 7; matrix products, arithmetic and copies ran while one was open for 6% -> 6% of each run, Pallas kernels for 9% -> 14%
where the time goes in v6:
time: 83.3 us; the launch traced here: 82.1 us
  starting transfers between devices  26.7 us (32%)
  Pallas kernels  22.6 us (27%)
  waiting for transfers between devices  22.6 us (27%)
  local copies, waits for them, and re-layouts  6.56 us (8%)
  other arithmetic  3.41 us (4%)
    ppermute x23, starting transfers between devices, swapped(): lax.ppermute(x, axis, [(i, i ^ bit) for i in range(lax.axis_size(axis))])  26.7 us
    ppermute x23, waiting for transfers between devices, swapped(): lax.ppermute(x, axis, [(i, i ^ bit) for i in range(lax.axis_size(axis))])  22.6 us
    pallas_call x1, Pallas kernels, project(): pl.pallas_call(body, out_shape=jax.ShapeDtypeStruct((views_n, blocks_n, s...  7.99 us
    pallas_call x2, Pallas kernels, gather_views(): pl.pallas_call(lambda *refs: gather_kernel(dims, parts_n, pieces_n, views...  7.29 us
    unnamed x46, local copies, waits for them, and re-layouts  4.21 us
    pallas_call x1, Pallas kernels, residual_windows(): pl.pallas_call(body, out_shape=[jax.ShapeDtypeStruct((views_n, WINDOW, ba...  3.15 us
    pallas_call x1, Pallas kernels, finish(): pl.pallas_call(lambda *refs: finish_kernel(parts_n, voxel_count, *refs),...  2.88 us
  transfers between devices with their start and end apart: 23, of which 7 were waited for; matrix products, arithmetic and copies ran while one was open for 6% of the time, Pallas kernels for 14%

profile of v6, /device:TPU:0, one launch (start us, length us, event | category | flops | bytes accessed | tf_op | source)
XLA Modules:
  0.0 82.1 jit_solution(13486841060766727410)
XLA Ops:
  0.0 0.8 constant_dynamic-slice_fusion.2
  0.8 1.2 %bitcast_bitcast_fusion = f32[2,23,16,128]{3,2,1,0:T(8,128)S(1)} fusion(f32[2,16,4096]{2,1,0:T(8,128)} %param.6), kind=kLoop, calls=%fused_computation.7 | loop fusion | bytes 753664 | tf_op jit(solution)/shard_map/transpose | solution.py:494
  2.1 3.0 %collective-permute-start.1 = (f32[2,24,16,128]{3,2,1,0:T(8,128)S(1)}, f32[2,24,16,128]{3,2,1,0:T(8,128)}, u32[]{:S(2)}, u32[]{:S(2)}) collective-permute-start(f32[2,24,16,128]{3,2,1,0:T(8,128)S(1)} %maximum_maximum_fusion.refs_6_), channel_id=1, source_target_pairs={{0,16},{8,24},{16,0},{24,8},{1,17},{9,25},{17,1},{25,9},{2,18},{10... | collective-permute-start | bytes 1179656 | tf_op jit(solution)/shard_map/ppermute | solution.py:464
  5.1 0.7 pad_maximum_fusion.2.refs_0_.refs_1_
  5.8 8.0 %project.1.refs_2_ = f32[2,23,16,128]{3,2,1,0:T(8,128)} custom-call(f32[4]{0:T(128)} %pad_maximum_fusion.2.refs_0_.refs_1_, f32[16,4,4096]{2,1,0:T(4,128)} %refs_5_.1), custom_call_target="tpu_custom_call" | custom-call | tf_op jit(solution)/shard_map/project/pallas_call | solution.py:100
  14.6 9.8 %collective-permute-done.4.refs_4_ = f32[2,23,16,128]{3,2,1,0:T(8,128)} collective-permute-done((f32[2,23,16,128]{3,2,1,0:T(8,128)}, f32[2,23,16,128]{3,2,1,0:T(8,128)}, u32[]{:S(2)}, u32[]{:S(2)}) %collective-permute-start.4) | collective-permute-done | bytes 376864 | tf_op jit(solution)/shard_map/ppermute | solution.py:464
  25.7 0.7 copy.15
  26.4 0.6 pad_add_fusion.1.refs_0_
  27.2 3.1 %residual_windows.1 = (f32[2,3,16,128]{3,2,1,0:T(8,128)}, f32[2,3,16,128]{3,2,1,0:T(8,128)}, f32[2,3,16,128]{3,2,1,0:T(8,128)}, f32[2,3,16,128]{3,2,1,0:T(8,128)...) custom-call(s32[10]{0:T(128)} %pad_add_fusion.1.refs_0_, ...), custom_call_target="tpu_custom_call" | custom-call | tf_op jit(solution)/shard_map/residual_windows/pallas_call | solution.py:315
  30.3 1.5 %collective-permute-start.6 = (f32[2,3,16,128]{3,2,1,0:T(8,128)}, f32[2,3,16,128]{3,2,1,0:T(8,128)S(1)}, u32[]{:S(2)}, u32[]{:S(2)}) collective-permute-start(f32[2,3,16,128]{3,2,1,0:T(8,128)} %get-tuple-element.18), channel_id=1, source_target_pairs={{0,1},{1,0},{2,3},{3,2},{4,5},{5,4},{6,7},{7,6},{8,9},{9,8},{10,11... | collective-permute-start | bytes 147464 | tf_op jit(solution)/shard_map/ppermute | solution.py:464
  31.9 1.6 %collective-permute-start.7 = (f32[2,3,16,128]{3,2,1,0:T(8,128)}, f32[2,3,16,128]{3,2,1,0:T(8,128)S(1)}, u32[]{:S(2)}, u32[]{:S(2)}) collective-permute-start(f32[2,3,16,128]{3,2,1,0:T(8,128)} %get-tuple-element.19), channel_id=1, source_target_pairs={{0,2},{1,3},{2,0},{3,1},{4,6},{5,7},{6,4},{7,5},{8,10},{9,11},{10,... | collective-permute-start | bytes 147464 | tf_op jit(solution)/shard_map/ppermute | solution.py:464
  33.8 3.5 %collective-permute-start.10 = (f32[2,3,16,128]{3,2,1,0:T(8,128)}, f32[2,3,16,128]{3,2,1,0:T(8,128)S(1)}, u32[]{:S(2)}, u32[]{:S(2)}) collective-permute-start(f32[2,3,16,128]{3,2,1,0:T(8,128)} %get-tuple-element.22), channel_id=1, source_target_pairs={{0,5},{1,4},{2,7},{3,6},{4,1},{5,0},{6,3},{7,2},{8,13},{9,12},{10,... | collective-permute-start | bytes 147464 | tf_op jit(solution)/shard_map/ppermute | solution.py:464
  37.4 1.4 %collective-permute-start.11 = (f32[2,3,16,128]{3,2,1,0:T(8,128)}, f32[2,3,16,128]{3,2,1,0:T(8,128)S(1)}, u32[]{:S(2)}, u32[]{:S(2)}) collective-permute-start(f32[2,3,16,128]{3,2,1,0:T(8,128)} %get-tuple-element.23), channel_id=1, source_target_pairs={{0,6},{1,7},{2,4},{3,5},{4,2},{5,3},{6,0},{7,1},{8,14},{9,15},{10,... | collective-permute-start | bytes 147464 | tf_op jit(solution)/shard_map/ppermute | solution.py:464
  38.7 0.8 fusion.24
  39.8 2.5 %collective-permute-start.12 = (f32[2,3,16,128]{3,2,1,0:T(8,128)}, f32[2,3,16,128]{3,2,1,0:T(8,128)S(1)}, u32[]{:S(2)}, u32[]{:S(2)}) collective-permute-start(f32[2,3,16,128]{3,2,1,0:T(8,128)} %get-tuple-element.24), channel_id=1, source_target_pairs={{0,7},{1,6},{2,5},{3,4},{4,3},{5,2},{6,1},{7,0},{8,15},{9,14},{10,... | collective-permute-start | bytes 147464 | tf_op jit(solution)/shard_map/ppermute | solution.py:464
  42.2 1.0 %fusion.7.refs_1_ = f32[4,16,512]{2,1,0:T(8,128)} fusion(s32[]{:T(128)S(6)} %select_n.98, f32[16,4,4096]{2,0,1:T(8,128)S(1)} %copy.8, s32[]{:T(128)S(6)} %add.69, f32[18,6,514]{2,0,1:T(8,128)S(1)} %select_maximum_fusion, f32[1,4,514]{2,0,1:T(1,128)S(1)} %pad.17, f32[16,4,514]{2,0,1:T(8,128)S(1)} %pad_dynamic-slice_fusion.3, s32[]{:T(128)S(6)} %add.68, ...), kind=kLoop, calls=%fused_computation.18 | loop fusion | flops 851968 | bytes 1589836 | tf_op jit(solution)/shard_map/transpose | solution.py:533
  43.9 3.5 %gather_views.2.refs_3_ = f32[4,16,512]{2,1,0:T(8,128)} custom-call(s32[10]{0:T(128)} %pad_add_fusion.1.refs_0_, f32[2,3,16,128]{3,2,1,0:T(8,128)} %get-tuple-element.17.refs_1_, f32[2,3,16,128]{3,2,1,0:T(8,128)} %copy-done.12, f32[2,3,16,128]{3,2,1,0:T(8,128)} %copy-done.13, f32[2,3,16,128]{3,2,1,0:T(8,128)} %copy-done.14), custom_call_target="tpu_custom_call" | custom-call | tf_op jit(solution)/shard_map/gather_views/pallas_call | solution.py:407
  48.0 3.8 %gather_views.3.refs_0_.refs_6_ = f32[17,4,512]{2,1,0:T(4,128)} custom-call(s32[10]{0:T(128)} %pad_add_fusion.1.refs_0_, f32[4,16,512]{2,1,0:T(8,128)} %fusion.7.refs_1_, f32[4,16,512]{2,1,0:T(8,128)} %bitcast.16, f32[4,16,512]{2,1,0:T(8,128)} %gather_views.2.refs_3_, f32[2,3,16,128]{3,2,1,0:T(8,128)} %copy-done.16, f32[2,3,16,128]{3,2,1,0:T(8,128)} %copy-done.10, ...), custom_call_target="tpu_custom_call" | custom-call | tf_op jit(solution)/shard_map/gather_views/pallas_call | solution.py:407
  51.9 2.9 %collective-permute-start.14 = (f32[17,4,512]{2,1,0:T(4,128)}, f32[17,4,512]{2,1,0:T(4,128)S(1)}, u32[]{:S(2)}, u32[]{:S(2)}) collective-permute-start(f32[17,4,512]{2,1,0:T(4,128)} %gather_views.3.refs_0_.refs_6_), channel_id=1, source_target_pairs={{0,4},{1,5},{2,6},{3,7},{4,0},{5,1},{6,2},{7,3},{8,12},{9,13},{10,... | collective-permute-start | bytes 417800 | tf_op jit(solution)/shard_map/ppermute | solution.py:464
  54.8 1.4 %collective-permute-start.15 = (f32[17,4,512]{2,1,0:T(4,128)}, f32[17,4,512]{2,1,0:T(4,128)S(1)}, u32[]{:S(2)}, u32[]{:S(2)}) collective-permute-start(f32[17,4,512]{2,1,0:T(4,128)} %gather_views.3.refs_0_.refs_6_), channel_id=1, source_target_pairs={{0,6},{1,7},{2,4},{3,5},{4,2},{5,3},{6,0},{7,1},{8,14},{9,15},{10,... | collective-permute-start | bytes 417800 | tf_op jit(solution)/shard_map/ppermute | solution.py:464
  56.1 1.5 %collective-permute-start.16 = (f32[17,4,512]{2,1,0:T(4,128)}, f32[17,4,512]{2,1,0:T(4,128)S(1)}, u32[]{:S(2)}, u32[]{:S(2)}) collective-permute-start(f32[17,4,512]{2,1,0:T(4,128)} %gather_views.3.refs_0_.refs_6_), channel_id=1, source_target_pairs={{0,1},{1,0},{2,3},{3,2},{4,5},{5,4},{6,7},{7,6},{8,9},{9,8},{10,11... | collective-permute-start | bytes 417800 | tf_op jit(solution)/shard_map/ppermute | solution.py:464
  57.7 2.0 %collective-permute-start.17 = (f32[17,4,512]{2,1,0:T(4,128)}, f32[17,4,512]{2,1,0:T(4,128)S(1)}, u32[]{:S(2)}, u32[]{:S(2)}) collective-permute-start(f32[17,4,512]{2,1,0:T(4,128)} %gather_views.3.refs_0_.refs_6_), channel_id=1, source_target_pairs={{0,3},{1,2},{2,1},{3,0},{4,7},{5,6},{6,5},{7,4},{8,11},{9,10},{10,... | collective-permute-start | bytes 417800 | tf_op jit(solution)/shard_map/ppermute | solution.py:464
  59.6 4.5 %collective-permute-done.14.refs_2_.refs_8_ = f32[17,4,512]{2,1,0:T(4,128)S(1)} collective-permute-done((f32[17,4,512]{2,1,0:T(4,128)}, f32[17,4,512]{2,1,0:T(4,128)S(1)}, u32[]{:S(2)}, u32[]{:S(2)}) %collective-permute-start.14) | collective-permute-done | bytes 139296 | tf_op jit(solution)/shard_map/ppermute | solution.py:464
  64.1 1.5 %collective-permute-start.18 = (f32[17,4,512]{2,1,0:T(4,128)S(1)}, f32[17,4,512]{2,1,0:T(4,128)S(1)}, u32[]{:S(2)}, u32[]{:S(2)}) collective-permute-start(f32[17,4,512]{2,1,0:T(4,128)S(1)} %collective-permute-done.14.refs_2_.refs_8_), channel_id=1, source_target_pairs={{0,1},{1,0},{2,3},{3,2},{4,5},{5,4},{6,7},{7,6},{8,9},{9,8},{10,11... | collective-permute-start | bytes 417800 | tf_op jit(solution)/shard_map/ppermute | solution.py:464
  66.2 2.1 %collective-permute-done.17.refs_5_.refs_11_ = f32[17,4,512]{2,1,0:T(4,128)S(1)} collective-permute-done((f32[17,4,512]{2,1,0:T(4,128)}, f32[17,4,512]{2,1,0:T(4,128)S(1)}, u32[]{:S(2)}, u32[]{:S(2)}) %collective-permute-start.17) | collective-permute-done | bytes 139296 | tf_op jit(solution)/shard_map/ppermute | solution.py:464
  68.3 2.8 %collective-permute-done.18.refs_6_.refs_12_ = f32[17,4,512]{2,1,0:T(4,128)S(1)} collective-permute-done((f32[17,4,512]{2,1,0:T(4,128)S(1)}, f32[17,4,512]{2,1,0:T(4,128)S(1)}, u32[]{:S(2)}, u32[]{:S(2)}) %collective-permute-start.18) | collective-permute-done | bytes 139296 | tf_op jit(solution)/shard_map/ppermute | solution.py:464
  71.1 1.5 %collective-permute-done.19.refs_7_.refs_13_ = f32[17,4,512]{2,1,0:T(4,128)S(1)} collective-permute-done((f32[17,4,512]{2,1,0:T(4,128)S(1)}, f32[17,4,512]{2,1,0:T(4,128)S(1)}, u32[]{:S(2)}, u32[]{:S(2)}) %collective-permute-start.19) | collective-permute-done | bytes 139296 | tf_op jit(solution)/shard_map/ppermute | solution.py:464
  72.6 0.7 copy-done.9
  73.3 1.3 %total.1.refs_1_ = f32[1,128]{1,0:T(1,128)} custom-call(f32[17,4,512]{2,1,0:T(4,128)} %gather_views.3.refs_0_.refs_6_, f32[17,4,512]{2,1,0:T(4,128)} %copy-done.5, f32[17,4,512]{2,1,0:T(4,128)} %copy-done.3, f32[17,4,512]{2,1,0:T(4,128)} %copy-done.4, f32[17,4,512]{2,1,0:T(4,128)} %copy-done.6, f32[17,4,512]{2,1,0:T(4,128)} %copy-done.7, ...), custom_call_target="tpu_custom_call" | custom-call | tf_op jit(solution)/shard_map/total/pallas_call | solution.py:427
  75.1 1.3 %collective-permute-start.22 = (f32[1,128]{1,0:T(1,128)}, f32[1,128]{1,0:T(1,128)S(1)}, u32[]{:S(2)}, u32[]{:S(2)}) collective-permute-start(f32[1,128]{1,0:T(1,128)} %total.1.refs_1_), channel_id=1, source_target_pairs={{0,24},{8,16},{16,8},{24,0},{1,25},{9,17},{17,9},{25,1},{2,26},{10... | collective-permute-start | bytes 1544 | tf_op jit(solution)/shard_map/ppermute | solution.py:464
  76.5 1.7 %collective-permute-done.21.refs_3_ = f32[1,128]{1,0:T(1,128)S(1)} collective-permute-done((f32[1,128]{1,0:T(1,128)}, f32[1,128]{1,0:T(1,128)S(1)}, u32[]{:S(2)}, u32[]{:S(2)}) %collective-permute-start.21) | collective-permute-done | bytes 544 | tf_op jit(solution)/shard_map/ppermute | solution.py:464
  79.3 2.9 %finish.1 = f32[16,4,4096]{2,1,0:T(4,128)} custom-call(s32[10]{0:T(128)} %pad_add_fusion.1.refs_0_, f32[1,128]{1,0:T(1,128)} %total.1.refs_1_, f32[1,128]{1,0:T(1,128)} %copy-done.18, f32[1,128]{1,0:T(1,128)} %copy-done.19, f32[1,128]{1,0:T(1,128)} %copy-done.20, f32[16,4,4096]{2,1,0:T(4,128)} %refs_5_.1, f32[17,4,512]{2,1,0:T(4,128)} %gather_views.3.refs_0_.refs_6_, ...), custom_call_target="tpu_custom_call" | custom-call | tf_op jit(solution)/shard_map/finish/pallas_call | solution.py:454
  (85 shorter events, 6.4 us)
Async XLA Ops:
  0.0 25.7 %copy-start = (f32[16,4,4096]{2,1,0:T(4,128)S(1)}, f32[16,4,4096]{2,1,0:T(4,128)}, u32[]{:S(2)}) copy-start(f32[16,4,4096]{2,1,0:T(4,128)} %param.7) | copy-start | bytes 3145732
  0.0 5.1 %copy-start.21 = (s32[2]{0:T(128)S(1)}, s32[2]{0:T(128)}, u32[]{:S(2)}) copy-start(s32[2]{0:T(128)} %param.8) | copy-start | bytes 28
  2.0 12.4 %copy-start.17 = (s32[2,4]{1,0:T(2,128)S(1)}, s32[2,4]{1,0:T(2,128)}, u32[]{:S(2)}) copy-start(s32[2,4]{1,0:T(2,128)} %param.9) | copy-start | bytes 100
  2.0 23.0 %copy-start.1 = (f32[16,4,4096]{2,1,0:T(4,128)S(1)}, f32[16,4,4096]{2,1,0:T(4,128)}, u32[]{:S(2)}) copy-start(f32[16,4,4096]{2,1,0:T(4,128)} %refs_5_.1) | copy-start | bytes 3145732
  2.1 23.5 %copy-start.2 = (f32[2,24,16,128]{3,2,1,0:T(8,128)}, f32[2,24,16,128]{3,2,1,0:T(8,128)S(1)}, u32[]{:S(2)}) copy-start(f32[2,24,16,128]{3,2,1,0:T(8,128)S(1)} %maximum_maximum_fusion.refs_6_) | copy-start | bytes 1179652
  2.1 22.3 %collective-permute-start.1 = (f32[2,24,16,128]{3,2,1,0:T(8,128)S(1)}, f32[2,24,16,128]{3,2,1,0:T(8,128)}, u32[]{:S(2)}, u32[]{:S(2)}) collective-permute-start(f32[2,24,16,128]{3,2,1,0:T(8,128)S(1)} %maximum_maximum_fusion.refs_6_), channel_id=1, source_target_pairs={{0,16},{8,24},{16,0},{24,8},{1,17},{9,25},{17,1},{25,9},{2,18},{10... | collective-permute-start | bytes 1179656 | tf_op jit(solution)/shard_map/ppermute | solution.py:464
  13.8 10.6 %collective-permute-start.4 = (f32[2,23,16,128]{3,2,1,0:T(8,128)}, f32[2,23,16,128]{3,2,1,0:T(8,128)}, u32[]{:S(2)}, u32[]{:S(2)}) collective-permute-start(f32[2,23,16,128]{3,2,1,0:T(8,128)} %project.1.refs_2_), channel_id=1, source_target_pairs={{0,16},{8,24},{16,0},{24,8},{1,17},{9,25},{17,1},{25,9},{2,18},{10... | collective-permute-start | bytes 1130504 | tf_op jit(solution)/shard_map/ppermute | solution.py:464
  13.9 13.3 %collective-permute-start.3 = (f32[2,23,16,128]{3,2,1,0:T(8,128)}, f32[2,23,16,128]{3,2,1,0:T(8,128)}, u32[]{:S(2)}, u32[]{:S(2)}) collective-permute-start(f32[2,23,16,128]{3,2,1,0:T(8,128)} %project.1.refs_2_), channel_id=1, source_target_pairs={{0,8},{8,0},{16,24},{24,16},{1,9},{9,1},{17,25},{25,17},{2,10},{10... | collective-permute-start | bytes 1130504 | tf_op jit(solution)/shard_map/ppermute | solution.py:464
  13.9 13.2 %collective-permute-start = (f32[2,24,16,128]{3,2,1,0:T(8,128)S(1)}, f32[2,24,16,128]{3,2,1,0:T(8,128)}, u32[]{:S(2)}, u32[]{:S(2)}) collective-permute-start(f32[2,24,16,128]{3,2,1,0:T(8,128)S(1)} %maximum_maximum_fusion.refs_6_), channel_id=1, source_target_pairs={{0,8},{8,0},{16,24},{24,16},{1,9},{9,1},{17,25},{25,17},{2,10},{10... | collective-permute-start | bytes 1179656 | tf_op jit(solution)/shard_map/ppermute | solution.py:464
  24.4 2.8 %collective-permute-start.5 = (f32[2,23,16,128]{3,2,1,0:T(8,128)}, f32[2,23,16,128]{3,2,1,0:T(8,128)}, u32[]{:S(2)}, u32[]{:S(2)}) collective-permute-start(f32[2,23,16,128]{3,2,1,0:T(8,128)} %collective-permute-done.4.refs_4_), channel_id=1, source_target_pairs={{0,8},{8,0},{16,24},{24,16},{1,9},{9,1},{17,25},{25,17},{2,10},{10... | collective-permute-start | bytes 1130504 | tf_op jit(solution)/shard_map/ppermute | solution.py:464
  24.4 2.8 %collective-permute-start.2 = (f32[2,24,16,128]{3,2,1,0:T(8,128)}, f32[2,24,16,128]{3,2,1,0:T(8,128)}, u32[]{:S(2)}, u32[]{:S(2)}) collective-permute-start(f32[2,24,16,128]{3,2,1,0:T(8,128)} %collective-permute-done.1.refs_8_), channel_id=1, source_target_pairs={{0,8},{8,0},{16,24},{24,16},{1,9},{9,1},{17,25},{25,17},{2,10},{10... | collective-permute-start | bytes 1179656 | tf_op jit(solution)/shard_map/ppermute | solution.py:464
  30.3 9.4 %collective-permute-start.6 = (f32[2,3,16,128]{3,2,1,0:T(8,128)}, f32[2,3,16,128]{3,2,1,0:T(8,128)S(1)}, u32[]{:S(2)}, u32[]{:S(2)}) collective-permute-start(f32[2,3,16,128]{3,2,1,0:T(8,128)} %get-tuple-element.18), channel_id=1, source_target_pairs={{0,1},{1,0},{2,3},{3,2},{4,5},{5,4},{6,7},{7,6},{8,9},{9,8},{10,11... | collective-permute-start | bytes 147464 | tf_op jit(solution)/shard_map/ppermute | solution.py:464
  31.9 10.3 %collective-permute-start.7 = (f32[2,3,16,128]{3,2,1,0:T(8,128)}, f32[2,3,16,128]{3,2,1,0:T(8,128)S(1)}, u32[]{:S(2)}, u32[]{:S(2)}) collective-permute-start(f32[2,3,16,128]{3,2,1,0:T(8,128)} %get-tuple-element.19), channel_id=1, source_target_pairs={{0,2},{1,3},{2,0},{3,1},{4,6},{5,7},{6,4},{7,5},{8,10},{9,11},{10,... | collective-permute-start | bytes 147464 | tf_op jit(solution)/shard_map/ppermute | solution.py:464
  33.5 9.8 %collective-permute-start.8 = (f32[2,3,16,128]{3,2,1,0:T(8,128)}, f32[2,3,16,128]{3,2,1,0:T(8,128)S(1)}, u32[]{:S(2)}, u32[]{:S(2)}) collective-permute-start(f32[2,3,16,128]{3,2,1,0:T(8,128)} %get-tuple-element.20), channel_id=1, source_target_pairs={{0,3},{1,2},{2,1},{3,0},{4,7},{5,6},{6,5},{7,4},{8,11},{9,10},{10,... | collective-permute-start | bytes 147464 | tf_op jit(solution)/shard_map/ppermute | solution.py:464
  33.8 13.5 %collective-permute-start.10 = (f32[2,3,16,128]{3,2,1,0:T(8,128)}, f32[2,3,16,128]{3,2,1,0:T(8,128)S(1)}, u32[]{:S(2)}, u32[]{:S(2)}) collective-permute-start(f32[2,3,16,128]{3,2,1,0:T(8,128)} %get-tuple-element.22), channel_id=1, source_target_pairs={{0,5},{1,4},{2,7},{3,6},{4,1},{5,0},{6,3},{7,2},{8,13},{9,12},{10,... | collective-permute-start | bytes 147464 | tf_op jit(solution)/shard_map/ppermute | solution.py:464
  37.4 10.0 %collective-permute-start.11 = (f32[2,3,16,128]{3,2,1,0:T(8,128)}, f32[2,3,16,128]{3,2,1,0:T(8,128)S(1)}, u32[]{:S(2)}, u32[]{:S(2)}) collective-permute-start(f32[2,3,16,128]{3,2,1,0:T(8,128)} %get-tuple-element.23), channel_id=1, source_target_pairs={{0,6},{1,7},{2,4},{3,5},{4,2},{5,3},{6,0},{7,1},{8,14},{9,15},{10,... | collective-permute-start | bytes 147464 | tf_op jit(solution)/shard_map/ppermute | solution.py:464
  39.8 7.6 %collective-permute-start.12 = (f32[2,3,16,128]{3,2,1,0:T(8,128)}, f32[2,3,16,128]{3,2,1,0:T(8,128)S(1)}, u32[]{:S(2)}, u32[]{:S(2)}) collective-permute-start(f32[2,3,16,128]{3,2,1,0:T(8,128)} %get-tuple-element.24), channel_id=1, source_target_pairs={{0,7},{1,6},{2,5},{3,4},{4,3},{5,2},{6,1},{7,0},{8,15},{9,14},{10,... | collective-permute-start | bytes 147464 | tf_op jit(solution)/shard_map/ppermute | solution.py:464
  42.2 5.2 %collective-permute-start.9 = (f32[2,3,16,128]{3,2,1,0:T(8,128)}, f32[2,3,16,128]{3,2,1,0:T(8,128)S(1)}, u32[]{:S(2)}, u32[]{:S(2)}) collective-permute-start(f32[2,3,16,128]{3,2,1,0:T(8,128)} %get-tuple-element.21), channel_id=1, source_target_pairs={{0,4},{1,5},{2,6},{3,7},{4,0},{5,1},{6,2},{7,3},{8,12},{9,13},{10,... | collective-permute-start | bytes 147464 | tf_op jit(solution)/shard_map/ppermute | solution.py:464
  51.9 12.2 %collective-permute-start.14 = (f32[17,4,512]{2,1,0:T(4,128)}, f32[17,4,512]{2,1,0:T(4,128)S(1)}, u32[]{:S(2)}, u32[]{:S(2)}) collective-permute-start(f32[17,4,512]{2,1,0:T(4,128)} %gather_views.3.refs_0_.refs_6_), channel_id=1, source_target_pairs={{0,4},{1,5},{2,6},{3,7},{4,0},{5,1},{6,2},{7,3},{8,12},{9,13},{10,... | collective-permute-start | bytes 417800 | tf_op jit(solution)/shard_map/ppermute | solution.py:464
  54.8 10.8 %collective-permute-start.15 = (f32[17,4,512]{2,1,0:T(4,128)}, f32[17,4,512]{2,1,0:T(4,128)S(1)}, u32[]{:S(2)}, u32[]{:S(2)}) collective-permute-start(f32[17,4,512]{2,1,0:T(4,128)} %gather_views.3.refs_0_.refs_6_), channel_id=1, source_target_pairs={{0,6},{1,7},{2,4},{3,5},{4,2},{5,3},{6,0},{7,1},{8,14},{9,15},{10,... | collective-permute-start | bytes 417800 | tf_op jit(solution)/shard_map/ppermute | solution.py:464
  56.1 10.0 %collective-permute-start.13 = (f32[17,4,512]{2,1,0:T(4,128)}, f32[17,4,512]{2,1,0:T(4,128)S(1)}, u32[]{:S(2)}, u32[]{:S(2)}) collective-permute-start(f32[17,4,512]{2,1,0:T(4,128)} %gather_views.3.refs_0_.refs_6_), channel_id=1, source_target_pairs={{0,2},{1,3},{2,0},{3,1},{4,6},{5,7},{6,4},{7,5},{8,10},{9,11},{10,... | collective-permute-start | bytes 417800 | tf_op jit(solution)/shard_map/ppermute | solution.py:464
  56.1 10.0 %collective-permute-start.16 = (f32[17,4,512]{2,1,0:T(4,128)}, f32[17,4,512]{2,1,0:T(4,128)S(1)}, u32[]{:S(2)}, u32[]{:S(2)}) collective-permute-start(f32[17,4,512]{2,1,0:T(4,128)} %gather_views.3.refs_0_.refs_6_), channel_id=1, source_target_pairs={{0,1},{1,0},{2,3},{3,2},{4,5},{5,4},{6,7},{7,6},{8,9},{9,8},{10,11... | collective-permute-start | bytes 417800 | tf_op jit(solution)/shard_map/ppermute | solution.py:464
  57.7 10.6 %collective-permute-start.17 = (f32[17,4,512]{2,1,0:T(4,128)}, f32[17,4,512]{2,1,0:T(4,128)S(1)}, u32[]{:S(2)}, u32[]{:S(2)}) collective-permute-start(f32[17,4,512]{2,1,0:T(4,128)} %gather_views.3.refs_0_.refs_6_), channel_id=1, source_target_pairs={{0,3},{1,2},{2,1},{3,0},{4,7},{5,6},{6,5},{7,4},{8,11},{9,10},{10,... | collective-permute-start | bytes 417800 | tf_op jit(solution)/shard_map/ppermute | solution.py:464
  64.1 8.5 %copy-start.3 = (f32[17,4,512]{2,1,0:T(4,128)}, f32[17,4,512]{2,1,0:T(4,128)S(1)}, u32[]{:S(2)}) copy-start(f32[17,4,512]{2,1,0:T(4,128)S(1)} %collective-permute-done.14.refs_2_.refs_8_) | copy-start | bytes 417796
  64.1 7.0 %collective-permute-start.18 = (f32[17,4,512]{2,1,0:T(4,128)S(1)}, f32[17,4,512]{2,1,0:T(4,128)S(1)}, u32[]{:S(2)}, u32[]{:S(2)}) collective-permute-start(f32[17,4,512]{2,1,0:T(4,128)S(1)} %collective-permute-done.14.refs_2_.refs_8_), channel_id=1, source_target_pairs={{0,1},{1,0},{2,3},{3,2},{4,5},{5,4},{6,7},{7,6},{8,9},{9,8},{10,11... | collective-permute-start | bytes 417800 | tf_op jit(solution)/shard_map/ppermute | solution.py:464
  65.6 7.0 %copy-start.4 = (f32[17,4,512]{2,1,0:T(4,128)}, f32[17,4,512]{2,1,0:T(4,128)S(1)}, u32[]{:S(2)}) copy-start(f32[17,4,512]{2,1,0:T(4,128)S(1)} %collective-permute-done.15.refs_3_.refs_9_) | copy-start | bytes 417796
  65.6 7.0 %collective-permute-start.19 = (f32[17,4,512]{2,1,0:T(4,128)S(1)}, f32[17,4,512]{2,1,0:T(4,128)S(1)}, u32[]{:S(2)}, u32[]{:S(2)}) collective-permute-start(f32[17,4,512]{2,1,0:T(4,128)S(1)} %collective-permute-done.15.refs_3_.refs_9_), channel_id=1, source_target_pairs={{0,1},{1,0},{2,3},{3,2},{4,5},{5,4},{6,7},{7,6},{8,9},{9,8},{10,11... | collective-permute-start | bytes 417800 | tf_op jit(solution)/shard_map/ppermute | solution.py:464
  66.1 6.4 %copy-start.5 = (f32[17,4,512]{2,1,0:T(4,128)}, f32[17,4,512]{2,1,0:T(4,128)S(1)}, u32[]{:S(2)}) copy-start(f32[17,4,512]{2,1,0:T(4,128)S(1)} %collective-permute-done.13.refs_1_.refs_7_) | copy-start | bytes 417796
  66.2 6.4 %copy-start.6 = (f32[17,4,512]{2,1,0:T(4,128)}, f32[17,4,512]{2,1,0:T(4,128)S(1)}, u32[]{:S(2)}) copy-start(f32[17,4,512]{2,1,0:T(4,128)S(1)} %collective-permute-done.16.refs_4_.refs_10_) | copy-start | bytes 417796
  74.6 1.9 %collective-permute-start.20 = (f32[1,128]{1,0:T(1,128)}, f32[1,128]{1,0:T(1,128)S(1)}, u32[]{:S(2)}, u32[]{:S(2)}) collective-permute-start(f32[1,128]{1,0:T(1,128)} %total.1.refs_1_), channel_id=1, source_target_pairs={{0,8},{8,0},{16,24},{24,16},{1,9},{9,1},{17,25},{25,17},{2,10},{10... | collective-permute-start | bytes 1544 | tf_op jit(solution)/shard_map/ppermute | solution.py:464
  74.6 3.6 %collective-permute-start.21 = (f32[1,128]{1,0:T(1,128)}, f32[1,128]{1,0:T(1,128)S(1)}, u32[]{:S(2)}, u32[]{:S(2)}) collective-permute-start(f32[1,128]{1,0:T(1,128)} %total.1.refs_1_), channel_id=1, source_target_pairs={{0,16},{8,24},{16,0},{24,8},{1,17},{9,25},{17,1},{25,9},{2,18},{10... | collective-permute-start | bytes 1544 | tf_op jit(solution)/shard_map/ppermute | solution.py:464
  75.1 3.2 %collective-permute-start.22 = (f32[1,128]{1,0:T(1,128)}, f32[1,128]{1,0:T(1,128)S(1)}, u32[]{:S(2)}, u32[]{:S(2)}) collective-permute-start(f32[1,128]{1,0:T(1,128)} %total.1.refs_1_), channel_id=1, source_target_pairs={{0,24},{8,16},{16,8},{24,0},{1,25},{9,17},{17,9},{25,1},{2,26},{10... | collective-permute-start | bytes 1544 | tf_op jit(solution)/shard_map/ppermute | solution.py:464
  (13 other events, 17.1 us)

commit v7 on v6

--- a/solution.py
+++ b/solution.py
@@ -270,26 +270,54 @@
     return jnp.clip(first, 0, (blocks - WINDOW) * LANES)
 
 
-def residual_kernel(dims, parts_n, ints_ref, trig_ref, *rest):
-    rows_n, cols_n, bins_n, base, blocks = dims
-    projs, sinos, outs = rest[:4], rest[4:8], rest[8 : 8 + parts_n]
-    pads = rest[8 + parts_n : 11 + parts_n]
-    sino, res = rest[11 + parts_n :]
-    views_n, _, band, _ = projs[0].shape
-    slab, part = ints_ref[0], ints_ref[1]
-    for other in range(1, 4):
-        pad = pads[other - 1]
-        pad[:, :, 0:band] = jnp.zeros((views_n, blocks, band, LANES), jnp.float32)
-        pad[:, :, 2 * band :] = jnp.zeros((views_n, blocks, band, LANES), jnp.float32)
-        pad[:, :, band : 2 * band] = projs[other][...]
+def fill_pad(pad, value):
+    views_n, blocks, band, _ = value.shape
+    edge = jnp.zeros((views_n, blocks, band, LANES), jnp.float32)
+    pad[:, :, 0:band] = edge
+    pad[:, :, 2 * band :] = edge
+    pad[:, :, band : 2 * band] = value[...]
+
+
+def near_kernel(ints_ref, proj_ref, near_ref, *rest):
+    sinos, out_ref, pad, sino = rest[:4], rest[4], rest[5], rest[6]
+    views_n, blocks, band, _ = proj_ref.shape
+    slab = ints_ref[0]
+    fill_pad(pad, near_ref)
     for other in range(4):
         rows = pl.ds(pl.multiple_of((slab ^ other) * band, band), band)
         sino[:, :, rows] = sinos[other][:, 0:blocks]
     for v in range(views_n):
-        value = projs[0][v]
-        for other in range(1, 4):
-            value = value + pads[other - 1][v, :, pl.ds(ints_ref[2 + 4 * v + other], band), :]
-        res[v, 0:blocks] = value - sino[v, :, pl.ds(ints_ref[2 + 4 * v], band), :]
+        value = proj_ref[v] + pad[v, :, pl.ds(ints_ref[3 + 4 * v], band), :]
+        out_ref[v] = value - sino[v, :, pl.ds(ints_ref[2 + 4 * v], band), :]
+
+
+def near_residual(ints, arrays):
+    views_n, blocks, band, _ = arrays[0].shape
+    vmem = pl.BlockSpec(memory_space=pltpu.VMEM)
+    return pl.pallas_call(
+        near_kernel,
+        out_shape=jax.ShapeDtypeStruct(arrays[0].shape, jnp.float32),
+        in_specs=[pl.BlockSpec(memory_space=pltpu.SMEM)] + [vmem] * len(arrays),
+        out_specs=vmem,
+        scratch_shapes=[
+            pltpu.VMEM((views_n, blocks, 3 * band, LANES), jnp.float32),
+            pltpu.VMEM((views_n, blocks, 4 * band, LANES), jnp.float32),
+        ],
+        name="near_residual",
+    )(ints, *arrays)
+
+
+def residual_kernel(dims, parts_n, ints_ref, trig_ref, base_ref, cross_ref, cross_pair_ref, *rest):
+    rows_n, cols_n, bins_n, base, blocks = dims
+    outs = rest[:parts_n]
+    cross_pad, cross_pair_pad, res = rest[parts_n:]
+    views_n, _, band, _ = base_ref.shape
+    part = ints_ref[1]
+    fill_pad(cross_pad, cross_ref)
+    fill_pad(cross_pair_pad, cross_pair_ref)
+    for v in range(views_n):
+        value = base_ref[v] + cross_pad[v, :, pl.ds(ints_ref[4 + 4 * v], band), :]
+        res[v, 0:blocks] = value + cross_pair_pad[v, :, pl.ds(ints_ref[5 + 4 * v], band), :]
         res[v, blocks] = jnp.zeros((band, LANES), jnp.float32)
     lane = lax.broadcasted_iota(jnp.int32, (band, LANES), 1)
     per_n = cols_n // parts_n
@@ -320,8 +348,6 @@
         scratch_shapes=[
             pltpu.VMEM((views_n, blocks, 3 * band, LANES), jnp.float32),
             pltpu.VMEM((views_n, blocks, 3 * band, LANES), jnp.float32),
-            pltpu.VMEM((views_n, blocks, 3 * band, LANES), jnp.float32),
-            pltpu.VMEM((views_n, blocks, 4 * band, LANES), jnp.float32),
             pltpu.VMEM((views_n, blocks + 1, band, LANES), jnp.float32),
         ],
         name="residual_windows",
@@ -334,7 +360,7 @@
         tv_ref, curv_ref, near_ref, *rest = rest
     pieces = rest[:pieces_n]
     if last:
-        out_ref, rows_ref, trig_ref, starts_ref = rest[pieces_n:]
+        out_ref, sum_ref, rows_ref, trig_ref, starts_ref = rest[pieces_n:]
     else:
         rows_ref, trig_ref, starts_ref = rest[pieces_n:]
     per_n = cols_n // parts_n
@@ -388,7 +414,9 @@
     if last:
         for row in range(rows_n):
             out_ref[0:16, row, :] = rows_ref[row]
-        out_ref[16] = jnp.full((rows_n, per_n), jnp.sum(squares), jnp.float32)
+        summed = jnp.sum(squares)
+        out_ref[16] = jnp.full((rows_n, per_n), summed, jnp.float32)
+        sum_ref[...] = jnp.full((1, LANES), summed, jnp.float32)
 
 
 def gather_views(dims, parts_n, ints, pieces, extra=()):
@@ -398,7 +426,7 @@
     pieces_n = len(pieces)
     last = len(extra) > 0
     rows = (rows_n, slices_n, per_n)
-    shape = (slices_n + 1, rows_n, per_n) if last else rows
+    shapes = [(slices_n + 1, rows_n, per_n), (1, LANES)] if last else [rows]
     vmem = pl.BlockSpec(memory_space=pltpu.VMEM)
     scratch = [
         pltpu.SMEM((2 * pieces_n * views_n,), jnp.float32),
@@ -406,32 +434,33 @@
     ]
     return pl.pallas_call(
         lambda *refs: gather_kernel(dims, parts_n, pieces_n, views_n, last, *refs),
-        out_shape=jax.ShapeDtypeStruct(shape, jnp.float32),
+        out_shape=[jax.ShapeDtypeStruct(x, jnp.float32) for x in shapes],
         in_specs=[pl.BlockSpec(memory_space=pltpu.SMEM)] + [vmem] * (pieces_n + len(extra)),
-        out_specs=vmem,
+        out_specs=[vmem] * len(shapes),
         scratch_shapes=([pltpu.VMEM(rows, jnp.float32)] if last else []) + scratch,
         name="gather_views",
     )(ints, *extra, *pieces)
 
 
-def total_kernel(*refs):
-    sums = [ref[0, 0:1, :] for ref in refs[:-1]]
+def total_kernel(pieces_n, *refs):
+    sums = [ref[0, 0:1, :] for ref in refs[:pieces_n]] + [ref[...] for ref in refs[pieces_n:-1]]
     while len(sums) > 1:
         sums = [a + b for a, b in zip(sums[0::2], sums[1::2])]
     refs[-1][...] = sums[0]
 
 
-def total(pieces):
+def total(pieces, distant):
     slices_n, rows_n, _ = pieces[0].shape
     last = pl.BlockSpec((1, rows_n, LANES), lambda i: (slices_n - 1, 0, 0))
-    return pl.pallas_call(
-        total_kernel,
+    line = pl.BlockSpec((1, LANES), lambda i: (0, 0))
+    return pl.pallas_call(
+        lambda *refs: total_kernel(len(pieces), *refs),
         grid=(1,),
         out_shape=jax.ShapeDtypeStruct((1, LANES), jnp.float32),
-        in_specs=[last] * len(pieces),
-        out_specs=pl.BlockSpec((1, LANES), lambda i: (0, 0)),
+        in_specs=[last] * len(pieces) + [line] * len(distant),
+        out_specs=line,
         name="total",
-    )(*pieces)
+    )(*pieces, *distant)
 
 
 def finish_kernel(parts_n, voxel_count, ints_ref, *rest):
@@ -501,7 +530,6 @@
     cross_pair_rows = swapped(cross_rows, "slab", 1)
     cross = swapped(proj, "slab", 2)
     near = swapped(proj, "slab", 1)
-    cross_pair = swapped(cross, "slab", 1)
 
     def of(k):
         return lax.dynamic_index_in_dim(offsets, k, 1, keepdims=False)
@@ -510,13 +538,11 @@
     shifts = [slices_n + jnp.clip(start - of(slab ^ k), -slices_n, slices_n) for k in (1, 2, 3)]
     table = jnp.stack([start] + shifts, axis=1).reshape(-1)
     ints = jnp.concatenate([jnp.stack([slab, part]).astype(jnp.int32), table])
-    windows = residual_windows(
-        dims,
-        parts_n,
-        ints,
-        trig,
-        [proj, near, cross, cross_pair, measured, pair_rows, cross_rows, cross_pair_rows],
-    )
+    rows = [measured, pair_rows, cross_rows, cross_pair_rows]
+    local_part = near_residual(ints, [proj, near] + rows)
+    local_part, cross = lax.optimization_barrier((local_part, cross))
+    cross_pair = swapped(cross, "slab", 1)
+    windows = residual_windows(dims, parts_n, ints, trig, [local_part, cross, cross_pair])
     pieces = [windows[0]] + [swapped(windows[r], "view", r) for r in range(1, parts_n)]
     def face_of(rows, which):
         return rows[which, blocks].reshape(1, rows_n, per_n)
@@ -531,10 +557,12 @@
     tv_grad = tv_padded(jnp.pad(block, ((0, 0), (1, 1), (0, 0))))
     curv = lax.dynamic_slice_in_dim(curvature, part * per_n, per_n, axis=2)
     tv = (tv_weight * tv_grad).transpose(1, 0, 2)
-    near_grad = gather_views(dims, parts_n, ints, pieces[: parts_n // 2])
+    (near_grad,) = gather_views(dims, parts_n, ints, pieces[: parts_n // 2])
     extra = (tv, curv.transpose(1, 0, 2), near_grad)
-    parts = gathered(gather_views(dims, parts_n, ints, pieces[parts_n // 2 :], extra))
-    squares = total(parts)
+    piece, squares = gather_views(dims, parts_n, ints, pieces[parts_n // 2 :], extra)
+    distant = [swapped(squares, "view", k) for k in SLOTS[6:]]
+    parts = gathered(piece)
+    squares = total(parts[:6], distant)
     sums = [squares] + [swapped(squares, "slab", k) for k in (1, 2, 3)]
     voxel_count = slices_n * slab_count * rows_n * cols_n
     return finish(voxel_count, ints, sums, volume, parts)

time: 83.3 us -> 87.3 us (1.048)
  local copies, waits for them, and re-layouts: 6.56 us -> 8.5 us
  Pallas kernels: 22.6 us -> 24.2 us
    pallas_call x1 -> x2, Pallas kernels: 1.29 us -> 3.78 us  [the longest x1 2.55 us: near_residual(): pl.pallas_call(near_kernel, out_shape=jax.ShapeDtypeStruct(arrays[0].shap...]
    unnamed x46 -> x54, local copies, waits for them, and re-layouts: 4.21 us -> 6.15 us
    ppermute x23 -> x25, starting transfers between devices: 26.7 us -> 27.5 us  [swapped(): lax.ppermute(x, axis, [(i, i ^ bit) for i in range(lax.axis_size(axis))])]
    ppermute x23 -> x25, waiting for transfers between devices: 22.6 us -> 23 us  [swapped(): lax.ppermute(x, axis, [(i, i ^ bit) for i in range(lax.axis_size(axis))])]
  transfers between devices with their start and end apart: 23 -> 25, of which waited for: 7 -> 7; matrix products, arithmetic and copies ran while one was open for 6% -> 6% of each run, Pallas kernels for 14% -> 18%
where the time goes in v7:
time: 87.3 us; the launch traced here: 86.9 us
  starting transfers between devices  27.5 us (32%)
  Pallas kernels  24.2 us (28%)
  waiting for transfers between devices  23 us (26%)
  local copies, waits for them, and re-layouts  8.5 us (10%)
  other arithmetic  3.39 us (4%)
    ppermute x25, starting transfers between devices, swapped(): lax.ppermute(x, axis, [(i, i ^ bit) for i in range(lax.axis_size(axis))])  27.5 us
    ppermute x25, waiting for transfers between devices, swapped(): lax.ppermute(x, axis, [(i, i ^ bit) for i in range(lax.axis_size(axis))])  23 us
    pallas_call x1, Pallas kernels, project(): pl.pallas_call(body, out_shape=jax.ShapeDtypeStruct((views_n, blocks_n, s...  7.97 us
    pallas_call x2, Pallas kernels, gather_views(): pl.pallas_call(lambda *refs: gather_kernel(dims, parts_n, pieces_n, views...  7.3 us
    unnamed x54, local copies, waits for them, and re-layouts  6.15 us
    pallas_call x1, Pallas kernels, finish(): pl.pallas_call(lambda *refs: finish_kernel(parts_n, voxel_count, *refs),...  2.88 us
    pallas_call x1, Pallas kernels, near_residual(): pl.pallas_call(near_kernel, out_shape=jax.ShapeDtypeStruct(arrays[0].shap...  2.55 us
    pallas_call x1, Pallas kernels, residual_windows(): pl.pallas_call(body, out_shape=[jax.ShapeDtypeStruct((views_n, WINDOW, ba...  2.29 us
  transfers between devices with their start and end apart: 25, of which 7 were waited for; matrix products, arithmetic and copies ran while one was open for 6% of the time, Pallas kernels for 18%

profile of v7, /device:TPU:0, one launch (start us, length us, event | category | flops | bytes accessed | tf_op | source)
XLA Modules:
  0.0 86.9 jit_solution(604436847956563431)
XLA Ops:
  0.0 0.8 constant_dynamic-slice_fusion.2
  0.8 1.2 %bitcast_bitcast_fusion = f32[2,23,16,128]{3,2,1,0:T(8,128)S(1)} fusion(f32[2,16,4096]{2,1,0:T(8,128)} %param.6), kind=kLoop, calls=%fused_computation.7 | loop fusion | bytes 753664 | tf_op jit(solution)/shard_map/transpose | solution.py:523
  2.1 3.0 %collective-permute-start.1 = (f32[2,24,16,128]{3,2,1,0:T(8,128)S(1)}, f32[2,24,16,128]{3,2,1,0:T(8,128)}, u32[]{:S(2)}, u32[]{:S(2)}) collective-permute-start(f32[2,24,16,128]{3,2,1,0:T(8,128)S(1)} %maximum_maximum_fusion.rest_0_), channel_id=1, source_target_pairs={{0,16},{8,24},{16,0},{24,8},{1,17},{9,25},{17,1},{25,9},{2,18},{10... | collective-permute-start | bytes 1179656 | tf_op jit(solution)/shard_map/ppermute | solution.py:493
  5.8 8.0 %project.1.proj_ref = f32[2,23,16,128]{3,2,1,0:T(8,128)} custom-call(f32[4]{0:T(128)} %pad_maximum_fusion.2.refs_0_.refs_1_, f32[16,4,4096]{2,1,0:T(4,128)} %refs_5_.1), custom_call_target="tpu_custom_call" | custom-call | tf_op jit(solution)/shard_map/project/pallas_call | solution.py:100
  16.7 0.7 copy-done.9
  17.5 2.6 %near_residual.1.refs_2_ = f32[2,23,16,128]{3,2,1,0:T(8,128)} custom-call(s32[10]{0:T(128)} %pad_add_fusion.1.ints_ref.refs_0_, f32[2,23,16,128]{3,2,1,0:T(8,128)} %project.1.proj_ref, f32[2,23,16,128]{3,2,1,0:T(8,128)} %collective-permute-done.3.near_ref, f32[2,24,16,128]{3,2,1,0:T(8,128)} %copy-done.2, f32[2,24,16,128]{3,2,1,0:T(8,128)} %copy-done.8, ...), custom_call_target="tpu_custom_call" | custom-call | tf_op jit(solution)/shard_map/near_residual/pallas_call | solution.py:297
  20.0 5.3 %collective-permute-done.4.refs_3_ = f32[2,23,16,128]{3,2,1,0:T(8,128)} collective-permute-done((f32[2,23,16,128]{3,2,1,0:T(8,128)}, f32[2,23,16,128]{3,2,1,0:T(8,128)}, u32[]{:S(2)}, u32[]{:S(2)}) %collective-permute-start.4) | collective-permute-done | bytes 376864 | tf_op jit(solution)/shard_map/ppermute | solution.py:493
  26.9 0.8 fusion.24
  27.8 2.3 %residual_windows.1 = (f32[2,3,16,128]{3,2,1,0:T(8,128)}, f32[2,3,16,128]{3,2,1,0:T(8,128)}, f32[2,3,16,128]{3,2,1,0:T(8,128)}, f32[2,3,16,128]{3,2,1,0:T(8,128)...) custom-call(s32[10]{0:T(128)} %pad_add_fusion.1.ints_ref.refs_0_, ...), custom_call_target="tpu_custom_call" | custom-call | tf_op jit(solution)/shard_map/residual_windows/pallas_call | solution.py:343
  30.1 1.5 %collective-permute-start.6 = (f32[2,3,16,128]{3,2,1,0:T(8,128)}, f32[2,3,16,128]{3,2,1,0:T(8,128)S(1)}, u32[]{:S(2)}, u32[]{:S(2)}) collective-permute-start(f32[2,3,16,128]{3,2,1,0:T(8,128)} %get-tuple-element.24), channel_id=1, source_target_pairs={{0,1},{1,0},{2,3},{3,2},{4,5},{5,4},{6,7},{7,6},{8,9},{9,8},{10,11... | collective-permute-start | bytes 147464 | tf_op jit(solution)/shard_map/ppermute | solution.py:493
  31.6 1.6 %collective-permute-start.7 = (f32[2,3,16,128]{3,2,1,0:T(8,128)}, f32[2,3,16,128]{3,2,1,0:T(8,128)S(1)}, u32[]{:S(2)}, u32[]{:S(2)}) collective-permute-start(f32[2,3,16,128]{3,2,1,0:T(8,128)} %get-tuple-element.25), channel_id=1, source_target_pairs={{0,2},{1,3},{2,0},{3,1},{4,6},{5,7},{6,4},{7,5},{8,10},{9,11},{10,... | collective-permute-start | bytes 147464 | tf_op jit(solution)/shard_map/ppermute | solution.py:493
  33.7 3.5 %collective-permute-start.10 = (f32[2,3,16,128]{3,2,1,0:T(8,128)}, f32[2,3,16,128]{3,2,1,0:T(8,128)S(1)}, u32[]{:S(2)}, u32[]{:S(2)}) collective-permute-start(f32[2,3,16,128]{3,2,1,0:T(8,128)} %get-tuple-element.28), channel_id=1, source_target_pairs={{0,5},{1,4},{2,7},{3,6},{4,1},{5,0},{6,3},{7,2},{8,13},{9,12},{10,... | collective-permute-start | bytes 147464 | tf_op jit(solution)/shard_map/ppermute | solution.py:493
  37.3 1.3 %collective-permute-start.11 = (f32[2,3,16,128]{3,2,1,0:T(8,128)}, f32[2,3,16,128]{3,2,1,0:T(8,128)S(1)}, u32[]{:S(2)}, u32[]{:S(2)}) collective-permute-start(f32[2,3,16,128]{3,2,1,0:T(8,128)} %get-tuple-element.29), channel_id=1, source_target_pairs={{0,6},{1,7},{2,4},{3,5},{4,2},{5,3},{6,0},{7,1},{8,14},{9,15},{10,... | collective-permute-start | bytes 147464 | tf_op jit(solution)/shard_map/ppermute | solution.py:493
  38.6 2.4 %collective-permute-start.12 = (f32[2,3,16,128]{3,2,1,0:T(8,128)}, f32[2,3,16,128]{3,2,1,0:T(8,128)S(1)}, u32[]{:S(2)}, u32[]{:S(2)}) collective-permute-start(f32[2,3,16,128]{3,2,1,0:T(8,128)} %get-tuple-element.30), channel_id=1, source_target_pairs={{0,7},{1,6},{2,5},{3,4},{4,3},{5,2},{6,1},{7,0},{8,15},{9,14},{10,... | collective-permute-start | bytes 147464 | tf_op jit(solution)/shard_map/ppermute | solution.py:493
  41.0 1.0 %fusion.7.refs_1_ = f32[4,16,512]{2,1,0:T(8,128)} fusion(s32[]{:T(128)S(6)} %select_n.98, f32[16,4,4096]{2,0,1:T(8,128)S(1)} %copy.8, s32[]{:T(128)S(6)} %add.69, f32[18,6,514]{2,0,1:T(8,128)S(1)} %select_maximum_fusion, f32[1,4,514]{2,0,1:T(1,128)S(1)} %pad.17, f32[16,4,514]{2,0,1:T(8,128)S(1)} %pad_dynamic-slice_fusion.3, s32[]{:T(128)S(6)} %add.68, ...), kind=kLoop, calls=%fused_computation.18 | loop fusion | flops 851968 | bytes 1589836 | tf_op jit(solution)/shard_map/transpose | solution.py:559
  42.7 3.5 %gather_views.2.refs_3_ = f32[4,16,512]{2,1,0:T(8,128)} custom-call(s32[10]{0:T(128)} %pad_add_fusion.1.ints_ref.refs_0_, f32[2,3,16,128]{3,2,1,0:T(8,128)} %get-tuple-element.23.refs_1_, f32[2,3,16,128]{3,2,1,0:T(8,128)} %copy-done.12, f32[2,3,16,128]{3,2,1,0:T(8,128)} %copy-done.13, f32[2,3,16,128]{3,2,1,0:T(8,128)} %copy-done.14), custom_call_target="tpu_custom_call" | custom-call | tf_op jit(solution)/shard_map/gather_views/pallas_call | solution.py:435
  46.2 1.0 %collective-permute-done.9.refs_4_ = f32[2,3,16,128]{3,2,1,0:T(8,128)S(1)} collective-permute-done((f32[2,3,16,128]{3,2,1,0:T(8,128)}, f32[2,3,16,128]{3,2,1,0:T(8,128)S(1)}, u32[]{:S(2)}, u32[]{:S(2)}) %collective-permute-start.9) | collective-permute-done | bytes 49184 | tf_op jit(solution)/shard_map/ppermute | solution.py:493
  47.8 3.8 %gather_views.3 = (f32[17,4,512]{2,1,0:T(4,128)}, f32[1,128]{1,0:T(1,128)}) custom-call(s32[10]{0:T(128)} %pad_add_fusion.1.ints_ref.refs_0_, f32[4,16,512]{2,1,0:T(8,128)} %fusion.7.refs_1_, f32[4,16,512]{2,1,0:T(8,128)} %bitcast.16, f32[4,16,512]{2,1,0:T(8,128)} %gather_views.2.refs_3_, f32[2,3,16,128]{3,2,1,0:T(8,128)} %copy-done.18, ...), custom_call_target="tpu_custom_call" | custom-call | tf_op jit(solution)/shard_map/gather_views/pallas_call | solution.py:435
  51.6 1.9 %collective-permute-start.14 = (f32[17,4,512]{2,1,0:T(4,128)}, f32[17,4,512]{2,1,0:T(4,128)S(1)}, u32[]{:S(2)}, u32[]{:S(2)}) collective-permute-start(f32[17,4,512]{2,1,0:T(4,128)} %get-tuple-element.31.refs_0_.refs_6_), channel_id=1, source_target_pairs={{0,4},{1,5},{2,6},{3,7},{4,0},{5,1},{6,2},{7,3},{8,12},{9,13},{10,... | collective-permute-start | bytes 417800 | tf_op jit(solution)/shard_map/ppermute | solution.py:493
  53.6 1.3 %collective-permute-start.15 = (f32[17,4,512]{2,1,0:T(4,128)}, f32[17,4,512]{2,1,0:T(4,128)S(1)}, u32[]{:S(2)}, u32[]{:S(2)}) collective-permute-start(f32[17,4,512]{2,1,0:T(4,128)} %get-tuple-element.31.refs_0_.refs_6_), channel_id=1, source_target_pairs={{0,6},{1,7},{2,4},{3,5},{4,2},{5,3},{6,0},{7,1},{8,14},{9,15},{10,... | collective-permute-start | bytes 417800 | tf_op jit(solution)/shard_map/ppermute | solution.py:493
  54.9 1.5 %collective-permute-start.18 = (f32[1,128]{1,0:T(1,128)}, f32[1,128]{1,0:T(1,128)S(1)}, u32[]{:S(2)}, u32[]{:S(2)}) collective-permute-start(f32[1,128]{1,0:T(1,128)} %get-tuple-element.32), channel_id=1, source_target_pairs={{0,5},{1,4},{2,7},{3,6},{4,1},{5,0},{6,3},{7,2},{8,13},{9,12},{10,... | collective-permute-start | bytes 1544 | tf_op jit(solution)/shard_map/ppermute | solution.py:493
  56.4 2.0 %collective-permute-start.19 = (f32[1,128]{1,0:T(1,128)}, f32[1,128]{1,0:T(1,128)S(1)}, u32[]{:S(2)}, u32[]{:S(2)}) collective-permute-start(f32[1,128]{1,0:T(1,128)} %get-tuple-element.32), channel_id=1, source_target_pairs={{0,7},{1,6},{2,5},{3,4},{4,3},{5,2},{6,1},{7,0},{8,15},{9,14},{10,... | collective-permute-start | bytes 1544 | tf_op jit(solution)/shard_map/ppermute | solution.py:493
  58.4 0.9 %collective-permute-start.13 = (f32[17,4,512]{2,1,0:T(4,128)}, f32[17,4,512]{2,1,0:T(4,128)S(1)}, u32[]{:S(2)}, u32[]{:S(2)}) collective-permute-start(f32[17,4,512]{2,1,0:T(4,128)} %get-tuple-element.31.refs_0_.refs_6_), channel_id=1, source_target_pairs={{0,2},{1,3},{2,0},{3,1},{4,6},{5,7},{6,4},{7,5},{8,10},{9,11},{10,... | collective-permute-start | bytes 417800 | tf_op jit(solution)/shard_map/ppermute | solution.py:493
  59.3 7.3 %collective-permute-done.18.refs_6_ = f32[1,128]{1,0:T(1,128)S(1)} collective-permute-done((f32[1,128]{1,0:T(1,128)}, f32[1,128]{1,0:T(1,128)S(1)}, u32[]{:S(2)}, u32[]{:S(2)}) %collective-permute-start.18) | collective-permute-done | bytes 544 | tf_op jit(solution)/shard_map/ppermute | solution.py:493
  66.6 1.3 %collective-permute-start.16 = (f32[17,4,512]{2,1,0:T(4,128)}, f32[17,4,512]{2,1,0:T(4,128)S(1)}, u32[]{:S(2)}, u32[]{:S(2)}) collective-permute-start(f32[17,4,512]{2,1,0:T(4,128)} %get-tuple-element.31.refs_0_.refs_6_), channel_id=1, source_target_pairs={{0,1},{1,0},{2,3},{3,2},{4,5},{5,4},{6,7},{7,6},{8,9},{9,8},{10,11... | collective-permute-start | bytes 417800 | tf_op jit(solution)/shard_map/ppermute | solution.py:493
  68.0 0.8 collective-permute-start.23
  68.8 1.3 %collective-permute-start.24 = (f32[17,4,512]{2,1,0:T(4,128)S(1)}, f32[17,4,512]{2,1,0:T(4,128)S(1)}, u32[]{:S(2)}, u32[]{:S(2)}) collective-permute-start(f32[17,4,512]{2,1,0:T(4,128)S(1)} %collective-permute-done.15.refs_3_.refs_9_), channel_id=1, source_target_pairs={{0,1},{1,0},{2,3},{3,2},{4,5},{5,4},{6,7},{7,6},{8,9},{9,8},{10,11... | collective-permute-start | bytes 417800 | tf_op jit(solution)/shard_map/ppermute | solution.py:493
  70.1 6.4 %collective-permute-done.16.refs_4_.refs_10_ = f32[17,4,512]{2,1,0:T(4,128)S(1)} collective-permute-done((f32[17,4,512]{2,1,0:T(4,128)}, f32[17,4,512]{2,1,0:T(4,128)S(1)}, u32[]{:S(2)}, u32[]{:S(2)}) %collective-permute-start.16) | collective-permute-done | bytes 139296 | tf_op jit(solution)/shard_map/ppermute | solution.py:493
  77.7 1.2 %total.1.refs_1_ = f32[1,128]{1,0:T(1,128)} custom-call(f32[17,4,512]{2,1,0:T(4,128)} %get-tuple-element.31.refs_0_.refs_6_, f32[17,4,512]{2,1,0:T(4,128)} %copy-done.5, f32[17,4,512]{2,1,0:T(4,128)} %copy-done.3, f32[17,4,512]{2,1,0:T(4,128)} %copy-done.4, f32[17,4,512]{2,1,0:T(4,128)} %copy-done.6, f32[17,4,512]{2,1,0:T(4,128)} %copy-done.7, ...), custom_call_target="tpu_custom_call" | custom-call | tf_op jit(solution)/shard_map/total/pallas_call | solution.py:456
  79.5 1.3 %collective-permute-start.22 = (f32[1,128]{1,0:T(1,128)}, f32[1,128]{1,0:T(1,128)S(1)}, u32[]{:S(2)}, u32[]{:S(2)}) collective-permute-start(f32[1,128]{1,0:T(1,128)} %total.1.refs_1_), channel_id=1, source_target_pairs={{0,24},{8,16},{16,8},{24,0},{1,25},{9,17},{17,9},{25,1},{2,26},{10... | collective-permute-start | bytes 1544 | tf_op jit(solution)/shard_map/ppermute | solution.py:493
  80.8 1.9 %collective-permute-done.21.refs_3_ = f32[1,128]{1,0:T(1,128)S(1)} collective-permute-done((f32[1,128]{1,0:T(1,128)}, f32[1,128]{1,0:T(1,128)S(1)}, u32[]{:S(2)}, u32[]{:S(2)}) %collective-permute-start.21) | collective-permute-done | bytes 544 | tf_op jit(solution)/shard_map/ppermute | solution.py:493
  84.0 2.9 %finish.1 = f32[16,4,4096]{2,1,0:T(4,128)} custom-call(s32[10]{0:T(128)} %pad_add_fusion.1.ints_ref.refs_0_, f32[1,128]{1,0:T(1,128)} %total.1.refs_1_, f32[1,128]{1,0:T(1,128)} %copy-done.20, f32[1,128]{1,0:T(1,128)} %copy-done.21, f32[1,128]{1,0:T(1,128)} %copy-done.22, f32[16,4,4096]{2,1,0:T(4,128)} %refs_5_.1, ...), custom_call_target="tpu_custom_call" | custom-call | tf_op jit(solution)/shard_map/finish/pallas_call | solution.py:483
  (98 shorter events, 10.2 us)
Async XLA Ops:
  0.0 25.4 %copy-start = (f32[16,4,4096]{2,1,0:T(4,128)S(1)}, f32[16,4,4096]{2,1,0:T(4,128)}, u32[]{:S(2)}) copy-start(f32[16,4,4096]{2,1,0:T(4,128)} %param.7) | copy-start | bytes 3145732
  2.0 12.4 %copy-start.19 = (s32[2,4]{1,0:T(2,128)S(1)}, s32[2,4]{1,0:T(2,128)}, u32[]{:S(2)}) copy-start(s32[2,4]{1,0:T(2,128)} %param.9) | copy-start | bytes 100
  2.0 14.4 %copy-start.2 = (f32[2,24,16,128]{3,2,1,0:T(8,128)}, f32[2,24,16,128]{3,2,1,0:T(8,128)S(1)}, u32[]{:S(2)}) copy-start(f32[2,24,16,128]{3,2,1,0:T(8,128)S(1)} %maximum_maximum_fusion.rest_0_) | copy-start | bytes 1179652
  2.1 12.4 %collective-permute-start.1 = (f32[2,24,16,128]{3,2,1,0:T(8,128)S(1)}, f32[2,24,16,128]{3,2,1,0:T(8,128)}, u32[]{:S(2)}, u32[]{:S(2)}) collective-permute-start(f32[2,24,16,128]{3,2,1,0:T(8,128)S(1)} %maximum_maximum_fusion.rest_0_), channel_id=1, source_target_pairs={{0,16},{8,24},{16,0},{24,8},{1,17},{9,25},{17,1},{25,9},{2,18},{10... | collective-permute-start | bytes 1179656 | tf_op jit(solution)/shard_map/ppermute | solution.py:493
  5.1 10.9 %collective-permute-start = (f32[2,24,16,128]{3,2,1,0:T(8,128)S(1)}, f32[2,24,16,128]{3,2,1,0:T(8,128)S(1)}, u32[]{:S(2)}, u32[]{:S(2)}) collective-permute-start(f32[2,24,16,128]{3,2,1,0:T(8,128)S(1)} %maximum_maximum_fusion.rest_0_), channel_id=1, source_target_pairs={{0,8},{8,0},{16,24},{24,16},{1,9},{9,1},{17,25},{25,17},{2,10},{10... | collective-permute-start | bytes 1179656 | tf_op jit(solution)/shard_map/ppermute | solution.py:493
  13.8 2.2 %collective-permute-start.3 = (f32[2,23,16,128]{3,2,1,0:T(8,128)}, f32[2,23,16,128]{3,2,1,0:T(8,128)}, u32[]{:S(2)}, u32[]{:S(2)}) collective-permute-start(f32[2,23,16,128]{3,2,1,0:T(8,128)} %project.1.proj_ref), channel_id=1, source_target_pairs={{0,8},{8,0},{16,24},{24,16},{1,9},{9,1},{17,25},{25,17},{2,10},{10... | collective-permute-start | bytes 1130504 | tf_op jit(solution)/shard_map/ppermute | solution.py:493
  14.3 11.1 %collective-permute-start.4 = (f32[2,23,16,128]{3,2,1,0:T(8,128)}, f32[2,23,16,128]{3,2,1,0:T(8,128)}, u32[]{:S(2)}, u32[]{:S(2)}) collective-permute-start(f32[2,23,16,128]{3,2,1,0:T(8,128)} %project.1.proj_ref), channel_id=1, source_target_pairs={{0,16},{8,24},{16,0},{24,8},{1,17},{9,25},{17,1},{25,9},{2,18},{10... | collective-permute-start | bytes 1130504 | tf_op jit(solution)/shard_map/ppermute | solution.py:493
  14.5 2.0 %collective-permute-start.2 = (f32[2,24,16,128]{3,2,1,0:T(8,128)}, f32[2,24,16,128]{3,2,1,0:T(8,128)S(1)}, u32[]{:S(2)}, u32[]{:S(2)}) collective-permute-start(f32[2,24,16,128]{3,2,1,0:T(8,128)} %collective-permute-done.1.rest_2_), channel_id=1, source_target_pairs={{0,8},{8,0},{16,24},{24,16},{1,9},{9,1},{17,25},{25,17},{2,10},{10... | collective-permute-start | bytes 1179656 | tf_op jit(solution)/shard_map/ppermute | solution.py:493
  15.4 10.0 %copy-start.1 = (f32[16,4,4096]{2,1,0:T(4,128)S(1)}, f32[16,4,4096]{2,1,0:T(4,128)}, u32[]{:S(2)}) copy-start(f32[16,4,4096]{2,1,0:T(4,128)} %refs_5_.1) | copy-start | bytes 3145732
  25.4 2.4 %collective-permute-start.5 = (f32[2,23,16,128]{3,2,1,0:T(8,128)}, f32[2,23,16,128]{3,2,1,0:T(8,128)}, u32[]{:S(2)}, u32[]{:S(2)}) collective-permute-start(f32[2,23,16,128]{3,2,1,0:T(8,128)} %collective-permute-done.4.refs_3_), channel_id=1, source_target_pairs={{0,8},{8,0},{16,24},{24,16},{1,9},{9,1},{17,25},{25,17},{2,10},{10... | collective-permute-start | bytes 1130504 | tf_op jit(solution)/shard_map/ppermute | solution.py:493
  30.1 8.5 %collective-permute-start.6 = (f32[2,3,16,128]{3,2,1,0:T(8,128)}, f32[2,3,16,128]{3,2,1,0:T(8,128)S(1)}, u32[]{:S(2)}, u32[]{:S(2)}) collective-permute-start(f32[2,3,16,128]{3,2,1,0:T(8,128)} %get-tuple-element.24), channel_id=1, source_target_pairs={{0,1},{1,0},{2,3},{3,2},{4,5},{5,4},{6,7},{7,6},{8,9},{9,8},{10,11... | collective-permute-start | bytes 147464 | tf_op jit(solution)/shard_map/ppermute | solution.py:493
  31.6 9.4 %collective-permute-start.7 = (f32[2,3,16,128]{3,2,1,0:T(8,128)}, f32[2,3,16,128]{3,2,1,0:T(8,128)S(1)}, u32[]{:S(2)}, u32[]{:S(2)}) collective-permute-start(f32[2,3,16,128]{3,2,1,0:T(8,128)} %get-tuple-element.25), channel_id=1, source_target_pairs={{0,2},{1,3},{2,0},{3,1},{4,6},{5,7},{6,4},{7,5},{8,10},{9,11},{10,... | collective-permute-start | bytes 147464 | tf_op jit(solution)/shard_map/ppermute | solution.py:493
  33.3 8.8 %collective-permute-start.8 = (f32[2,3,16,128]{3,2,1,0:T(8,128)}, f32[2,3,16,128]{3,2,1,0:T(8,128)S(1)}, u32[]{:S(2)}, u32[]{:S(2)}) collective-permute-start(f32[2,3,16,128]{3,2,1,0:T(8,128)} %get-tuple-element.26), channel_id=1, source_target_pairs={{0,3},{1,2},{2,1},{3,0},{4,7},{5,6},{6,5},{7,4},{8,11},{9,10},{10,... | collective-permute-start | bytes 147464 | tf_op jit(solution)/shard_map/ppermute | solution.py:493
  33.7 12.4 %collective-permute-start.10 = (f32[2,3,16,128]{3,2,1,0:T(8,128)}, f32[2,3,16,128]{3,2,1,0:T(8,128)S(1)}, u32[]{:S(2)}, u32[]{:S(2)}) collective-permute-start(f32[2,3,16,128]{3,2,1,0:T(8,128)} %get-tuple-element.28), channel_id=1, source_target_pairs={{0,5},{1,4},{2,7},{3,6},{4,1},{5,0},{6,3},{7,2},{8,13},{9,12},{10,... | collective-permute-start | bytes 147464 | tf_op jit(solution)/shard_map/ppermute | solution.py:493
  37.3 8.9 %collective-permute-start.11 = (f32[2,3,16,128]{3,2,1,0:T(8,128)}, f32[2,3,16,128]{3,2,1,0:T(8,128)S(1)}, u32[]{:S(2)}, u32[]{:S(2)}) collective-permute-start(f32[2,3,16,128]{3,2,1,0:T(8,128)} %get-tuple-element.29), channel_id=1, source_target_pairs={{0,6},{1,7},{2,4},{3,5},{4,2},{5,3},{6,0},{7,1},{8,14},{9,15},{10,... | collective-permute-start | bytes 147464 | tf_op jit(solution)/shard_map/ppermute | solution.py:493
  38.6 7.6 %collective-permute-start.12 = (f32[2,3,16,128]{3,2,1,0:T(8,128)}, f32[2,3,16,128]{3,2,1,0:T(8,128)S(1)}, u32[]{:S(2)}, u32[]{:S(2)}) collective-permute-start(f32[2,3,16,128]{3,2,1,0:T(8,128)} %get-tuple-element.30), channel_id=1, source_target_pairs={{0,7},{1,6},{2,5},{3,4},{4,3},{5,2},{6,1},{7,0},{8,15},{9,14},{10,... | collective-permute-start | bytes 147464 | tf_op jit(solution)/shard_map/ppermute | solution.py:493
  41.0 6.2 %collective-permute-start.9 = (f32[2,3,16,128]{3,2,1,0:T(8,128)}, f32[2,3,16,128]{3,2,1,0:T(8,128)S(1)}, u32[]{:S(2)}, u32[]{:S(2)}) collective-permute-start(f32[2,3,16,128]{3,2,1,0:T(8,128)} %get-tuple-element.27), channel_id=1, source_target_pairs={{0,4},{1,5},{2,6},{3,7},{4,0},{5,1},{6,2},{7,3},{8,12},{9,13},{10,... | collective-permute-start | bytes 147464 | tf_op jit(solution)/shard_map/ppermute | solution.py:493
  51.6 16.3 %collective-permute-start.14 = (f32[17,4,512]{2,1,0:T(4,128)}, f32[17,4,512]{2,1,0:T(4,128)S(1)}, u32[]{:S(2)}, u32[]{:S(2)}) collective-permute-start(f32[17,4,512]{2,1,0:T(4,128)} %get-tuple-element.31.refs_0_.refs_6_), channel_id=1, source_target_pairs={{0,4},{1,5},{2,6},{3,7},{4,0},{5,1},{6,2},{7,3},{8,12},{9,13},{10,... | collective-permute-start | bytes 417800 | tf_op jit(solution)/shard_map/ppermute | solution.py:493
  53.6 15.2 %collective-permute-start.15 = (f32[17,4,512]{2,1,0:T(4,128)}, f32[17,4,512]{2,1,0:T(4,128)S(1)}, u32[]{:S(2)}, u32[]{:S(2)}) collective-permute-start(f32[17,4,512]{2,1,0:T(4,128)} %get-tuple-element.31.refs_0_.refs_6_), channel_id=1, source_target_pairs={{0,6},{1,7},{2,4},{3,5},{4,2},{5,3},{6,0},{7,1},{8,14},{9,15},{10,... | collective-permute-start | bytes 417800 | tf_op jit(solution)/shard_map/ppermute | solution.py:493
  54.9 11.7 %collective-permute-start.18 = (f32[1,128]{1,0:T(1,128)}, f32[1,128]{1,0:T(1,128)S(1)}, u32[]{:S(2)}, u32[]{:S(2)}) collective-permute-start(f32[1,128]{1,0:T(1,128)} %get-tuple-element.32), channel_id=1, source_target_pairs={{0,5},{1,4},{2,7},{3,6},{4,1},{5,0},{6,3},{7,2},{8,13},{9,12},{10,... | collective-permute-start | bytes 1544 | tf_op jit(solution)/shard_map/ppermute | solution.py:493
  56.4 11.6 %collective-permute-start.19 = (f32[1,128]{1,0:T(1,128)}, f32[1,128]{1,0:T(1,128)S(1)}, u32[]{:S(2)}, u32[]{:S(2)}) collective-permute-start(f32[1,128]{1,0:T(1,128)} %get-tuple-element.32), channel_id=1, source_target_pairs={{0,7},{1,6},{2,5},{3,4},{4,3},{5,2},{6,1},{7,0},{8,15},{9,14},{10,... | collective-permute-start | bytes 1544 | tf_op jit(solution)/shard_map/ppermute | solution.py:493
  58.4 11.7 %collective-permute-start.13 = (f32[17,4,512]{2,1,0:T(4,128)}, f32[17,4,512]{2,1,0:T(4,128)S(1)}, u32[]{:S(2)}, u32[]{:S(2)}) collective-permute-start(f32[17,4,512]{2,1,0:T(4,128)} %get-tuple-element.31.refs_0_.refs_6_), channel_id=1, source_target_pairs={{0,2},{1,3},{2,0},{3,1},{4,6},{5,7},{6,4},{7,5},{8,10},{9,11},{10,... | collective-permute-start | bytes 417800 | tf_op jit(solution)/shard_map/ppermute | solution.py:493
  66.6 9.8 %copy-start.23 = (f32[1,128]{1,0:T(1,128)}, f32[1,128]{1,0:T(1,128)S(1)}, u32[]{:S(2)}) copy-start(f32[1,128]{1,0:T(1,128)S(1)} %collective-permute-done.18.refs_6_) | copy-start | bytes 1540
  66.6 9.8 %collective-permute-start.16 = (f32[17,4,512]{2,1,0:T(4,128)}, f32[17,4,512]{2,1,0:T(4,128)S(1)}, u32[]{:S(2)}, u32[]{:S(2)}) collective-permute-start(f32[17,4,512]{2,1,0:T(4,128)} %get-tuple-element.31.refs_0_.refs_6_), channel_id=1, source_target_pairs={{0,1},{1,0},{2,3},{3,2},{4,5},{5,4},{6,7},{7,6},{8,9},{9,8},{10,11... | collective-permute-start | bytes 417800 | tf_op jit(solution)/shard_map/ppermute | solution.py:493
  67.9 8.5 %copy-start.24 = (f32[1,128]{1,0:T(1,128)}, f32[1,128]{1,0:T(1,128)S(1)}, u32[]{:S(2)}) copy-start(f32[1,128]{1,0:T(1,128)S(1)} %collective-permute-done.19.refs_7_) | copy-start | bytes 1540
  67.9 8.5 %collective-permute-start.17 = (f32[17,4,512]{2,1,0:T(4,128)}, f32[17,4,512]{2,1,0:T(4,128)S(1)}, u32[]{:S(2)}, u32[]{:S(2)}) collective-permute-start(f32[17,4,512]{2,1,0:T(4,128)} %get-tuple-element.31.refs_0_.refs_6_), channel_id=1, source_target_pairs={{0,3},{1,2},{2,1},{3,0},{4,7},{5,6},{6,5},{7,4},{8,11},{9,10},{10,... | collective-permute-start | bytes 417800 | tf_op jit(solution)/shard_map/ppermute | solution.py:493
  67.9 8.5 %copy-start.3 = (f32[17,4,512]{2,1,0:T(4,128)}, f32[17,4,512]{2,1,0:T(4,128)S(1)}, u32[]{:S(2)}) copy-start(f32[17,4,512]{2,1,0:T(4,128)S(1)} %collective-permute-done.14.refs_2_.refs_8_) | copy-start | bytes 417796
  68.0 14.8 %collective-permute-start.23 = (f32[17,4,512]{2,1,0:T(4,128)S(1)}, f32[17,4,512]{2,1,0:T(4,128)S(1)}, u32[]{:S(2)}, u32[]{:S(2)}) collective-permute-start(f32[17,4,512]{2,1,0:T(4,128)S(1)} %collective-permute-done.14.refs_2_.refs_8_), channel_id=1, source_target_pairs={{0,1},{1,0},{2,3},{3,2},{4,5},{5,4},{6,7},{7,6},{8,9},{9,8},{10,11... | collective-permute-start | bytes 417800 | tf_op jit(solution)/shard_map/ppermute | solution.py:493
  68.8 14.0 %collective-permute-start.24 = (f32[17,4,512]{2,1,0:T(4,128)S(1)}, f32[17,4,512]{2,1,0:T(4,128)S(1)}, u32[]{:S(2)}, u32[]{:S(2)}) collective-permute-start(f32[17,4,512]{2,1,0:T(4,128)S(1)} %collective-permute-done.15.refs_3_.refs_9_), channel_id=1, source_target_pairs={{0,1},{1,0},{2,3},{3,2},{4,5},{5,4},{6,7},{7,6},{8,9},{9,8},{10,11... | collective-permute-start | bytes 417800 | tf_op jit(solution)/shard_map/ppermute | solution.py:493
  79.0 1.9 %collective-permute-start.20 = (f32[1,128]{1,0:T(1,128)}, f32[1,128]{1,0:T(1,128)S(1)}, u32[]{:S(2)}, u32[]{:S(2)}) collective-permute-start(f32[1,128]{1,0:T(1,128)} %total.1.refs_1_), channel_id=1, source_target_pairs={{0,8},{8,0},{16,24},{24,16},{1,9},{9,1},{17,25},{25,17},{2,10},{10... | collective-permute-start | bytes 1544 | tf_op jit(solution)/shard_map/ppermute | solution.py:493
  79.0 3.8 %collective-permute-start.21 = (f32[1,128]{1,0:T(1,128)}, f32[1,128]{1,0:T(1,128)S(1)}, u32[]{:S(2)}, u32[]{:S(2)}) collective-permute-start(f32[1,128]{1,0:T(1,128)} %total.1.refs_1_), channel_id=1, source_target_pairs={{0,16},{8,24},{16,0},{24,8},{1,17},{9,25},{17,1},{25,9},{2,18},{10... | collective-permute-start | bytes 1544 | tf_op jit(solution)/shard_map/ppermute | solution.py:493
  79.5 3.2 %collective-permute-start.22 = (f32[1,128]{1,0:T(1,128)}, f32[1,128]{1,0:T(1,128)S(1)}, u32[]{:S(2)}, u32[]{:S(2)}) collective-permute-start(f32[1,128]{1,0:T(1,128)} %total.1.refs_1_), channel_id=1, source_target_pairs={{0,24},{8,16},{16,8},{24,0},{1,25},{9,17},{17,9},{25,1},{2,26},{10... | collective-permute-start | bytes 1544 | tf_op jit(solution)/shard_map/ppermute | solution.py:493
  (19 other events, 35.2 us)

commit v8 on v7

--- a/solution.py
+++ b/solution.py
@@ -360,7 +360,7 @@
         tv_ref, curv_ref, near_ref, *rest = rest
     pieces = rest[:pieces_n]
     if last:
-        out_ref, sum_ref, rows_ref, trig_ref, starts_ref = rest[pieces_n:]
+        out_ref, rows_ref, trig_ref, starts_ref = rest[pieces_n:]
     else:
         rows_ref, trig_ref, starts_ref = rest[pieces_n:]
     per_n = cols_n // parts_n
@@ -414,9 +414,7 @@
     if last:
         for row in range(rows_n):
             out_ref[0:16, row, :] = rows_ref[row]
-        summed = jnp.sum(squares)
-        out_ref[16] = jnp.full((rows_n, per_n), summed, jnp.float32)
-        sum_ref[...] = jnp.full((1, LANES), summed, jnp.float32)
+        out_ref[16] = jnp.full((rows_n, per_n), jnp.sum(squares), jnp.float32)
 
 
 def gather_views(dims, parts_n, ints, pieces, extra=()):
@@ -426,7 +424,7 @@
     pieces_n = len(pieces)
     last = len(extra) > 0
     rows = (rows_n, slices_n, per_n)
-    shapes = [(slices_n + 1, rows_n, per_n), (1, LANES)] if last else [rows]
+    shape = (slices_n + 1, rows_n, per_n) if last else rows
     vmem = pl.BlockSpec(memory_space=pltpu.VMEM)
     scratch = [
         pltpu.SMEM((2 * pieces_n * views_n,), jnp.float32),
@@ -434,33 +432,32 @@
     ]
     return pl.pallas_call(
         lambda *refs: gather_kernel(dims, parts_n, pieces_n, views_n, last, *refs),
-        out_shape=[jax.ShapeDtypeStruct(x, jnp.float32) for x in shapes],
+        out_shape=jax.ShapeDtypeStruct(shape, jnp.float32),
         in_specs=[pl.BlockSpec(memory_space=pltpu.SMEM)] + [vmem] * (pieces_n + len(extra)),
-        out_specs=[vmem] * len(shapes),
+        out_specs=vmem,
         scratch_shapes=([pltpu.VMEM(rows, jnp.float32)] if last else []) + scratch,
         name="gather_views",
     )(ints, *extra, *pieces)
 
 
-def total_kernel(pieces_n, *refs):
-    sums = [ref[0, 0:1, :] for ref in refs[:pieces_n]] + [ref[...] for ref in refs[pieces_n:-1]]
+def total_kernel(*refs):
+    sums = [ref[0, 0:1, :] for ref in refs[:-1]]
     while len(sums) > 1:
         sums = [a + b for a, b in zip(sums[0::2], sums[1::2])]
     refs[-1][...] = sums[0]
 
 
-def total(pieces, distant):
+def total(pieces):
     slices_n, rows_n, _ = pieces[0].shape
     last = pl.BlockSpec((1, rows_n, LANES), lambda i: (slices_n - 1, 0, 0))
-    line = pl.BlockSpec((1, LANES), lambda i: (0, 0))
-    return pl.pallas_call(
-        lambda *refs: total_kernel(len(pieces), *refs),
+    return pl.pallas_call(
+        total_kernel,
         grid=(1,),
         out_shape=jax.ShapeDtypeStruct((1, LANES), jnp.float32),
-        in_specs=[last] * len(pieces) + [line] * len(distant),
-        out_specs=line,
+        in_specs=[last] * len(pieces),
+        out_specs=pl.BlockSpec((1, LANES), lambda i: (0, 0)),
         name="total",
-    )(*pieces, *distant)
+    )(*pieces)
 
 
 def finish_kernel(parts_n, voxel_count, ints_ref, *rest):
@@ -538,12 +535,6 @@
     shifts = [slices_n + jnp.clip(start - of(slab ^ k), -slices_n, slices_n) for k in (1, 2, 3)]
     table = jnp.stack([start] + shifts, axis=1).reshape(-1)
     ints = jnp.concatenate([jnp.stack([slab, part]).astype(jnp.int32), table])
-    rows = [measured, pair_rows, cross_rows, cross_pair_rows]
-    local_part = near_residual(ints, [proj, near] + rows)
-    local_part, cross = lax.optimization_barrier((local_part, cross))
-    cross_pair = swapped(cross, "slab", 1)
-    windows = residual_windows(dims, parts_n, ints, trig, [local_part, cross, cross_pair])
-    pieces = [windows[0]] + [swapped(windows[r], "view", r) for r in range(1, parts_n)]
     def face_of(rows, which):
         return rows[which, blocks].reshape(1, rows_n, per_n)
 
@@ -557,12 +548,17 @@
     tv_grad = tv_padded(jnp.pad(block, ((0, 0), (1, 1), (0, 0))))
     curv = lax.dynamic_slice_in_dim(curvature, part * per_n, per_n, axis=2)
     tv = (tv_weight * tv_grad).transpose(1, 0, 2)
-    (near_grad,) = gather_views(dims, parts_n, ints, pieces[: parts_n // 2])
-    extra = (tv, curv.transpose(1, 0, 2), near_grad)
-    piece, squares = gather_views(dims, parts_n, ints, pieces[parts_n // 2 :], extra)
-    distant = [swapped(squares, "view", k) for k in SLOTS[6:]]
-    parts = gathered(piece)
-    squares = total(parts[:6], distant)
+    curv = curv.transpose(1, 0, 2)
+    rows = [measured, pair_rows, cross_rows, cross_pair_rows]
+    local_part = near_residual(ints, [proj, near] + rows)
+    local_part, cross, tv, curv = lax.optimization_barrier((local_part, cross, tv, curv))
+    cross_pair = swapped(cross, "slab", 1)
+    windows = residual_windows(dims, parts_n, ints, trig, [local_part, cross, cross_pair])
+    pieces = [windows[0]] + [swapped(windows[r], "view", r) for r in range(1, parts_n)]
+    near_grad = gather_views(dims, parts_n, ints, pieces[: parts_n // 2])
+    extra = (tv, curv, near_grad)
+    parts = gathered(gather_views(dims, parts_n, ints, pieces[parts_n // 2 :], extra))
+    squares = total(parts)
     sums = [squares] + [swapped(squares, "slab", k) for k in (1, 2, 3)]
     voxel_count = slices_n * slab_count * rows_n * cols_n
     return finish(voxel_count, ints, sums, volume, parts)

time: 87.3 us -> 82.8 us (0.948)
  starting transfers between devices: 27.5 us -> 23.6 us
  waiting for transfers between devices: 23 us -> 21.9 us
    ppermute x25 -> x23, starting transfers between devices: 27.5 us -> 23.6 us  [swapped(): lax.ppermute(x, axis, [(i, i ^ bit) for i in range(lax.axis_size(axis))])]
    ppermute x25 -> x23, waiting for transfers between devices: 23 us -> 21.9 us  [swapped(): lax.ppermute(x, axis, [(i, i ^ bit) for i in range(lax.axis_size(axis))])]
    unnamed x54 -> x48, local copies, waits for them, and re-layouts: 6.15 us -> 5.89 us
  transfers between devices with their start and end apart: 25 -> 23, of which waited for: 7 -> 11; matrix products, arithmetic and copies ran while one was open for 6% -> 8% of each run, Pallas kernels for 18% -> 17%
where the time goes in v8:
time: 82.8 us; the launch traced here: 82.3 us
  Pallas kernels  24.3 us (29%)
  starting transfers between devices  23.6 us (29%)
  waiting for transfers between devices  21.9 us (26%)
  local copies, waits for them, and re-layouts  8.9 us (11%)
  other arithmetic  3.37 us (4%)
    ppermute x23, starting transfers between devices, swapped(): lax.ppermute(x, axis, [(i, i ^ bit) for i in range(lax.axis_size(axis))])  23.6 us
    ppermute x23, waiting for transfers between devices, swapped(): lax.ppermute(x, axis, [(i, i ^ bit) for i in range(lax.axis_size(axis))])  21.9 us
    pallas_call x1, Pallas kernels, project(): pl.pallas_call(body, out_shape=jax.ShapeDtypeStruct((views_n, blocks_n, s...  7.95 us
    pallas_call x2, Pallas kernels, gather_views(): pl.pallas_call(lambda *refs: gather_kernel(dims, parts_n, pieces_n, views...  7.28 us
    unnamed x48, local copies, waits for them, and re-layouts  5.89 us
    pallas_call x1, Pallas kernels, finish(): pl.pallas_call(lambda *refs: finish_kernel(parts_n, voxel_count, *refs),...  2.88 us
    pallas_call x1, Pallas kernels, near_residual(): pl.pallas_call(near_kernel, out_shape=jax.ShapeDtypeStruct(arrays[0].shap...  2.58 us
    pallas_call x1, Pallas kernels, residual_windows(): pl.pallas_call(body, out_shape=[jax.ShapeDtypeStruct((views_n, WINDOW, ba...  2.31 us
  transfers between devices with their start and end apart: 23, of which 11 were waited for; matrix products, arithmetic and copies ran while one was open for 8% of the time, Pallas kernels for 17%

profile of v8, /device:TPU:0, one launch (start us, length us, event | category | flops | bytes accessed | tf_op | source)
XLA Modules:
  0.0 82.3 jit_solution(658228310930414447)
XLA Ops:
  0.0 0.8 constant_dynamic-slice_fusion.2
  0.8 1.2 %bitcast_bitcast_fusion = f32[2,23,16,128]{3,2,1,0:T(8,128)S(1)} fusion(f32[2,16,4096]{2,1,0:T(8,128)} %param.6), kind=kLoop, calls=%fused_computation.7 | loop fusion | bytes 753664 | tf_op jit(solution)/shard_map/transpose | solution.py:520
  2.6 2.6 %collective-permute-start.2 = (f32[2,24,16,128]{3,2,1,0:T(8,128)S(1)}, f32[2,24,16,128]{3,2,1,0:T(8,128)}, u32[]{:S(2)}, u32[]{:S(2)}) collective-permute-start(f32[2,24,16,128]{3,2,1,0:T(8,128)S(1)} %maximum_maximum_fusion.rest_0_), channel_id=1, source_target_pairs={{0,16},{8,24},{16,0},{24,8},{1,17},{9,25},{17,1},{25,9},{2,18},{10... | collective-permute-start | bytes 1179656 | tf_op jit(solution)/shard_map/ppermute | solution.py:490
  5.9 7.9 %project.1.proj_ref = f32[2,23,16,128]{3,2,1,0:T(8,128)} custom-call(f32[4]{0:T(128)} %pad_maximum_fusion.2.refs_0_.refs_1_, f32[16,4,4096]{2,1,0:T(4,128)} %refs_5_.1), custom_call_target="tpu_custom_call" | custom-call | tf_op jit(solution)/shard_map/project/pallas_call | solution.py:100
  17.0 1.6 %copy.15 = f32[16,4,512]{2,0,1:T(8,128)} copy(f32[16,4,512]{2,1,0:T(4,128)} %constant_dynamic-slice_fusion) | data formatting | bytes 262144
  18.8 0.8 fusion.24
  19.7 2.6 %near_residual.1.refs_2_ = f32[2,23,16,128]{3,2,1,0:T(8,128)} custom-call(s32[10]{0:T(128)} %pad_add_fusion.1.ints_ref.refs_0_, f32[2,23,16,128]{3,2,1,0:T(8,128)} %project.1.proj_ref, f32[2,23,16,128]{3,2,1,0:T(8,128)} %collective-permute-done.near_ref, f32[2,24,16,128]{3,2,1,0:T(8,128)} %copy-done.2, f32[2,24,16,128]{3,2,1,0:T(8,128)} %collective-permute-done.1.rest_1_, ...), custom_call_target="tpu_custom_call" | custom-call | tf_op jit(solution)/shard_map/near_residual/pallas_call | solution.py:297
  22.3 1.0 %fusion.7.refs_1_ = f32[4,16,512]{2,1,0:T(8,128)} fusion(s32[]{:T(128)S(6)} %select_n.99, f32[16,4,4096]{2,0,1:T(8,128)S(1)} %copy.9, s32[]{:T(128)S(6)} %add.69, f32[18,6,514]{2,0,1:T(8,128)S(1)} %select_maximum_fusion, f32[1,4,514]{2,0,1:T(1,128)S(1)} %pad.17, f32[16,4,514]{2,0,1:T(8,128)S(1)} %pad_dynamic-slice_fusion.3, s32[]{:T(128)S(6)} %add.68, ...), kind=kLoop, calls=%fused_computation.18 | loop fusion | flops 851968 | bytes 1589836 | tf_op jit(solution)/shard_map/transpose | solution.py:550
  23.4 2.0 %collective-permute-done.4.refs_3_ = f32[2,23,16,128]{3,2,1,0:T(8,128)} collective-permute-done((f32[2,23,16,128]{3,2,1,0:T(8,128)}, f32[2,23,16,128]{3,2,1,0:T(8,128)}, u32[]{:S(2)}, u32[]{:S(2)}) %collective-permute-start.4) | collective-permute-done | bytes 376864 | tf_op jit(solution)/shard_map/ppermute | solution.py:490
  25.4 1.9 %collective-permute-done.5.refs_4_ = f32[2,23,16,128]{3,2,1,0:T(8,128)S(1)} collective-permute-done((f32[2,23,16,128]{3,2,1,0:T(8,128)}, f32[2,23,16,128]{3,2,1,0:T(8,128)S(1)}, u32[]{:S(2)}, u32[]{:S(2)}) %collective-permute-start.5) | collective-permute-done | bytes 376864 | tf_op jit(solution)/shard_map/ppermute | solution.py:490
  28.0 2.3 %residual_windows.1 = (f32[2,3,16,128]{3,2,1,0:T(8,128)}, f32[2,3,16,128]{3,2,1,0:T(8,128)}, f32[2,3,16,128]{3,2,1,0:T(8,128)}, f32[2,3,16,128]{3,2,1,0:T(8,128)...) custom-call(s32[10]{0:T(128)} %pad_add_fusion.1.ints_ref.refs_0_, ...), custom_call_target="tpu_custom_call" | custom-call | tf_op jit(solution)/shard_map/residual_windows/pallas_call | solution.py:343
  30.4 1.5 %collective-permute-start.6 = (f32[2,3,16,128]{3,2,1,0:T(8,128)}, f32[2,3,16,128]{3,2,1,0:T(8,128)S(1)}, u32[]{:S(2)}, u32[]{:S(2)}) collective-permute-start(f32[2,3,16,128]{3,2,1,0:T(8,128)} %get-tuple-element.26), channel_id=1, source_target_pairs={{0,1},{1,0},{2,3},{3,2},{4,5},{5,4},{6,7},{7,6},{8,9},{9,8},{10,11... | collective-permute-start | bytes 147464 | tf_op jit(solution)/shard_map/ppermute | solution.py:490
  31.9 1.6 %collective-permute-start.7 = (f32[2,3,16,128]{3,2,1,0:T(8,128)}, f32[2,3,16,128]{3,2,1,0:T(8,128)S(1)}, u32[]{:S(2)}, u32[]{:S(2)}) collective-permute-start(f32[2,3,16,128]{3,2,1,0:T(8,128)} %get-tuple-element.27), channel_id=1, source_target_pairs={{0,2},{1,3},{2,0},{3,1},{4,6},{5,7},{6,4},{7,5},{8,10},{9,11},{10,... | collective-permute-start | bytes 147464 | tf_op jit(solution)/shard_map/ppermute | solution.py:490
  33.8 2.6 %collective-permute-start.9 = (f32[2,3,16,128]{3,2,1,0:T(8,128)}, f32[2,3,16,128]{3,2,1,0:T(8,128)S(1)}, u32[]{:S(2)}, u32[]{:S(2)}) collective-permute-start(f32[2,3,16,128]{3,2,1,0:T(8,128)} %get-tuple-element.29), channel_id=1, source_target_pairs={{0,4},{1,5},{2,6},{3,7},{4,0},{5,1},{6,2},{7,3},{8,12},{9,13},{10,... | collective-permute-start | bytes 147464 | tf_op jit(solution)/shard_map/ppermute | solution.py:490
  36.4 1.3 %collective-permute-start.10 = (f32[2,3,16,128]{3,2,1,0:T(8,128)}, f32[2,3,16,128]{3,2,1,0:T(8,128)S(1)}, u32[]{:S(2)}, u32[]{:S(2)}) collective-permute-start(f32[2,3,16,128]{3,2,1,0:T(8,128)} %get-tuple-element.30), channel_id=1, source_target_pairs={{0,5},{1,4},{2,7},{3,6},{4,1},{5,0},{6,3},{7,2},{8,13},{9,12},{10,... | collective-permute-start | bytes 147464 | tf_op jit(solution)/shard_map/ppermute | solution.py:490
  37.7 3.6 %collective-permute-start.11 = (f32[2,3,16,128]{3,2,1,0:T(8,128)}, f32[2,3,16,128]{3,2,1,0:T(8,128)S(1)}, u32[]{:S(2)}, u32[]{:S(2)}) collective-permute-start(f32[2,3,16,128]{3,2,1,0:T(8,128)} %get-tuple-element.31), channel_id=1, source_target_pairs={{0,6},{1,7},{2,4},{3,5},{4,2},{5,3},{6,0},{7,1},{8,14},{9,15},{10,... | collective-permute-start | bytes 147464 | tf_op jit(solution)/shard_map/ppermute | solution.py:490
  42.1 3.5 %gather_views.2.refs_3_ = f32[4,16,512]{2,1,0:T(8,128)} custom-call(s32[10]{0:T(128)} %pad_add_fusion.1.ints_ref.refs_0_, f32[2,3,16,128]{3,2,1,0:T(8,128)} %get-tuple-element.25.refs_1_, f32[2,3,16,128]{3,2,1,0:T(8,128)} %copy-done.13, f32[2,3,16,128]{3,2,1,0:T(8,128)} %copy-done.15, f32[2,3,16,128]{3,2,1,0:T(8,128)} %copy-done.16), custom_call_target="tpu_custom_call" | custom-call | tf_op jit(solution)/shard_map/gather_views/pallas_call | solution.py:433
  45.6 2.7 %collective-permute-done.12.refs_7_ = f32[2,3,16,128]{3,2,1,0:T(8,128)S(1)} collective-permute-done((f32[2,3,16,128]{3,2,1,0:T(8,128)}, f32[2,3,16,128]{3,2,1,0:T(8,128)S(1)}, u32[]{:S(2)}, u32[]{:S(2)}) %collective-permute-start.12) | collective-permute-done | bytes 49184 | tf_op jit(solution)/shard_map/ppermute | solution.py:490
  49.0 3.8 %gather_views.3.refs_0_.refs_6_ = f32[17,4,512]{2,1,0:T(4,128)} custom-call(s32[10]{0:T(128)} %pad_add_fusion.1.ints_ref.refs_0_, f32[4,16,512]{2,1,0:T(8,128)} %fusion.7.refs_1_, f32[4,16,512]{2,1,0:T(8,128)} %bitcast.16, f32[4,16,512]{2,1,0:T(8,128)} %gather_views.2.refs_3_, f32[2,3,16,128]{3,2,1,0:T(8,128)} %copy-done.11, f32[2,3,16,128]{3,2,1,0:T(8,128)} %copy-done.12, ...), custom_call_target="tpu_custom_call" | custom-call | tf_op jit(solution)/shard_map/gather_views/pallas_call | solution.py:433
  53.3 1.0 %collective-permute-start.15 = (f32[17,4,512]{2,1,0:T(4,128)}, f32[17,4,512]{2,1,0:T(4,128)S(1)}, u32[]{:S(2)}, u32[]{:S(2)}) collective-permute-start(f32[17,4,512]{2,1,0:T(4,128)} %gather_views.3.refs_0_.refs_6_), channel_id=1, source_target_pairs={{0,6},{1,7},{2,4},{3,5},{4,2},{5,3},{6,0},{7,1},{8,14},{9,15},{10,... | collective-permute-start | bytes 417800 | tf_op jit(solution)/shard_map/ppermute | solution.py:490
  54.3 2.0 %collective-permute-start.13 = (f32[17,4,512]{2,1,0:T(4,128)}, f32[17,4,512]{2,1,0:T(4,128)S(1)}, u32[]{:S(2)}, u32[]{:S(2)}) collective-permute-start(f32[17,4,512]{2,1,0:T(4,128)} %gather_views.3.refs_0_.refs_6_), channel_id=1, source_target_pairs={{0,2},{1,3},{2,0},{3,1},{4,6},{5,7},{6,4},{7,5},{8,10},{9,11},{10,... | collective-permute-start | bytes 417800 | tf_op jit(solution)/shard_map/ppermute | solution.py:490
  56.8 1.0 %collective-permute-start.17 = (f32[17,4,512]{2,1,0:T(4,128)}, f32[17,4,512]{2,1,0:T(4,128)S(1)}, u32[]{:S(2)}, u32[]{:S(2)}) collective-permute-start(f32[17,4,512]{2,1,0:T(4,128)} %gather_views.3.refs_0_.refs_6_), channel_id=1, source_target_pairs={{0,3},{1,2},{2,1},{3,0},{4,7},{5,6},{6,5},{7,4},{8,11},{9,10},{10,... | collective-permute-start | bytes 417800 | tf_op jit(solution)/shard_map/ppermute | solution.py:490
  57.8 5.8 %collective-permute-done.14.refs_2_.refs_8_ = f32[17,4,512]{2,1,0:T(4,128)S(1)} collective-permute-done((f32[17,4,512]{2,1,0:T(4,128)}, f32[17,4,512]{2,1,0:T(4,128)S(1)}, u32[]{:S(2)}, u32[]{:S(2)}) %collective-permute-start.14) | collective-permute-done | bytes 139296 | tf_op jit(solution)/shard_map/ppermute | solution.py:490
  63.6 1.2 %collective-permute-start.18 = (f32[17,4,512]{2,1,0:T(4,128)S(1)}, f32[17,4,512]{2,1,0:T(4,128)S(1)}, u32[]{:S(2)}, u32[]{:S(2)}) collective-permute-start(f32[17,4,512]{2,1,0:T(4,128)S(1)} %collective-permute-done.14.refs_2_.refs_8_), channel_id=1, source_target_pairs={{0,1},{1,0},{2,3},{3,2},{4,5},{5,4},{6,7},{7,6},{8,9},{9,8},{10,11... | collective-permute-start | bytes 417800 | tf_op jit(solution)/shard_map/ppermute | solution.py:490
  64.8 0.8 %collective-permute-start.19 = (f32[17,4,512]{2,1,0:T(4,128)S(1)}, f32[17,4,512]{2,1,0:T(4,128)S(1)}, u32[]{:S(2)}, u32[]{:S(2)}) collective-permute-start(f32[17,4,512]{2,1,0:T(4,128)S(1)} %collective-permute-done.15.refs_3_.refs_9_), channel_id=1, source_target_pairs={{0,1},{1,0},{2,3},{3,2},{4,5},{5,4},{6,7},{7,6},{8,9},{9,8},{10,11... | collective-permute-start | bytes 417800 | tf_op jit(solution)/shard_map/ppermute | solution.py:490
  65.7 1.5 %collective-permute-done.17.refs_5_.refs_11_ = f32[17,4,512]{2,1,0:T(4,128)S(1)} collective-permute-done((f32[17,4,512]{2,1,0:T(4,128)}, f32[17,4,512]{2,1,0:T(4,128)S(1)}, u32[]{:S(2)}, u32[]{:S(2)}) %collective-permute-start.17) | collective-permute-done | bytes 139296 | tf_op jit(solution)/shard_map/ppermute | solution.py:490
  67.1 3.0 %collective-permute-done.18.refs_6_.refs_12_ = f32[17,4,512]{2,1,0:T(4,128)S(1)} collective-permute-done((f32[17,4,512]{2,1,0:T(4,128)S(1)}, f32[17,4,512]{2,1,0:T(4,128)S(1)}, u32[]{:S(2)}, u32[]{:S(2)}) %collective-permute-start.18) | collective-permute-done | bytes 139296 | tf_op jit(solution)/shard_map/ppermute | solution.py:490
  70.1 2.7 %collective-permute-done.19.refs_7_.refs_13_ = f32[17,4,512]{2,1,0:T(4,128)S(1)} collective-permute-done((f32[17,4,512]{2,1,0:T(4,128)S(1)}, f32[17,4,512]{2,1,0:T(4,128)S(1)}, u32[]{:S(2)}, u32[]{:S(2)}) %collective-permute-start.19) | collective-permute-done | bytes 139296 | tf_op jit(solution)/shard_map/ppermute | solution.py:490
  73.5 1.3 %total.1.refs_1_ = f32[1,128]{1,0:T(1,128)} custom-call(f32[17,4,512]{2,1,0:T(4,128)} %gather_views.3.refs_0_.refs_6_, f32[17,4,512]{2,1,0:T(4,128)} %copy-done.5, f32[17,4,512]{2,1,0:T(4,128)} %copy-done.3, f32[17,4,512]{2,1,0:T(4,128)} %copy-done.4, f32[17,4,512]{2,1,0:T(4,128)} %copy-done.6, f32[17,4,512]{2,1,0:T(4,128)} %copy-done.7, ...), custom_call_target="tpu_custom_call" | custom-call | tf_op jit(solution)/shard_map/total/pallas_call | solution.py:453
  75.3 1.3 %collective-permute-start.22 = (f32[1,128]{1,0:T(1,128)}, f32[1,128]{1,0:T(1,128)S(1)}, u32[]{:S(2)}, u32[]{:S(2)}) collective-permute-start(f32[1,128]{1,0:T(1,128)} %total.1.refs_1_), channel_id=1, source_target_pairs={{0,24},{8,16},{16,8},{24,0},{1,25},{9,17},{17,9},{25,1},{2,26},{10... | collective-permute-start | bytes 1544 | tf_op jit(solution)/shard_map/ppermute | solution.py:490
  76.6 1.7 %collective-permute-done.21.refs_3_ = f32[1,128]{1,0:T(1,128)S(1)} collective-permute-done((f32[1,128]{1,0:T(1,128)}, f32[1,128]{1,0:T(1,128)S(1)}, u32[]{:S(2)}, u32[]{:S(2)}) %collective-permute-start.21) | collective-permute-done | bytes 544 | tf_op jit(solution)/shard_map/ppermute | solution.py:490
  79.4 2.9 %finish.1 = f32[16,4,4096]{2,1,0:T(4,128)} custom-call(s32[10]{0:T(128)} %pad_add_fusion.1.ints_ref.refs_0_, f32[1,128]{1,0:T(1,128)} %total.1.refs_1_, f32[1,128]{1,0:T(1,128)} %copy-done.19, f32[1,128]{1,0:T(1,128)} %copy-done.20, f32[1,128]{1,0:T(1,128)} %copy-done.21, f32[16,4,4096]{2,1,0:T(4,128)} %refs_5_.1, ...), custom_call_target="tpu_custom_call" | custom-call | tf_op jit(solution)/shard_map/finish/pallas_call | solution.py:480
  (88 shorter events, 10.7 us)
Async XLA Ops:
  0.0 15.1 %copy-start = (f32[16,4,4096]{2,1,0:T(4,128)S(1)}, f32[16,4,4096]{2,1,0:T(4,128)}, u32[]{:S(2)}) copy-start(f32[16,4,4096]{2,1,0:T(4,128)} %param.7) | copy-start | bytes 3145732
  2.0 12.3 %copy-start.18 = (s32[2,4]{1,0:T(2,128)S(1)}, s32[2,4]{1,0:T(2,128)}, u32[]{:S(2)}) copy-start(s32[2,4]{1,0:T(2,128)} %param.9) | copy-start | bytes 100
  2.0 15.0 %copy-start.2 = (f32[2,24,16,128]{3,2,1,0:T(8,128)}, f32[2,24,16,128]{3,2,1,0:T(8,128)S(1)}, u32[]{:S(2)}) copy-start(f32[2,24,16,128]{3,2,1,0:T(8,128)S(1)} %maximum_maximum_fusion.rest_0_) | copy-start | bytes 1179652
  2.1 14.3 %copy-start.1 = (f32[16,4,4096]{2,1,0:T(4,128)S(1)}, f32[16,4,4096]{2,1,0:T(4,128)}, u32[]{:S(2)}) copy-start(f32[16,4,4096]{2,1,0:T(4,128)} %refs_5_.1) | copy-start | bytes 3145732
  2.1 16.7 %collective-permute-start.1 = (f32[2,24,16,128]{3,2,1,0:T(8,128)S(1)}, f32[2,24,16,128]{3,2,1,0:T(8,128)}, u32[]{:S(2)}, u32[]{:S(2)}) collective-permute-start(f32[2,24,16,128]{3,2,1,0:T(8,128)S(1)} %maximum_maximum_fusion.rest_0_), channel_id=1, source_target_pairs={{0,8},{8,0},{16,24},{24,16},{1,9},{9,1},{17,25},{25,17},{2,10},{10... | collective-permute-start | bytes 1179656 | tf_op jit(solution)/shard_map/ppermute | solution.py:490
  2.6 12.4 %collective-permute-start.2 = (f32[2,24,16,128]{3,2,1,0:T(8,128)S(1)}, f32[2,24,16,128]{3,2,1,0:T(8,128)}, u32[]{:S(2)}, u32[]{:S(2)}) collective-permute-start(f32[2,24,16,128]{3,2,1,0:T(8,128)S(1)} %maximum_maximum_fusion.rest_0_), channel_id=1, source_target_pairs={{0,16},{8,24},{16,0},{24,8},{1,17},{9,25},{17,1},{25,9},{2,18},{10... | collective-permute-start | bytes 1179656 | tf_op jit(solution)/shard_map/ppermute | solution.py:490
  13.8 5.9 %collective-permute-start = (f32[2,23,16,128]{3,2,1,0:T(8,128)}, f32[2,23,16,128]{3,2,1,0:T(8,128)}, u32[]{:S(2)}, u32[]{:S(2)}) collective-permute-start(f32[2,23,16,128]{3,2,1,0:T(8,128)} %project.1.proj_ref), channel_id=1, source_target_pairs={{0,8},{8,0},{16,24},{24,16},{1,9},{9,1},{17,25},{25,17},{2,10},{10... | collective-permute-start | bytes 1130504 | tf_op jit(solution)/shard_map/ppermute | solution.py:490
  14.1 11.3 %collective-permute-start.4 = (f32[2,23,16,128]{3,2,1,0:T(8,128)}, f32[2,23,16,128]{3,2,1,0:T(8,128)}, u32[]{:S(2)}, u32[]{:S(2)}) collective-permute-start(f32[2,23,16,128]{3,2,1,0:T(8,128)} %project.1.proj_ref), channel_id=1, source_target_pairs={{0,16},{8,24},{16,0},{24,8},{1,17},{9,25},{17,1},{25,9},{2,18},{10... | collective-permute-start | bytes 1130504 | tf_op jit(solution)/shard_map/ppermute | solution.py:490
  15.0 3.8 %collective-permute-start.3 = (f32[2,24,16,128]{3,2,1,0:T(8,128)}, f32[2,24,16,128]{3,2,1,0:T(8,128)}, u32[]{:S(2)}, u32[]{:S(2)}) collective-permute-start(f32[2,24,16,128]{3,2,1,0:T(8,128)} %collective-permute-done.2.rest_2_), channel_id=1, source_target_pairs={{0,8},{8,0},{16,24},{24,16},{1,9},{9,1},{17,25},{25,17},{2,10},{10... | collective-permute-start | bytes 1179656 | tf_op jit(solution)/shard_map/ppermute | solution.py:490
  25.4 1.9 %collective-permute-start.5 = (f32[2,23,16,128]{3,2,1,0:T(8,128)}, f32[2,23,16,128]{3,2,1,0:T(8,128)S(1)}, u32[]{:S(2)}, u32[]{:S(2)}) collective-permute-start(f32[2,23,16,128]{3,2,1,0:T(8,128)} %collective-permute-done.4.refs_3_), channel_id=1, source_target_pairs={{0,8},{8,0},{16,24},{24,16},{1,9},{9,1},{17,25},{25,17},{2,10},{10... | collective-permute-start | bytes 1130504 | tf_op jit(solution)/shard_map/ppermute | solution.py:490
  30.4 7.4 %collective-permute-start.6 = (f32[2,3,16,128]{3,2,1,0:T(8,128)}, f32[2,3,16,128]{3,2,1,0:T(8,128)S(1)}, u32[]{:S(2)}, u32[]{:S(2)}) collective-permute-start(f32[2,3,16,128]{3,2,1,0:T(8,128)} %get-tuple-element.26), channel_id=1, source_target_pairs={{0,1},{1,0},{2,3},{3,2},{4,5},{5,4},{6,7},{7,6},{8,9},{9,8},{10,11... | collective-permute-start | bytes 147464 | tf_op jit(solution)/shard_map/ppermute | solution.py:490
  31.9 9.5 %collective-permute-start.7 = (f32[2,3,16,128]{3,2,1,0:T(8,128)}, f32[2,3,16,128]{3,2,1,0:T(8,128)S(1)}, u32[]{:S(2)}, u32[]{:S(2)}) collective-permute-start(f32[2,3,16,128]{3,2,1,0:T(8,128)} %get-tuple-element.27), channel_id=1, source_target_pairs={{0,2},{1,3},{2,0},{3,1},{4,6},{5,7},{6,4},{7,5},{8,10},{9,11},{10,... | collective-permute-start | bytes 147464 | tf_op jit(solution)/shard_map/ppermute | solution.py:490
  33.4 8.1 %collective-permute-start.8 = (f32[2,3,16,128]{3,2,1,0:T(8,128)}, f32[2,3,16,128]{3,2,1,0:T(8,128)S(1)}, u32[]{:S(2)}, u32[]{:S(2)}) collective-permute-start(f32[2,3,16,128]{3,2,1,0:T(8,128)} %get-tuple-element.28), channel_id=1, source_target_pairs={{0,3},{1,2},{2,1},{3,0},{4,7},{5,6},{6,5},{7,4},{8,11},{9,10},{10,... | collective-permute-start | bytes 147464 | tf_op jit(solution)/shard_map/ppermute | solution.py:490
  33.8 11.8 %collective-permute-start.9 = (f32[2,3,16,128]{3,2,1,0:T(8,128)}, f32[2,3,16,128]{3,2,1,0:T(8,128)S(1)}, u32[]{:S(2)}, u32[]{:S(2)}) collective-permute-start(f32[2,3,16,128]{3,2,1,0:T(8,128)} %get-tuple-element.29), channel_id=1, source_target_pairs={{0,4},{1,5},{2,6},{3,7},{4,0},{5,1},{6,2},{7,3},{8,12},{9,13},{10,... | collective-permute-start | bytes 147464 | tf_op jit(solution)/shard_map/ppermute | solution.py:490
  36.4 9.2 %collective-permute-start.10 = (f32[2,3,16,128]{3,2,1,0:T(8,128)}, f32[2,3,16,128]{3,2,1,0:T(8,128)S(1)}, u32[]{:S(2)}, u32[]{:S(2)}) collective-permute-start(f32[2,3,16,128]{3,2,1,0:T(8,128)} %get-tuple-element.30), channel_id=1, source_target_pairs={{0,5},{1,4},{2,7},{3,6},{4,1},{5,0},{6,3},{7,2},{8,13},{9,12},{10,... | collective-permute-start | bytes 147464 | tf_op jit(solution)/shard_map/ppermute | solution.py:490
  37.7 7.9 %collective-permute-start.11 = (f32[2,3,16,128]{3,2,1,0:T(8,128)}, f32[2,3,16,128]{3,2,1,0:T(8,128)S(1)}, u32[]{:S(2)}, u32[]{:S(2)}) collective-permute-start(f32[2,3,16,128]{3,2,1,0:T(8,128)} %get-tuple-element.31), channel_id=1, source_target_pairs={{0,6},{1,7},{2,4},{3,5},{4,2},{5,3},{6,0},{7,1},{8,14},{9,15},{10,... | collective-permute-start | bytes 147464 | tf_op jit(solution)/shard_map/ppermute | solution.py:490
  41.3 7.0 %collective-permute-start.12 = (f32[2,3,16,128]{3,2,1,0:T(8,128)}, f32[2,3,16,128]{3,2,1,0:T(8,128)S(1)}, u32[]{:S(2)}, u32[]{:S(2)}) collective-permute-start(f32[2,3,16,128]{3,2,1,0:T(8,128)} %get-tuple-element.32), channel_id=1, source_target_pairs={{0,7},{1,6},{2,5},{3,4},{4,3},{5,2},{6,1},{7,0},{8,15},{9,14},{10,... | collective-permute-start | bytes 147464 | tf_op jit(solution)/shard_map/ppermute | solution.py:490
  52.8 10.8 %collective-permute-start.14 = (f32[17,4,512]{2,1,0:T(4,128)}, f32[17,4,512]{2,1,0:T(4,128)S(1)}, u32[]{:S(2)}, u32[]{:S(2)}) collective-permute-start(f32[17,4,512]{2,1,0:T(4,128)} %gather_views.3.refs_0_.refs_6_), channel_id=1, source_target_pairs={{0,4},{1,5},{2,6},{3,7},{4,0},{5,1},{6,2},{7,3},{8,12},{9,13},{10,... | collective-permute-start | bytes 417800 | tf_op jit(solution)/shard_map/ppermute | solution.py:490
  53.3 11.5 %collective-permute-start.15 = (f32[17,4,512]{2,1,0:T(4,128)}, f32[17,4,512]{2,1,0:T(4,128)S(1)}, u32[]{:S(2)}, u32[]{:S(2)}) collective-permute-start(f32[17,4,512]{2,1,0:T(4,128)} %gather_views.3.refs_0_.refs_6_), channel_id=1, source_target_pairs={{0,6},{1,7},{2,4},{3,5},{4,2},{5,3},{6,0},{7,1},{8,14},{9,15},{10,... | collective-permute-start | bytes 417800 | tf_op jit(solution)/shard_map/ppermute | solution.py:490
  54.3 11.4 %collective-permute-start.13 = (f32[17,4,512]{2,1,0:T(4,128)}, f32[17,4,512]{2,1,0:T(4,128)S(1)}, u32[]{:S(2)}, u32[]{:S(2)}) collective-permute-start(f32[17,4,512]{2,1,0:T(4,128)} %gather_views.3.refs_0_.refs_6_), channel_id=1, source_target_pairs={{0,2},{1,3},{2,0},{3,1},{4,6},{5,7},{6,4},{7,5},{8,10},{9,11},{10,... | collective-permute-start | bytes 417800 | tf_op jit(solution)/shard_map/ppermute | solution.py:490
  56.3 9.4 %collective-permute-start.16 = (f32[17,4,512]{2,1,0:T(4,128)}, f32[17,4,512]{2,1,0:T(4,128)S(1)}, u32[]{:S(2)}, u32[]{:S(2)}) collective-permute-start(f32[17,4,512]{2,1,0:T(4,128)} %gather_views.3.refs_0_.refs_6_), channel_id=1, source_target_pairs={{0,1},{1,0},{2,3},{3,2},{4,5},{5,4},{6,7},{7,6},{8,9},{9,8},{10,11... | collective-permute-start | bytes 417800 | tf_op jit(solution)/shard_map/ppermute | solution.py:490
  56.8 10.4 %collective-permute-start.17 = (f32[17,4,512]{2,1,0:T(4,128)}, f32[17,4,512]{2,1,0:T(4,128)S(1)}, u32[]{:S(2)}, u32[]{:S(2)}) collective-permute-start(f32[17,4,512]{2,1,0:T(4,128)} %gather_views.3.refs_0_.refs_6_), channel_id=1, source_target_pairs={{0,3},{1,2},{2,1},{3,0},{4,7},{5,6},{6,5},{7,4},{8,11},{9,10},{10,... | collective-permute-start | bytes 417800 | tf_op jit(solution)/shard_map/ppermute | solution.py:490
  63.6 9.2 %copy-start.3 = (f32[17,4,512]{2,1,0:T(4,128)}, f32[17,4,512]{2,1,0:T(4,128)S(1)}, u32[]{:S(2)}) copy-start(f32[17,4,512]{2,1,0:T(4,128)S(1)} %collective-permute-done.14.refs_2_.refs_8_) | copy-start | bytes 417796
  63.6 6.6 %collective-permute-start.18 = (f32[17,4,512]{2,1,0:T(4,128)S(1)}, f32[17,4,512]{2,1,0:T(4,128)S(1)}, u32[]{:S(2)}, u32[]{:S(2)}) collective-permute-start(f32[17,4,512]{2,1,0:T(4,128)S(1)} %collective-permute-done.14.refs_2_.refs_8_), channel_id=1, source_target_pairs={{0,1},{1,0},{2,3},{3,2},{4,5},{5,4},{6,7},{7,6},{8,9},{9,8},{10,11... | collective-permute-start | bytes 417800 | tf_op jit(solution)/shard_map/ppermute | solution.py:490
  64.7 8.0 %copy-start.4 = (f32[17,4,512]{2,1,0:T(4,128)}, f32[17,4,512]{2,1,0:T(4,128)S(1)}, u32[]{:S(2)}) copy-start(f32[17,4,512]{2,1,0:T(4,128)S(1)} %collective-permute-done.15.refs_3_.refs_9_) | copy-start | bytes 417796
  64.8 8.0 %collective-permute-start.19 = (f32[17,4,512]{2,1,0:T(4,128)S(1)}, f32[17,4,512]{2,1,0:T(4,128)S(1)}, u32[]{:S(2)}, u32[]{:S(2)}) collective-permute-start(f32[17,4,512]{2,1,0:T(4,128)S(1)} %collective-permute-done.15.refs_3_.refs_9_), channel_id=1, source_target_pairs={{0,1},{1,0},{2,3},{3,2},{4,5},{5,4},{6,7},{7,6},{8,9},{9,8},{10,11... | collective-permute-start | bytes 417800 | tf_op jit(solution)/shard_map/ppermute | solution.py:490
  65.7 7.1 %copy-start.5 = (f32[17,4,512]{2,1,0:T(4,128)}, f32[17,4,512]{2,1,0:T(4,128)S(1)}, u32[]{:S(2)}) copy-start(f32[17,4,512]{2,1,0:T(4,128)S(1)} %collective-permute-done.13.refs_1_.refs_7_) | copy-start | bytes 417796
  65.7 7.1 %copy-start.6 = (f32[17,4,512]{2,1,0:T(4,128)}, f32[17,4,512]{2,1,0:T(4,128)S(1)}, u32[]{:S(2)}) copy-start(f32[17,4,512]{2,1,0:T(4,128)S(1)} %collective-permute-done.16.refs_4_.refs_10_) | copy-start | bytes 417796
  67.1 5.7 %copy-start.7 = (f32[17,4,512]{2,1,0:T(4,128)}, f32[17,4,512]{2,1,0:T(4,128)S(1)}, u32[]{:S(2)}) copy-start(f32[17,4,512]{2,1,0:T(4,128)S(1)} %collective-permute-done.17.refs_5_.refs_11_) | copy-start | bytes 417796
  74.7 1.9 %collective-permute-start.20 = (f32[1,128]{1,0:T(1,128)}, f32[1,128]{1,0:T(1,128)S(1)}, u32[]{:S(2)}, u32[]{:S(2)}) collective-permute-start(f32[1,128]{1,0:T(1,128)} %total.1.refs_1_), channel_id=1, source_target_pairs={{0,8},{8,0},{16,24},{24,16},{1,9},{9,1},{17,25},{25,17},{2,10},{10... | collective-permute-start | bytes 1544 | tf_op jit(solution)/shard_map/ppermute | solution.py:490
  74.8 3.6 %collective-permute-start.21 = (f32[1,128]{1,0:T(1,128)}, f32[1,128]{1,0:T(1,128)S(1)}, u32[]{:S(2)}, u32[]{:S(2)}) collective-permute-start(f32[1,128]{1,0:T(1,128)} %total.1.refs_1_), channel_id=1, source_target_pairs={{0,16},{8,24},{16,0},{24,8},{1,17},{9,25},{17,1},{25,9},{2,18},{10... | collective-permute-start | bytes 1544 | tf_op jit(solution)/shard_map/ppermute | solution.py:490
  75.3 3.2 %collective-permute-start.22 = (f32[1,128]{1,0:T(1,128)}, f32[1,128]{1,0:T(1,128)S(1)}, u32[]{:S(2)}, u32[]{:S(2)}) collective-permute-start(f32[1,128]{1,0:T(1,128)} %total.1.refs_1_), channel_id=1, source_target_pairs={{0,24},{8,16},{16,8},{24,0},{1,25},{9,17},{17,9},{25,1},{2,26},{10... | collective-permute-start | bytes 1544 | tf_op jit(solution)/shard_map/ppermute | solution.py:490
  (14 other events, 26.0 us)

commit v9 on v8

--- a/solution.py
+++ b/solution.py
@@ -466,22 +466,26 @@
     squares = sums[0][...] + sums[1][...] + (sums[2][...] + sums[3][...])
     rms = jnp.sqrt(squares / float(voxel_count) + epsilon)
     factor = jnp.max(jnp.minimum(1.0, step_limit / rms))
-    slices_n, _, per_n = pieces[0].shape
+    per_n = pieces[0].shape[2]
     part = ints_ref[1]
     for r in range(parts_n):
         cols = pl.ds(pl.multiple_of((part ^ SLOTS[r]) * per_n, per_n), per_n)
-        out_ref[:, :, cols] = vol_ref[:, :, cols] - factor * pieces[r][0 : slices_n - 1]
+        out_ref[:, :, cols] = vol_ref[:, :, cols] - factor * pieces[r][...]
 
 
 def finish(voxel_count, ints, sums, volume, pieces):
     parts_n = len(pieces)
-    vmem = pl.BlockSpec(memory_space=pltpu.VMEM)
-    smem = pl.BlockSpec(memory_space=pltpu.SMEM)
+    slices_n, rows_n, cols_n = volume.shape
+    step = slices_n // 4
+    line = pl.BlockSpec((1, LANES), lambda i: (0, 0))
+    wide = pl.BlockSpec((step, rows_n, cols_n), lambda i: (i, 0, 0))
+    piece = pl.BlockSpec((step, rows_n, cols_n // parts_n), lambda i: (i, 0, 0))
     return pl.pallas_call(
         lambda *refs: finish_kernel(parts_n, voxel_count, *refs),
+        grid=(slices_n // step,),
         out_shape=jax.ShapeDtypeStruct(volume.shape, volume.dtype),
-        in_specs=[smem] + [vmem] * (parts_n + 5),
-        out_specs=vmem,
+        in_specs=[pl.BlockSpec(memory_space=pltpu.SMEM)] + [line] * 4 + [wide] + [piece] * parts_n,
+        out_specs=wide,
         name="finish",
     )(ints, *sums, volume, *pieces)
 

time: 82.8 us -> 83.6 us (level)
  Pallas kernels: 24.3 us -> 25.2 us
    pallas_call x1, Pallas kernels: 2.88 us -> 3.75 us  [finish(): pl.pallas_call(lambda *refs: finish_kernel(parts_n, voxel_count, *refs),...]
where the time goes in v9:
time: 83.6 us; the launch traced here: 83.2 us
  Pallas kernels  25.2 us (30%)
  starting transfers between devices  23.6 us (28%)
  waiting for transfers between devices  21.9 us (26%)
  local copies, waits for them, and re-layouts  8.88 us (11%)
  other arithmetic  3.37 us (4%)
    ppermute x23, starting transfers between devices, swapped(): lax.ppermute(x, axis, [(i, i ^ bit) for i in range(lax.axis_size(axis))])  23.6 us
    ppermute x23, waiting for transfers between devices, swapped(): lax.ppermute(x, axis, [(i, i ^ bit) for i in range(lax.axis_size(axis))])  21.9 us
    pallas_call x1, Pallas kernels, project(): pl.pallas_call(body, out_shape=jax.ShapeDtypeStruct((views_n, blocks_n, s...  7.94 us
    pallas_call x2, Pallas kernels, gather_views(): pl.pallas_call(lambda *refs: gather_kernel(dims, parts_n, pieces_n, views...  7.28 us
    unnamed x48, local copies, waits for them, and re-layouts  5.86 us
    pallas_call x1, Pallas kernels, finish(): pl.pallas_call(lambda *refs: finish_kernel(parts_n, voxel_count, *refs),...  3.75 us
    pallas_call x1, Pallas kernels, near_residual(): pl.pallas_call(near_kernel, out_shape=jax.ShapeDtypeStruct(arrays[0].shap...  2.58 us
    pallas_call x1, Pallas kernels, residual_windows(): pl.pallas_call(body, out_shape=[jax.ShapeDtypeStruct((views_n, WINDOW, ba...  2.31 us
  transfers between devices with their start and end apart: 23, of which 11 were waited for; matrix products, arithmetic and copies ran while one was open for 8% of the time, Pallas kernels for 17%

profile of v9, /device:TPU:0, one launch (start us, length us, event | category | flops | bytes accessed | tf_op | source)
XLA Modules:
  0.0 83.2 jit_solution(17343427963134518844)
XLA Ops:
  0.0 0.8 constant_dynamic-slice_fusion.2
  0.8 1.2 %bitcast_bitcast_fusion = f32[2,23,16,128]{3,2,1,0:T(8,128)S(1)} fusion(f32[2,16,4096]{2,1,0:T(8,128)} %param.6), kind=kLoop, calls=%fused_computation.7 | loop fusion | bytes 753664 | tf_op jit(solution)/shard_map/transpose | solution.py:524
  2.6 2.6 %collective-permute-start.2 = (f32[2,24,16,128]{3,2,1,0:T(8,128)S(1)}, f32[2,24,16,128]{3,2,1,0:T(8,128)}, u32[]{:S(2)}, u32[]{:S(2)}) collective-permute-start(f32[2,24,16,128]{3,2,1,0:T(8,128)S(1)} %maximum_maximum_fusion.rest_0_), channel_id=1, source_target_pairs={{0,16},{8,24},{16,0},{24,8},{1,17},{9,25},{17,1},{25,9},{2,18},{10... | collective-permute-start | bytes 1179656 | tf_op jit(solution)/shard_map/ppermute | solution.py:494
  5.9 7.9 %project.1.proj_ref = f32[2,23,16,128]{3,2,1,0:T(8,128)} custom-call(f32[4]{0:T(128)} %pad_maximum_fusion.2.refs_0_.refs_1_, f32[16,4,4096]{2,1,0:T(4,128)} %refs_5_.1), custom_call_target="tpu_custom_call" | custom-call | tf_op jit(solution)/shard_map/project/pallas_call | solution.py:100
  17.0 1.6 %copy.15 = f32[16,4,512]{2,0,1:T(8,128)} copy(f32[16,4,512]{2,1,0:T(4,128)} %constant_dynamic-slice_fusion) | data formatting | bytes 262144
  18.8 0.8 fusion.24
  19.7 2.6 %near_residual.1.refs_2_ = f32[2,23,16,128]{3,2,1,0:T(8,128)} custom-call(s32[10]{0:T(128)} %pad_add_fusion.1.ints_ref.refs_0_, f32[2,23,16,128]{3,2,1,0:T(8,128)} %project.1.proj_ref, f32[2,23,16,128]{3,2,1,0:T(8,128)} %collective-permute-done.near_ref, f32[2,24,16,128]{3,2,1,0:T(8,128)} %copy-done.2, f32[2,24,16,128]{3,2,1,0:T(8,128)} %collective-permute-done.1.rest_1_, ...), custom_call_target="tpu_custom_call" | custom-call | tf_op jit(solution)/shard_map/near_residual/pallas_call | solution.py:297
  22.3 1.0 %fusion.7.refs_1_ = f32[4,16,512]{2,1,0:T(8,128)} fusion(s32[]{:T(128)S(6)} %select_n.99, f32[16,4,4096]{2,0,1:T(8,128)S(1)} %copy.9, s32[]{:T(128)S(6)} %add.69, f32[18,6,514]{2,0,1:T(8,128)S(1)} %select_maximum_fusion, f32[1,4,514]{2,0,1:T(1,128)S(1)} %pad.17, f32[16,4,514]{2,0,1:T(8,128)S(1)} %pad_dynamic-slice_fusion.3, s32[]{:T(128)S(6)} %add.68, ...), kind=kLoop, calls=%fused_computation.18 | loop fusion | flops 851968 | bytes 1589836 | tf_op jit(solution)/shard_map/transpose | solution.py:554
  23.4 2.0 %collective-permute-done.4.refs_3_ = f32[2,23,16,128]{3,2,1,0:T(8,128)} collective-permute-done((f32[2,23,16,128]{3,2,1,0:T(8,128)}, f32[2,23,16,128]{3,2,1,0:T(8,128)}, u32[]{:S(2)}, u32[]{:S(2)}) %collective-permute-start.4) | collective-permute-done | bytes 376864 | tf_op jit(solution)/shard_map/ppermute | solution.py:494
  25.4 1.9 %collective-permute-done.5.refs_4_ = f32[2,23,16,128]{3,2,1,0:T(8,128)S(1)} collective-permute-done((f32[2,23,16,128]{3,2,1,0:T(8,128)}, f32[2,23,16,128]{3,2,1,0:T(8,128)S(1)}, u32[]{:S(2)}, u32[]{:S(2)}) %collective-permute-start.5) | collective-permute-done | bytes 376864 | tf_op jit(solution)/shard_map/ppermute | solution.py:494
  28.0 2.3 %residual_windows.1 = (f32[2,3,16,128]{3,2,1,0:T(8,128)}, f32[2,3,16,128]{3,2,1,0:T(8,128)}, f32[2,3,16,128]{3,2,1,0:T(8,128)}, f32[2,3,16,128]{3,2,1,0:T(8,128)...) custom-call(s32[10]{0:T(128)} %pad_add_fusion.1.ints_ref.refs_0_, ...), custom_call_target="tpu_custom_call" | custom-call | tf_op jit(solution)/shard_map/residual_windows/pallas_call | solution.py:343
  30.3 1.5 %collective-permute-start.6 = (f32[2,3,16,128]{3,2,1,0:T(8,128)}, f32[2,3,16,128]{3,2,1,0:T(8,128)S(1)}, u32[]{:S(2)}, u32[]{:S(2)}) collective-permute-start(f32[2,3,16,128]{3,2,1,0:T(8,128)} %get-tuple-element.26), channel_id=1, source_target_pairs={{0,1},{1,0},{2,3},{3,2},{4,5},{5,4},{6,7},{7,6},{8,9},{9,8},{10,11... | collective-permute-start | bytes 147464 | tf_op jit(solution)/shard_map/ppermute | solution.py:494
  31.9 1.6 %collective-permute-start.7 = (f32[2,3,16,128]{3,2,1,0:T(8,128)}, f32[2,3,16,128]{3,2,1,0:T(8,128)S(1)}, u32[]{:S(2)}, u32[]{:S(2)}) collective-permute-start(f32[2,3,16,128]{3,2,1,0:T(8,128)} %get-tuple-element.27), channel_id=1, source_target_pairs={{0,2},{1,3},{2,0},{3,1},{4,6},{5,7},{6,4},{7,5},{8,10},{9,11},{10,... | collective-permute-start | bytes 147464 | tf_op jit(solution)/shard_map/ppermute | solution.py:494
  33.8 2.6 %collective-permute-start.9 = (f32[2,3,16,128]{3,2,1,0:T(8,128)}, f32[2,3,16,128]{3,2,1,0:T(8,128)S(1)}, u32[]{:S(2)}, u32[]{:S(2)}) collective-permute-start(f32[2,3,16,128]{3,2,1,0:T(8,128)} %get-tuple-element.29), channel_id=1, source_target_pairs={{0,4},{1,5},{2,6},{3,7},{4,0},{5,1},{6,2},{7,3},{8,12},{9,13},{10,... | collective-permute-start | bytes 147464 | tf_op jit(solution)/shard_map/ppermute | solution.py:494
  36.4 1.3 %collective-permute-start.10 = (f32[2,3,16,128]{3,2,1,0:T(8,128)}, f32[2,3,16,128]{3,2,1,0:T(8,128)S(1)}, u32[]{:S(2)}, u32[]{:S(2)}) collective-permute-start(f32[2,3,16,128]{3,2,1,0:T(8,128)} %get-tuple-element.30), channel_id=1, source_target_pairs={{0,5},{1,4},{2,7},{3,6},{4,1},{5,0},{6,3},{7,2},{8,13},{9,12},{10,... | collective-permute-start | bytes 147464 | tf_op jit(solution)/shard_map/ppermute | solution.py:494
  37.7 3.6 %collective-permute-start.11 = (f32[2,3,16,128]{3,2,1,0:T(8,128)}, f32[2,3,16,128]{3,2,1,0:T(8,128)S(1)}, u32[]{:S(2)}, u32[]{:S(2)}) collective-permute-start(f32[2,3,16,128]{3,2,1,0:T(8,128)} %get-tuple-element.31), channel_id=1, source_target_pairs={{0,6},{1,7},{2,4},{3,5},{4,2},{5,3},{6,0},{7,1},{8,14},{9,15},{10,... | collective-permute-start | bytes 147464 | tf_op jit(solution)/shard_map/ppermute | solution.py:494
  42.1 3.5 %gather_views.2.refs_3_ = f32[4,16,512]{2,1,0:T(8,128)} custom-call(s32[10]{0:T(128)} %pad_add_fusion.1.ints_ref.refs_0_, f32[2,3,16,128]{3,2,1,0:T(8,128)} %get-tuple-element.25.refs_1_, f32[2,3,16,128]{3,2,1,0:T(8,128)} %copy-done.13, f32[2,3,16,128]{3,2,1,0:T(8,128)} %copy-done.15, f32[2,3,16,128]{3,2,1,0:T(8,128)} %copy-done.16), custom_call_target="tpu_custom_call" | custom-call | tf_op jit(solution)/shard_map/gather_views/pallas_call | solution.py:433
  45.6 2.7 %collective-permute-done.12.refs_7_ = f32[2,3,16,128]{3,2,1,0:T(8,128)S(1)} collective-permute-done((f32[2,3,16,128]{3,2,1,0:T(8,128)}, f32[2,3,16,128]{3,2,1,0:T(8,128)S(1)}, u32[]{:S(2)}, u32[]{:S(2)}) %collective-permute-start.12) | collective-permute-done | bytes 49184 | tf_op jit(solution)/shard_map/ppermute | solution.py:494
  49.0 3.8 %gather_views.3.refs_0_.refs_6_ = f32[17,4,512]{2,1,0:T(4,128)} custom-call(s32[10]{0:T(128)} %pad_add_fusion.1.ints_ref.refs_0_, f32[4,16,512]{2,1,0:T(8,128)} %fusion.7.refs_1_, f32[4,16,512]{2,1,0:T(8,128)} %bitcast.16, f32[4,16,512]{2,1,0:T(8,128)} %gather_views.2.refs_3_, f32[2,3,16,128]{3,2,1,0:T(8,128)} %copy-done.11, f32[2,3,16,128]{3,2,1,0:T(8,128)} %copy-done.12, ...), custom_call_target="tpu_custom_call" | custom-call | tf_op jit(solution)/shard_map/gather_views/pallas_call | solution.py:433
  53.3 1.0 %collective-permute-start.15 = (f32[17,4,512]{2,1,0:T(4,128)}, f32[17,4,512]{2,1,0:T(4,128)S(1)}, u32[]{:S(2)}, u32[]{:S(2)}) collective-permute-start(f32[17,4,512]{2,1,0:T(4,128)} %gather_views.3.refs_0_.refs_6_), channel_id=1, source_target_pairs={{0,6},{1,7},{2,4},{3,5},{4,2},{5,3},{6,0},{7,1},{8,14},{9,15},{10,... | collective-permute-start | bytes 417800 | tf_op jit(solution)/shard_map/ppermute | solution.py:494
  54.3 2.0 %collective-permute-start.13 = (f32[17,4,512]{2,1,0:T(4,128)}, f32[17,4,512]{2,1,0:T(4,128)S(1)}, u32[]{:S(2)}, u32[]{:S(2)}) collective-permute-start(f32[17,4,512]{2,1,0:T(4,128)} %gather_views.3.refs_0_.refs_6_), channel_id=1, source_target_pairs={{0,2},{1,3},{2,0},{3,1},{4,6},{5,7},{6,4},{7,5},{8,10},{9,11},{10,... | collective-permute-start | bytes 417800 | tf_op jit(solution)/shard_map/ppermute | solution.py:494
  56.8 1.0 %collective-permute-start.17 = (f32[17,4,512]{2,1,0:T(4,128)}, f32[17,4,512]{2,1,0:T(4,128)S(1)}, u32[]{:S(2)}, u32[]{:S(2)}) collective-permute-start(f32[17,4,512]{2,1,0:T(4,128)} %gather_views.3.refs_0_.refs_6_), channel_id=1, source_target_pairs={{0,3},{1,2},{2,1},{3,0},{4,7},{5,6},{6,5},{7,4},{8,11},{9,10},{10,... | collective-permute-start | bytes 417800 | tf_op jit(solution)/shard_map/ppermute | solution.py:494
  57.8 5.8 %collective-permute-done.14.refs_2_.refs_8_ = f32[17,4,512]{2,1,0:T(4,128)S(1)} collective-permute-done((f32[17,4,512]{2,1,0:T(4,128)}, f32[17,4,512]{2,1,0:T(4,128)S(1)}, u32[]{:S(2)}, u32[]{:S(2)}) %collective-permute-start.14) | collective-permute-done | bytes 139296 | tf_op jit(solution)/shard_map/ppermute | solution.py:494
  63.6 1.2 %collective-permute-start.18 = (f32[17,4,512]{2,1,0:T(4,128)S(1)}, f32[17,4,512]{2,1,0:T(4,128)S(1)}, u32[]{:S(2)}, u32[]{:S(2)}) collective-permute-start(f32[17,4,512]{2,1,0:T(4,128)S(1)} %collective-permute-done.14.refs_2_.refs_8_), channel_id=1, source_target_pairs={{0,1},{1,0},{2,3},{3,2},{4,5},{5,4},{6,7},{7,6},{8,9},{9,8},{10,11... | collective-permute-start | bytes 417800 | tf_op jit(solution)/shard_map/ppermute | solution.py:494
  64.8 0.8 %collective-permute-start.19 = (f32[17,4,512]{2,1,0:T(4,128)S(1)}, f32[17,4,512]{2,1,0:T(4,128)S(1)}, u32[]{:S(2)}, u32[]{:S(2)}) collective-permute-start(f32[17,4,512]{2,1,0:T(4,128)S(1)} %collective-permute-done.15.refs_3_.refs_9_), channel_id=1, source_target_pairs={{0,1},{1,0},{2,3},{3,2},{4,5},{5,4},{6,7},{7,6},{8,9},{9,8},{10,11... | collective-permute-start | bytes 417800 | tf_op jit(solution)/shard_map/ppermute | solution.py:494
  65.7 1.5 %collective-permute-done.17.refs_5_.refs_11_ = f32[17,4,512]{2,1,0:T(4,128)S(1)} collective-permute-done((f32[17,4,512]{2,1,0:T(4,128)}, f32[17,4,512]{2,1,0:T(4,128)S(1)}, u32[]{:S(2)}, u32[]{:S(2)}) %collective-permute-start.17) | collective-permute-done | bytes 139296 | tf_op jit(solution)/shard_map/ppermute | solution.py:494
  67.1 3.0 %collective-permute-done.18.refs_6_.refs_12_ = f32[17,4,512]{2,1,0:T(4,128)S(1)} collective-permute-done((f32[17,4,512]{2,1,0:T(4,128)S(1)}, f32[17,4,512]{2,1,0:T(4,128)S(1)}, u32[]{:S(2)}, u32[]{:S(2)}) %collective-permute-start.18) | collective-permute-done | bytes 139296 | tf_op jit(solution)/shard_map/ppermute | solution.py:494
  70.1 2.6 %collective-permute-done.19.refs_7_.refs_13_ = f32[17,4,512]{2,1,0:T(4,128)S(1)} collective-permute-done((f32[17,4,512]{2,1,0:T(4,128)S(1)}, f32[17,4,512]{2,1,0:T(4,128)S(1)}, u32[]{:S(2)}, u32[]{:S(2)}) %collective-permute-start.19) | collective-permute-done | bytes 139296 | tf_op jit(solution)/shard_map/ppermute | solution.py:494
  73.4 1.3 %total.1.refs_1_ = f32[1,128]{1,0:T(1,128)} custom-call(f32[17,4,512]{2,1,0:T(4,128)} %gather_views.3.refs_0_.refs_6_, f32[17,4,512]{2,1,0:T(4,128)} %copy-done.5, f32[17,4,512]{2,1,0:T(4,128)} %copy-done.3, f32[17,4,512]{2,1,0:T(4,128)} %copy-done.4, f32[17,4,512]{2,1,0:T(4,128)} %copy-done.6, f32[17,4,512]{2,1,0:T(4,128)} %copy-done.7, ...), custom_call_target="tpu_custom_call" | custom-call | tf_op jit(solution)/shard_map/total/pallas_call | solution.py:453
  75.3 1.3 %collective-permute-start.22 = (f32[1,128]{1,0:T(1,128)}, f32[1,128]{1,0:T(1,128)S(1)}, u32[]{:S(2)}, u32[]{:S(2)}) collective-permute-start(f32[1,128]{1,0:T(1,128)} %total.1.refs_1_), channel_id=1, source_target_pairs={{0,24},{8,16},{16,8},{24,0},{1,25},{9,17},{17,9},{25,1},{2,26},{10... | collective-permute-start | bytes 1544 | tf_op jit(solution)/shard_map/ppermute | solution.py:494
  76.6 1.7 %collective-permute-done.21.refs_3_ = f32[1,128]{1,0:T(1,128)S(1)} collective-permute-done((f32[1,128]{1,0:T(1,128)}, f32[1,128]{1,0:T(1,128)S(1)}, u32[]{:S(2)}, u32[]{:S(2)}) %collective-permute-start.21) | collective-permute-done | bytes 544 | tf_op jit(solution)/shard_map/ppermute | solution.py:494
  79.4 3.8 %finish.1 = f32[16,4,4096]{2,1,0:T(4,128)} custom-call(s32[10]{0:T(128)} %pad_add_fusion.1.ints_ref.refs_0_, f32[1,128]{1,0:T(1,128)} %total.1.refs_1_, f32[1,128]{1,0:T(1,128)} %copy-done.19, f32[1,128]{1,0:T(1,128)} %copy-done.20, f32[1,128]{1,0:T(1,128)} %copy-done.21, f32[16,4,4096]{2,1,0:T(4,128)} %refs_5_.1, ...), custom_call_target="tpu_custom_call" | custom-call | tf_op jit(solution)/shard_map/finish/pallas_call | solution.py:483
  (88 shorter events, 10.8 us)
Async XLA Ops:
  0.0 15.1 %copy-start = (f32[16,4,4096]{2,1,0:T(4,128)S(1)}, f32[16,4,4096]{2,1,0:T(4,128)}, u32[]{:S(2)}) copy-start(f32[16,4,4096]{2,1,0:T(4,128)} %param.7) | copy-start | bytes 3145732
  2.0 12.3 %copy-start.18 = (s32[2,4]{1,0:T(2,128)S(1)}, s32[2,4]{1,0:T(2,128)}, u32[]{:S(2)}) copy-start(s32[2,4]{1,0:T(2,128)} %param.9) | copy-start | bytes 100
  2.0 15.0 %copy-start.2 = (f32[2,24,16,128]{3,2,1,0:T(8,128)}, f32[2,24,16,128]{3,2,1,0:T(8,128)S(1)}, u32[]{:S(2)}) copy-start(f32[2,24,16,128]{3,2,1,0:T(8,128)S(1)} %maximum_maximum_fusion.rest_0_) | copy-start | bytes 1179652
  2.1 14.3 %copy-start.1 = (f32[16,4,4096]{2,1,0:T(4,128)S(1)}, f32[16,4,4096]{2,1,0:T(4,128)}, u32[]{:S(2)}) copy-start(f32[16,4,4096]{2,1,0:T(4,128)} %refs_5_.1) | copy-start | bytes 3145732
  2.1 16.7 %collective-permute-start.1 = (f32[2,24,16,128]{3,2,1,0:T(8,128)S(1)}, f32[2,24,16,128]{3,2,1,0:T(8,128)}, u32[]{:S(2)}, u32[]{:S(2)}) collective-permute-start(f32[2,24,16,128]{3,2,1,0:T(8,128)S(1)} %maximum_maximum_fusion.rest_0_), channel_id=1, source_target_pairs={{0,8},{8,0},{16,24},{24,16},{1,9},{9,1},{17,25},{25,17},{2,10},{10... | collective-permute-start | bytes 1179656 | tf_op jit(solution)/shard_map/ppermute | solution.py:494
  2.6 12.4 %collective-permute-start.2 = (f32[2,24,16,128]{3,2,1,0:T(8,128)S(1)}, f32[2,24,16,128]{3,2,1,0:T(8,128)}, u32[]{:S(2)}, u32[]{:S(2)}) collective-permute-start(f32[2,24,16,128]{3,2,1,0:T(8,128)S(1)} %maximum_maximum_fusion.rest_0_), channel_id=1, source_target_pairs={{0,16},{8,24},{16,0},{24,8},{1,17},{9,25},{17,1},{25,9},{2,18},{10... | collective-permute-start | bytes 1179656 | tf_op jit(solution)/shard_map/ppermute | solution.py:494
  13.8 5.9 %collective-permute-start = (f32[2,23,16,128]{3,2,1,0:T(8,128)}, f32[2,23,16,128]{3,2,1,0:T(8,128)}, u32[]{:S(2)}, u32[]{:S(2)}) collective-permute-start(f32[2,23,16,128]{3,2,1,0:T(8,128)} %project.1.proj_ref), channel_id=1, source_target_pairs={{0,8},{8,0},{16,24},{24,16},{1,9},{9,1},{17,25},{25,17},{2,10},{10... | collective-permute-start | bytes 1130504 | tf_op jit(solution)/shard_map/ppermute | solution.py:494
  14.1 11.3 %collective-permute-start.4 = (f32[2,23,16,128]{3,2,1,0:T(8,128)}, f32[2,23,16,128]{3,2,1,0:T(8,128)}, u32[]{:S(2)}, u32[]{:S(2)}) collective-permute-start(f32[2,23,16,128]{3,2,1,0:T(8,128)} %project.1.proj_ref), channel_id=1, source_target_pairs={{0,16},{8,24},{16,0},{24,8},{1,17},{9,25},{17,1},{25,9},{2,18},{10... | collective-permute-start | bytes 1130504 | tf_op jit(solution)/shard_map/ppermute | solution.py:494
  15.0 3.8 %collective-permute-start.3 = (f32[2,24,16,128]{3,2,1,0:T(8,128)}, f32[2,24,16,128]{3,2,1,0:T(8,128)}, u32[]{:S(2)}, u32[]{:S(2)}) collective-permute-start(f32[2,24,16,128]{3,2,1,0:T(8,128)} %collective-permute-done.2.rest_2_), channel_id=1, source_target_pairs={{0,8},{8,0},{16,24},{24,16},{1,9},{9,1},{17,25},{25,17},{2,10},{10... | collective-permute-start | bytes 1179656 | tf_op jit(solution)/shard_map/ppermute | solution.py:494
  25.4 1.9 %collective-permute-start.5 = (f32[2,23,16,128]{3,2,1,0:T(8,128)}, f32[2,23,16,128]{3,2,1,0:T(8,128)S(1)}, u32[]{:S(2)}, u32[]{:S(2)}) collective-permute-start(f32[2,23,16,128]{3,2,1,0:T(8,128)} %collective-permute-done.4.refs_3_), channel_id=1, source_target_pairs={{0,8},{8,0},{16,24},{24,16},{1,9},{9,1},{17,25},{25,17},{2,10},{10... | collective-permute-start | bytes 1130504 | tf_op jit(solution)/shard_map/ppermute | solution.py:494
  30.3 7.4 %collective-permute-start.6 = (f32[2,3,16,128]{3,2,1,0:T(8,128)}, f32[2,3,16,128]{3,2,1,0:T(8,128)S(1)}, u32[]{:S(2)}, u32[]{:S(2)}) collective-permute-start(f32[2,3,16,128]{3,2,1,0:T(8,128)} %get-tuple-element.26), channel_id=1, source_target_pairs={{0,1},{1,0},{2,3},{3,2},{4,5},{5,4},{6,7},{7,6},{8,9},{9,8},{10,11... | collective-permute-start | bytes 147464 | tf_op jit(solution)/shard_map/ppermute | solution.py:494
  31.9 9.5 %collective-permute-start.7 = (f32[2,3,16,128]{3,2,1,0:T(8,128)}, f32[2,3,16,128]{3,2,1,0:T(8,128)S(1)}, u32[]{:S(2)}, u32[]{:S(2)}) collective-permute-start(f32[2,3,16,128]{3,2,1,0:T(8,128)} %get-tuple-element.27), channel_id=1, source_target_pairs={{0,2},{1,3},{2,0},{3,1},{4,6},{5,7},{6,4},{7,5},{8,10},{9,11},{10,... | collective-permute-start | bytes 147464 | tf_op jit(solution)/shard_map/ppermute | solution.py:494
  33.4 8.1 %collective-permute-start.8 = (f32[2,3,16,128]{3,2,1,0:T(8,128)}, f32[2,3,16,128]{3,2,1,0:T(8,128)S(1)}, u32[]{:S(2)}, u32[]{:S(2)}) collective-permute-start(f32[2,3,16,128]{3,2,1,0:T(8,128)} %get-tuple-element.28), channel_id=1, source_target_pairs={{0,3},{1,2},{2,1},{3,0},{4,7},{5,6},{6,5},{7,4},{8,11},{9,10},{10,... | collective-permute-start | bytes 147464 | tf_op jit(solution)/shard_map/ppermute | solution.py:494
  33.8 11.8 %collective-permute-start.9 = (f32[2,3,16,128]{3,2,1,0:T(8,128)}, f32[2,3,16,128]{3,2,1,0:T(8,128)S(1)}, u32[]{:S(2)}, u32[]{:S(2)}) collective-permute-start(f32[2,3,16,128]{3,2,1,0:T(8,128)} %get-tuple-element.29), channel_id=1, source_target_pairs={{0,4},{1,5},{2,6},{3,7},{4,0},{5,1},{6,2},{7,3},{8,12},{9,13},{10,... | collective-permute-start | bytes 147464 | tf_op jit(solution)/shard_map/ppermute | solution.py:494
  36.4 9.2 %collective-permute-start.10 = (f32[2,3,16,128]{3,2,1,0:T(8,128)}, f32[2,3,16,128]{3,2,1,0:T(8,128)S(1)}, u32[]{:S(2)}, u32[]{:S(2)}) collective-permute-start(f32[2,3,16,128]{3,2,1,0:T(8,128)} %get-tuple-element.30), channel_id=1, source_target_pairs={{0,5},{1,4},{2,7},{3,6},{4,1},{5,0},{6,3},{7,2},{8,13},{9,12},{10,... | collective-permute-start | bytes 147464 | tf_op jit(solution)/shard_map/ppermute | solution.py:494
  37.7 7.9 %collective-permute-start.11 = (f32[2,3,16,128]{3,2,1,0:T(8,128)}, f32[2,3,16,128]{3,2,1,0:T(8,128)S(1)}, u32[]{:S(2)}, u32[]{:S(2)}) collective-permute-start(f32[2,3,16,128]{3,2,1,0:T(8,128)} %get-tuple-element.31), channel_id=1, source_target_pairs={{0,6},{1,7},{2,4},{3,5},{4,2},{5,3},{6,0},{7,1},{8,14},{9,15},{10,... | collective-permute-start | bytes 147464 | tf_op jit(solution)/shard_map/ppermute | solution.py:494
  41.3 7.0 %collective-permute-start.12 = (f32[2,3,16,128]{3,2,1,0:T(8,128)}, f32[2,3,16,128]{3,2,1,0:T(8,128)S(1)}, u32[]{:S(2)}, u32[]{:S(2)}) collective-permute-start(f32[2,3,16,128]{3,2,1,0:T(8,128)} %get-tuple-element.32), channel_id=1, source_target_pairs={{0,7},{1,6},{2,5},{3,4},{4,3},{5,2},{6,1},{7,0},{8,15},{9,14},{10,... | collective-permute-start | bytes 147464 | tf_op jit(solution)/shard_map/ppermute | solution.py:494
  52.8 10.8 %collective-permute-start.14 = (f32[17,4,512]{2,1,0:T(4,128)}, f32[17,4,512]{2,1,0:T(4,128)S(1)}, u32[]{:S(2)}, u32[]{:S(2)}) collective-permute-start(f32[17,4,512]{2,1,0:T(4,128)} %gather_views.3.refs_0_.refs_6_), channel_id=1, source_target_pairs={{0,4},{1,5},{2,6},{3,7},{4,0},{5,1},{6,2},{7,3},{8,12},{9,13},{10,... | collective-permute-start | bytes 417800 | tf_op jit(solution)/shard_map/ppermute | solution.py:494
  53.3 11.5 %collective-permute-start.15 = (f32[17,4,512]{2,1,0:T(4,128)}, f32[17,4,512]{2,1,0:T(4,128)S(1)}, u32[]{:S(2)}, u32[]{:S(2)}) collective-permute-start(f32[17,4,512]{2,1,0:T(4,128)} %gather_views.3.refs_0_.refs_6_), channel_id=1, source_target_pairs={{0,6},{1,7},{2,4},{3,5},{4,2},{5,3},{6,0},{7,1},{8,14},{9,15},{10,... | collective-permute-start | bytes 417800 | tf_op jit(solution)/shard_map/ppermute | solution.py:494
  54.3 11.4 %collective-permute-start.13 = (f32[17,4,512]{2,1,0:T(4,128)}, f32[17,4,512]{2,1,0:T(4,128)S(1)}, u32[]{:S(2)}, u32[]{:S(2)}) collective-permute-start(f32[17,4,512]{2,1,0:T(4,128)} %gather_views.3.refs_0_.refs_6_), channel_id=1, source_target_pairs={{0,2},{1,3},{2,0},{3,1},{4,6},{5,7},{6,4},{7,5},{8,10},{9,11},{10,... | collective-permute-start | bytes 417800 | tf_op jit(solution)/shard_map/ppermute | solution.py:494
  56.3 9.4 %collective-permute-start.16 = (f32[17,4,512]{2,1,0:T(4,128)}, f32[17,4,512]{2,1,0:T(4,128)S(1)}, u32[]{:S(2)}, u32[]{:S(2)}) collective-permute-start(f32[17,4,512]{2,1,0:T(4,128)} %gather_views.3.refs_0_.refs_6_), channel_id=1, source_target_pairs={{0,1},{1,0},{2,3},{3,2},{4,5},{5,4},{6,7},{7,6},{8,9},{9,8},{10,11... | collective-permute-start | bytes 417800 | tf_op jit(solution)/shard_map/ppermute | solution.py:494
  56.8 10.4 %collective-permute-start.17 = (f32[17,4,512]{2,1,0:T(4,128)}, f32[17,4,512]{2,1,0:T(4,128)S(1)}, u32[]{:S(2)}, u32[]{:S(2)}) collective-permute-start(f32[17,4,512]{2,1,0:T(4,128)} %gather_views.3.refs_0_.refs_6_), channel_id=1, source_target_pairs={{0,3},{1,2},{2,1},{3,0},{4,7},{5,6},{6,5},{7,4},{8,11},{9,10},{10,... | collective-permute-start | bytes 417800 | tf_op jit(solution)/shard_map/ppermute | solution.py:494
  63.6 9.2 %copy-start.3 = (f32[17,4,512]{2,1,0:T(4,128)}, f32[17,4,512]{2,1,0:T(4,128)S(1)}, u32[]{:S(2)}) copy-start(f32[17,4,512]{2,1,0:T(4,128)S(1)} %collective-permute-done.14.refs_2_.refs_8_) | copy-start | bytes 417796
  63.6 6.5 %collective-permute-start.18 = (f32[17,4,512]{2,1,0:T(4,128)S(1)}, f32[17,4,512]{2,1,0:T(4,128)S(1)}, u32[]{:S(2)}, u32[]{:S(2)}) collective-permute-start(f32[17,4,512]{2,1,0:T(4,128)S(1)} %collective-permute-done.14.refs_2_.refs_8_), channel_id=1, source_target_pairs={{0,1},{1,0},{2,3},{3,2},{4,5},{5,4},{6,7},{7,6},{8,9},{9,8},{10,11... | collective-permute-start | bytes 417800 | tf_op jit(solution)/shard_map/ppermute | solution.py:494
  64.7 8.0 %copy-start.4 = (f32[17,4,512]{2,1,0:T(4,128)}, f32[17,4,512]{2,1,0:T(4,128)S(1)}, u32[]{:S(2)}) copy-start(f32[17,4,512]{2,1,0:T(4,128)S(1)} %collective-permute-done.15.refs_3_.refs_9_) | copy-start | bytes 417796
  64.8 8.0 %collective-permute-start.19 = (f32[17,4,512]{2,1,0:T(4,128)S(1)}, f32[17,4,512]{2,1,0:T(4,128)S(1)}, u32[]{:S(2)}, u32[]{:S(2)}) collective-permute-start(f32[17,4,512]{2,1,0:T(4,128)S(1)} %collective-permute-done.15.refs_3_.refs_9_), channel_id=1, source_target_pairs={{0,1},{1,0},{2,3},{3,2},{4,5},{5,4},{6,7},{7,6},{8,9},{9,8},{10,11... | collective-permute-start | bytes 417800 | tf_op jit(solution)/shard_map/ppermute | solution.py:494
  65.7 7.1 %copy-start.5 = (f32[17,4,512]{2,1,0:T(4,128)}, f32[17,4,512]{2,1,0:T(4,128)S(1)}, u32[]{:S(2)}) copy-start(f32[17,4,512]{2,1,0:T(4,128)S(1)} %collective-permute-done.13.refs_1_.refs_7_) | copy-start | bytes 417796
  65.7 7.1 %copy-start.6 = (f32[17,4,512]{2,1,0:T(4,128)}, f32[17,4,512]{2,1,0:T(4,128)S(1)}, u32[]{:S(2)}) copy-start(f32[17,4,512]{2,1,0:T(4,128)S(1)} %collective-permute-done.16.refs_4_.refs_10_) | copy-start | bytes 417796
  67.1 5.6 %copy-start.7 = (f32[17,4,512]{2,1,0:T(4,128)}, f32[17,4,512]{2,1,0:T(4,128)S(1)}, u32[]{:S(2)}) copy-start(f32[17,4,512]{2,1,0:T(4,128)S(1)} %collective-permute-done.17.refs_5_.refs_11_) | copy-start | bytes 417796
  74.7 1.9 %collective-permute-start.20 = (f32[1,128]{1,0:T(1,128)}, f32[1,128]{1,0:T(1,128)S(1)}, u32[]{:S(2)}, u32[]{:S(2)}) collective-permute-start(f32[1,128]{1,0:T(1,128)} %total.1.refs_1_), channel_id=1, source_target_pairs={{0,8},{8,0},{16,24},{24,16},{1,9},{9,1},{17,25},{25,17},{2,10},{10... | collective-permute-start | bytes 1544 | tf_op jit(solution)/shard_map/ppermute | solution.py:494
  74.7 3.6 %collective-permute-start.21 = (f32[1,128]{1,0:T(1,128)}, f32[1,128]{1,0:T(1,128)S(1)}, u32[]{:S(2)}, u32[]{:S(2)}) collective-permute-start(f32[1,128]{1,0:T(1,128)} %total.1.refs_1_), channel_id=1, source_target_pairs={{0,16},{8,24},{16,0},{24,8},{1,17},{9,25},{17,1},{25,9},{2,18},{10... | collective-permute-start | bytes 1544 | tf_op jit(solution)/shard_map/ppermute | solution.py:494
  75.3 3.2 %collective-permute-start.22 = (f32[1,128]{1,0:T(1,128)}, f32[1,128]{1,0:T(1,128)S(1)}, u32[]{:S(2)}, u32[]{:S(2)}) collective-permute-start(f32[1,128]{1,0:T(1,128)} %total.1.refs_1_), channel_id=1, source_target_pairs={{0,24},{8,16},{16,8},{24,0},{1,25},{9,17},{17,9},{25,1},{2,26},{10... | collective-permute-start | bytes 1544 | tf_op jit(solution)/shard_map/ppermute | solution.py:494
  (14 other events, 26.0 us)
